TPU v7x, 32 devices: a whole 2x2x4 slice. The times are simulated.
32 devices in a mesh: dom: 4 (over y, x), edge: 8 (over z, core).
Axes of the slice: x: 2, y: 2, z: 4, core: 2. Of those that a mesh axis runs over, the one named last changes fastest.
Arguments:
- src_table: float32 [400, 16384], P(None, ('dom', 'edge')), may hold values from -2.5 to 2.5
- src_state: float32 [16384], P(('dom', 'edge')), may hold values from 0.001 to 1
- dst_table: float32 [400, 16384], P(None, ('dom', 'edge')), may hold values from -2.5 to 2.5
- dst_state: float32 [16384], P(('dom', 'edge')), may hold values from 0.001 to 1
- relation: float32 [400, 16], replicated, may hold values from -4 to 4
- edge_src: int32 [131072], P(('dom', 'edge')), may hold values from 0 to 511
- edge_dst: int32 [131072], P(('dom', 'edge')), may hold values from 0 to 511
- edge_rel: int32 [131072], P(('dom', 'edge')), may hold values from 0 to 15
- matching: int32 [4], replicated, may hold values from 0 to 3, as said below
- neg_rows: int32 [32, 8, 256], P(('dom', 'edge')), may hold values from 0 to 511
- quotas: int32 [32, 8], P(('dom', 'edge')), may hold values from 0 to 2, as said below
Outputs:
- src_out: float32 [400, 16384], P(None, ('dom', 'edge'))
- src_state_out: float32 [16384], P(('dom', 'edge'))
- dst_out: float32 [400, 16384], P(None, ('dom', 'edge'))
- dst_state_out: float32 [16384], P(('dom', 'edge'))
- relation_out: float32 [400, 16], replicated
Inputs may be any that keep to these rules, and one draw needn't show every extreme that they name: matching names every partition exactly once. `quotas`: each device's 8 entries sum to exactly 12; for each index of dom, one index of edge is given 2 blocks by every device of that index of dom.
All inputs are finite; a program needn't handle non-finite values.
Results may differ from a plain program's by a relative error of at most 0.0011.
Values may be sent and summed in bfloat16 or wider, within the bound.
No kernel may reach another device: no remote copies, remote signals or barrier semaphores. Data moves between devices by JAX's collectives and lax.ppermute only.
A program may use at most 128 MiB of HBM per device.

v0:
```python
import math

import jax
import jax.numpy as jnp
from jax import lax
from jax.sharding import PartitionSpec as P

DIM = 400
NREL = 16
BLOCK = 128
QMAX = 2
QTOTAL = 12
NNEG = 1536
SLOTS = 256


learn_rate = 0.1
rel_rate = 0.02


def complex_product(one_side, other_side):
    half_dim = one_side.shape[0] // 2
    real_part = (
        one_side[:half_dim] * other_side[:half_dim] - one_side[half_dim:] * other_side[half_dim:]
    )
    imag_part = (
        one_side[:half_dim] * other_side[half_dim:] + one_side[half_dim:] * other_side[:half_dim]
    )
    return jnp.concatenate([real_part, imag_part], axis=0)


def conj_product(gradient, operand):
    half_dim = gradient.shape[0] // 2
    real_part = gradient[:half_dim] * operand[:half_dim] + gradient[half_dim:] * operand[half_dim:]
    imag_part = gradient[half_dim:] * operand[:half_dim] - gradient[:half_dim] * operand[half_dim:]
    return jnp.concatenate([real_part, imag_part], axis=0)


def block_plan(quota_row, edge_count):
    block_ends = jnp.cumsum(quota_row)
    starts = block_ends - quota_row
    positions = jnp.arange(QTOTAL, dtype=jnp.int32)
    owner_of = jnp.sum((block_ends[None, :] <= positions[:, None]).astype(jnp.int32), axis=1)
    matches = owner_of[:, None] == jnp.arange(edge_count, dtype=jnp.int32)[None, :]
    first_block = jnp.sum(jnp.where(matches, starts[None, :], 0), axis=1)
    return (owner_of, owner_of * QMAX + positions - first_block)


def adagrad(table_in, state_in, gradient):
    new_state = state_in + jnp.mean(gradient * gradient, axis=-2)
    return (table_in - learn_rate * gradient / jnp.sqrt(new_state)[..., None, :], new_state)


def shards(
    src_table,
    src_state,
    dst_table,
    dst_state,
    relation,
    edge_src,
    edge_dst,
    edge_rel,
    matching,
    neg_rows,
    quotas,
):
    edge_count = lax.axis_size("edge")
    row_count = src_table.shape[1]
    held_state = dst_state.reshape(1, row_count)
    partner = lax.dynamic_index_in_dim(matching, lax.axis_index("dom"), 0, False)
    pieces = (
        lax.all_gather(dst_table, "dom", axis=1, tiled=True),
        lax.all_gather(held_state, "dom", axis=1, tiled=True),
    )
    piece_cols = pieces[0].shape[1]
    offset = partner * row_count
    inside = jnp.logical_and(offset >= 0, offset < piece_cols)
    anchor = jnp.clip(offset, 0, piece_cols - row_count)
    table_part = lax.dynamic_slice_in_dim(pieces[0], anchor, row_count, 1)
    state_part = lax.dynamic_slice_in_dim(pieces[1], anchor, row_count, 1)
    part_table = jnp.where(inside, table_part, jnp.zeros_like(dst_table))
    part_state = jnp.where(inside, state_part, jnp.zeros_like(held_state))
    own_requests = neg_rows.reshape(edge_count, SLOTS)
    requested = lax.all_to_all(own_requests, "edge", split_axis=0, concat_axis=0, tiled=True)
    served = part_table.astype(jnp.bfloat16)[:, requested]
    fetched = lax.all_to_all(served, "edge", split_axis=1, concat_axis=1, tiled=True)
    owner_of, block_at = block_plan(quotas.reshape(edge_count), edge_count)
    negatives = fetched.reshape(DIM, edge_count * QMAX, BLOCK)[:, block_at].reshape(DIM, NNEG)
    weight = 1.0 / math.sqrt(NNEG)
    labels = jnp.arange(NREL, dtype=jnp.int32)
    edge_total = edge_src.shape[0]
    edge_rows = min(edge_total, 512)
    groups = edge_total // edge_rows
    edge_sets = (
        edge_src.reshape(groups, edge_rows),
        edge_dst.reshape(groups, edge_rows),
        edge_rel.reshape(groups, edge_rows),
    )

    def edge_block(totals, pieces):
        src_grad, dst_grad, neg_grad, rel_grad = totals
        src_ids, dst_ids, rel_ids = pieces
        onehot = (rel_ids[None, :] == labels[:, None]).astype(jnp.float32)
        rel_edges = jnp.dot(relation, onehot, precision=lax.Precision.HIGHEST)
        src_rows = src_table[:, src_ids]
        dst_rows = part_table[:, dst_ids]
        queries = complex_product(src_rows, rel_edges)
        positive = jnp.sum(queries * dst_rows, axis=0)
        pos_coef = -jax.nn.sigmoid(-positive)
        query_b = queries.astype(jnp.bfloat16)
        scores = lax.dot_general(
            query_b, negatives, (((0,), (0,)), ((), ())), preferred_element_type=jnp.float32
        )
        neg_coef = (weight * jax.nn.sigmoid(scores)).astype(jnp.bfloat16)
        neg_grad = neg_grad + jnp.dot(query_b, neg_coef, preferred_element_type=jnp.float32)
        query_grad = pos_coef[None, :] * dst_rows + lax.dot_general(
            negatives, neg_coef, (((1,), (1,)), ((), ())), preferred_element_type=jnp.float32
        )
        src_grad = src_grad.at[:, src_ids].add(conj_product(query_grad, rel_edges))
        dst_grad = dst_grad.at[:, dst_ids].add(pos_coef[None, :] * queries)
        rel_grad = rel_grad + jnp.dot(
            conj_product(query_grad, src_rows), onehot.T, precision=lax.Precision.HIGHEST
        )
        return ((src_grad, dst_grad, neg_grad, rel_grad), None)

    start_totals = (
        jnp.zeros((DIM, row_count), jnp.float32),
        jnp.zeros((DIM, row_count), jnp.float32),
        jnp.zeros((DIM, NNEG), jnp.float32),
        jnp.zeros((DIM, NREL), jnp.float32),
    )
    summed, unused_out = lax.scan(edge_block, start_totals, edge_sets)
    src_grad, dst_grad, neg_grad, rel_grad = summed
    live_rows = own_requests.reshape(edge_count * QMAX, BLOCK)[block_at]
    columns = (owner_of[:, None] * row_count + live_rows).reshape(NNEG)
    dense = jnp.zeros((DIM, edge_count * row_count), jnp.float32).at[:, columns].add(neg_grad)
    dst_grad = dst_grad + lax.psum_scatter(dense, "edge", scatter_dimension=1, tiled=True)
    rel_total = lax.psum(rel_grad, ("dom", "edge"))
    src_out, src_state_out = adagrad(src_table, src_state, src_grad)
    dst_out, dst_state_new = adagrad(part_table, part_state.reshape(row_count), dst_grad)
    relation_out = relation - rel_rate * rel_total
    return (src_out, src_state_out, dst_out, dst_state_new, relation_out)


def solution(mesh):
    in_specs = (
        P(None, ("dom", "edge")),
        P(("dom", "edge")),
        P(None, ("dom", "edge")),
        P(("dom", "edge")),
        P(),
        P(("dom", "edge")),
        P(("dom", "edge")),
        P(("dom", "edge")),
        P(),
        P(("dom", "edge"), None, None),
        P(("dom", "edge"), None),
    )
    out_specs = (
        P(None, ("dom", "edge")),
        P(("dom", "edge")),
        P(None, ("dom", "edge")),
        P(("dom", "edge")),
        P(),
    )
    return jax.shard_map(shards, mesh=mesh, in_specs=in_specs, out_specs=out_specs, check_vma=False)
```

profile of v0, /device:TPU:0, one launch (start us, length us, event | category | flops | bytes accessed | tf_op | source)
XLA Modules:
  0.0 651.4 jit_solution(17470633159199048808)
XLA Ops:
  10.3 6.4 all-to-all-start
  22.3 42.9 %all-gather.4.cloned.1.call-done = f32[400,2048]{0,1:T(8,128)} async-done(((f32[400,512]{0,1:T(8,128)}), f32[400,2048]{0,1:T(8,128)}) %all-gather.4.cloned.1.call-update) | async-done | bytes 3276816 | tf_op jit(solution)/shard_map/all_gather | solution.py:72
  66.6 9.2 %gather_fusion.2 = bf16[2048,400]{1,0:T(8,128)(2,1)} fusion(bf16[400,512]{0,1:T(8,128)(2,1)S(1)} %get-tuple-element.233, s32[2048]{0:T(1024)S(1)} %broadcast_clamp_fusion), kind=kCustom, calls=%fused_computation.2 | custom fusion | bytes 3284992 | tf_op jit(solution)/shard_map/gather | solution.py:85
  79.6 4.7 all-to-all-start.1
  90.7 32.9 %all-to-all-done.1 = bf16[400,8,256]{2,0,1:T(8,128)(2,1)S(1)} async-done(((bf16[400,8,256]{2,0,1:T(8,128)(2,1)}), bf16[400,8,256]{2,0,1:T(8,128)(2,1)S(1)}, u32[]{:S(2)}, u32[]{:S(2)}) %all-to-all-start.1) | async-done | bytes 1638432 | tf_op jit(solution)/shard_map/all_to_all | solution.py:86
  133.0 398.8 %while.17 = (s32[]{:T(128)}, f32[400,512]{0,1:T(8,128)S(1)}, f32[400,512]{0,1:T(8,128)S(1)}, f32[400,1536]{1,0:T(8,128)}, f32[400,16]{0,1:T(8,128)}, /*index=5*/...) while((s32[]{:T(128)}, f32[400,512]{0,1:T(8,128)S(1)}, ...), condition=%wide.region_7.8_spmd.clone, body=%wide.region_3.7_spmd.clone.sunk | while | flops 1977010688 | bytes 71210600 | solution.py:132
  177.6 4.7 scatter_fusion
  227.5 4.7 scatter_fusion
  264.7 4.6 scatter_fusion.1
  277.5 4.7 scatter_fusion
  314.6 4.6 scatter_fusion.1
  327.4 4.7 scatter_fusion
  364.6 4.6 scatter_fusion.1
  377.3 4.7 scatter_fusion
  414.5 4.6 scatter_fusion.1
  427.2 4.7 scatter_fusion
  464.4 4.6 scatter_fusion.1
  477.1 4.7 scatter_fusion
  514.3 4.6 scatter_fusion.1
  527.1 4.7 scatter_fusion
  535.2 13.9 %scatter_custom_fusion.2 = f32[400,4096]{0,1:T(8,128)} fusion(s32[1536]{0:T(1024)} %fusion.19, f32[1536,400]{1,0:T(8,128)} %copy.75, f32[]{:T(128)} %constant.30.clone.1), kind=kCustom, calls=%fused_computation.46 | custom fusion | flops 614400 | bytes 6554112 | tf_op jit(solution)/shard_map/scatter-add | solution.py:136
  549.9 8.0 %all-gather.1 = f32[4,1,512]{2,1,0:T(1,128)S(1)} all-gather(f32[1,1,512]{2,1,0:T(1,128)S(1)} %bitcast.114), channel_id=2, replica_groups=mesh['dom'=4,'edge'=8] {'dom'}, dimensions={0}, use_global_device_ids=true | all-gather | bytes 10240 | tf_op jit(solution)/shard_map/all_gather | solution.py:73
  557.9 38.6 %psum.7 = f32[400,16]{0,1:T(8,128)S(1)} all-reduce(f32[400,16]{0,1:T(8,128)S(1)} %copy-done.11), channel_id=1, replica_groups=mesh['dom'=4,'edge'=8] {'dom','edge'}, use_global_device_ids=true, to_apply=%region_12.13 | all-reduce | flops 6400 | bytes 51200 | tf_op jit(solution)/shard_map/psum | solution.py:138
  597.1 40.8 %reduce-scatter.2.cloned.1.call-done = f32[400,512]{0,1:T(8,128)} async-done(((f32[400,4096]{0,1:T(8,128)}), f32[400,512]{0,1:T(8,128)}) %reduce-scatter.2.cloned.1.call-update) | async-done | bytes 819216 | tf_op jit(solution)/shard_map/reduce_scatter | solution.py:137
  (497 shorter events, 372.2 us)
Async XLA Ops:
  7.2 9.5 %copy-start.28 = (s32[4]{0:T(128)S(1)}, s32[4]{0:T(128)}, u32[]{:S(2)}) copy-start(s32[4]{0:T(128)} %param.21) | copy-start | bytes 52
  7.2 58.0 %all-gather.4.cloned.1.call-start = ((), (), s32[]{:S(2)}) async-start(), calls=%async_computation.3 | async-start | bytes 5242880 | tf_op jit(solution)/shard_map/all_gather | solution.py:72
  10.3 12.0 %all-to-all-start = ((s32[8,1,256]{2,1,0:T(1,128)}), s32[8,1,256]{2,1,0:T(1,128)S(1)}, u32[]{:S(2)}, u32[]{:S(2)}) async-start(s32[8,1,256]{2,1,0:T(1,128)} %all_to_all.11), calls=%async_computation | async-start | bytes 16384 | tf_op jit(solution)/shard_map/all_to_all | solution.py:84
  79.6 5.7 copy-start.15
  79.6 7.0 %copy-start.24 = (s32[4096]{0:T(1024)S(1)}, s32[4096]{0:T(1024)}, u32[]{:S(2)}) copy-start(s32[4096]{0:T(1024)} %param.18) | copy-start | bytes 49156
  79.6 7.6 %copy-start.25 = (s32[4096]{0:T(1024)S(1)}, s32[4096]{0:T(1024)}, u32[]{:S(2)}) copy-start(s32[4096]{0:T(1024)} %param.20) | copy-start | bytes 49156
  79.6 43.9 %all-to-all-start.1 = ((bf16[400,8,256]{2,0,1:T(8,128)(2,1)}), bf16[400,8,256]{2,0,1:T(8,128)(2,1)S(1)}, u32[]{:S(2)}, u32[]{:S(2)}) async-start(bf16[400,8,256]{2,0,1:T(8,128)(2,1)} %bitcast.5), calls=%async_computation.1 | async-start | bytes 3276800 | tf_op jit(solution)/shard_map/all_to_all | solution.py:86
  84.4 553.5 %reduce-scatter.2.cloned.1.call-start = ((), (), s32[]{:S(2)}) async-start(), calls=%async_computation.4 | async-start | bytes 9437184 | tf_op jit(solution)/shard_map/reduce_scatter | solution.py:137
  133.2 8.3 %copy-start.21 = (s32[8,512]{1,0:T(8,128)}, s32[8,512]{1,0:T(8,128)S(1)}, u32[]{:S(2)}) copy-start(s32[8,512]{1,0:T(8,128)S(1)} %get-tuple-element.371) | copy-start | bytes 49156 | tf_op jit(solution)/shard_map/while
  177.6 4.7 copy-start.22
  182.3 8.3 %copy-start.21 = (s32[8,512]{1,0:T(8,128)}, s32[8,512]{1,0:T(8,128)S(1)}, u32[]{:S(2)}) copy-start(s32[8,512]{1,0:T(8,128)S(1)} %get-tuple-element.371) | copy-start | bytes 49156 | tf_op jit(solution)/shard_map/while
  227.5 4.7 copy-start.22
  232.2 8.3 %copy-start.21 = (s32[8,512]{1,0:T(8,128)}, s32[8,512]{1,0:T(8,128)S(1)}, u32[]{:S(2)}) copy-start(s32[8,512]{1,0:T(8,128)S(1)} %get-tuple-element.371) | copy-start | bytes 49156 | tf_op jit(solution)/shard_map/while
  277.5 4.7 copy-start.22
  282.2 8.3 %copy-start.21 = (s32[8,512]{1,0:T(8,128)}, s32[8,512]{1,0:T(8,128)S(1)}, u32[]{:S(2)}) copy-start(s32[8,512]{1,0:T(8,128)S(1)} %get-tuple-element.371) | copy-start | bytes 49156 | tf_op jit(solution)/shard_map/while
  327.4 4.7 copy-start.22
  332.1 8.3 %copy-start.21 = (s32[8,512]{1,0:T(8,128)}, s32[8,512]{1,0:T(8,128)S(1)}, u32[]{:S(2)}) copy-start(s32[8,512]{1,0:T(8,128)S(1)} %get-tuple-element.371) | copy-start | bytes 49156 | tf_op jit(solution)/shard_map/while
  377.3 4.7 copy-start.22
  382.0 8.3 %copy-start.21 = (s32[8,512]{1,0:T(8,128)}, s32[8,512]{1,0:T(8,128)S(1)}, u32[]{:S(2)}) copy-start(s32[8,512]{1,0:T(8,128)S(1)} %get-tuple-element.371) | copy-start | bytes 49156 | tf_op jit(solution)/shard_map/while
  427.2 4.7 copy-start.22
  431.9 8.3 %copy-start.21 = (s32[8,512]{1,0:T(8,128)}, s32[8,512]{1,0:T(8,128)S(1)}, u32[]{:S(2)}) copy-start(s32[8,512]{1,0:T(8,128)S(1)} %get-tuple-element.371) | copy-start | bytes 49156 | tf_op jit(solution)/shard_map/while
  481.8 8.3 %copy-start.21 = (s32[8,512]{1,0:T(8,128)}, s32[8,512]{1,0:T(8,128)S(1)}, u32[]{:S(2)}) copy-start(s32[8,512]{1,0:T(8,128)S(1)} %get-tuple-element.371) | copy-start | bytes 49156 | tf_op jit(solution)/shard_map/while
  549.2 8.7 %copy-start.11 = (f32[400,16]{0,1:T(8,128)S(1)}, f32[400,16]{0,1:T(8,128)}, u32[]{:S(2)}) copy-start(f32[400,16]{0,1:T(8,128)} %get-tuple-element.392) | copy-start | bytes 76804
  549.2 47.3 %copy-start.14 = (f32[400,16]{0,1:T(8,128)S(1)}, f32[400,16]{0,1:T(8,128)}, u32[]{:S(2)}) copy-start(f32[400,16]{0,1:T(8,128)} %param.17) | copy-start | bytes 76804
  (121 other events, 320.3 us)
Sparse Core Ops, SparseCore 0:
  9.8 55.2 all-gather.3
  549.3 88.5 reduce-scatter.1
where the time goes:
time: 656 us; the launch traced here: 651 us
  local copies, waits for them, and re-layouts  192 us (29%)
  other arithmetic  175 us (27%)
  waiting for transfers between devices  121 us (18%)
  matrix products  89.3 us (14%)
  blocking collectives  46.6 us (7%)
  between operations  14.9 us (2%)
  starting transfers between devices  11.2 us (2%)
    gather x16, local copies, waits for them, and re-layouts, edge_block(): src_rows = src_table[:, src_ids]  50.9 us
    all_gather x1, waiting for transfers between devices, shards(): lax.all_gather(dst_table, 'dom', axis=1, tiled=True)  42.9 us
    reduce_scatter x1, waiting for transfers between devices, shards(): lax.psum_scatter(dense, 'edge', scatter_dimension=1, tiled=True)  40.8 us
    gather x16, local copies, waits for them, and re-layouts, edge_block(): dst_rows = part_table[:, dst_ids]  39 us
    psum x1, blocking collectives, shards(): rel_total = lax.psum(rel_grad, ('dom', 'edge'))  38.6 us
    scatter-add x8, other arithmetic, edge_block(): src_grad = src_grad.at[:, src_ids].add(conj_product(query_grad, rel_edges))  37.2 us
    scatter-add x8, other arithmetic, edge_block(): dst_grad = dst_grad.at[:, dst_ids].add(pos_coef[None, :] * queries)  37.2 us
    dot_general x8, matrix products, edge_block(): jnp.dot(query_b, neg_coef, preferred_element_type=jnp.float32)  36.3 us
  transfers between devices with their start and end apart: 4, of which 4 were waited for; matrix products, arithmetic and copies ran while one was open for 1% of the time, Pallas kernels for 0%

commit v1 on v0

v1 whole, which is shorter than its diff:
```python
import math

import jax
import jax.numpy as jnp
from jax import lax
from jax.experimental import pallas as pl
from jax.experimental.pallas import tpu as pltpu
from jax.sharding import PartitionSpec as P

BLOCK = 128
QMAX = 2
QTOTAL = 12
NNEG = QTOTAL * BLOCK
CORES = 2
LEARN_RATE = 0.1
REL_RATE = 0.02

bf16 = jnp.bfloat16
f32 = jnp.float32
MIB = 2**20


def dot_nn(lhs, rhs):
    return lax.dot_general(lhs, rhs, (((1,), (0,)), ((), ())), preferred_element_type=f32)


def dot_nt(lhs, rhs):
    return lax.dot_general(lhs, rhs, (((1,), (1,)), ((), ())), preferred_element_type=f32)


def split2(value):
    high = value.astype(bf16)
    return high, (value - high.astype(f32)).astype(bf16)


def select_rows(ids, rows):
    places = lax.broadcasted_iota(jnp.int32, (rows, ids.shape[1]), 0)
    return jnp.where(places == ids, 1.0, 0.0).astype(bf16)


def product(one, other):
    half = one.shape[0] // 2
    a, b, c, d = one[:half], one[half:], other[:half], other[half:]
    return jnp.concatenate([a * c - b * d, a * d + b * c], axis=0)


def back(grad, value):
    half = grad.shape[0] // 2
    a, b, c, d = grad[:half], grad[half:], value[:half], value[half:]
    return jnp.concatenate([a * c + b * d, b * c - a * d], axis=0)


def whole(shape):
    return pl.BlockSpec(shape, lambda *_: (0,) * len(shape))


def lanes(rows, width):
    return pl.BlockSpec((rows, width), lambda i, *_: (0, i))


def params(mib):
    return pltpu.CompilerParams(
        vmem_limit_bytes=mib * MIB, dimension_semantics=("arbitrary",)
    )


def cost(flops, moved):
    return pl.CostEstimate(flops=int(flops), bytes_accessed=int(moved), transcendentals=0)


def split_relation(relation):
    high = lax.reduce_precision(relation, 8, 7)
    rest = relation - high
    mid = lax.reduce_precision(rest, 8, 7)
    low = rest - mid
    parts = jnp.concatenate([high, mid, low], axis=1).astype(bf16)
    return jnp.pad(parts, ((0, 0), (0, (-parts.shape[1]) % 128)))


def relation_rows(rel_parts, ids, count):
    width = rel_parts.shape[1]
    places = lax.broadcasted_iota(jnp.int32, (width, ids.shape[1]), 0)
    hit = jnp.logical_and(places % count == ids, places < 3 * count)
    return dot_nn(rel_parts, jnp.where(hit, 1.0, 0.0).astype(bf16))


def make_queries(src_table, rel_parts, src_ids, rel_ids, rel_count, chunk):
    dim, rows = src_table.shape
    edges = src_ids.shape[1]

    def body(table, parts, src, rel, query, query_b, high, low):
        @pl.when(pl.program_id(0) == 0)
        def _():
            high[...], low[...] = split2(table[...])

        pick = select_rows(src[...], rows)
        src_rows = dot_nn(high[...], pick) + dot_nn(low[...], pick)
        value = product(src_rows, relation_rows(parts[...], rel[...], rel_count))
        query[...] = value
        query_b[...] = value.astype(bf16)

    return pl.pallas_call(
        body,
        name="make_queries",
        grid=(edges // chunk,),
        in_specs=[whole((dim, rows)), whole(rel_parts.shape), lanes(1, chunk), lanes(1, chunk)],
        out_specs=[lanes(dim, chunk), lanes(dim, chunk)],
        out_shape=[
            jax.ShapeDtypeStruct((dim, edges), f32),
            jax.ShapeDtypeStruct((dim, edges), bf16),
        ],
        scratch_shapes=[pltpu.VMEM((dim, rows), bf16)] * 2,
        compiler_params=params(40),
        cost_estimate=cost(4 * dim * rows * edges, 6 * dim * edges),
    )(src_table, rel_parts, src_ids, rel_ids)


def positives(part_high, query, dst_ids, chunk):
    dim, rows = part_high.shape
    edges = dst_ids.shape[1]

    def body(table, query_in, dst, query_grad, dst_grad):
        @pl.when(pl.program_id(0) == 0)
        def _():
            dst_grad[...] = jnp.zeros_like(dst_grad)

        pick = select_rows(dst[...], rows)
        dst_rows = dot_nn(table[...], pick)
        value = query_in[...]
        positive = jnp.sum(value * dst_rows, axis=0, keepdims=True)
        coef = -jax.nn.sigmoid(-positive)
        query_grad[...] = coef * dst_rows
        high, low = split2(coef * value)
        dst_grad[...] += dot_nt(high, pick) + dot_nt(low, pick)

    return pl.pallas_call(
        body,
        name="positives",
        grid=(edges // chunk,),
        in_specs=[whole((dim, rows)), lanes(dim, chunk), lanes(1, chunk)],
        out_specs=[lanes(dim, chunk), whole((dim, rows))],
        out_shape=[
            jax.ShapeDtypeStruct((dim, edges), f32),
            jax.ShapeDtypeStruct((dim, rows), f32),
        ],
        compiler_params=params(40),
        cost_estimate=cost(6 * dim * rows * edges, 8 * dim * edges),
    )(part_high, query, dst_ids)


def negative_wave(plan, tables, neg_ids, query_b, query_grad, chunk):
    count = len(tables)
    dim, rows = tables[0].shape
    edges = query_b.shape[1]
    half_weight = 0.5 / math.sqrt(NNEG)

    def body(plan_ref, *refs):
        table_refs = refs[:count]
        ids, query_ref, grad_in = refs[count : count + 3]
        grad_out = refs[count + 3]
        shard_grads = refs[count + 4 : 2 * count + 4]
        neg, neg_t, neg_grad = refs[2 * count + 4 :]
        step = pl.program_id(0)

        @pl.when(step == 0)
        def _():
            base = jnp.int32(0)
            for s in range(count):
                for b in range(QMAX):

                    @pl.when(plan_ref[s] > b)
                    def _(s=s, b=b, base=base):
                        pick = select_rows(ids[plan_ref[count + s], b : b + 1, :], rows)
                        value = dot_nn(table_refs[s][...], pick)
                        neg[base + b] = value.astype(bf16)
                        neg_t[base + b] = value.T.astype(bf16)

                base = base + plan_ref[s]

            @pl.when(base % 2 == 1)
            def _():
                neg[base] = jnp.zeros((dim, BLOCK), bf16)
                neg_t[base] = jnp.zeros((BLOCK, dim), bf16)

            def clear(j, carry):
                neg_grad[j] = jnp.zeros((dim, BLOCK), f32)
                return carry

            lax.fori_loop(0, base + base % 2, clear, 0)

        total = plan_ref[0]
        for s in range(1, count):
            total = total + plan_ref[s]
        grad_out[...] = grad_in[...]

        def pair(p, carry):
            left, right = 2 * p, 2 * p + 1
            columns = jnp.concatenate([neg[left], neg[right]], axis=1)
            columns_t = jnp.concatenate([neg_t[left], neg_t[right]], axis=0)
            scores = dot_nn(columns_t, query_ref[...])
            coef = (half_weight * jnp.tanh(0.5 * scores) + half_weight).astype(bf16)
            grad_out[...] += dot_nn(columns, coef)
            added = dot_nt(query_ref[...], coef)
            neg_grad[left] += added[:, :BLOCK]
            neg_grad[right] += added[:, BLOCK:]
            return carry

        lax.fori_loop(0, (total + 1) // 2, pair, 0)

        @pl.when(step == pl.num_programs(0) - 1)
        def _():
            base = jnp.int32(0)
            for s in range(count):
                shard_grads[s][...] = jnp.zeros((dim, rows), bf16)
                for b in range(QMAX):

                    @pl.when(plan_ref[s] > b)
                    def _(s=s, b=b, base=base):
                        pick = select_rows(ids[plan_ref[count + s], b : b + 1, :], rows)
                        high, low = split2(neg_grad[base + b])
                        value = dot_nt(high, pick) + dot_nt(low, pick)
                        if b:
                            value = value + shard_grads[s][...].astype(f32)
                        shard_grads[s][...] = value.astype(bf16)

                base = base + plan_ref[s]

    slots = QMAX * count
    return pl.pallas_call(
        body,
        name="negative_wave",
        grid_spec=pltpu.PrefetchScalarGridSpec(
            num_scalar_prefetch=1,
            grid=(edges // chunk,),
            in_specs=[whole((dim, rows))] * count
            + [whole(neg_ids.shape), lanes(dim, chunk), lanes(dim, chunk)],
            out_specs=[lanes(dim, chunk)] + [whole((dim, rows))] * count,
            scratch_shapes=[
                pltpu.VMEM((slots, dim, BLOCK), bf16),
                pltpu.VMEM((slots, BLOCK, dim), bf16),
                pltpu.VMEM((slots, dim, BLOCK), f32),
            ],
        ),
        out_shape=[jax.ShapeDtypeStruct((dim, edges), f32)]
        + [jax.ShapeDtypeStruct((dim, rows), bf16)] * count,
        input_output_aliases={count + 3: 0},
        compiler_params=params(40),
        cost_estimate=cost(6 * dim * 1.5 * count * BLOCK * edges, 10 * dim * edges),
    )(plan, *tables, neg_ids, query_b, query_grad)


def source_side(src_table, src_state, rel_parts, src_ids, rel_ids, query_grad, rel_count, chunk):
    dim, rows = src_table.shape
    edges = src_ids.shape[1]

    def body(table, state, parts, src, rel, grad_in, out, state_out, rel_out, high, low, acc):
        step = pl.program_id(0)

        @pl.when(step == 0)
        def _():
            high[...], low[...] = split2(table[...])
            acc[...] = jnp.zeros_like(acc)
            rel_out[...] = jnp.zeros_like(rel_out)

        pick = select_rows(src[...], rows)
        src_rows = dot_nn(high[...], pick) + dot_nn(low[...], pick)
        grad = grad_in[...]
        upper, lower = split2(back(grad, relation_rows(parts[...], rel[...], rel_count)))
        acc[...] += dot_nt(upper, pick) + dot_nt(lower, pick)
        kinds = select_rows(rel[...], rel_count)
        upper, lower = split2(back(grad, src_rows))
        rel_out[...] += dot_nt(kinds, upper) + dot_nt(kinds, lower)

        @pl.when(step == pl.num_programs(0) - 1)
        def _():
            total = acc[...]
            new_state = state[...] + jnp.sum(total * total, axis=0, keepdims=True) / dim
            state_out[...] = new_state
            out[...] = table[...] - LEARN_RATE * total / jnp.sqrt(new_state)

    return pl.pallas_call(
        body,
        name="source_side",
        grid=(edges // chunk,),
        in_specs=[
            whole((dim, rows)),
            whole((1, rows)),
            whole(rel_parts.shape),
            lanes(1, chunk),
            lanes(1, chunk),
            lanes(dim, chunk),
        ],
        out_specs=[whole((dim, rows)), whole((1, rows)), whole((rel_count, dim))],
        out_shape=[
            jax.ShapeDtypeStruct((dim, rows), f32),
            jax.ShapeDtypeStruct((1, rows), f32),
            jax.ShapeDtypeStruct((rel_count, dim), f32),
        ],
        scratch_shapes=[pltpu.VMEM((dim, rows), bf16)] * 2 + [pltpu.VMEM((dim, rows), f32)],
        compiler_params=params(40),
        cost_estimate=cost(8 * dim * rows * edges, 4 * dim * edges),
    )(src_table, src_state, rel_parts, src_ids, rel_ids, query_grad)


def destination_side(high, low, state, own_grad, grads):
    dim, rows = own_grad.shape
    count = len(grads)

    def body(*refs):
        high_ref, low_ref, state_ref, own_ref = refs[:4]
        out, state_out = refs[4 + count :]
        total = own_ref[...]
        for ref in refs[4 : 4 + count]:
            total = total + ref[...].astype(f32)
        new_state = state_ref[...] + jnp.sum(total * total, axis=0, keepdims=True) / dim
        state_out[...] = new_state
        table = high_ref[...].astype(f32) + low_ref[...].astype(f32)
        out[...] = table - LEARN_RATE * total / jnp.sqrt(new_state)

    width = min(rows, 128)
    return pl.pallas_call(
        body,
        name="destination_side",
        grid=(rows // width,),
        in_specs=[lanes(dim, width)] * 2
        + [lanes(1, width)]
        + [lanes(dim, width)] * (count + 1),
        out_specs=[lanes(dim, width), lanes(1, width)],
        out_shape=[
            jax.ShapeDtypeStruct((dim, rows), f32),
            jax.ShapeDtypeStruct((1, rows), f32),
        ],
        compiler_params=params(24),
        cost_estimate=cost(8 * dim * rows, (12 + 2 * count) * dim * rows),
    )(high, low, state, own_grad, *grads)


def grid_of(count):
    across = math.isqrt(count)
    while count % across:
        across -= 1
    return count // across, across


def choose(index, options):
    result = options[0]
    for k in range(1, len(options)):
        result = jnp.where(index == k, options[k], result)
    return result


def route(value, matching, x_first):
    count = lax.axis_size("dom")
    down, across = grid_of(count)
    axes = [(across, 1), (down, across)]
    (n1, stride1), (n2, stride2) = axes if x_first else axes[::-1]
    here = lax.axis_index("dom")

    def moved(device, n, stride, shift):
        place = (device // stride) % n
        return device + ((place + shift) % n - place) * stride

    def shifted(array, n, stride, shift):
        pairs = [(d, moved(d, n, stride, shift)) for d in range(count)]
        return lax.ppermute(array, "dom", pairs)

    held = [value] + [shifted(value, n1, stride1, k) for k in range(1, n1)]

    def wanted_by(device):
        source = jnp.take(matching, device)
        behind = ((here // stride1) % n1 - (source // stride1) % n1) % n1
        return choose(behind, held)

    found = [wanted_by(here)]
    for m in range(1, n2):
        found.append(shifted(wanted_by(moved(here, n2, stride2, m)), n2, stride2, m))
    source = jnp.take(matching, here)
    return choose(((here // stride2) % n2 - (source // stride2) % n2) % n2, found)


def route_halves(value, matching):
    half = value.shape[1] // 2
    parts = [route(value[:, :half], matching, True), route(value[:, half:], matching, False)]
    return jnp.concatenate(parts, axis=1)


def total_over_mesh(value):
    for axis in ("edge", "dom"):
        count = lax.axis_size(axis)
        step = 1
        while step < count:
            value = value + lax.ppermute(value, axis, [(i, i ^ step) for i in range(count)])
            step *= 2
    return value


def shards(
    src_table,
    src_state,
    dst_table,
    dst_state,
    relation,
    edge_src,
    edge_dst,
    edge_rel,
    matching,
    neg_rows,
    quotas,
):
    edge_count = lax.axis_size("edge")
    chips = edge_count // CORES
    dim, row_count = src_table.shape
    rel_count = relation.shape[1]
    edges = edge_src.shape[0]
    chunk = min(edges, 512)
    wave_chunk = min(edges, 1024)
    here = lax.axis_index("edge")

    src_ids = edge_src.reshape(1, edges)
    dst_ids = edge_dst.reshape(1, edges)
    rel_ids = edge_rel.reshape(1, edges)
    neg_ids = neg_rows.reshape(edge_count, QMAX, BLOCK)
    quota = quotas.reshape(edge_count)
    rel_parts = split_relation(relation)

    table_high = lax.reduce_precision(dst_table, 8, 7)
    table_low = (dst_table - table_high).astype(bf16)
    part_high = route_halves(table_high.astype(bf16), matching)
    table_low, held_state, part_high = lax.optimization_barrier((table_low, dst_state, part_high))
    part_low = route_halves(table_low, matching)
    part_state = route(held_state.reshape(1, row_count), matching, True)

    query, query_b = make_queries(src_table, rel_parts, src_ids, rel_ids, rel_count, chunk)
    query_grad, own_grad = positives(part_high, query, dst_ids, chunk)

    swap = [(i, i ^ 1) for i in range(edge_count)]

    def plan_of(places):
        live, at = [], []
        for place in places:
            inside = jnp.logical_and(place >= 0, place < edge_count)
            place = jnp.clip(place, 0, edge_count - 1)
            live.append(jnp.where(inside, jnp.take(quota, place), 0))
            at.append(place)
        return jnp.stack(live + at).astype(jnp.int32)

    other = here + 1 - 2 * (here % CORES)
    tables = [part_high, lax.ppermute(part_high, "edge", swap)]
    query_grad, mine, theirs = negative_wave(
        plan_of([here, other]), tables, neg_ids, query_b, query_grad, wave_chunk
    )
    arrived = [mine, lax.ppermute(theirs, "edge", swap)]

    from_below = from_above = part_high
    for s in range(1, chips):
        last = edge_count - CORES
        up = [(i, i + CORES) for i in range(CORES * (s - 1), last)]
        down = [(i + CORES, i) for i in range(0, last - CORES * (s - 1))]
        from_below = lax.ppermute(from_below, "edge", up)
        from_above = lax.ppermute(from_above, "edge", down)
        tables = [
            from_below,
            from_above,
            lax.ppermute(from_below, "edge", swap),
            lax.ppermute(from_above, "edge", swap),
        ]
        far = CORES * s
        plan = plan_of([here - far, here + far, other - far, other + far])
        query_grad, below, above, below_other, above_other = negative_wave(
            plan, tables, neg_ids, query_b, query_grad, wave_chunk
        )
        below = below.astype(f32) + lax.ppermute(below_other, "edge", swap).astype(f32)
        above = above.astype(f32) + lax.ppermute(above_other, "edge", swap).astype(f32)
        to_below = [(i, i - far) for i in range(far, edge_count)]
        to_above = [(i, i + far) for i in range(edge_count - far)]
        arrived.append(lax.ppermute(below.astype(bf16), "edge", to_below))
        arrived.append(lax.ppermute(above.astype(bf16), "edge", to_above))

    src_out, src_state_out, rel_grad = source_side(
        src_table,
        src_state.reshape(1, row_count),
        rel_parts,
        src_ids,
        rel_ids,
        query_grad,
        rel_count,
        chunk,
    )
    relation_out = relation - REL_RATE * total_over_mesh(rel_grad).T
    dst_out, dst_state_out = destination_side(part_high, part_low, part_state, own_grad, arrived)
    return (
        src_out,
        src_state_out.reshape(row_count),
        dst_out,
        dst_state_out.reshape(row_count),
        relation_out,
    )


def solution(mesh):
    in_specs = (
        P(None, ("dom", "edge")),
        P(("dom", "edge")),
        P(None, ("dom", "edge")),
        P(("dom", "edge")),
        P(),
        P(("dom", "edge")),
        P(("dom", "edge")),
        P(("dom", "edge")),
        P(),
        P(("dom", "edge"), None, None),
        P(("dom", "edge"), None),
    )
    out_specs = (
        P(None, ("dom", "edge")),
        P(("dom", "edge")),
        P(None, ("dom", "edge")),
        P(("dom", "edge")),
        P(),
    )
    return jax.shard_map(shards, mesh=mesh, in_specs=in_specs, out_specs=out_specs, check_vma=False)
```

time: 656 us -> 218 us (0.33)
  local copies, waits for them, and re-layouts: 192 us -> 17.2 us
  other arithmetic: 175 us -> 7.34 us
  matrix products: 89.3 us -> 0 us
  Pallas kernels: 0 us -> 77.7 us
  waiting for transfers between devices: 121 us -> 50.7 us
  blocking collectives: 46.6 us -> 0 us
  starting transfers between devices: 11.2 us -> 52.4 us
    gather x36 -> x0, local copies, waits for them, and re-layouts: 106 us -> none  [the longest x16 50.9 us: edge_block(): src_rows = src_table[:, src_ids]]
    dot_general x40 -> x0, matrix products: 89.3 us -> none  [the longest x8 36.3 us: edge_block(): jnp.dot(query_b, neg_coef, preferred_element_type=jnp.float32)]
    scatter-add x17 -> x0, other arithmetic: 88.4 us -> none  [the longest x8 37.2 us: edge_block(): src_grad = src_grad.at[:, src_ids].add(conj_product(query_grad, rel_edges))]
    pallas_call x0 -> x8, Pallas kernels: none -> 77.7 us  [the longest x4 43.7 us: negative_wave(): pl.pallas_call(body, name='negative_wave', grid_spec=pltpu.PrefetchScalar...]
    ppermute x0 -> x41, starting transfers between devices: none -> 52.4 us  [the longest x3 16.1 us: shards(): arrived.append(lax.ppermute(above.astype(bf16), 'edge', to_above))]
    ppermute x0 -> x41, waiting for transfers between devices: none -> 50.7 us  [the longest x3 19.9 us: shards(): arrived.append(lax.ppermute(below.astype(bf16), 'edge', to_below))]
    all_gather x1 -> x0, waiting for transfers between devices: 42.9 us -> none  [shards(): lax.all_gather(dst_table, 'dom', axis=1, tiled=True)]
    reduce_scatter x1 -> x0, waiting for transfers between devices: 40.8 us -> none  [shards(): lax.psum_scatter(dense, 'edge', scatter_dimension=1, tiled=True)]
  transfers between devices with their start and end apart: 4 -> 41, of which waited for: 4 -> 13; matrix products, arithmetic and copies ran while one was open for 1% -> 3% of each run, Pallas kernels for 0% -> 35%
where the time goes in v1:
time: 218 us; the launch traced here: 217 us
  Pallas kernels  77.7 us (36%)
  starting transfers between devices  52.4 us (24%)
  waiting for transfers between devices  50.7 us (23%)
  local copies, waits for them, and re-layouts  17.2 us (8%)
  between operations  12 us (6%)
  other arithmetic  7.34 us (3%)
    pallas_call x4, Pallas kernels, negative_wave(): pl.pallas_call(body, name='negative_wave', grid_spec=pltpu.PrefetchScalar...  43.7 us
    ppermute x3, waiting for transfers between devices, shards(): arrived.append(lax.ppermute(below.astype(bf16), 'edge', to_below))  19.9 us
    ppermute x10, waiting for transfers between devices, shifted(): return lax.ppermute(array, 'dom', pairs)  17.3 us
    ppermute x3, starting transfers between devices, shards(): arrived.append(lax.ppermute(above.astype(bf16), 'edge', to_above))  16.1 us
    pallas_call x1, Pallas kernels, source_side(): pl.pallas_call(body, name='source_side', grid=(edges // chunk,), in_specs...  14.8 us
    unnamed x38, local copies, waits for them, and re-layouts  13.7 us
    ppermute x10, starting transfers between devices, shifted(): return lax.ppermute(array, 'dom', pairs)  12.8 us
    ppermute x5, waiting for transfers between devices, total_over_mesh(): lax.ppermute(value, axis, [(i, i ^ step) for i in range(count)])  10.2 us
  transfers between devices with their start and end apart: 41, of which 13 were waited for; matrix products, arithmetic and copies ran while one was open for 3% of the time, Pallas kernels for 35%

profile of v1, /device:TPU:0, one launch (start us, length us, event | category | flops | bytes accessed | tf_op | source)
XLA Modules:
  0.0 217.4 jit_solution(8774272011163450498)
XLA Ops:
  2.7 3.0 %collective-permute-start = (bf16[400,256]{1,0:T(8,128)(2,1)S(1)}, bf16[400,256]{1,0:T(8,128)(2,1)S(1)}, u32[]{:S(2)}, u32[]{:S(2)}) collective-permute-start(bf16[400,256]{1,0:T(8,128)(2,1)S(1)} %slice.101), channel_id=1, source_target_pairs={{0,8},{8,0},{16,24},{24,16},{1,9},{9,1},{17,25},{25,17},{2,10},{10... | collective-permute-start | bytes 614408 | tf_op jit(solution)/shard_map/ppermute | solution.py:365
  7.7 3.0 %collective-permute-done = bf16[400,256]{1,0:T(8,128)(2,1)S(1)} collective-permute-done((bf16[400,256]{1,0:T(8,128)(2,1)S(1)}, bf16[400,256]{1,0:T(8,128)(2,1)S(1)}, u32[]{:S(2)}, u32[]{:S(2)}) %collective-permute-start) | collective-permute-done | bytes 204832 | tf_op jit(solution)/shard_map/ppermute | solution.py:365
  15.2 3.6 %collective-permute-done.1 = bf16[400,256]{1,0:T(8,128)(2,1)S(1)} collective-permute-done((bf16[400,256]{1,0:T(8,128)(2,1)S(1)}, bf16[400,256]{1,0:T(8,128)(2,1)S(1)}, u32[]{:S(2)}, u32[]{:S(2)}) %collective-permute-start.1) | collective-permute-done | bytes 204832 | tf_op jit(solution)/shard_map/ppermute | solution.py:365
  18.8 2.7 %collective-permute-done.2 = bf16[400,256]{1,0:T(8,128)(2,1)S(1)} collective-permute-done((bf16[400,256]{1,0:T(8,128)(2,1)S(1)}, bf16[400,256]{1,0:T(8,128)(2,1)S(1)}, u32[]{:S(2)}, u32[]{:S(2)}) %collective-permute-start.2) | collective-permute-done | bytes 204832 | tf_op jit(solution)/shard_map/ppermute | solution.py:365
  26.4 7.0 %make_queries.1 = (f32[400,4096]{1,0:T(8,128)S(1)}, bf16[400,4096]{1,0:T(8,128)(2,1)S(1)}) custom-call(f32[400,512]{1,0:T(8,128)S(1)} %copy-done, bf16[400,128]{1,0:T(8,128)(2,1)S(1)} %pad.4.parts, s32[1,4096]{1,0:T(1,128)S(1)} %bitcast.72, s32[1,4096]{1,0:T(1,128)S(1)} %bitcast.74), custom_call_target="tpu_custom_call" | custom-call | flops 3355443200 | bytes 9830400 | tf_op jit(solution)/shard_map/make_queries/pallas_call | solution.py:102
  33.5 2.7 %copy-done.10 = f32[400,4096]{1,0:T(8,128)} copy-done((f32[400,4096]{1,0:T(8,128)}, f32[400,4096]{1,0:T(8,128)S(1)}, u32[]{:S(2)}) %copy-start.10) | copy-done | bytes 6553624
  48.3 3.5 %collective-permute-start.4 = (bf16[400,512]{1,0:T(8,128)(2,1)S(1)}, bf16[400,512]{1,0:T(8,128)(2,1)S(1)}, u32[]{:S(2)}, u32[]{:S(2)}) collective-permute-start(bf16[400,512]{1,0:T(8,128)(2,1)S(1)} %pad_maximum_fusion.table.refs_0_), channel_id=1, source_target_pairs={{0,2},{1,3},{2,4},{3,5},{4,6},{5,7},{8,10},{9,11},{10,12},{11,13},... | collective-permute-start | bytes 1228808 | tf_op jit(solution)/shard_map/ppermute | solution.py:459
  56.1 2.9 %copy-done.11 = f32[400,4096]{1,0:T(8,128)S(1)} copy-done((f32[400,4096]{1,0:T(8,128)S(1)}, f32[400,4096]{1,0:T(8,128)}, u32[]{:S(2)}) %copy-start.11) | copy-done | bytes 6553624
  59.0 9.6 %positives.1 = (f32[400,4096]{1,0:T(8,128)S(1)}, f32[400,512]{1,0:T(8,128)S(1)}) custom-call(bf16[400,512]{1,0:T(8,128)(2,1)S(1)} %pad_maximum_fusion.table.refs_0_, f32[400,4096]{1,0:T(8,128)S(1)} %copy-done.11, s32[1,4096]{1,0:T(1,128)S(1)} %bitcast.71), custom_call_target="tpu_custom_call" | custom-call | flops 5033164800 | bytes 13107200 | tf_op jit(solution)/shard_map/positives/pallas_call | solution.py:136
  68.7 2.7 %copy-done.8 = f32[400,4096]{1,0:T(8,128)} copy-done((f32[400,4096]{1,0:T(8,128)}, f32[400,4096]{1,0:T(8,128)S(1)}, u32[]{:S(2)}) %copy-start.8) | copy-done | bytes 6553624
  77.2 3.7 %collective-permute-done.18 = bf16[400,256]{1,0:T(8,128)(2,1)S(1)} collective-permute-done((bf16[400,256]{1,0:T(8,128)(2,1)S(1)}, bf16[400,256]{1,0:T(8,128)(2,1)S(1)}, u32[]{:S(2)}, u32[]{:S(2)}) %collective-permute-start.18) | collective-permute-done | bytes 204832 | tf_op jit(solution)/shard_map/ppermute | solution.py:365
  80.9 2.8 %collective-permute-done.19 = bf16[400,256]{1,0:T(8,128)(2,1)S(1)} collective-permute-done((bf16[400,256]{1,0:T(8,128)(2,1)S(1)}, bf16[400,256]{1,0:T(8,128)(2,1)S(1)}, u32[]{:S(2)}, u32[]{:S(2)}) %collective-permute-start.19) | collective-permute-done | bytes 204832 | tf_op jit(solution)/shard_map/ppermute | solution.py:365
  85.7 2.9 %copy-done.9 = f32[400,4096]{1,0:T(8,128)S(1)} copy-done((f32[400,4096]{1,0:T(8,128)S(1)}, f32[400,4096]{1,0:T(8,128)}, u32[]{:S(2)}) %copy-start.9) | copy-done | bytes 6553624
  88.6 7.3 %negative_wave.4 = (f32[400,4096]{1,0:T(8,128)S(1)}, bf16[400,512]{1,0:T(8,128)(2,1)S(1)}, bf16[400,512]{1,0:T(8,128)(2,1)S(1)}) custom-call(s32[4]{0:T(128)S(1)} %pad_add_fusion.plan_ref, bf16[400,512]{1,0:T(8,128)(2,1)S(1)} %pad_maximum_fusion.table.refs_0_, bf16[400,512]{1,0:T(8,128)(2,1)S(1)} %collective-permute-done.16.refs_1_, ...), custom_call_target="tpu_custom_call", output_to_operand_aliasing={{0}: (5, {})} | custom-call | flops 3774873600 | bytes 16384000 | tf_op jit(solution)/shard_map/negative_wave/pallas_call | solution.py:229
  100.9 11.8 %negative_wave.5 = (f32[400,4096]{1,0:T(8,128)S(1)}, bf16[400,512]{1,0:T(8,128)(2,1)S(1)}, bf16[400,512]{1,0:T(8,128)(2,1)S(1)}, bf16[400,512]{1,0:T(8,128)(2,1)S(1)}, bf16[400,512]{1,0:T(8,128)(2,1)S(1)}) custom-call(s32[8]{0:T(128)S(1)} %stack.82.plan_ref, bf16[400,512]{1,0:T(8,128)(2,1)S(1)} %collective-permute-done.4.refs_0_, ...), custom_call_target="tpu_custom_call", output_to_operand_aliasing={{0}: (7, {})} | custom-call | flops 7549747200 | bytes 16384000 | tf_op jit(solution)/shard_map/negative_wave/pallas_call | solution.py:229
  116.3 12.5 %negative_wave.6 = (f32[400,4096]{1,0:T(8,128)S(1)}, bf16[400,512]{1,0:T(8,128)(2,1)S(1)}, bf16[400,512]{1,0:T(8,128)(2,1)S(1)}, bf16[400,512]{1,0:T(8,128)(2,1)S(1)}, bf16[400,512]{1,0:T(8,128)(2,1)S(1)}) custom-call(s32[8]{0:T(128)S(1)} %stack.77.plan_ref, bf16[400,512]{1,0:T(8,128)(2,1)S(1)} %collective-permute-done.5.refs_0_, ...), custom_call_target="tpu_custom_call", output_to_operand_aliasing={{0}: (7, {})} | custom-call | flops 7549747200 | bytes 16384000 | tf_op jit(solution)/shard_map/negative_wave/pallas_call | solution.py:229
  129.4 12.0 %negative_wave.7 = (f32[400,4096]{1,0:T(8,128)S(1)}, bf16[400,512]{1,0:T(8,128)(2,1)S(1)}, bf16[400,512]{1,0:T(8,128)(2,1)S(1)}, bf16[400,512]{1,0:T(8,128)(2,1)S(1)}, bf16[400,512]{1,0:T(8,128)(2,1)S(1)}) custom-call(s32[8]{0:T(128)S(1)} %stack.72.plan_ref, bf16[400,512]{1,0:T(8,128)(2,1)S(1)} %collective-permute-done.6.refs_0_, ...), custom_call_target="tpu_custom_call", output_to_operand_aliasing={{0}: (7, {})} | custom-call | flops 7549747200 | bytes 16384000 | tf_op jit(solution)/shard_map/negative_wave/pallas_call | solution.py:229
  141.4 14.8 %source_side.1 = (f32[400,512]{1,0:T(8,128)}, f32[1,512]{1,0:T(1,128)}, f32[16,400]{1,0:T(8,128)S(1)}) custom-call(f32[400,512]{1,0:T(8,128)S(1)} %copy-done.1, f32[1,512]{1,0:T(1,128)S(1)} %bitcast.76, bf16[400,128]{1,0:T(8,128)(2,1)S(1)} %pad.4.parts, s32[1,4096]{1,0:T(1,128)S(1)} %bitcast.73, s32[1,4096]{1,0:T(1,128)S(1)} %bitcast.75, ...), custom_call_target="tpu_custom_call" | custom-call | flops 6710886400 | bytes 6553600 | tf_op jit(solution)/shard_map/source_side/pallas_call | solution.py:281
  157.8 3.8 %collective-permute-done.37 = f32[16,400]{1,0:T(8,128)S(1)} collective-permute-done((f32[16,400]{1,0:T(8,128)S(1)}, f32[16,400]{1,0:T(8,128)S(1)}, u32[]{:S(2)}, u32[]{:S(2)}) %collective-permute-start.37) | collective-permute-done | bytes 25632 | tf_op jit(solution)/shard_map/ppermute | solution.py:392
  163.3 3.4 %collective-permute-done.38 = f32[16,400]{1,0:T(8,128)S(1)} collective-permute-done((f32[16,400]{1,0:T(8,128)S(1)}, f32[16,400]{1,0:T(8,128)S(1)}, u32[]{:S(2)}, u32[]{:S(2)}) %collective-permute-start.38) | collective-permute-done | bytes 25632 | tf_op jit(solution)/shard_map/ppermute | solution.py:392
  171.3 3.9 %collective-permute-start.27 = (bf16[400,512]{1,0:T(8,128)(2,1)S(1)}, bf16[400,512]{1,0:T(8,128)(2,1)S(1)}, u32[]{:S(2)}, u32[]{:S(2)}) collective-permute-start(bf16[400,512]{1,0:T(8,128)(2,1)S(1)} %add_convert_fusion.4), channel_id=1, source_target_pairs={{0,2},{1,3},{2,4},{3,5},{4,6},{5,7},{8,10},{9,11},{10,12},{11,13},... | collective-permute-start | bytes 1228808 | tf_op jit(solution)/shard_map/ppermute | solution.py:477
  177.8 7.2 %collective-permute-start.31 = (bf16[400,512]{1,0:T(8,128)(2,1)S(1)}, bf16[400,512]{1,0:T(8,128)(2,1)S(1)}, u32[]{:S(2)}, u32[]{:S(2)}) collective-permute-start(bf16[400,512]{1,0:T(8,128)(2,1)S(1)} %add_convert_fusion.2), channel_id=1, source_target_pairs={{0,4},{1,5},{2,6},{3,7},{8,12},{9,13},{10,14},{11,15},{16,20},{17,... | collective-permute-start | bytes 1228808 | tf_op jit(solution)/shard_map/ppermute | solution.py:477
  186.3 5.0 %collective-permute-start.35 = (bf16[400,512]{1,0:T(8,128)(2,1)S(1)}, bf16[400,512]{1,0:T(8,128)(2,1)S(1)}, u32[]{:S(2)}, u32[]{:S(2)}) collective-permute-start(bf16[400,512]{1,0:T(8,128)(2,1)S(1)} %add_convert_fusion), channel_id=1, source_target_pairs={{0,6},{1,7},{8,14},{9,15},{16,22},{17,23},{24,30},{25,31}} | collective-permute-start | bytes 1228808 | tf_op jit(solution)/shard_map/ppermute | solution.py:477
  194.8 19.9 %collective-permute-done.29.refs_8_ = bf16[400,512]{1,0:T(8,128)(2,1)S(1)} collective-permute-done((bf16[400,512]{1,0:T(8,128)(2,1)S(1)}, bf16[400,512]{1,0:T(8,128)(2,1)S(1)}, u32[]{:S(2)}, u32[]{:S(2)}) %collective-permute-start.29) | collective-permute-done | bytes 409632 | tf_op jit(solution)/shard_map/ppermute | solution.py:476
  (139 shorter events, 53.7 us)
Async XLA Ops:
  22.4 23.7 %collective-permute-start.3 = (bf16[400,256]{1,0:T(8,128)(2,1)}, bf16[400,256]{1,0:T(8,128)(2,1)}, u32[]{:S(2)}, u32[]{:S(2)}) collective-permute-start(bf16[400,256]{1,0:T(8,128)(2,1)} %get-tuple-element.259), channel_id=1, source_target_pairs={{0,8},{8,0},{16,24},{24,16},{1,9},{9,1},{17,25},{25,17},{2,10},{10... | collective-permute-start | bytes 614408 | tf_op jit(solution)/shard_map/ppermute | solution.py:365
  48.2 36.9 %collective-permute-start.16 = (bf16[400,512]{1,0:T(8,128)(2,1)S(1)}, bf16[400,512]{1,0:T(8,128)(2,1)S(1)}, u32[]{:S(2)}, u32[]{:S(2)}) collective-permute-start(bf16[400,512]{1,0:T(8,128)(2,1)S(1)} %pad_maximum_fusion.table.refs_0_), channel_id=1, source_target_pairs={{0,1},{1,0},{2,3},{3,2},{4,5},{5,4},{6,7},{7,6},{8,9},{9,8},{10,11... | collective-permute-start | bytes 1228808 | tf_op jit(solution)/shard_map/ppermute | solution.py:448
  48.3 28.2 %collective-permute-start.4 = (bf16[400,512]{1,0:T(8,128)(2,1)S(1)}, bf16[400,512]{1,0:T(8,128)(2,1)S(1)}, u32[]{:S(2)}, u32[]{:S(2)}) collective-permute-start(bf16[400,512]{1,0:T(8,128)(2,1)S(1)} %pad_maximum_fusion.table.refs_0_), channel_id=1, source_target_pairs={{0,2},{1,3},{2,4},{3,5},{4,6},{5,7},{8,10},{9,11},{10,12},{11,13},... | collective-permute-start | bytes 1228808 | tf_op jit(solution)/shard_map/ppermute | solution.py:459
  51.8 24.8 %collective-permute-start.7 = (bf16[400,512]{1,0:T(8,128)(2,1)S(1)}, bf16[400,512]{1,0:T(8,128)(2,1)S(1)}, u32[]{:S(2)}, u32[]{:S(2)}) collective-permute-start(bf16[400,512]{1,0:T(8,128)(2,1)S(1)} %pad_maximum_fusion.table.refs_0_), channel_id=1, source_target_pairs={{2,0},{3,1},{4,2},{5,3},{6,4},{7,5},{10,8},{11,9},{12,10},{13,11},... | collective-permute-start | bytes 1228808 | tf_op jit(solution)/shard_map/ppermute | solution.py:460
  54.0 18.8 %collective-permute-start.17 = (bf16[400,256]{1,0:T(8,128)(2,1)S(1)}, bf16[400,256]{1,0:T(8,128)(2,1)S(1)}, u32[]{:S(2)}, u32[]{:S(2)}) collective-permute-start(bf16[400,256]{1,0:T(8,128)(2,1)S(1)} %slice.14), channel_id=1, source_target_pairs={{0,8},{8,0},{16,24},{24,16},{1,9},{9,1},{17,25},{25,17},{2,10},{10... | collective-permute-start | bytes 614408 | tf_op jit(solution)/shard_map/ppermute | solution.py:365
  54.6 16.7 %collective-permute-start.21 = (f32[1,512]{1,0:T(1,128)S(1)}, f32[1,512]{1,0:T(1,128)S(1)}, u32[]{:S(2)}, u32[]{:S(2)}) collective-permute-start(f32[1,512]{1,0:T(1,128)S(1)} %bitcast.77), channel_id=1, source_target_pairs={{0,8},{8,0},{16,24},{24,16},{1,9},{9,1},{17,25},{25,17},{2,10},{10... | collective-permute-start | bytes 6152 | tf_op jit(solution)/shard_map/ppermute | solution.py:365
  76.5 22.1 %collective-permute-start.14 = (bf16[400,512]{1,0:T(8,128)(2,1)S(1)}, bf16[400,512]{1,0:T(8,128)(2,1)S(1)}, u32[]{:S(2)}, u32[]{:S(2)}) collective-permute-start(bf16[400,512]{1,0:T(8,128)(2,1)S(1)} %collective-permute-done.4.refs_0_), channel_id=1, source_target_pairs={{0,1},{1,0},{2,3},{3,2},{4,5},{5,4},{6,7},{7,6},{8,9},{9,8},{10,11... | collective-permute-start | bytes 1228808 | tf_op jit(solution)/shard_map/ppermute | solution.py:464
  76.6 19.4 %collective-permute-start.5 = (bf16[400,512]{1,0:T(8,128)(2,1)S(1)}, bf16[400,512]{1,0:T(8,128)(2,1)S(1)}, u32[]{:S(2)}, u32[]{:S(2)}) collective-permute-start(bf16[400,512]{1,0:T(8,128)(2,1)S(1)} %collective-permute-done.4.refs_0_), channel_id=1, source_target_pairs={{2,4},{3,5},{4,6},{5,7},{10,12},{11,13},{12,14},{13,15},{18,20},{1... | collective-permute-start | bytes 1228808 | tf_op jit(solution)/shard_map/ppermute | solution.py:459
  80.9 18.5 %collective-permute-start.15 = (bf16[400,512]{1,0:T(8,128)(2,1)S(1)}, bf16[400,512]{1,0:T(8,128)(2,1)S(1)}, u32[]{:S(2)}, u32[]{:S(2)}) collective-permute-start(bf16[400,512]{1,0:T(8,128)(2,1)S(1)} %collective-permute-done.7.refs_1_), channel_id=1, source_target_pairs={{0,1},{1,0},{2,3},{3,2},{4,5},{5,4},{6,7},{7,6},{8,9},{9,8},{10,11... | collective-permute-start | bytes 1228808 | tf_op jit(solution)/shard_map/ppermute | solution.py:465
  83.7 15.5 %collective-permute-start.8 = (bf16[400,512]{1,0:T(8,128)(2,1)S(1)}, bf16[400,512]{1,0:T(8,128)(2,1)S(1)}, u32[]{:S(2)}, u32[]{:S(2)}) collective-permute-start(bf16[400,512]{1,0:T(8,128)(2,1)S(1)} %collective-permute-done.7.refs_1_), channel_id=1, source_target_pairs={{2,0},{3,1},{4,2},{5,3},{10,8},{11,9},{12,10},{13,11},{18,16},{19,... | collective-permute-start | bytes 1228808 | tf_op jit(solution)/shard_map/ppermute | solution.py:460
  85.1 92.7 %collective-permute-start.20 = (bf16[400,256]{1,0:T(8,128)(2,1)S(1)}, bf16[400,256]{1,0:T(8,128)(2,1)S(1)}, u32[]{:S(2)}, u32[]{:S(2)}) collective-permute-start(bf16[400,256]{1,0:T(8,128)(2,1)S(1)} %get-tuple-element.255), channel_id=1, source_target_pairs={{0,8},{8,0},{16,24},{24,16},{1,9},{9,1},{17,25},{25,17},{2,10},{10... | collective-permute-start | bytes 614408 | tf_op jit(solution)/shard_map/ppermute | solution.py:365
  95.9 16.7 %collective-permute-start.12 = (bf16[400,512]{1,0:T(8,128)(2,1)S(1)}, bf16[400,512]{1,0:T(8,128)(2,1)S(1)}, u32[]{:S(2)}, u32[]{:S(2)}) collective-permute-start(bf16[400,512]{1,0:T(8,128)(2,1)S(1)} %collective-permute-done.5.refs_0_), channel_id=1, source_target_pairs={{0,1},{1,0},{2,3},{3,2},{4,5},{5,4},{6,7},{7,6},{8,9},{9,8},{10,11... | collective-permute-start | bytes 1228808 | tf_op jit(solution)/shard_map/ppermute | solution.py:464
  98.6 15.4 %collective-permute-start.6 = (bf16[400,512]{1,0:T(8,128)(2,1)S(1)}, bf16[400,512]{1,0:T(8,128)(2,1)S(1)}, u32[]{:S(2)}, u32[]{:S(2)}) collective-permute-start(bf16[400,512]{1,0:T(8,128)(2,1)S(1)} %collective-permute-done.5.refs_0_), channel_id=1, source_target_pairs={{4,6},{5,7},{12,14},{13,15},{20,22},{21,23},{28,30},{29,31}} | collective-permute-start | bytes 1228808 | tf_op jit(solution)/shard_map/ppermute | solution.py:459
  99.4 16.9 %collective-permute-start.9 = (bf16[400,512]{1,0:T(8,128)(2,1)S(1)}, bf16[400,512]{1,0:T(8,128)(2,1)S(1)}, u32[]{:S(2)}, u32[]{:S(2)}) collective-permute-start(bf16[400,512]{1,0:T(8,128)(2,1)S(1)} %collective-permute-done.8.refs_1_), channel_id=1, source_target_pairs={{2,0},{3,1},{10,8},{11,9},{18,16},{19,17},{26,24},{27,25}} | collective-permute-start | bytes 1228808 | tf_op jit(solution)/shard_map/ppermute | solution.py:460
  112.7 72.3 %collective-permute-start.23 = (bf16[400,512]{1,0:T(8,128)(2,1)S(1)}, bf16[400,512]{1,0:T(8,128)(2,1)S(1)}, u32[]{:S(2)}, u32[]{:S(2)}) collective-permute-start(bf16[400,512]{1,0:T(8,128)(2,1)S(1)} %get-tuple-element.49), channel_id=1, source_target_pairs={{0,1},{1,0},{2,3},{3,2},{4,5},{5,4},{6,7},{7,6},{8,9},{9,8},{10,11... | collective-permute-start | bytes 1228808 | tf_op jit(solution)/shard_map/ppermute | solution.py:452
  113.9 42.3 %collective-permute-start.26 = (bf16[400,512]{1,0:T(8,128)(2,1)S(1)}, bf16[400,512]{1,0:T(8,128)(2,1)S(1)}, u32[]{:S(2)}, u32[]{:S(2)}) collective-permute-start(bf16[400,512]{1,0:T(8,128)(2,1)S(1)} %get-tuple-element.53), channel_id=1, source_target_pairs={{0,1},{1,0},{2,3},{3,2},{4,5},{5,4},{6,7},{7,6},{8,9},{9,8},{10,11... | collective-permute-start | bytes 1228808 | tf_op jit(solution)/shard_map/ppermute | solution.py:473
  128.8 28.8 %collective-permute-start.24 = (bf16[400,512]{1,0:T(8,128)(2,1)S(1)}, bf16[400,512]{1,0:T(8,128)(2,1)S(1)}, u32[]{:S(2)}, u32[]{:S(2)}) collective-permute-start(bf16[400,512]{1,0:T(8,128)(2,1)S(1)} %get-tuple-element.51), channel_id=1, source_target_pairs={{0,1},{1,0},{2,3},{3,2},{4,5},{5,4},{6,7},{7,6},{8,9},{9,8},{10,11... | collective-permute-start | bytes 1228808 | tf_op jit(solution)/shard_map/ppermute | solution.py:472
  128.9 32.7 %collective-permute-start.30 = (bf16[400,512]{1,0:T(8,128)(2,1)S(1)}, bf16[400,512]{1,0:T(8,128)(2,1)S(1)}, u32[]{:S(2)}, u32[]{:S(2)}) collective-permute-start(bf16[400,512]{1,0:T(8,128)(2,1)S(1)} %get-tuple-element.57), channel_id=1, source_target_pairs={{0,1},{1,0},{2,3},{3,2},{4,5},{5,4},{6,7},{7,6},{8,9},{9,8},{10,11... | collective-permute-start | bytes 1228808 | tf_op jit(solution)/shard_map/ppermute | solution.py:473
  171.3 15.0 %collective-permute-start.27 = (bf16[400,512]{1,0:T(8,128)(2,1)S(1)}, bf16[400,512]{1,0:T(8,128)(2,1)S(1)}, u32[]{:S(2)}, u32[]{:S(2)}) collective-permute-start(bf16[400,512]{1,0:T(8,128)(2,1)S(1)} %add_convert_fusion.4), channel_id=1, source_target_pairs={{0,2},{1,3},{2,4},{3,5},{4,6},{5,7},{8,10},{9,11},{10,12},{11,13},... | collective-permute-start | bytes 1228808 | tf_op jit(solution)/shard_map/ppermute | solution.py:477
  175.3 18.0 %collective-permute-start.25 = (bf16[400,512]{1,0:T(8,128)(2,1)S(1)}, bf16[400,512]{1,0:T(8,128)(2,1)S(1)}, u32[]{:S(2)}, u32[]{:S(2)}) collective-permute-start(bf16[400,512]{1,0:T(8,128)(2,1)S(1)} %add_convert_fusion.5), channel_id=1, source_target_pairs={{2,0},{3,1},{4,2},{5,3},{6,4},{7,5},{10,8},{11,9},{12,10},{13,11},... | collective-permute-start | bytes 1228808 | tf_op jit(solution)/shard_map/ppermute | solution.py:476
  177.8 17.0 %collective-permute-start.31 = (bf16[400,512]{1,0:T(8,128)(2,1)S(1)}, bf16[400,512]{1,0:T(8,128)(2,1)S(1)}, u32[]{:S(2)}, u32[]{:S(2)}) collective-permute-start(bf16[400,512]{1,0:T(8,128)(2,1)S(1)} %add_convert_fusion.2), channel_id=1, source_target_pairs={{0,4},{1,5},{2,6},{3,7},{8,12},{9,13},{10,14},{11,15},{16,20},{17,... | collective-permute-start | bytes 1228808 | tf_op jit(solution)/shard_map/ppermute | solution.py:477
  185.0 29.7 %collective-permute-start.29 = (bf16[400,512]{1,0:T(8,128)(2,1)S(1)}, bf16[400,512]{1,0:T(8,128)(2,1)S(1)}, u32[]{:S(2)}, u32[]{:S(2)}) collective-permute-start(bf16[400,512]{1,0:T(8,128)(2,1)S(1)} %add_convert_fusion.3), channel_id=1, source_target_pairs={{4,0},{5,1},{6,2},{7,3},{12,8},{13,9},{14,10},{15,11},{20,16},{21,... | collective-permute-start | bytes 1228808 | tf_op jit(solution)/shard_map/ppermute | solution.py:476
  186.3 28.4 %collective-permute-start.35 = (bf16[400,512]{1,0:T(8,128)(2,1)S(1)}, bf16[400,512]{1,0:T(8,128)(2,1)S(1)}, u32[]{:S(2)}, u32[]{:S(2)}) collective-permute-start(bf16[400,512]{1,0:T(8,128)(2,1)S(1)} %add_convert_fusion), channel_id=1, source_target_pairs={{0,6},{1,7},{8,14},{9,15},{16,22},{17,23},{24,30},{25,31}} | collective-permute-start | bytes 1228808 | tf_op jit(solution)/shard_map/ppermute | solution.py:477
  191.3 23.4 %collective-permute-start.33 = (bf16[400,512]{1,0:T(8,128)(2,1)S(1)}, bf16[400,512]{1,0:T(8,128)(2,1)S(1)}, u32[]{:S(2)}, u32[]{:S(2)}) collective-permute-start(bf16[400,512]{1,0:T(8,128)(2,1)S(1)} %add_convert_fusion.1), channel_id=1, source_target_pairs={{6,0},{7,1},{14,8},{15,9},{22,16},{23,17},{30,24},{31,25}} | collective-permute-start | bytes 1228808 | tf_op jit(solution)/shard_map/ppermute | solution.py:476
  (36 other events, 371.9 us)

commit v2 on v1

v2 whole, which is shorter than its diff:
```python
import math

import jax
import jax.numpy as jnp
from jax import lax
from jax.experimental import pallas as pl
from jax.experimental.pallas import tpu as pltpu
from jax.sharding import PartitionSpec as P

BLOCK = 128
QMAX = 2
QTOTAL = 12
NNEG = QTOTAL * BLOCK
CORES = 2
LEARN_RATE = 0.1
REL_RATE = 0.02


bf16 = jnp.bfloat16
f32 = jnp.float32
MIB = 2**20


def dot_nn(lhs, rhs):
    return lax.dot_general(lhs, rhs, (((1,), (0,)), ((), ())), preferred_element_type=f32)


def dot_nt(lhs, rhs):
    return lax.dot_general(lhs, rhs, (((1,), (1,)), ((), ())), preferred_element_type=f32)


def split2(value):
    high = value.astype(bf16)
    return high, (value - high.astype(f32)).astype(bf16)


def select_rows(ids, rows):
    places = lax.broadcasted_iota(jnp.int32, (rows, ids.shape[1]), 0)
    return jnp.where(places == ids, 1.0, 0.0).astype(bf16)


def product(one, other):
    half = one.shape[0] // 2
    a, b, c, d = one[:half], one[half:], other[:half], other[half:]
    return jnp.concatenate([a * c - b * d, a * d + b * c], axis=0)


def back(grad, value):
    half = grad.shape[0] // 2
    a, b, c, d = grad[:half], grad[half:], value[:half], value[half:]
    return jnp.concatenate([a * c + b * d, b * c - a * d], axis=0)


def whole(shape):
    return pl.BlockSpec(shape, lambda *_: (0,) * len(shape))


def lanes(rows, width):
    return pl.BlockSpec((rows, width), lambda i, *_: (0, i))


def params(mib):
    return pltpu.CompilerParams(
        vmem_limit_bytes=mib * MIB, dimension_semantics=("arbitrary",)
    )


def in_hbm(array):
    return pltpu.with_memory_space_constraint(array, pltpu.HBM)


def cost(flops, moved):
    return pl.CostEstimate(flops=int(flops), bytes_accessed=int(moved), transcendentals=0)


def split_relation(relation):
    high = lax.reduce_precision(relation, 8, 7)
    rest = relation - high
    mid = lax.reduce_precision(rest, 8, 7)
    low = rest - mid
    parts = jnp.concatenate([high, mid, low], axis=1).astype(bf16)
    return jnp.pad(parts, ((0, 0), (0, (-parts.shape[1]) % 128)))


def relation_rows(rel_parts, ids, count):
    width = rel_parts.shape[1]
    places = lax.broadcasted_iota(jnp.int32, (width, ids.shape[1]), 0)
    hit = jnp.logical_and(places % count == ids, places < 3 * count)
    return dot_nn(rel_parts, jnp.where(hit, 1.0, 0.0).astype(bf16))


def make_queries(src_table, rel_parts, src_ids, rel_ids, rel_count, chunk):
    dim, rows = src_table.shape
    edges = src_ids.shape[1]

    def body(table, parts, src, rel, query, query_b, high, low):
        @pl.when(pl.program_id(0) == 0)
        def _():
            high[...], low[...] = split2(table[...])

        pick = select_rows(src[...], rows)
        src_rows = dot_nn(high[...], pick) + dot_nn(low[...], pick)
        value = product(src_rows, relation_rows(parts[...], rel[...], rel_count))
        query[...] = value
        query_b[...] = value.astype(bf16)

    return pl.pallas_call(
        body,
        name="make_queries",
        grid=(edges // chunk,),
        in_specs=[whole((dim, rows)), whole(rel_parts.shape), lanes(1, chunk), lanes(1, chunk)],
        out_specs=[lanes(dim, chunk), lanes(dim, chunk)],
        out_shape=[pltpu.HBM((dim, edges), f32), pltpu.HBM((dim, edges), bf16)],
        scratch_shapes=[pltpu.VMEM((dim, rows), bf16)] * 2,
        compiler_params=params(16),
        cost_estimate=cost(4 * dim * rows * edges, 6 * dim * edges),
    )(src_table, rel_parts, src_ids, rel_ids)


def positives(part_high, query, dst_ids, chunk):
    dim, rows = part_high.shape
    edges = dst_ids.shape[1]

    def body(table, query_in, dst, query_grad, dst_grad):
        @pl.when(pl.program_id(0) == 0)
        def _():
            dst_grad[...] = jnp.zeros_like(dst_grad)

        pick = select_rows(dst[...], rows)
        dst_rows = dot_nn(table[...], pick)
        value = query_in[...]
        positive = jnp.sum(value * dst_rows, axis=0, keepdims=True)
        coef = -jax.nn.sigmoid(-positive)
        query_grad[...] = coef * dst_rows
        high, low = split2(coef * value)
        dst_grad[...] += dot_nt(high, pick) + dot_nt(low, pick)

    return pl.pallas_call(
        body,
        name="positives",
        grid=(edges // chunk,),
        in_specs=[whole((dim, rows)), lanes(dim, chunk), lanes(1, chunk)],
        out_specs=[lanes(dim, chunk), whole((dim, rows))],
        out_shape=[pltpu.HBM((dim, edges), f32), jax.ShapeDtypeStruct((dim, rows), f32)],
        compiler_params=params(16),
        cost_estimate=cost(6 * dim * rows * edges, 8 * dim * edges),
    )(part_high, in_hbm(query), dst_ids)


def negative_wave(tables, shifts, here, quota, neg_ids, query_b, query_grad, chunk):
    count = len(tables)
    dim, rows = tables[0].shape
    edges = query_b.shape[1]
    edge_count = neg_ids.shape[0]
    half_weight = 0.5 / math.sqrt(NNEG)
    own = [s for s in range(count) if shifts[s][0]]
    others = [s for s in range(count) if not shifts[s][0]]

    def body(here_ref, quota_ref, *refs):
        table_refs = refs[:count]
        ids, query_ref, grad_in, grad_out = refs[count : count + 4]
        own_refs = refs[count + 4 : count + 4 + len(own)]
        other_ref, neg, neg_t, neg_grad = refs[count + 4 + len(own) :]

        place = here_ref[0]
        across = place + 1 - 2 * (place % CORES)
        live, at, base = [], [], [jnp.int32(0)]
        for lane, shift in shifts:
            spot = (place if lane else across) + shift
            inside = jnp.logical_and(spot >= 0, spot < edge_count)
            spot = jnp.clip(spot, 0, edge_count - 1)
            at.append(spot)
            live.append(jnp.where(inside, quota_ref[0, spot], 0))
            base.append(base[-1] + live[-1])
        total = base[-1]

        step = pl.program_id(0)

        def picks(s, wide):
            parts = [select_rows(ids[at[s], b : b + 1, :], rows) for b in range(wide)]
            return jnp.concatenate(parts, axis=1) if wide > 1 else parts[0]

        def when_live(s, wide):
            return pl.when(jnp.logical_and(live[s] == wide, step == 0))

        def when_done(s, wide):
            return pl.when(jnp.logical_and(live[s] == wide, step == pl.num_programs(0) - 1))

        for s in range(count):
            for wide in range(1, QMAX + 1):

                @when_live(s, wide)
                def _(s=s, wide=wide):
                    value = dot_nn(table_refs[s][...], picks(s, wide))
                    for b in range(wide):
                        part = value[:, b * BLOCK : (b + 1) * BLOCK]
                        neg[base[s] + b] = part.astype(bf16)
                        neg_t[base[s] + b] = part.T.astype(bf16)
                        neg_grad[base[s] + b] = jnp.zeros((dim, BLOCK), f32)

        @pl.when(jnp.logical_and(total % 2 == 1, step == 0))
        def _():
            neg[total] = jnp.zeros((dim, BLOCK), bf16)
            neg_t[total] = jnp.zeros((BLOCK, dim), bf16)
            neg_grad[total] = jnp.zeros((dim, BLOCK), f32)

        @pl.when(total == 0)
        def _():
            grad_out[...] = grad_in[...]

        def pair(p, carry):
            left, right = 2 * p, 2 * p + 1
            columns = jnp.concatenate([neg[left], neg[right]], axis=1)
            columns_t = jnp.concatenate([neg_t[left], neg_t[right]], axis=0)
            query = query_ref[...]
            scores = dot_nn(columns_t, query)
            coef = (half_weight * jnp.tanh(0.5 * scores) + half_weight).astype(bf16)
            before = jnp.where(p == 0, grad_in[...], grad_out[...])
            grad_out[...] = before + dot_nn(columns, coef)
            added = dot_nt(query, coef)
            neg_grad[left] += added[:, :BLOCK]
            neg_grad[right] += added[:, BLOCK:]
            return carry

        lax.fori_loop(0, (total + 1) // 2, pair, 0)

        for s in range(count):

            def put(value, s=s):
                if s in own:
                    own_refs[own.index(s)][...] = value
                else:
                    other_ref[others.index(s)] = value

            @when_done(s, 0)
            def _(put=put):
                put(jnp.zeros((dim, rows), bf16))

            for wide in range(1, QMAX + 1):

                @when_done(s, wide)
                def _(s=s, wide=wide, put=put):
                    parts = [neg_grad[base[s] + b] for b in range(wide)]
                    value = jnp.concatenate(parts, axis=1) if wide > 1 else parts[0]
                    high, low = split2(value)
                    pick = picks(s, wide)
                    put((dot_nt(high, pick) + dot_nt(low, pick)).astype(bf16))

    slots = QMAX * count
    smem = pl.BlockSpec(memory_space=pltpu.SMEM)
    shard = jax.ShapeDtypeStruct((dim, rows), bf16)
    return pl.pallas_call(
        body,
        grid=(edges // chunk,),
        in_specs=[smem, smem]
        + [whole((dim, rows))] * count
        + [whole(neg_ids.shape), lanes(dim, chunk), lanes(dim, chunk)],
        out_specs=[lanes(dim, chunk)]
        + [whole((dim, rows))] * len(own)
        + [whole((len(others), dim, rows))],
        scratch_shapes=[
            pltpu.VMEM((slots, dim, BLOCK), bf16),
            pltpu.VMEM((slots, BLOCK, dim), bf16),
            pltpu.VMEM((slots, dim, BLOCK), f32),
        ],
        out_shape=[pltpu.HBM((dim, edges), f32)]
        + [shard] * len(own)
        + [jax.ShapeDtypeStruct((len(others), dim, rows), bf16)],
        input_output_aliases={count + 4: 0},
        compiler_params=params(32),
        cost_estimate=cost(6 * dim * 1.5 * count * BLOCK * edges, 10 * dim * edges),
    )(here, quota, *tables, neg_ids, in_hbm(query_b), in_hbm(query_grad))


def source_side(src_table, src_state, rel_parts, src_ids, rel_ids, query_grad, rel_count, chunk):
    dim, rows = src_table.shape
    edges = src_ids.shape[1]

    def body(table, state, parts, src, rel, grad_in, out, state_out, rel_out, high, low, acc):
        step = pl.program_id(0)

        @pl.when(step == 0)
        def _():
            high[...], low[...] = split2(table[...])
            acc[...] = jnp.zeros_like(acc)
            rel_out[...] = jnp.zeros_like(rel_out)

        pick = select_rows(src[...], rows)
        src_rows = dot_nn(high[...], pick) + dot_nn(low[...], pick)
        grad = grad_in[...]
        upper, lower = split2(back(grad, relation_rows(parts[...], rel[...], rel_count)))
        acc[...] += dot_nt(upper, pick) + dot_nt(lower, pick)
        kinds = select_rows(rel[...], rel_count)
        upper, lower = split2(back(grad, src_rows))
        rel_out[...] += dot_nt(kinds, upper) + dot_nt(kinds, lower)

        @pl.when(step == pl.num_programs(0) - 1)
        def _():
            total = acc[...]
            new_state = state[...] + jnp.sum(total * total, axis=0, keepdims=True) / dim
            state_out[...] = new_state
            out[...] = table[...] - LEARN_RATE * total / jnp.sqrt(new_state)

    return pl.pallas_call(
        body,
        name="source_side",
        grid=(edges // chunk,),
        in_specs=[
            whole((dim, rows)),
            whole((1, rows)),
            whole(rel_parts.shape),
            lanes(1, chunk),
            lanes(1, chunk),
            lanes(dim, chunk),
        ],
        out_specs=[whole((dim, rows)), whole((1, rows)), whole((rel_count, dim))],
        out_shape=[
            jax.ShapeDtypeStruct((dim, rows), f32),
            jax.ShapeDtypeStruct((1, rows), f32),
            jax.ShapeDtypeStruct((rel_count, dim), f32),
        ],
        scratch_shapes=[pltpu.VMEM((dim, rows), bf16)] * 2 + [pltpu.VMEM((dim, rows), f32)],
        compiler_params=params(16),
        cost_estimate=cost(8 * dim * rows * edges, 4 * dim * edges),
    )(src_table, src_state, rel_parts, src_ids, rel_ids, in_hbm(query_grad))


def destination_side(high, low_state, own_grad, grads):
    dim, rows = own_grad.shape
    count = len(grads)

    def body(*refs):
        high_ref, low_ref, own_ref = refs[:3]
        out, state_out = refs[3 + count :]
        total = own_ref[...]
        for ref in refs[3 : 3 + count]:
            total = total + (ref[0] if len(ref.shape) == 3 else ref[...]).astype(f32)
        packed = low_ref[...].astype(f32)
        state = packed[dim : dim + 1] + packed[dim + 1 : dim + 2] + packed[dim + 2 : dim + 3]
        new_state = state + jnp.sum(total * total, axis=0, keepdims=True) / dim
        state_out[...] = new_state
        table = high_ref[...].astype(f32) + packed[:dim]
        out[...] = table - LEARN_RATE * total / jnp.sqrt(new_state)

    width = min(rows, 128)

    def column(array):
        if array.ndim == 3:
            return pl.BlockSpec((1, dim, width), lambda i: (0, 0, i))
        return lanes(array.shape[0], width)

    operands = [high, low_state, own_grad, *grads]
    return pl.pallas_call(
        body,
        name="destination_side",
        grid=(rows // width,),
        in_specs=[column(array) for array in operands],
        out_specs=[lanes(dim, width), lanes(1, width)],
        out_shape=[
            jax.ShapeDtypeStruct((dim, rows), f32),
            jax.ShapeDtypeStruct((1, rows), f32),
        ],
        compiler_params=params(16),
        cost_estimate=cost(8 * dim * rows, (12 + 2 * count) * dim * rows),
    )(*operands)


def split_table(table, state):
    dim, rows = table.shape
    half = rows // 2
    tail = 16

    def body(table_ref, state_ref, left, right, rest):
        value = table_ref[...]
        high, low = split2(value)
        left[...] = high[:, :half]
        right[...] = high[:, half:]
        rest[:dim] = low
        first, _ = split2(state_ref[...])
        left_over = state_ref[...] - first.astype(f32)
        second, third = split2(left_over)
        parts = [first.astype(f32), second.astype(f32), third.astype(f32)]
        parts.append(jnp.zeros((tail - 3, rows), f32))
        rest[dim:] = jnp.concatenate(parts, axis=0).astype(bf16)

    return pl.pallas_call(
        body,
        name="split_table",
        in_specs=[pl.BlockSpec(memory_space=pltpu.VMEM)] * 2,
        out_specs=[pl.BlockSpec(memory_space=pltpu.VMEM)] * 3,
        out_shape=[
            jax.ShapeDtypeStruct((dim, half), bf16),
            jax.ShapeDtypeStruct((dim, rows - half), bf16),
            jax.ShapeDtypeStruct((dim + tail, rows), bf16),
        ],
        compiler_params=pltpu.CompilerParams(vmem_limit_bytes=16 * MIB),
        cost_estimate=cost(4 * dim * rows, 8 * dim * rows),
    )(table, state)


def grid_of(count):
    across = math.isqrt(count)
    while count % across:
        across -= 1
    return count // across, across


def moved(device, n, stride, shift):
    place = (device // stride) % n
    return device + ((place + shift) % n - place) * stride


def shifted(array, n, stride, shift):
    count = lax.axis_size("dom")
    return lax.ppermute(array, "dom", [(d, moved(d, n, stride, shift)) for d in range(count)])


def copy_chosen(index, options, out, columns):
    for k in range(len(options)):

        @pl.when(index == k)
        def _(k=k):
            out[:, columns] = options[k][...]


def route(values, matching, here):
    down, across = grid_of(lax.axis_size("dom"))
    axes = [(across, 1), (down, across)]
    orders = [axes, axes[::-1]][: len(values)]
    rows = values[0].shape[0]
    widths = [value.shape[1] for value in values]
    starts = [sum(widths[:i]) for i in range(len(widths))]
    vmem = pl.BlockSpec(memory_space=pltpu.VMEM)
    smem = pl.BlockSpec(memory_space=pltpu.SMEM)

    held = []
    for i, ((n1, stride1), _) in enumerate(orders):
        held.append([values[i]] + [shifted(values[i], n1, stride1, k) for k in range(1, n1)])
    flat = [array for group in held for array in group]

    def grouped(refs, groups):
        result, used = [], 0
        for group in groups:
            result.append(refs[used : used + len(group)])
            used += len(group)
        return result, refs[used:]

    def behind(place, source, n, stride):
        return ((place // stride) % n - (source // stride) % n + n) % n

    def pass_on(match_ref, here_ref, *refs):
        place = here_ref[0]
        held_refs, outs = grouped(refs, held)
        used = 0
        for i, ((n1, stride1), (n2, stride2)) in enumerate(orders):
            for m in range(1, n2):
                source = match_ref[moved(place, n2, stride2, m)]
                picked = behind(place, source, n1, stride1)
                copy_chosen(picked, held_refs[i], outs[used], slice(None))
                used += 1

    hops = [(i, m) for i in range(len(orders)) for m in range(1, orders[i][1][0])]
    passed = pl.pallas_call(
        pass_on,
        in_specs=[smem, smem] + [vmem] * len(flat),
        out_specs=[vmem] * len(hops),
        out_shape=[jax.ShapeDtypeStruct((rows, widths[i]), bf16) for i, _ in hops],
        compiler_params=pltpu.CompilerParams(vmem_limit_bytes=16 * MIB),
        cost_estimate=cost(0, 4 * rows * sum(widths)),
    )(matching, here, *flat)
    found = [[] for _ in orders]
    for (i, m), array in zip(hops, passed):
        found[i].append(shifted(array, *orders[i][1], m))
    flat_found = [array for group in found for array in group]

    def merge(match_ref, here_ref, *refs):
        place = here_ref[0]
        held_refs, rest = grouped(refs, held)
        found_refs, (out,) = grouped(rest, found)
        source = match_ref[place]
        for i, ((n1, stride1), (n2, stride2)) in enumerate(orders):
            columns = slice(starts[i], starts[i] + widths[i])
            near = behind(place, source, n1, stride1)
            far = behind(place, source, n2, stride2)
            index = jnp.where(far == 0, near, n1 - 1 + far)
            copy_chosen(index, list(held_refs[i]) + list(found_refs[i]), out, columns)

    return pl.pallas_call(
        merge,
        in_specs=[smem, smem] + [vmem] * (len(flat) + len(flat_found)),
        out_specs=vmem,
        out_shape=jax.ShapeDtypeStruct((rows, sum(widths)), bf16),
        compiler_params=pltpu.CompilerParams(vmem_limit_bytes=24 * MIB),
        cost_estimate=cost(0, 4 * rows * sum(widths)),
    )(matching, here, *flat, *flat_found)


def total_over_mesh(value):
    for axis in ("edge", "dom"):
        count = lax.axis_size(axis)
        step = 1
        while step < count:
            value = value + lax.ppermute(value, axis, [(i, i ^ step) for i in range(count)])
            step *= 2
    return value


def shards(
    src_table,
    src_state,
    dst_table,
    dst_state,
    relation,
    edge_src,
    edge_dst,
    edge_rel,
    matching,
    neg_rows,
    quotas,
):
    edge_count = lax.axis_size("edge")
    chips = edge_count // CORES
    _, row_count = src_table.shape
    rel_count = relation.shape[1]
    edges = edge_src.shape[0]
    chunk = min(edges, 512)
    wave_chunk = min(edges, 1024)
    here = lax.axis_index("edge").reshape(1).astype(jnp.int32)
    place = lax.axis_index("dom").reshape(1).astype(jnp.int32)

    src_ids = edge_src.reshape(1, edges)
    dst_ids = edge_dst.reshape(1, edges)
    rel_ids = edge_rel.reshape(1, edges)
    neg_ids = neg_rows.reshape(edge_count, QMAX, BLOCK)
    rel_parts = split_relation(relation)

    left, right, rest = split_table(dst_table, dst_state.reshape(1, row_count))
    part_high = route([left, right], matching, place)
    rest, part_high = lax.optimization_barrier((rest, part_high))
    low_state = route([rest], matching, place)

    query, query_b = make_queries(src_table, rel_parts, src_ids, rel_ids, rel_count, chunk)
    query_grad, own_grad = positives(part_high, query, dst_ids, chunk)

    swap = [(i, i ^ 1) for i in range(edge_count)]

    def swapped(array):
        return lax.ppermute(array, "edge", swap)

    query_grad, mine, theirs = negative_wave(
        [part_high, swapped(part_high)],
        [(True, 0), (False, 0)],
        here,
        quotas,
        neg_ids,
        query_b,
        query_grad,
        wave_chunk,
    )
    arrived = [mine, swapped(theirs)]

    from_below = from_above = part_high
    for s in range(1, chips):
        last = edge_count - CORES
        up = [(i, i + CORES) for i in range(CORES * (s - 1), last)]
        down = [(i + CORES, i) for i in range(0, last - CORES * (s - 1))]
        from_below = lax.ppermute(from_below, "edge", up)
        from_above = lax.ppermute(from_above, "edge", down)
        tables = [from_below, from_above, swapped(from_below), swapped(from_above)]
        far = CORES * s
        shifts = [(True, -far), (True, far), (False, -far), (False, far)]
        query_grad, below, above, theirs = negative_wave(
            tables, shifts, here, quotas, neg_ids, query_b, query_grad, wave_chunk
        )
        theirs = swapped(theirs).astype(f32)
        pairs = [(i, i - far) for i in range(far, edge_count)]
        arrived.append(lax.ppermute((below.astype(f32) + theirs[0]).astype(bf16), "edge", pairs))
        pairs = [(i, i + far) for i in range(edge_count - far)]
        arrived.append(lax.ppermute((above.astype(f32) + theirs[1]).astype(bf16), "edge", pairs))

    src_out, src_state_out, rel_grad = source_side(
        src_table,
        src_state.reshape(1, row_count),
        rel_parts,
        src_ids,
        rel_ids,
        query_grad,
        rel_count,
        chunk,
    )
    relation_out = relation - REL_RATE * total_over_mesh(rel_grad).T
    dst_out, dst_state_out = destination_side(part_high, low_state, own_grad, arrived)
    return (
        src_out,
        src_state_out.reshape(row_count),
        dst_out,
        dst_state_out.reshape(row_count),
        relation_out,
    )


def solution(mesh):
    in_specs = (
        P(None, ("dom", "edge")),
        P(("dom", "edge")),
        P(None, ("dom", "edge")),
        P(("dom", "edge")),
        P(),
        P(("dom", "edge")),
        P(("dom", "edge")),
        P(("dom", "edge")),
        P(),
        P(("dom", "edge"), None, None),
        P(("dom", "edge"), None),
    )
    out_specs = (
        P(None, ("dom", "edge")),
        P(("dom", "edge")),
        P(None, ("dom", "edge")),
        P(("dom", "edge")),
        P(),
    )

    return jax.shard_map(shards, mesh=mesh, in_specs=in_specs, out_specs=out_specs, check_vma=False)
```

time: 218 us -> 184 us (0.84)
  waiting for transfers between devices: 50.7 us -> 36.9 us
  local copies, waits for them, and re-layouts: 17.2 us -> 4.02 us
  between operations: 12 us -> 1.04 us
  Pallas kernels: 77.7 us -> 88.6 us
  other arithmetic: 7.34 us -> 2.99 us
  starting transfers between devices: 52.4 us -> 49.6 us
    unnamed x38 -> x24, local copies, waits for them, and re-layouts: 13.7 us -> 3.17 us
    ppermute x30 -> x23, waiting for transfers between devices: 38.7 us -> 29.7 us  [the longest x3 19.9 us: shards(): lax.ppermute((below.astype(f32) + theirs[0]).astype(bf16), 'edge', pairs)]
    ppermute x30 -> x23, starting transfers between devices: 38.2 us -> 29.4 us  [the longest x3 13.3 us: shards(): lax.ppermute((above.astype(f32) + theirs[1]).astype(bf16), 'edge', pairs)]
    pallas_call x4 -> x9, Pallas kernels: 43.7 us -> 51.3 us  [the longest x4 48.7 us: negative_wave(): pl.pallas_call(body, grid=(edges // chunk,), in_specs=[smem, smem] + [who...]
    ppermute x5, starting transfers between devices: 5.27 us -> 10.2 us  [total_over_mesh(): lax.ppermute(value, axis, [(i, i ^ step) for i in range(count)])]
    ppermute x5, waiting for transfers between devices: 10.2 us -> 5.85 us  [total_over_mesh(): lax.ppermute(value, axis, [(i, i ^ step) for i in range(count)])]
    another operation x5 -> x0, local copies, waits for them, and re-layouts: 2.36 us -> none  [the longest x1 1.36 us: wanted_by(): source = jnp.take(matching, device)]
    select_n x8 -> x0, other arithmetic: 2.22 us -> none  [choose(): result = jnp.where(index == k, options[k], result)]
  transfers between devices with their start and end apart: 41 -> 34, of which waited for: 13 -> 11; matrix products, arithmetic and copies ran while one was open for 3% -> 2% of each run, Pallas kernels for 35% -> 46%
where the time goes in v2:
time: 184 us; the launch traced here: 183 us
  Pallas kernels  88.6 us (48%)
  starting transfers between devices  49.6 us (27%)
  waiting for transfers between devices  36.9 us (20%)
  local copies, waits for them, and re-layouts  4.02 us (2%)
  other arithmetic  2.99 us (2%)
    pallas_call x4, Pallas kernels, negative_wave(): pl.pallas_call(body, grid=(edges // chunk,), in_specs=[smem, smem] + [who...  48.7 us
    ppermute x3, waiting for transfers between devices, shards(): lax.ppermute((below.astype(f32) + theirs[0]).astype(bf16), 'edge', pairs)  19.9 us
    pallas_call x1, Pallas kernels, source_side(): pl.pallas_call(body, name='source_side', grid=(edges // chunk,), in_specs...  15.5 us
    ppermute x3, starting transfers between devices, shards(): lax.ppermute((above.astype(f32) + theirs[1]).astype(bf16), 'edge', pairs)  13.3 us
    pallas_call x1, Pallas kernels, positives(): pl.pallas_call(body, name='positives', grid=(edges // chunk,), in_specs=[...  10.6 us
    ppermute x5, starting transfers between devices, total_over_mesh(): lax.ppermute(value, axis, [(i, i ^ step) for i in range(count)])  10.2 us
    ppermute x6, waiting for transfers between devices, shifted(): lax.ppermute(array, 'dom', [(d, moved(d, n, stride, shift)) for d in rang...  8.77 us
    pallas_call x1, Pallas kernels, make_queries(): pl.pallas_call(body, name='make_queries', grid=(edges // chunk,), in_spec...  8.45 us
  transfers between devices with their start and end apart: 34, of which 11 were waited for; matrix products, arithmetic and copies ran while one was open for 2% of the time, Pallas kernels for 46%

profile of v2, /device:TPU:0, one launch (start us, length us, event | category | flops | bytes accessed | tf_op | source)
XLA Modules:
  0.0 183.1 jit_solution(7527031243693278984)
XLA Ops:
  2.6 3.0 %collective-permute-start = (bf16[400,256]{1,0:T(8,128)(2,1)S(1)}, bf16[400,256]{1,0:T(8,128)(2,1)S(1)}, u32[]{:S(2)}, u32[]{:S(2)}) collective-permute-start(bf16[400,256]{1,0:T(8,128)(2,1)S(1)} %get-tuple-element.37.refs_0_), channel_id=1, source_target_pairs={{0,8},{8,0},{16,24},{24,16},{1,9},{9,1},{17,25},{25,17},{2,10},{10... | collective-permute-start | bytes 614408 | tf_op jit(solution)/shard_map/ppermute | solution.py:415
  5.6 1.5 collective-permute-start.1
  7.9 2.9 %collective-permute-done.refs_1_ = bf16[400,256]{1,0:T(8,128)(2,1)S(1)} collective-permute-done((bf16[400,256]{1,0:T(8,128)(2,1)S(1)}, bf16[400,256]{1,0:T(8,128)(2,1)S(1)}, u32[]{:S(2)}, u32[]{:S(2)}) %collective-permute-start) | collective-permute-done | bytes 204832 | tf_op jit(solution)/shard_map/ppermute | solution.py:415
  13.5 1.6 collective-permute-start.2
  16.4 2.9 %collective-permute-done.2.refs_4_ = bf16[400,256]{1,0:T(8,128)(2,1)S(1)} collective-permute-done((bf16[400,256]{1,0:T(8,128)(2,1)S(1)}, bf16[400,256]{1,0:T(8,128)(2,1)S(1)}, u32[]{:S(2)}, u32[]{:S(2)}) %collective-permute-start.2) | collective-permute-done | bytes 204832 | tf_op jit(solution)/shard_map/ppermute | solution.py:415
  23.4 4.6 %collective-permute-start.4 = (bf16[400,512]{1,0:T(8,128)(2,1)S(1)}, bf16[400,512]{1,0:T(8,128)(2,1)S(1)}, u32[]{:S(2)}, u32[]{:S(2)}) collective-permute-start(bf16[400,512]{1,0:T(8,128)(2,1)S(1)} %shard_map.147.table.refs_0_), channel_id=1, source_target_pairs={{0,2},{1,3},{2,4},{3,5},{4,6},{5,7},{8,10},{9,11},{10,12},{11,13},... | collective-permute-start | bytes 1228808 | tf_op jit(solution)/shard_map/ppermute | solution.py:567
  28.2 8.5 %make_queries.1 = (f32[400,4096]{1,0:T(8,128)}, bf16[400,4096]{1,0:T(8,128)(2,1)}) custom-call(f32[400,512]{1,0:T(8,128)S(1)} %copy-done.5, bf16[400,128]{1,0:T(8,128)(2,1)S(1)} %pad.4.parts, s32[1,4096]{1,0:T(1,128)S(1)} %bitcast.49, s32[1,4096]{1,0:T(1,128)S(1)} %bitcast.51), custom_call_target="tpu_custom_call" | custom-call | flops 3355443200 | bytes 9830400 | tf_op jit(solution)/shard_map/make_queries/pallas_call | solution.py:107
  39.3 10.6 %positives.1 = (f32[400,4096]{1,0:T(8,128)}, f32[400,512]{1,0:T(8,128)S(1)}) custom-call(bf16[400,512]{1,0:T(8,128)(2,1)S(1)} %shard_map.147.table.refs_0_, f32[400,4096]{1,0:T(8,128)} %get-tuple-element.43.query_in, s32[1,4096]{1,0:T(1,128)S(1)} %bitcast.48), custom_call_target="tpu_custom_call" | custom-call | flops 5033164800 | bytes 13107200 | tf_op jit(solution)/shard_map/positives/pallas_call | solution.py:138
  50.5 12.5 %shard_map.148 = (f32[400,4096]{1,0:T(8,128)}, bf16[400,512]{1,0:T(8,128)(2,1)S(1)}, bf16[1,400,512]{2,1,0:T(8,128)(2,1)S(1)}) custom-call(s32[1]{0:T(128)} %bitcast.3.here_ref, s32[1,8]{1,0:T(1,128)S(1)} %copy-done.10, bf16[400,512]{1,0:T(8,128)(2,1)S(1)} %shard_map.147.table.refs_0_, ...), custom_call_target="tpu_custom_call", output_to_operand_aliasing={{0}: (6, {})} | custom-call | flops 3774873600 | bytes 16384000 | tf_op jit(solution)/shard_map/pallas_call | solution.py:252
  65.8 12.8 %shard_map.149 = (f32[400,4096]{1,0:T(8,128)}, bf16[400,512]{1,0:T(8,128)(2,1)S(1)}, bf16[400,512]{1,0:T(8,128)(2,1)S(1)}, bf16[2,400,512]{2,1,0:T(8,128)(2,1)S(1)}) custom-call(s32[1]{0:T(128)} %bitcast.3.here_ref, s32[1,8]{1,0:T(1,128)S(1)} %copy-done.10, bf16[400,512]{1,0:T(8,128)(2,1)S(1)} %collective-permute-done.4.refs_0_, ...), custom_call_target="tpu_custom_call", output_to_operand_aliasing={{0}: (8, {})} | custom-call | flops 7549747200 | bytes 16384000 | tf_op jit(solution)/shard_map/pallas_call | solution.py:252
  80.4 12.8 %shard_map.150 = (f32[400,4096]{1,0:T(8,128)}, bf16[400,512]{1,0:T(8,128)(2,1)S(1)}, bf16[400,512]{1,0:T(8,128)(2,1)S(1)}, bf16[2,400,512]{2,1,0:T(8,128)(2,1)S(1)}) custom-call(s32[1]{0:T(128)} %bitcast.3.here_ref, s32[1,8]{1,0:T(1,128)S(1)} %copy-done.10, bf16[400,512]{1,0:T(8,128)(2,1)S(1)} %collective-permute-done.5.refs_0_, ...), custom_call_target="tpu_custom_call", output_to_operand_aliasing={{0}: (8, {})} | custom-call | flops 7549747200 | bytes 16384000 | tf_op jit(solution)/shard_map/pallas_call | solution.py:252
  93.2 10.7 %shard_map.151 = (f32[400,4096]{1,0:T(8,128)}, bf16[400,512]{1,0:T(8,128)(2,1)S(1)}, bf16[400,512]{1,0:T(8,128)(2,1)S(1)}, bf16[2,400,512]{2,1,0:T(8,128)(2,1)S(1)}) custom-call(s32[1]{0:T(128)} %bitcast.3.here_ref, s32[1,8]{1,0:T(1,128)S(1)} %copy-done.10, bf16[400,512]{1,0:T(8,128)(2,1)S(1)} %collective-permute-done.6.refs_0_, ...), custom_call_target="tpu_custom_call", output_to_operand_aliasing={{0}: (8, {})} | custom-call | flops 7549747200 | bytes 16384000 | tf_op jit(solution)/shard_map/pallas_call | solution.py:252
  103.9 2.8 %collective-permute-start.26 = (bf16[2,400,512]{2,1,0:T(8,128)(2,1)S(1)}, bf16[2,400,512]{2,1,0:T(8,128)(2,1)S(1)}, u32[]{:S(2)}, u32[]{:S(2)}) collective-permute-start(bf16[2,400,512]{2,1,0:T(8,128)(2,1)S(1)} %get-tuple-element.62), channel_id=1, source_target_pairs={{0,1},{1,0},{2,3},{3,2},{4,5},{5,4},{6,7},{7,6},{8,9},{9,8},{10,11... | collective-permute-start | bytes 2457608 | tf_op jit(solution)/shard_map/ppermute | solution.py:548
  106.7 15.5 %source_side.1 = (f32[400,512]{1,0:T(8,128)}, f32[1,512]{1,0:T(1,128)}, f32[16,400]{1,0:T(8,128)S(1)}) custom-call(f32[400,512]{1,0:T(8,128)S(1)} %copy-done.5, f32[1,512]{1,0:T(1,128)S(1)} %bitcast.53, bf16[400,128]{1,0:T(8,128)(2,1)S(1)} %pad.4.parts, s32[1,4096]{1,0:T(1,128)S(1)} %bitcast.50, s32[1,4096]{1,0:T(1,128)S(1)} %bitcast.52, ...), custom_call_target="tpu_custom_call" | custom-call | flops 6710886400 | bytes 6553600 | tf_op jit(solution)/shard_map/source_side/pallas_call | solution.py:304
  123.4 2.6 %collective-permute-start.30 = (f32[16,400]{1,0:T(8,128)S(1)}, f32[16,400]{1,0:T(8,128)S(1)}, u32[]{:S(2)}, u32[]{:S(2)}) collective-permute-start(f32[16,400]{1,0:T(8,128)S(1)} %add.41), channel_id=1, source_target_pairs={{0,2},{1,3},{2,0},{3,1},{4,6},{5,7},{6,4},{7,5},{8,10},{9,11},{10,... | collective-permute-start | bytes 76808 | tf_op jit(solution)/shard_map/ppermute | solution.py:503
  126.0 1.9 %collective-permute-done.30 = f32[16,400]{1,0:T(8,128)S(1)} collective-permute-done((f32[16,400]{1,0:T(8,128)S(1)}, f32[16,400]{1,0:T(8,128)S(1)}, u32[]{:S(2)}, u32[]{:S(2)}) %collective-permute-start.30) | collective-permute-done | bytes 25632 | tf_op jit(solution)/shard_map/ppermute | solution.py:503
  127.9 2.3 %collective-permute-start.31 = (f32[16,400]{1,0:T(8,128)S(1)}, f32[16,400]{1,0:T(8,128)S(1)}, u32[]{:S(2)}, u32[]{:S(2)}) collective-permute-start(f32[16,400]{1,0:T(8,128)S(1)} %add.42), channel_id=1, source_target_pairs={{0,4},{1,5},{2,6},{3,7},{4,0},{5,1},{6,2},{7,3},{8,12},{9,13},{10,... | collective-permute-start | bytes 76808 | tf_op jit(solution)/shard_map/ppermute | solution.py:503
  132.7 4.2 %collective-permute-start.32 = (f32[16,400]{1,0:T(8,128)S(1)}, f32[16,400]{1,0:T(8,128)S(1)}, u32[]{:S(2)}, u32[]{:S(2)}) collective-permute-start(f32[16,400]{1,0:T(8,128)S(1)} %add.43), channel_id=1, source_target_pairs={{0,8},{8,0},{16,24},{24,16},{1,9},{9,1},{17,25},{25,17},{2,10},{10... | collective-permute-start | bytes 76808 | tf_op jit(solution)/shard_map/ppermute | solution.py:503
  137.2 1.6 collective-permute-done.32
  138.8 2.0 %collective-permute-start.22 = (bf16[400,512]{1,0:T(8,128)(2,1)S(1)}, bf16[400,512]{1,0:T(8,128)(2,1)S(1)}, u32[]{:S(2)}, u32[]{:S(2)}) collective-permute-start(bf16[400,512]{1,0:T(8,128)(2,1)S(1)} %get-tuple-element.71), channel_id=1, source_target_pairs={{0,2},{1,3},{2,4},{3,5},{4,6},{5,7},{8,10},{9,11},{10,12},{11,13},... | collective-permute-start | bytes 1228808 | tf_op jit(solution)/shard_map/ppermute | solution.py:579
  144.4 6.3 %collective-permute-start.25 = (bf16[400,512]{1,0:T(8,128)(2,1)S(1)}, bf16[400,512]{1,0:T(8,128)(2,1)S(1)}, u32[]{:S(2)}, u32[]{:S(2)}) collective-permute-start(bf16[400,512]{1,0:T(8,128)(2,1)S(1)} %get-tuple-element.69), channel_id=1, source_target_pairs={{0,4},{1,5},{2,6},{3,7},{8,12},{9,13},{10,14},{11,15},{16,20},{17,... | collective-permute-start | bytes 1228808 | tf_op jit(solution)/shard_map/ppermute | solution.py:579
  152.0 5.0 %collective-permute-start.28 = (bf16[400,512]{1,0:T(8,128)(2,1)S(1)}, bf16[400,512]{1,0:T(8,128)(2,1)S(1)}, u32[]{:S(2)}, u32[]{:S(2)}) collective-permute-start(bf16[400,512]{1,0:T(8,128)(2,1)S(1)} %get-tuple-element.67), channel_id=1, source_target_pairs={{0,6},{1,7},{8,14},{9,15},{16,22},{17,23},{24,30},{25,31}} | collective-permute-start | bytes 1228808 | tf_op jit(solution)/shard_map/ppermute | solution.py:579
  160.5 19.9 %collective-permute-done.24.refs_7_ = bf16[400,512]{1,0:T(8,128)(2,1)S(1)} collective-permute-done((bf16[400,512]{1,0:T(8,128)(2,1)S(1)}, bf16[400,512]{1,0:T(8,128)(2,1)S(1)}, u32[]{:S(2)}, u32[]{:S(2)}) %collective-permute-start.24) | collective-permute-done | bytes 409632 | tf_op jit(solution)/shard_map/ppermute | solution.py:577
  180.5 2.6 %destination_side.1 = (f32[400,512]{1,0:T(8,128)}, f32[1,512]{1,0:T(1,128)}) custom-call(bf16[400,512]{1,0:T(8,128)(2,1)S(1)} %shard_map.147.table.refs_0_, bf16[416,512]{1,0:T(8,128)(2,1)S(1)} %shard_map.153.refs_1_, f32[400,512]{1,0:T(8,128)S(1)} %get-tuple-element.52.refs_2_, bf16[400,512]{1,0:T(8,128)(2,1)S(1)} %get-tuple-element.53.refs_3_, ...), custom_call_target="tpu_custom_call" | custom-call | flops 1638400 | bytes 5734400 | tf_op jit(solution)/shard_map/destination_side/pallas_call | solution.py:353
  (97 shorter events, 31.0 us)
Async XLA Ops:
  22.1 14.6 %collective-permute-start.7 = (bf16[400,512]{1,0:T(8,128)(2,1)S(1)}, bf16[400,512]{1,0:T(8,128)(2,1)S(1)}, u32[]{:S(2)}, u32[]{:S(2)}) collective-permute-start(bf16[400,512]{1,0:T(8,128)(2,1)S(1)} %shard_map.147.table.refs_0_), channel_id=1, source_target_pairs={{2,0},{3,1},{4,2},{5,3},{6,4},{7,5},{10,8},{11,9},{12,10},{13,11},... | collective-permute-start | bytes 1228808 | tf_op jit(solution)/shard_map/ppermute | solution.py:568
  23.4 15.1 %collective-permute-start.4 = (bf16[400,512]{1,0:T(8,128)(2,1)S(1)}, bf16[400,512]{1,0:T(8,128)(2,1)S(1)}, u32[]{:S(2)}, u32[]{:S(2)}) collective-permute-start(bf16[400,512]{1,0:T(8,128)(2,1)S(1)} %shard_map.147.table.refs_0_), channel_id=1, source_target_pairs={{0,2},{1,3},{2,4},{3,5},{4,6},{5,7},{8,10},{9,11},{10,12},{11,13},... | collective-permute-start | bytes 1228808 | tf_op jit(solution)/shard_map/ppermute | solution.py:567
  36.6 13.3 %collective-permute-start.16 = (bf16[400,512]{1,0:T(8,128)(2,1)S(1)}, bf16[400,512]{1,0:T(8,128)(2,1)S(1)}, u32[]{:S(2)}, u32[]{:S(2)}) collective-permute-start(bf16[400,512]{1,0:T(8,128)(2,1)S(1)} %shard_map.147.table.refs_0_), channel_id=1, source_target_pairs={{0,1},{1,0},{2,3},{3,2},{4,5},{5,4},{6,7},{7,6},{8,9},{9,8},{10,11... | collective-permute-start | bytes 1228808 | tf_op jit(solution)/shard_map/ppermute | solution.py:548
  36.7 26.6 %collective-permute-start.15 = (bf16[400,512]{1,0:T(8,128)(2,1)S(1)}, bf16[400,512]{1,0:T(8,128)(2,1)S(1)}, u32[]{:S(2)}, u32[]{:S(2)}) collective-permute-start(bf16[400,512]{1,0:T(8,128)(2,1)S(1)} %collective-permute-done.7.refs_1_), channel_id=1, source_target_pairs={{0,1},{1,0},{2,3},{3,2},{4,5},{5,4},{6,7},{7,6},{8,9},{9,8},{10,11... | collective-permute-start | bytes 1228808 | tf_op jit(solution)/shard_map/ppermute | solution.py:548
  37.2 25.8 %collective-permute-start.8 = (bf16[400,512]{1,0:T(8,128)(2,1)S(1)}, bf16[400,512]{1,0:T(8,128)(2,1)S(1)}, u32[]{:S(2)}, u32[]{:S(2)}) collective-permute-start(bf16[400,512]{1,0:T(8,128)(2,1)S(1)} %collective-permute-done.7.refs_1_), channel_id=1, source_target_pairs={{2,0},{3,1},{4,2},{5,3},{10,8},{11,9},{12,10},{13,11},{18,16},{19,... | collective-permute-start | bytes 1228808 | tf_op jit(solution)/shard_map/ppermute | solution.py:568
  38.5 26.4 %collective-permute-start.14 = (bf16[400,512]{1,0:T(8,128)(2,1)S(1)}, bf16[400,512]{1,0:T(8,128)(2,1)S(1)}, u32[]{:S(2)}, u32[]{:S(2)}) collective-permute-start(bf16[400,512]{1,0:T(8,128)(2,1)S(1)} %collective-permute-done.4.refs_0_), channel_id=1, source_target_pairs={{0,1},{1,0},{2,3},{3,2},{4,5},{5,4},{6,7},{7,6},{8,9},{9,8},{10,11... | collective-permute-start | bytes 1228808 | tf_op jit(solution)/shard_map/ppermute | solution.py:548
  38.6 25.9 %collective-permute-start.5 = (bf16[400,512]{1,0:T(8,128)(2,1)S(1)}, bf16[400,512]{1,0:T(8,128)(2,1)S(1)}, u32[]{:S(2)}, u32[]{:S(2)}) collective-permute-start(bf16[400,512]{1,0:T(8,128)(2,1)S(1)} %collective-permute-done.4.refs_0_), channel_id=1, source_target_pairs={{2,4},{3,5},{4,6},{5,7},{10,12},{11,13},{12,14},{13,15},{18,20},{1... | collective-permute-start | bytes 1228808 | tf_op jit(solution)/shard_map/ppermute | solution.py:567
  49.9 80.3 %collective-permute-start.17 = (bf16[416,512]{1,0:T(8,128)(2,1)S(1)}, bf16[416,512]{1,0:T(8,128)(2,1)S(1)}, u32[]{:S(2)}, u32[]{:S(2)}) collective-permute-start(bf16[416,512]{1,0:T(8,128)(2,1)S(1)} %get-tuple-element.51.refs_0_), channel_id=1, source_target_pairs={{0,8},{8,0},{16,24},{24,16},{1,9},{9,1},{17,25},{25,17},{2,10},{10... | collective-permute-start | bytes 1277960 | tf_op jit(solution)/shard_map/ppermute | solution.py:415
  63.0 15.5 %collective-permute-start.13 = (bf16[400,512]{1,0:T(8,128)(2,1)S(1)}, bf16[400,512]{1,0:T(8,128)(2,1)S(1)}, u32[]{:S(2)}, u32[]{:S(2)}) collective-permute-start(bf16[400,512]{1,0:T(8,128)(2,1)S(1)} %collective-permute-done.8.refs_1_), channel_id=1, source_target_pairs={{0,1},{1,0},{2,3},{3,2},{4,5},{5,4},{6,7},{7,6},{8,9},{9,8},{10,11... | collective-permute-start | bytes 1228808 | tf_op jit(solution)/shard_map/ppermute | solution.py:548
  63.2 16.7 %collective-permute-start.9 = (bf16[400,512]{1,0:T(8,128)(2,1)S(1)}, bf16[400,512]{1,0:T(8,128)(2,1)S(1)}, u32[]{:S(2)}, u32[]{:S(2)}) collective-permute-start(bf16[400,512]{1,0:T(8,128)(2,1)S(1)} %collective-permute-done.8.refs_1_), channel_id=1, source_target_pairs={{2,0},{3,1},{10,8},{11,9},{18,16},{19,17},{26,24},{27,25}} | collective-permute-start | bytes 1228808 | tf_op jit(solution)/shard_map/ppermute | solution.py:568
  64.5 15.9 %collective-permute-start.12 = (bf16[400,512]{1,0:T(8,128)(2,1)S(1)}, bf16[400,512]{1,0:T(8,128)(2,1)S(1)}, u32[]{:S(2)}, u32[]{:S(2)}) collective-permute-start(bf16[400,512]{1,0:T(8,128)(2,1)S(1)} %collective-permute-done.5.refs_0_), channel_id=1, source_target_pairs={{0,1},{1,0},{2,3},{3,2},{4,5},{5,4},{6,7},{7,6},{8,9},{9,8},{10,11... | collective-permute-start | bytes 1228808 | tf_op jit(solution)/shard_map/ppermute | solution.py:548
  64.9 15.0 %collective-permute-start.6 = (bf16[400,512]{1,0:T(8,128)(2,1)S(1)}, bf16[400,512]{1,0:T(8,128)(2,1)S(1)}, u32[]{:S(2)}, u32[]{:S(2)}) collective-permute-start(bf16[400,512]{1,0:T(8,128)(2,1)S(1)} %collective-permute-done.5.refs_0_), channel_id=1, source_target_pairs={{4,6},{5,7},{12,14},{13,15},{20,22},{21,23},{28,30},{29,31}} | collective-permute-start | bytes 1228808 | tf_op jit(solution)/shard_map/ppermute | solution.py:567
  78.5 52.3 %collective-permute-start.20 = (bf16[2,400,512]{2,1,0:T(8,128)(2,1)S(1)}, bf16[2,400,512]{2,1,0:T(8,128)(2,1)S(1)}, u32[]{:S(2)}, u32[]{:S(2)}) collective-permute-start(bf16[2,400,512]{2,1,0:T(8,128)(2,1)S(1)} %get-tuple-element.56), channel_id=1, source_target_pairs={{0,1},{1,0},{2,3},{3,2},{4,5},{5,4},{6,7},{7,6},{8,9},{9,8},{10,11... | collective-permute-start | bytes 2457608 | tf_op jit(solution)/shard_map/ppermute | solution.py:548
  79.9 13.3 %collective-permute-start.11 = (bf16[400,512]{1,0:T(8,128)(2,1)S(1)}, bf16[400,512]{1,0:T(8,128)(2,1)S(1)}, u32[]{:S(2)}, u32[]{:S(2)}) collective-permute-start(bf16[400,512]{1,0:T(8,128)(2,1)S(1)} %collective-permute-done.9.refs_1_), channel_id=1, source_target_pairs={{0,1},{1,0},{2,3},{3,2},{4,5},{5,4},{6,7},{7,6},{8,9},{9,8},{10,11... | collective-permute-start | bytes 1228808 | tf_op jit(solution)/shard_map/ppermute | solution.py:548
  93.2 47.7 %collective-permute-start.23 = (bf16[2,400,512]{2,1,0:T(8,128)(2,1)S(1)}, bf16[2,400,512]{2,1,0:T(8,128)(2,1)S(1)}, u32[]{:S(2)}, u32[]{:S(2)}) collective-permute-start(bf16[2,400,512]{2,1,0:T(8,128)(2,1)S(1)} %get-tuple-element.59), channel_id=1, source_target_pairs={{0,1},{1,0},{2,3},{3,2},{4,5},{5,4},{6,7},{7,6},{8,9},{9,8},{10,11... | collective-permute-start | bytes 2457608 | tf_op jit(solution)/shard_map/ppermute | solution.py:548
  103.9 38.8 %collective-permute-start.26 = (bf16[2,400,512]{2,1,0:T(8,128)(2,1)S(1)}, bf16[2,400,512]{2,1,0:T(8,128)(2,1)S(1)}, u32[]{:S(2)}, u32[]{:S(2)}) collective-permute-start(bf16[2,400,512]{2,1,0:T(8,128)(2,1)S(1)} %get-tuple-element.62), channel_id=1, source_target_pairs={{0,1},{1,0},{2,3},{3,2},{4,5},{5,4},{6,7},{7,6},{8,9},{9,8},{10,11... | collective-permute-start | bytes 2457608 | tf_op jit(solution)/shard_map/ppermute | solution.py:548
  130.2 14.2 %collective-permute-start.19 = (bf16[1,400,512]{2,1,0:T(8,128)(2,1)S(1)}, bf16[1,400,512]{2,1,0:T(8,128)(2,1)S(1)}, u32[]{:S(2)}, u32[]{:S(2)}) collective-permute-start(bf16[1,400,512]{2,1,0:T(8,128)(2,1)S(1)} %get-tuple-element.54), channel_id=1, source_target_pairs={{0,1},{1,0},{2,3},{3,2},{4,5},{5,4},{6,7},{7,6},{8,9},{9,8},{10,11... | collective-permute-start | bytes 1228808 | tf_op jit(solution)/shard_map/ppermute | solution.py:548
  130.8 19.9 %collective-permute-start.18 = (bf16[416,512]{1,0:T(8,128)(2,1)S(1)}, bf16[416,512]{1,0:T(8,128)(2,1)S(1)}, u32[]{:S(2)}, u32[]{:S(2)}) collective-permute-start(bf16[416,512]{1,0:T(8,128)(2,1)S(1)} %shard_map.152), channel_id=1, source_target_pairs={{0,16},{8,24},{16,0},{24,8},{1,17},{9,25},{17,1},{25,9},{2,18},{10... | collective-permute-start | bytes 1277960 | tf_op jit(solution)/shard_map/ppermute | solution.py:415
  138.8 18.2 %collective-permute-start.22 = (bf16[400,512]{1,0:T(8,128)(2,1)S(1)}, bf16[400,512]{1,0:T(8,128)(2,1)S(1)}, u32[]{:S(2)}, u32[]{:S(2)}) collective-permute-start(bf16[400,512]{1,0:T(8,128)(2,1)S(1)} %get-tuple-element.71), channel_id=1, source_target_pairs={{0,2},{1,3},{2,4},{3,5},{4,6},{5,7},{8,10},{9,11},{10,12},{11,13},... | collective-permute-start | bytes 1228808 | tf_op jit(solution)/shard_map/ppermute | solution.py:579
  140.8 18.7 %collective-permute-start.21 = (bf16[400,512]{1,0:T(8,128)(2,1)S(1)}, bf16[400,512]{1,0:T(8,128)(2,1)S(1)}, u32[]{:S(2)}, u32[]{:S(2)}) collective-permute-start(bf16[400,512]{1,0:T(8,128)(2,1)S(1)} %get-tuple-element.72), channel_id=1, source_target_pairs={{2,0},{3,1},{4,2},{5,3},{6,4},{7,5},{10,8},{11,9},{12,10},{13,11},... | collective-permute-start | bytes 1228808 | tf_op jit(solution)/shard_map/ppermute | solution.py:577
  144.4 16.2 %collective-permute-start.25 = (bf16[400,512]{1,0:T(8,128)(2,1)S(1)}, bf16[400,512]{1,0:T(8,128)(2,1)S(1)}, u32[]{:S(2)}, u32[]{:S(2)}) collective-permute-start(bf16[400,512]{1,0:T(8,128)(2,1)S(1)} %get-tuple-element.69), channel_id=1, source_target_pairs={{0,4},{1,5},{2,6},{3,7},{8,12},{9,13},{10,14},{11,15},{16,20},{17,... | collective-permute-start | bytes 1228808 | tf_op jit(solution)/shard_map/ppermute | solution.py:579
  150.7 29.7 %collective-permute-start.24 = (bf16[400,512]{1,0:T(8,128)(2,1)S(1)}, bf16[400,512]{1,0:T(8,128)(2,1)S(1)}, u32[]{:S(2)}, u32[]{:S(2)}) collective-permute-start(bf16[400,512]{1,0:T(8,128)(2,1)S(1)} %get-tuple-element.70), channel_id=1, source_target_pairs={{4,0},{5,1},{6,2},{7,3},{12,8},{13,9},{14,10},{15,11},{20,16},{21,... | collective-permute-start | bytes 1228808 | tf_op jit(solution)/shard_map/ppermute | solution.py:577
  152.0 28.4 %collective-permute-start.28 = (bf16[400,512]{1,0:T(8,128)(2,1)S(1)}, bf16[400,512]{1,0:T(8,128)(2,1)S(1)}, u32[]{:S(2)}, u32[]{:S(2)}) collective-permute-start(bf16[400,512]{1,0:T(8,128)(2,1)S(1)} %get-tuple-element.67), channel_id=1, source_target_pairs={{0,6},{1,7},{8,14},{9,15},{16,22},{17,23},{24,30},{25,31}} | collective-permute-start | bytes 1228808 | tf_op jit(solution)/shard_map/ppermute | solution.py:579
  157.0 23.4 %collective-permute-start.27 = (bf16[400,512]{1,0:T(8,128)(2,1)S(1)}, bf16[400,512]{1,0:T(8,128)(2,1)S(1)}, u32[]{:S(2)}, u32[]{:S(2)}) collective-permute-start(bf16[400,512]{1,0:T(8,128)(2,1)S(1)} %get-tuple-element.68), channel_id=1, source_target_pairs={{6,0},{7,1},{14,8},{15,9},{22,16},{23,17},{30,24},{31,25}} | collective-permute-start | bytes 1228808 | tf_op jit(solution)/shard_map/ppermute | solution.py:577
  (22 other events, 221.2 us)

commit v3 on v2

--- a/solution.py
+++ b/solution.py
@@ -114,7 +114,7 @@
         scratch_shapes=[pltpu.VMEM((dim, rows), bf16)] * 2,
         compiler_params=params(16),
         cost_estimate=cost(4 * dim * rows * edges, 6 * dim * edges),
-    )(src_table, rel_parts, src_ids, rel_ids)
+    )(in_hbm(src_table), rel_parts, in_hbm(src_ids), in_hbm(rel_ids))
 
 
 def positives(part_high, query, dst_ids, chunk):
@@ -132,8 +132,7 @@
         positive = jnp.sum(value * dst_rows, axis=0, keepdims=True)
         coef = -jax.nn.sigmoid(-positive)
         query_grad[...] = coef * dst_rows
-        high, low = split2(coef * value)
-        dst_grad[...] += dot_nt(high, pick) + dot_nt(low, pick)
+        dst_grad[...] += dot_nt((coef * value).astype(bf16), pick)
 
     return pl.pallas_call(
         body,
@@ -144,7 +143,7 @@
         out_shape=[pltpu.HBM((dim, edges), f32), jax.ShapeDtypeStruct((dim, rows), f32)],
         compiler_params=params(16),
         cost_estimate=cost(6 * dim * rows * edges, 8 * dim * edges),
-    )(part_high, in_hbm(query), dst_ids)
+    )(part_high, in_hbm(query), in_hbm(dst_ids))
 
 
 def negative_wave(tables, shifts, here, quota, neg_ids, query_b, query_grad, chunk):
@@ -272,27 +271,49 @@
     )(here, quota, *tables, neg_ids, in_hbm(query_b), in_hbm(query_grad))
 
 
+def relation_side(src_table, src_ids, rel_ids, query_grad, rel_count, chunk):
+    dim, rows = src_table.shape
+    edges = src_ids.shape[1]
+
+    def body(table, src, rel, grad_in, rel_out, high, low):
+        @pl.when(pl.program_id(0) == 0)
+        def _():
+            high[...], low[...] = split2(table[...])
+            rel_out[...] = jnp.zeros_like(rel_out)
+
+        pick = select_rows(src[...], rows)
+        src_rows = dot_nn(high[...], pick) + dot_nn(low[...], pick)
+        kinds = select_rows(rel[...], rel_count)
+        upper, lower = split2(back(grad_in[...], src_rows))
+        rel_out[...] += dot_nt(kinds, upper) + dot_nt(kinds, lower)
+
+    return pl.pallas_call(
+        body,
+        name="relation_side",
+        grid=(edges // chunk,),
+        in_specs=[whole((dim, rows)), lanes(1, chunk), lanes(1, chunk), lanes(dim, chunk)],
+        out_specs=whole((rel_count, dim)),
+        out_shape=jax.ShapeDtypeStruct((rel_count, dim), f32),
+        scratch_shapes=[pltpu.VMEM((dim, rows), bf16)] * 2,
+        compiler_params=params(24),
+        cost_estimate=cost(4 * dim * rows * edges, 4 * dim * edges),
+    )(in_hbm(src_table), in_hbm(src_ids), in_hbm(rel_ids), in_hbm(query_grad))
+
+
 def source_side(src_table, src_state, rel_parts, src_ids, rel_ids, query_grad, rel_count, chunk):
     dim, rows = src_table.shape
     edges = src_ids.shape[1]
 
-    def body(table, state, parts, src, rel, grad_in, out, state_out, rel_out, high, low, acc):
+    def body(table, state, parts, src, rel, grad_in, out, state_out, acc):
         step = pl.program_id(0)
 
         @pl.when(step == 0)
         def _():
-            high[...], low[...] = split2(table[...])
             acc[...] = jnp.zeros_like(acc)
-            rel_out[...] = jnp.zeros_like(rel_out)
 
         pick = select_rows(src[...], rows)
-        src_rows = dot_nn(high[...], pick) + dot_nn(low[...], pick)
-        grad = grad_in[...]
-        upper, lower = split2(back(grad, relation_rows(parts[...], rel[...], rel_count)))
-        acc[...] += dot_nt(upper, pick) + dot_nt(lower, pick)
-        kinds = select_rows(rel[...], rel_count)
-        upper, lower = split2(back(grad, src_rows))
-        rel_out[...] += dot_nt(kinds, upper) + dot_nt(kinds, lower)
+        term = back(grad_in[...], relation_rows(parts[...], rel[...], rel_count))
+        acc[...] += dot_nt(term.astype(bf16), pick)
 
         @pl.when(step == pl.num_programs(0) - 1)
         def _():
@@ -313,16 +334,22 @@
             lanes(1, chunk),
             lanes(dim, chunk),
         ],
-        out_specs=[whole((dim, rows)), whole((1, rows)), whole((rel_count, dim))],
+        out_specs=[whole((dim, rows)), whole((1, rows))],
         out_shape=[
             jax.ShapeDtypeStruct((dim, rows), f32),
             jax.ShapeDtypeStruct((1, rows), f32),
-            jax.ShapeDtypeStruct((rel_count, dim), f32),
         ],
-        scratch_shapes=[pltpu.VMEM((dim, rows), bf16)] * 2 + [pltpu.VMEM((dim, rows), f32)],
-        compiler_params=params(16),
-        cost_estimate=cost(8 * dim * rows * edges, 4 * dim * edges),
-    )(src_table, src_state, rel_parts, src_ids, rel_ids, in_hbm(query_grad))
+        scratch_shapes=[pltpu.VMEM((dim, rows), f32)],
+        compiler_params=params(24),
+        cost_estimate=cost(4 * dim * rows * edges, 4 * dim * edges),
+    )(
+        in_hbm(src_table),
+        in_hbm(src_state),
+        rel_parts,
+        in_hbm(src_ids),
+        in_hbm(rel_ids),
+        in_hbm(query_grad),
+    )
 
 
 def destination_side(high, low_state, own_grad, grads):
@@ -386,16 +413,17 @@
     return pl.pallas_call(
         body,
         name="split_table",
-        in_specs=[pl.BlockSpec(memory_space=pltpu.VMEM)] * 2,
-        out_specs=[pl.BlockSpec(memory_space=pltpu.VMEM)] * 3,
+        grid=(1,),
+        in_specs=[whole((dim, rows)), whole((1, rows))],
+        out_specs=[whole((dim, half)), whole((dim, rows - half)), whole((dim + tail, rows))],
         out_shape=[
             jax.ShapeDtypeStruct((dim, half), bf16),
             jax.ShapeDtypeStruct((dim, rows - half), bf16),
             jax.ShapeDtypeStruct((dim + tail, rows), bf16),
         ],
-        compiler_params=pltpu.CompilerParams(vmem_limit_bytes=16 * MIB),
+        compiler_params=params(16),
         cost_estimate=cost(4 * dim * rows, 8 * dim * rows),
-    )(table, state)
+    )(in_hbm(table), in_hbm(state))
 
 
 def grid_of(count):
@@ -500,7 +528,8 @@
         count = lax.axis_size(axis)
         step = 1
         while step < count:
-            value = value + lax.ppermute(value, axis, [(i, i ^ step) for i in range(count)])
+            other = lax.ppermute(value, axis, [(i, i ^ step) for i in range(count)])
+            value = value + other
             step *= 2
     return value
 
@@ -523,8 +552,8 @@
     _, row_count = src_table.shape
     rel_count = relation.shape[1]
     edges = edge_src.shape[0]
-    chunk = min(edges, 512)
-    wave_chunk = min(edges, 1024)
+    chunk = min(edges, 1024)
+    wave_chunk = min(edges, 2048)
     here = lax.axis_index("edge").reshape(1).astype(jnp.int32)
     place = lax.axis_index("dom").reshape(1).astype(jnp.int32)
 
@@ -547,38 +576,44 @@
     def swapped(array):
         return lax.ppermute(array, "edge", swap)
 
-    query_grad, mine, theirs = negative_wave(
-        [part_high, swapped(part_high)],
-        [(True, 0), (False, 0)],
-        here,
-        quotas,
-        neg_ids,
-        query_b,
-        query_grad,
-        wave_chunk,
-    )
-    arrived = [mine, swapped(theirs)]
-
+    near = swapped(part_high)
     from_below = from_above = part_high
-    for s in range(1, chips):
-        last = edge_count - CORES
-        up = [(i, i + CORES) for i in range(CORES * (s - 1), last)]
-        down = [(i + CORES, i) for i in range(0, last - CORES * (s - 1))]
-        from_below = lax.ppermute(from_below, "edge", up)
-        from_above = lax.ppermute(from_above, "edge", down)
-        tables = [from_below, from_above, swapped(from_below), swapped(from_above)]
-        far = CORES * s
-        shifts = [(True, -far), (True, far), (False, -far), (False, far)]
-        query_grad, below, above, theirs = negative_wave(
+    arrived = []
+    for group in groups_of(chips):
+        tables, shifts = [], []
+        for s in group:
+            if s == 0:
+                tables += [part_high, near]
+                shifts += [(True, 0), (False, 0)]
+                continue
+            last = edge_count - CORES
+            up = [(i, i + CORES) for i in range(CORES * (s - 1), last)]
+            down = [(i + CORES, i) for i in range(0, last - CORES * (s - 1))]
+            from_below = lax.ppermute(from_below, "edge", up)
+            from_above = lax.ppermute(from_above, "edge", down)
+            far = CORES * s
+            tables += [from_below, from_above]
+            tables += [swapped(from_below), swapped(from_above)]
+            shifts += [(True, -far), (True, far), (False, -far), (False, far)]
+        query_grad, *mine, theirs = negative_wave(
             tables, shifts, here, quotas, neg_ids, query_b, query_grad, wave_chunk
         )
         theirs = swapped(theirs).astype(f32)
-        pairs = [(i, i - far) for i in range(far, edge_count)]
-        arrived.append(lax.ppermute((below.astype(f32) + theirs[0]).astype(bf16), "edge", pairs))
-        pairs = [(i, i + far) for i in range(edge_count - far)]
-        arrived.append(lax.ppermute((above.astype(f32) + theirs[1]).astype(bf16), "edge", pairs))
-
-    src_out, src_state_out, rel_grad = source_side(
+        at = 0
+        for s in group:
+            far = CORES * s
+            below = [(i, i - far) for i in range(far, edge_count)]
+            above = [(i, i + far) for i in range(edge_count - far)]
+            for pairs in (below, above):
+                total = mine[at].astype(f32) + theirs[at]
+                at += 1
+                if s == 0:
+                    arrived.append(total)
+                    break
+                arrived.append(lax.ppermute(total.astype(bf16), "edge", pairs))
+
+    rel_grad = relation_side(src_table, src_ids, rel_ids, query_grad, rel_count, chunk)
+    src_out, src_state_out = source_side(
         src_table,
         src_state.reshape(1, row_count),
         rel_parts,
@@ -597,6 +632,10 @@
         dst_state_out.reshape(row_count),
         relation_out,
     )
+
+
+def groups_of(chips):
+    return [list(range(min(2, chips)))] + [[s] for s in range(2, chips)]
 
 
 def solution(mesh):

time: 184 us -> 168 us (0.913)
  the two profiles are of different devices: /device:TPU:0 before, /device:TPU:22 now
where the time goes in v3:
time: 168 us; the launch traced here: 167 us
  Pallas kernels  83.9 us (50%)
  waiting for transfers between devices  39.4 us (23%)
  starting transfers between devices  38.1 us (23%)
  other arithmetic  3.15 us (2%)
    pallas_call x3, Pallas kernels, negative_wave(): pl.pallas_call(body, grid=(edges // chunk,), in_specs=[smem, smem] + [who...  44.9 us
    ppermute x6, waiting for transfers between devices, shards(): arrived.append(lax.ppermute(total.astype(bf16), 'edge', pairs))  17.5 us
    ppermute x6, starting transfers between devices, shards(): arrived.append(lax.ppermute(total.astype(bf16), 'edge', pairs))  14.1 us
    ppermute x5, waiting for transfers between devices, total_over_mesh(): other = lax.ppermute(value, axis, [(i, i ^ step) for i in range(count)])  12.4 us
    ppermute x6, waiting for transfers between devices, shifted(): lax.ppermute(array, 'dom', [(d, moved(d, n, stride, shift)) for d in rang...  9.53 us
    pallas_call x1, Pallas kernels, relation_side(): pl.pallas_call(body, name='relation_side', grid=(edges // chunk,), in_spe...  8.77 us
    pallas_call x1, Pallas kernels, make_queries(): pl.pallas_call(body, name='make_queries', grid=(edges // chunk,), in_spec...  8.58 us
    ppermute x3, starting transfers between devices, shards(): from_below = lax.ppermute(from_below, 'edge', up)  8.3 us
  transfers between devices with their start and end apart: 33, of which 11 were waited for; matrix products, arithmetic and copies ran while one was open for 2% of the time, Pallas kernels for 47%

profile of v3, /device:TPU:22, one launch (start us, length us, event | category | flops | bytes accessed | tf_op | source)
XLA Modules:
  0.0 167.1 jit_solution(14528254991621828155)
XLA Ops:
  3.0 5.8 %collective-permute-done.refs_1_ = bf16[400,256]{1,0:T(8,128)(2,1)S(1)} collective-permute-done((bf16[400,256]{1,0:T(8,128)(2,1)S(1)}, bf16[400,256]{1,0:T(8,128)(2,1)S(1)}, u32[]{:S(2)}, u32[]{:S(2)}) %collective-permute-start) | collective-permute-done | bytes 204832 | tf_op jit(solution)/shard_map/ppermute | solution.py:443
  13.2 3.0 %collective-permute-done.2.refs_4_ = bf16[400,256]{1,0:T(8,128)(2,1)S(1)} collective-permute-done((bf16[400,256]{1,0:T(8,128)(2,1)S(1)}, bf16[400,256]{1,0:T(8,128)(2,1)S(1)}, u32[]{:S(2)}, u32[]{:S(2)}) %collective-permute-start.2) | collective-permute-done | bytes 204832 | tf_op jit(solution)/shard_map/ppermute | solution.py:443
  18.0 3.5 %collective-permute-start.4 = (bf16[400,512]{1,0:T(8,128)(2,1)S(1)}, bf16[400,512]{1,0:T(8,128)(2,1)S(1)}, u32[]{:S(2)}, u32[]{:S(2)}) collective-permute-start(bf16[400,512]{1,0:T(8,128)(2,1)S(1)} %shard_map.147.table.refs_0_), channel_id=1, source_target_pairs={{0,2},{1,3},{2,4},{3,5},{4,6},{5,7},{8,10},{9,11},{10,12},{11,13},... | collective-permute-start | bytes 1228808 | tf_op jit(solution)/shard_map/ppermute | solution.py:592
  21.5 2.4 %collective-permute-start.7 = (bf16[400,512]{1,0:T(8,128)(2,1)S(1)}, bf16[400,512]{1,0:T(8,128)(2,1)S(1)}, u32[]{:S(2)}, u32[]{:S(2)}) collective-permute-start(bf16[400,512]{1,0:T(8,128)(2,1)S(1)} %shard_map.147.table.refs_0_), channel_id=1, source_target_pairs={{2,0},{3,1},{4,2},{5,3},{6,4},{7,5},{10,8},{11,9},{12,10},{13,11},... | collective-permute-start | bytes 1228808 | tf_op jit(solution)/shard_map/ppermute | solution.py:593
  25.6 8.6 %make_queries.1 = (f32[400,4096]{1,0:T(8,128)}, bf16[400,4096]{1,0:T(8,128)(2,1)}) custom-call(f32[400,512]{1,0:T(8,128)} %table.5, bf16[400,128]{1,0:T(8,128)(2,1)S(1)} %pad.4.parts, s32[1,4096]{1,0:T(1,128)} %bitcast.53, s32[1,4096]{1,0:T(1,128)} %bitcast.56), custom_call_target="tpu_custom_call" | custom-call | flops 3355443200 | bytes 9830400 | tf_op jit(solution)/shard_map/make_queries/pallas_call | solution.py:107
  34.7 3.5 %collective-permute-start.5 = (bf16[400,512]{1,0:T(8,128)(2,1)S(1)}, bf16[400,512]{1,0:T(8,128)(2,1)S(1)}, u32[]{:S(2)}, u32[]{:S(2)}) collective-permute-start(bf16[400,512]{1,0:T(8,128)(2,1)S(1)} %collective-permute-done.4.refs_2_), channel_id=1, source_target_pairs={{2,4},{3,5},{4,6},{5,7},{10,12},{11,13},{12,14},{13,15},{18,20},{1... | collective-permute-start | bytes 1228808 | tf_op jit(solution)/shard_map/ppermute | solution.py:592
  38.3 2.4 %collective-permute-start.8 = (bf16[400,512]{1,0:T(8,128)(2,1)S(1)}, bf16[400,512]{1,0:T(8,128)(2,1)S(1)}, u32[]{:S(2)}, u32[]{:S(2)}) collective-permute-start(bf16[400,512]{1,0:T(8,128)(2,1)S(1)} %collective-permute-done.7.refs_3_), channel_id=1, source_target_pairs={{2,0},{3,1},{4,2},{5,3},{10,8},{11,9},{12,10},{13,11},{18,16},{19,... | collective-permute-start | bytes 1228808 | tf_op jit(solution)/shard_map/ppermute | solution.py:593
  40.7 8.0 %positives.1 = (f32[400,4096]{1,0:T(8,128)}, f32[400,512]{1,0:T(8,128)S(1)}) custom-call(bf16[400,512]{1,0:T(8,128)(2,1)S(1)} %shard_map.147.table.refs_0_, f32[400,4096]{1,0:T(8,128)} %get-tuple-element.40.query_in, s32[1,4096]{1,0:T(1,128)} %bitcast.52), custom_call_target="tpu_custom_call" | custom-call | flops 5033164800 | bytes 13107200 | tf_op jit(solution)/shard_map/positives/pallas_call | solution.py:137
  49.3 1.6 collective-permute-start.18
  53.7 25.6 %shard_map.148 = (f32[400,4096]{1,0:T(8,128)}, bf16[400,512]{1,0:T(8,128)(2,1)S(1)}, bf16[400,512]{1,0:T(8,128)(2,1)S(1)}, bf16[400,512]{1,0:T(8,128)(2,1)S(1)}, bf16[3,400,512]{2,1,0:T(8,128)(2,1)S(1)}) custom-call(s32[1]{0:T(128)} %bitcast.3.here_ref, s32[1,8]{1,0:T(1,128)S(1)} %copy-done.3, ...), custom_call_target="tpu_custom_call", output_to_operand_aliasing={{0}: (10, {})} | custom-call | flops 11324620800 | bytes 16384000 | tf_op jit(solution)/shard_map/pallas_call | solution.py:251
  79.9 12.8 %shard_map.149 = (f32[400,4096]{1,0:T(8,128)}, bf16[400,512]{1,0:T(8,128)(2,1)S(1)}, bf16[400,512]{1,0:T(8,128)(2,1)S(1)}, bf16[2,400,512]{2,1,0:T(8,128)(2,1)S(1)}) custom-call(s32[1]{0:T(128)} %bitcast.3.here_ref, s32[1,8]{1,0:T(1,128)S(1)} %copy-done.3, bf16[400,512]{1,0:T(8,128)(2,1)S(1)} %collective-permute-done.5.refs_0_, ...), custom_call_target="tpu_custom_call", output_to_operand_aliasing={{0}: (8, {})} | custom-call | flops 7549747200 | bytes 16384000 | tf_op jit(solution)/shard_map/pallas_call | solution.py:251
  93.0 6.5 %shard_map.150 = (f32[400,4096]{1,0:T(8,128)}, bf16[400,512]{1,0:T(8,128)(2,1)S(1)}, bf16[400,512]{1,0:T(8,128)(2,1)S(1)}, bf16[2,400,512]{2,1,0:T(8,128)(2,1)S(1)}) custom-call(s32[1]{0:T(128)} %bitcast.3.here_ref, s32[1,8]{1,0:T(1,128)S(1)} %copy-done.3, bf16[400,512]{1,0:T(8,128)(2,1)S(1)} %collective-permute-done.6.refs_0_, ...), custom_call_target="tpu_custom_call", output_to_operand_aliasing={{0}: (8, {})} | custom-call | flops 7549747200 | bytes 16384000 | tf_op jit(solution)/shard_map/pallas_call | solution.py:251
  99.8 8.8 %relation_side.1 = f32[16,400]{1,0:T(8,128)S(1)} custom-call(f32[400,512]{1,0:T(8,128)} %table.5, s32[1,4096]{1,0:T(1,128)} %bitcast.54, s32[1,4096]{1,0:T(1,128)} %bitcast.57, f32[400,4096]{1,0:T(8,128)} %get-tuple-element.44.grad_in), custom_call_target="tpu_custom_call" | custom-call | flops 3355443200 | bytes 6553600 | tf_op jit(solution)/shard_map/relation_side/pallas_call | solution.py:290
  109.8 3.9 %collective-permute-done.29 = f32[16,400]{1,0:T(8,128)S(1)} collective-permute-done((f32[16,400]{1,0:T(8,128)S(1)}, f32[16,400]{1,0:T(8,128)S(1)}, u32[]{:S(2)}, u32[]{:S(2)}) %collective-permute-start.29) | collective-permute-done | bytes 25632 | tf_op jit(solution)/shard_map/ppermute | solution.py:531
  114.3 4.2 %collective-permute-done.30 = f32[16,400]{1,0:T(8,128)S(1)} collective-permute-done((f32[16,400]{1,0:T(8,128)S(1)}, f32[16,400]{1,0:T(8,128)S(1)}, u32[]{:S(2)}, u32[]{:S(2)}) %collective-permute-start.30) | collective-permute-done | bytes 25632 | tf_op jit(solution)/shard_map/ppermute | solution.py:531
  119.2 3.3 %collective-permute-done.31 = f32[16,400]{1,0:T(8,128)S(1)} collective-permute-done((f32[16,400]{1,0:T(8,128)S(1)}, f32[16,400]{1,0:T(8,128)S(1)}, u32[]{:S(2)}, u32[]{:S(2)}) %collective-permute-start.31) | collective-permute-done | bytes 25632 | tf_op jit(solution)/shard_map/ppermute | solution.py:531
  123.6 5.2 %collective-permute-start.23 = (bf16[400,512]{1,0:T(8,128)(2,1)S(1)}, bf16[400,512]{1,0:T(8,128)(2,1)S(1)}, u32[]{:S(2)}, u32[]{:S(2)}) collective-permute-start(bf16[400,512]{1,0:T(8,128)(2,1)S(1)} %get-tuple-element.67), channel_id=1, source_target_pairs={{4,0},{5,1},{6,2},{7,3},{12,8},{13,9},{14,10},{15,11},{20,16},{21,... | collective-permute-start | bytes 1228808 | tf_op jit(solution)/shard_map/ppermute | solution.py:613
  130.9 4.3 %collective-permute-start.20 = (bf16[400,512]{1,0:T(8,128)(2,1)S(1)}, bf16[400,512]{1,0:T(8,128)(2,1)S(1)}, u32[]{:S(2)}, u32[]{:S(2)}) collective-permute-start(bf16[400,512]{1,0:T(8,128)(2,1)S(1)} %get-tuple-element.62), channel_id=1, source_target_pairs={{2,0},{3,1},{4,2},{5,3},{6,4},{7,5},{10,8},{11,9},{12,10},{13,11},... | collective-permute-start | bytes 1228808 | tf_op jit(solution)/shard_map/ppermute | solution.py:613
  135.3 1.9 %collective-permute-start.21 = (bf16[400,512]{1,0:T(8,128)(2,1)S(1)}, bf16[400,512]{1,0:T(8,128)(2,1)S(1)}, u32[]{:S(2)}, u32[]{:S(2)}) collective-permute-start(bf16[400,512]{1,0:T(8,128)(2,1)S(1)} %get-tuple-element.61), channel_id=1, source_target_pairs={{0,2},{1,3},{2,4},{3,5},{4,6},{5,7},{8,10},{9,11},{10,12},{11,13},... | collective-permute-start | bytes 1228808 | tf_op jit(solution)/shard_map/ppermute | solution.py:613
  138.4 7.8 %collective-permute-done.23.refs_6_ = bf16[400,512]{1,0:T(8,128)(2,1)S(1)} collective-permute-done((bf16[400,512]{1,0:T(8,128)(2,1)S(1)}, bf16[400,512]{1,0:T(8,128)(2,1)S(1)}, u32[]{:S(2)}, u32[]{:S(2)}) %collective-permute-start.23) | collective-permute-done | bytes 409632 | tf_op jit(solution)/shard_map/ppermute | solution.py:613
  146.9 7.3 %source_side.1 = (f32[400,512]{1,0:T(8,128)}, f32[1,512]{1,0:T(1,128)}) custom-call(f32[400,512]{1,0:T(8,128)} %table.5, f32[1,512]{1,0:T(1,128)} %bitcast.59, bf16[400,128]{1,0:T(8,128)(2,1)S(1)} %pad.4.parts, s32[1,4096]{1,0:T(1,128)} %bitcast.55, s32[1,4096]{1,0:T(1,128)} %bitcast.58, f32[400,4096]{1,0:T(8,128)} %get-tuple-element.44.grad_in), custom_call_target="tpu_custom_call" | custom-call | flops 3355443200 | bytes 6553600 | tf_op jit(solution)/shard_map/source_side/pallas_call | solution.py:325
  154.8 5.5 %collective-permute-done.20.refs_4_ = bf16[400,512]{1,0:T(8,128)(2,1)S(1)} collective-permute-done((bf16[400,512]{1,0:T(8,128)(2,1)S(1)}, bf16[400,512]{1,0:T(8,128)(2,1)S(1)}, u32[]{:S(2)}, u32[]{:S(2)}) %collective-permute-start.20) | collective-permute-done | bytes 409632 | tf_op jit(solution)/shard_map/ppermute | solution.py:613
  160.4 4.1 %collective-permute-done.21.refs_5_ = bf16[400,512]{1,0:T(8,128)(2,1)S(1)} collective-permute-done((bf16[400,512]{1,0:T(8,128)(2,1)S(1)}, bf16[400,512]{1,0:T(8,128)(2,1)S(1)}, u32[]{:S(2)}, u32[]{:S(2)}) %collective-permute-start.21) | collective-permute-done | bytes 409632 | tf_op jit(solution)/shard_map/ppermute | solution.py:613
  164.5 2.6 %destination_side.1 = (f32[400,512]{1,0:T(8,128)}, f32[1,512]{1,0:T(1,128)}) custom-call(bf16[400,512]{1,0:T(8,128)(2,1)S(1)} %shard_map.147.table.refs_0_, bf16[416,512]{1,0:T(8,128)(2,1)S(1)} %shard_map.152.refs_1_, f32[400,512]{1,0:T(8,128)S(1)} %get-tuple-element.48.refs_2_, f32[400,512]{1,0:T(8,128)S(1)} %get-tuple-element.63.refs_3_, ...), custom_call_target="tpu_custom_call" | custom-call | flops 1638400 | bytes 5324800 | tf_op jit(solution)/shard_map/destination_side/pallas_call | solution.py:380
  (83 shorter events, 23.5 us)
Async XLA Ops:
  18.0 16.2 %collective-permute-start.4 = (bf16[400,512]{1,0:T(8,128)(2,1)S(1)}, bf16[400,512]{1,0:T(8,128)(2,1)S(1)}, u32[]{:S(2)}, u32[]{:S(2)}) collective-permute-start(bf16[400,512]{1,0:T(8,128)(2,1)S(1)} %shard_map.147.table.refs_0_), channel_id=1, source_target_pairs={{0,2},{1,3},{2,4},{3,5},{4,6},{5,7},{8,10},{9,11},{10,12},{11,13},... | collective-permute-start | bytes 1228808 | tf_op jit(solution)/shard_map/ppermute | solution.py:592
  21.5 16.7 %collective-permute-start.7 = (bf16[400,512]{1,0:T(8,128)(2,1)S(1)}, bf16[400,512]{1,0:T(8,128)(2,1)S(1)}, u32[]{:S(2)}, u32[]{:S(2)}) collective-permute-start(bf16[400,512]{1,0:T(8,128)(2,1)S(1)} %shard_map.147.table.refs_0_), channel_id=1, source_target_pairs={{2,0},{3,1},{4,2},{5,3},{6,4},{7,5},{10,8},{11,9},{12,10},{13,11},... | collective-permute-start | bytes 1228808 | tf_op jit(solution)/shard_map/ppermute | solution.py:593
  23.8 14.4 %collective-permute-start.17 = (bf16[416,512]{1,0:T(8,128)(2,1)S(1)}, bf16[416,512]{1,0:T(8,128)(2,1)S(1)}, u32[]{:S(2)}, u32[]{:S(2)}) collective-permute-start(bf16[416,512]{1,0:T(8,128)(2,1)S(1)} %get-tuple-element.47.refs_0_), channel_id=1, source_target_pairs={{0,8},{8,0},{16,24},{24,16},{1,9},{9,1},{17,25},{25,17},{2,10},{10... | collective-permute-start | bytes 1277960 | tf_op jit(solution)/shard_map/ppermute | solution.py:443
  34.2 15.1 %collective-permute-start.14 = (bf16[400,512]{1,0:T(8,128)(2,1)S(1)}, bf16[400,512]{1,0:T(8,128)(2,1)S(1)}, u32[]{:S(2)}, u32[]{:S(2)}) collective-permute-start(bf16[400,512]{1,0:T(8,128)(2,1)S(1)} %shard_map.147.table.refs_0_), channel_id=1, source_target_pairs={{0,1},{1,0},{2,3},{3,2},{4,5},{5,4},{6,7},{7,6},{8,9},{9,8},{10,11... | collective-permute-start | bytes 1228808 | tf_op jit(solution)/shard_map/ppermute | solution.py:577
  34.2 16.8 %collective-permute-start.15 = (bf16[400,512]{1,0:T(8,128)(2,1)S(1)}, bf16[400,512]{1,0:T(8,128)(2,1)S(1)}, u32[]{:S(2)}, u32[]{:S(2)}) collective-permute-start(bf16[400,512]{1,0:T(8,128)(2,1)S(1)} %collective-permute-done.4.refs_2_), channel_id=1, source_target_pairs={{0,1},{1,0},{2,3},{3,2},{4,5},{5,4},{6,7},{7,6},{8,9},{9,8},{10,11... | collective-permute-start | bytes 1228808 | tf_op jit(solution)/shard_map/ppermute | solution.py:577
  34.7 16.2 %collective-permute-start.5 = (bf16[400,512]{1,0:T(8,128)(2,1)S(1)}, bf16[400,512]{1,0:T(8,128)(2,1)S(1)}, u32[]{:S(2)}, u32[]{:S(2)}) collective-permute-start(bf16[400,512]{1,0:T(8,128)(2,1)S(1)} %collective-permute-done.4.refs_2_), channel_id=1, source_target_pairs={{2,4},{3,5},{4,6},{5,7},{10,12},{11,13},{12,14},{13,15},{18,20},{1... | collective-permute-start | bytes 1228808 | tf_op jit(solution)/shard_map/ppermute | solution.py:592
  38.2 14.6 %collective-permute-start.16 = (bf16[400,512]{1,0:T(8,128)(2,1)S(1)}, bf16[400,512]{1,0:T(8,128)(2,1)S(1)}, u32[]{:S(2)}, u32[]{:S(2)}) collective-permute-start(bf16[400,512]{1,0:T(8,128)(2,1)S(1)} %collective-permute-done.7.refs_3_), channel_id=1, source_target_pairs={{0,1},{1,0},{2,3},{3,2},{4,5},{5,4},{6,7},{7,6},{8,9},{9,8},{10,11... | collective-permute-start | bytes 1228808 | tf_op jit(solution)/shard_map/ppermute | solution.py:577
  38.3 14.0 %collective-permute-start.8 = (bf16[400,512]{1,0:T(8,128)(2,1)S(1)}, bf16[400,512]{1,0:T(8,128)(2,1)S(1)}, u32[]{:S(2)}, u32[]{:S(2)}) collective-permute-start(bf16[400,512]{1,0:T(8,128)(2,1)S(1)} %collective-permute-done.7.refs_3_), channel_id=1, source_target_pairs={{2,0},{3,1},{4,2},{5,3},{10,8},{11,9},{12,10},{13,11},{18,16},{19,... | collective-permute-start | bytes 1228808 | tf_op jit(solution)/shard_map/ppermute | solution.py:593
  49.3 69.2 %collective-permute-start.18 = (bf16[416,512]{1,0:T(8,128)(2,1)S(1)}, bf16[416,512]{1,0:T(8,128)(2,1)S(1)}, u32[]{:S(2)}, u32[]{:S(2)}) collective-permute-start(bf16[416,512]{1,0:T(8,128)(2,1)S(1)} %shard_map.151), channel_id=1, source_target_pairs={{0,16},{8,24},{16,0},{24,8},{1,17},{9,25},{17,1},{25,9},{2,18},{10... | collective-permute-start | bytes 1277960 | tf_op jit(solution)/shard_map/ppermute | solution.py:443
  50.9 28.4 %collective-permute-start.12 = (bf16[400,512]{1,0:T(8,128)(2,1)S(1)}, bf16[400,512]{1,0:T(8,128)(2,1)S(1)}, u32[]{:S(2)}, u32[]{:S(2)}) collective-permute-start(bf16[400,512]{1,0:T(8,128)(2,1)S(1)} %collective-permute-done.5.refs_0_), channel_id=1, source_target_pairs={{0,1},{1,0},{2,3},{3,2},{4,5},{5,4},{6,7},{7,6},{8,9},{9,8},{10,11... | collective-permute-start | bytes 1228808 | tf_op jit(solution)/shard_map/ppermute | solution.py:577
  50.9 28.4 %collective-permute-start.6 = (bf16[400,512]{1,0:T(8,128)(2,1)S(1)}, bf16[400,512]{1,0:T(8,128)(2,1)S(1)}, u32[]{:S(2)}, u32[]{:S(2)}) collective-permute-start(bf16[400,512]{1,0:T(8,128)(2,1)S(1)} %collective-permute-done.5.refs_0_), channel_id=1, source_target_pairs={{4,6},{5,7},{12,14},{13,15},{20,22},{21,23},{28,30},{29,31}} | collective-permute-start | bytes 1228808 | tf_op jit(solution)/shard_map/ppermute | solution.py:592
  52.3 27.6 %collective-permute-start.13 = (bf16[400,512]{1,0:T(8,128)(2,1)S(1)}, bf16[400,512]{1,0:T(8,128)(2,1)S(1)}, u32[]{:S(2)}, u32[]{:S(2)}) collective-permute-start(bf16[400,512]{1,0:T(8,128)(2,1)S(1)} %collective-permute-done.8.refs_1_), channel_id=1, source_target_pairs={{0,1},{1,0},{2,3},{3,2},{4,5},{5,4},{6,7},{7,6},{8,9},{9,8},{10,11... | collective-permute-start | bytes 1228808 | tf_op jit(solution)/shard_map/ppermute | solution.py:577
  52.8 27.0 %collective-permute-start.9 = (bf16[400,512]{1,0:T(8,128)(2,1)S(1)}, bf16[400,512]{1,0:T(8,128)(2,1)S(1)}, u32[]{:S(2)}, u32[]{:S(2)}) collective-permute-start(bf16[400,512]{1,0:T(8,128)(2,1)S(1)} %collective-permute-done.8.refs_1_), channel_id=1, source_target_pairs={{2,0},{3,1},{10,8},{11,9},{18,16},{19,17},{26,24},{27,25}} | collective-permute-start | bytes 1228808 | tf_op jit(solution)/shard_map/ppermute | solution.py:593
  79.3 50.8 %collective-permute-start.19 = (bf16[3,400,512]{2,1,0:T(8,128)(2,1)S(1)}, bf16[3,400,512]{2,1,0:T(8,128)(2,1)S(1)}, u32[]{:S(2)}, u32[]{:S(2)}) collective-permute-start(bf16[3,400,512]{2,1,0:T(8,128)(2,1)S(1)} %get-tuple-element.50), channel_id=1, source_target_pairs={{0,1},{1,0},{2,3},{3,2},{4,5},{5,4},{6,7},{7,6},{8,9},{9,8},{10,11... | collective-permute-start | bytes 3686408 | tf_op jit(solution)/shard_map/ppermute | solution.py:577
  79.3 13.7 %collective-permute-start.10 = (bf16[400,512]{1,0:T(8,128)(2,1)S(1)}, bf16[400,512]{1,0:T(8,128)(2,1)S(1)}, u32[]{:S(2)}, u32[]{:S(2)}) collective-permute-start(bf16[400,512]{1,0:T(8,128)(2,1)S(1)} %collective-permute-done.6.refs_0_), channel_id=1, source_target_pairs={{0,1},{1,0},{2,3},{3,2},{4,5},{5,4},{6,7},{7,6},{8,9},{9,8},{10,11... | collective-permute-start | bytes 1228808 | tf_op jit(solution)/shard_map/ppermute | solution.py:577
  92.7 30.4 %collective-permute-start.22 = (bf16[2,400,512]{2,1,0:T(8,128)(2,1)S(1)}, bf16[2,400,512]{2,1,0:T(8,128)(2,1)S(1)}, u32[]{:S(2)}, u32[]{:S(2)}) collective-permute-start(bf16[2,400,512]{2,1,0:T(8,128)(2,1)S(1)} %get-tuple-element.54), channel_id=1, source_target_pairs={{0,1},{1,0},{2,3},{3,2},{4,5},{5,4},{6,7},{7,6},{8,9},{9,8},{10,11... | collective-permute-start | bytes 2457608 | tf_op jit(solution)/shard_map/ppermute | solution.py:577
  99.5 35.7 %collective-permute-start.25 = (bf16[2,400,512]{2,1,0:T(8,128)(2,1)S(1)}, bf16[2,400,512]{2,1,0:T(8,128)(2,1)S(1)}, u32[]{:S(2)}, u32[]{:S(2)}) collective-permute-start(bf16[2,400,512]{2,1,0:T(8,128)(2,1)S(1)} %get-tuple-element.57), channel_id=1, source_target_pairs={{0,1},{1,0},{2,3},{3,2},{4,5},{5,4},{6,7},{7,6},{8,9},{9,8},{10,11... | collective-permute-start | bytes 2457608 | tf_op jit(solution)/shard_map/ppermute | solution.py:577
  122.4 15.3 %collective-permute-start.32 = (f32[16,400]{1,0:T(8,128)S(1)}, f32[16,400]{1,0:T(8,128)S(1)}, u32[]{:S(2)}, u32[]{:S(2)}) collective-permute-start(f32[16,400]{1,0:T(8,128)S(1)} %add.48), channel_id=1, source_target_pairs={{0,16},{8,24},{16,0},{24,8},{1,17},{9,25},{17,1},{25,9},{2,18},{10... | collective-permute-start | bytes 76808 | tf_op jit(solution)/shard_map/ppermute | solution.py:531
  123.6 22.5 %collective-permute-start.23 = (bf16[400,512]{1,0:T(8,128)(2,1)S(1)}, bf16[400,512]{1,0:T(8,128)(2,1)S(1)}, u32[]{:S(2)}, u32[]{:S(2)}) collective-permute-start(bf16[400,512]{1,0:T(8,128)(2,1)S(1)} %get-tuple-element.67), channel_id=1, source_target_pairs={{4,0},{5,1},{6,2},{7,3},{12,8},{13,9},{14,10},{15,11},{20,16},{21,... | collective-permute-start | bytes 1228808 | tf_op jit(solution)/shard_map/ppermute | solution.py:613
  128.9 26.0 %collective-permute-start.24 = (bf16[400,512]{1,0:T(8,128)(2,1)S(1)}, bf16[400,512]{1,0:T(8,128)(2,1)S(1)}, u32[]{:S(2)}, u32[]{:S(2)}) collective-permute-start(bf16[400,512]{1,0:T(8,128)(2,1)S(1)} %get-tuple-element.66), channel_id=1, source_target_pairs={{0,4},{1,5},{2,6},{3,7},{8,12},{9,13},{10,14},{11,15},{16,20},{17,... | collective-permute-start | bytes 1228808 | tf_op jit(solution)/shard_map/ppermute | solution.py:613
  130.9 29.5 %collective-permute-start.20 = (bf16[400,512]{1,0:T(8,128)(2,1)S(1)}, bf16[400,512]{1,0:T(8,128)(2,1)S(1)}, u32[]{:S(2)}, u32[]{:S(2)}) collective-permute-start(bf16[400,512]{1,0:T(8,128)(2,1)S(1)} %get-tuple-element.62), channel_id=1, source_target_pairs={{2,0},{3,1},{4,2},{5,3},{6,4},{7,5},{10,8},{11,9},{12,10},{13,11},... | collective-permute-start | bytes 1228808 | tf_op jit(solution)/shard_map/ppermute | solution.py:613
  135.3 29.3 %collective-permute-start.21 = (bf16[400,512]{1,0:T(8,128)(2,1)S(1)}, bf16[400,512]{1,0:T(8,128)(2,1)S(1)}, u32[]{:S(2)}, u32[]{:S(2)}) collective-permute-start(bf16[400,512]{1,0:T(8,128)(2,1)S(1)} %get-tuple-element.61), channel_id=1, source_target_pairs={{0,2},{1,3},{2,4},{3,5},{4,6},{5,7},{8,10},{9,11},{10,12},{11,13},... | collective-permute-start | bytes 1228808 | tf_op jit(solution)/shard_map/ppermute | solution.py:613
  137.7 26.8 %collective-permute-start.26 = (bf16[400,512]{1,0:T(8,128)(2,1)S(1)}, bf16[400,512]{1,0:T(8,128)(2,1)S(1)}, u32[]{:S(2)}, u32[]{:S(2)}) collective-permute-start(bf16[400,512]{1,0:T(8,128)(2,1)S(1)} %get-tuple-element.65), channel_id=1, source_target_pairs={{6,0},{7,1},{14,8},{15,9},{22,16},{23,17},{30,24},{31,25}} | collective-permute-start | bytes 1228808 | tf_op jit(solution)/shard_map/ppermute | solution.py:613
  146.2 18.3 %collective-permute-start.27 = (bf16[400,512]{1,0:T(8,128)(2,1)S(1)}, bf16[400,512]{1,0:T(8,128)(2,1)S(1)}, u32[]{:S(2)}, u32[]{:S(2)}) collective-permute-start(bf16[400,512]{1,0:T(8,128)(2,1)S(1)} %get-tuple-element.64), channel_id=1, source_target_pairs={{0,6},{1,7},{8,14},{9,15},{16,22},{17,23},{24,30},{25,31}} | collective-permute-start | bytes 1228808 | tf_op jit(solution)/shard_map/ppermute | solution.py:613
  (15 other events, 106.7 us)

commit v4 on v3

--- a/solution.py
+++ b/solution.py
@@ -93,13 +93,14 @@
     dim, rows = src_table.shape
     edges = src_ids.shape[1]
 
-    def body(table, parts, src, rel, query, query_b, high, low):
+    def body(table, parts, src, rel, query, query_b, rows_out, high, low):
         @pl.when(pl.program_id(0) == 0)
         def _():
             high[...], low[...] = split2(table[...])
 
         pick = select_rows(src[...], rows)
         src_rows = dot_nn(high[...], pick) + dot_nn(low[...], pick)
+        rows_out[...] = src_rows
         value = product(src_rows, relation_rows(parts[...], rel[...], rel_count))
         query[...] = value
         query_b[...] = value.astype(bf16)
@@ -109,10 +110,14 @@
         name="make_queries",
         grid=(edges // chunk,),
         in_specs=[whole((dim, rows)), whole(rel_parts.shape), lanes(1, chunk), lanes(1, chunk)],
-        out_specs=[lanes(dim, chunk), lanes(dim, chunk)],
-        out_shape=[pltpu.HBM((dim, edges), f32), pltpu.HBM((dim, edges), bf16)],
+        out_specs=[lanes(dim, chunk)] * 3,
+        out_shape=[
+            pltpu.HBM((dim, edges), f32),
+            pltpu.HBM((dim, edges), bf16),
+            pltpu.HBM((dim, edges), f32),
+        ],
         scratch_shapes=[pltpu.VMEM((dim, rows), bf16)] * 2,
-        compiler_params=params(16),
+        compiler_params=params(32),
         cost_estimate=cost(4 * dim * rows * edges, 6 * dim * edges),
     )(in_hbm(src_table), rel_parts, in_hbm(src_ids), in_hbm(rel_ids))
 
@@ -141,35 +146,28 @@
         in_specs=[whole((dim, rows)), lanes(dim, chunk), lanes(1, chunk)],
         out_specs=[lanes(dim, chunk), whole((dim, rows))],
         out_shape=[pltpu.HBM((dim, edges), f32), jax.ShapeDtypeStruct((dim, rows), f32)],
-        compiler_params=params(16),
+        compiler_params=params(32),
         cost_estimate=cost(6 * dim * rows * edges, 8 * dim * edges),
     )(part_high, in_hbm(query), in_hbm(dst_ids))
 
 
-def negative_wave(tables, shifts, here, quota, neg_ids, query_b, query_grad, chunk):
+def negative_wave(tables, chip, quota, neg_ids, query_b, query_grad, lane, chunk):
     count = len(tables)
     dim, rows = tables[0].shape
     edges = query_b.shape[1]
-    edge_count = neg_ids.shape[0]
     half_weight = 0.5 / math.sqrt(NNEG)
-    own = [s for s in range(count) if shifts[s][0]]
-    others = [s for s in range(count) if not shifts[s][0]]
-
-    def body(here_ref, quota_ref, *refs):
+
+    def body(chip_ref, lane_ref, quota_ref, *refs):
         table_refs = refs[:count]
         ids, query_ref, grad_in, grad_out = refs[count : count + 4]
-        own_refs = refs[count + 4 : count + 4 + len(own)]
-        other_ref, neg, neg_t, neg_grad = refs[count + 4 + len(own) :]
-
-        place = here_ref[0]
-        across = place + 1 - 2 * (place % CORES)
+        grad_refs = refs[count + 4 : 2 * count + 4]
+        neg, neg_t, neg_grad = refs[2 * count + 4 :]
+
         live, at, base = [], [], [jnp.int32(0)]
-        for lane, shift in shifts:
-            spot = (place if lane else across) + shift
-            inside = jnp.logical_and(spot >= 0, spot < edge_count)
-            spot = jnp.clip(spot, 0, edge_count - 1)
+        for s in range(count):
+            spot = CORES * chip_ref[0] + (lane_ref[0] + s) % CORES
             at.append(spot)
-            live.append(jnp.where(inside, quota_ref[0, spot], 0))
+            live.append(quota_ref[0, spot])
             base.append(base[-1] + live[-1])
         total = base[-1]
 
@@ -225,25 +223,19 @@
 
         for s in range(count):
 
-            def put(value, s=s):
-                if s in own:
-                    own_refs[own.index(s)][...] = value
-                else:
-                    other_ref[others.index(s)] = value
-
             @when_done(s, 0)
-            def _(put=put):
-                put(jnp.zeros((dim, rows), bf16))
+            def _(s=s):
+                grad_refs[s][...] = jnp.zeros((dim, rows), bf16)
 
             for wide in range(1, QMAX + 1):
 
                 @when_done(s, wide)
-                def _(s=s, wide=wide, put=put):
+                def _(s=s, wide=wide):
                     parts = [neg_grad[base[s] + b] for b in range(wide)]
                     value = jnp.concatenate(parts, axis=1) if wide > 1 else parts[0]
                     high, low = split2(value)
                     pick = picks(s, wide)
-                    put((dot_nt(high, pick) + dot_nt(low, pick)).astype(bf16))
+                    grad_refs[s][...] = (dot_nt(high, pick) + dot_nt(low, pick)).astype(bf16)
 
     slots = QMAX * count
     smem = pl.BlockSpec(memory_space=pltpu.SMEM)
@@ -251,53 +243,44 @@
     return pl.pallas_call(
         body,
         grid=(edges // chunk,),
-        in_specs=[smem, smem]
+        in_specs=[smem, smem, smem]
         + [whole((dim, rows))] * count
         + [whole(neg_ids.shape), lanes(dim, chunk), lanes(dim, chunk)],
-        out_specs=[lanes(dim, chunk)]
-        + [whole((dim, rows))] * len(own)
-        + [whole((len(others), dim, rows))],
+        out_specs=[lanes(dim, chunk)] + [whole((dim, rows))] * count,
         scratch_shapes=[
             pltpu.VMEM((slots, dim, BLOCK), bf16),
             pltpu.VMEM((slots, BLOCK, dim), bf16),
             pltpu.VMEM((slots, dim, BLOCK), f32),
         ],
-        out_shape=[pltpu.HBM((dim, edges), f32)]
-        + [shard] * len(own)
-        + [jax.ShapeDtypeStruct((len(others), dim, rows), bf16)],
-        input_output_aliases={count + 4: 0},
+        out_shape=[pltpu.HBM((dim, edges), f32)] + [shard] * count,
+        input_output_aliases={count + 5: 0},
         compiler_params=params(32),
         cost_estimate=cost(6 * dim * 1.5 * count * BLOCK * edges, 10 * dim * edges),
-    )(here, quota, *tables, neg_ids, in_hbm(query_b), in_hbm(query_grad))
-
-
-def relation_side(src_table, src_ids, rel_ids, query_grad, rel_count, chunk):
-    dim, rows = src_table.shape
-    edges = src_ids.shape[1]
-
-    def body(table, src, rel, grad_in, rel_out, high, low):
+    )(chip, lane, quota, *tables, neg_ids, in_hbm(query_b), in_hbm(query_grad))
+
+
+def relation_side(src_rows, rel_ids, query_grad, rel_count, chunk):
+    dim, edges = src_rows.shape
+
+    def body(rows_in, rel, grad_in, rel_out):
         @pl.when(pl.program_id(0) == 0)
         def _():
-            high[...], low[...] = split2(table[...])
             rel_out[...] = jnp.zeros_like(rel_out)
 
-        pick = select_rows(src[...], rows)
-        src_rows = dot_nn(high[...], pick) + dot_nn(low[...], pick)
         kinds = select_rows(rel[...], rel_count)
-        upper, lower = split2(back(grad_in[...], src_rows))
+        upper, lower = split2(back(grad_in[...], rows_in[...]))
         rel_out[...] += dot_nt(kinds, upper) + dot_nt(kinds, lower)
 
     return pl.pallas_call(
         body,
         name="relation_side",
         grid=(edges // chunk,),
-        in_specs=[whole((dim, rows)), lanes(1, chunk), lanes(1, chunk), lanes(dim, chunk)],
+        in_specs=[lanes(dim, chunk), lanes(1, chunk), lanes(dim, chunk)],
         out_specs=whole((rel_count, dim)),
         out_shape=jax.ShapeDtypeStruct((rel_count, dim), f32),
-        scratch_shapes=[pltpu.VMEM((dim, rows), bf16)] * 2,
         compiler_params=params(24),
-        cost_estimate=cost(4 * dim * rows * edges, 4 * dim * edges),
-    )(in_hbm(src_table), in_hbm(src_ids), in_hbm(rel_ids), in_hbm(query_grad))
+        cost_estimate=cost(4 * dim * rel_count * edges, 8 * dim * edges),
+    )(in_hbm(src_rows), in_hbm(rel_ids), in_hbm(query_grad))
 
 
 def source_side(src_table, src_state, rel_parts, src_ids, rel_ids, query_grad, rel_count, chunk):
@@ -361,7 +344,7 @@
         out, state_out = refs[3 + count :]
         total = own_ref[...]
         for ref in refs[3 : 3 + count]:
-            total = total + (ref[0] if len(ref.shape) == 3 else ref[...]).astype(f32)
+            total = total + ref[...].astype(f32)
         packed = low_ref[...].astype(f32)
         state = packed[dim : dim + 1] + packed[dim + 1 : dim + 2] + packed[dim + 2 : dim + 3]
         new_state = state + jnp.sum(total * total, axis=0, keepdims=True) / dim
@@ -371,17 +354,12 @@
 
     width = min(rows, 128)
 
-    def column(array):
-        if array.ndim == 3:
-            return pl.BlockSpec((1, dim, width), lambda i: (0, 0, i))
-        return lanes(array.shape[0], width)
-
     operands = [high, low_state, own_grad, *grads]
     return pl.pallas_call(
         body,
         name="destination_side",
         grid=(rows // width,),
-        in_specs=[column(array) for array in operands],
+        in_specs=[lanes(array.shape[0], width) for array in operands],
         out_specs=[lanes(dim, width), lanes(1, width)],
         out_shape=[
             jax.ShapeDtypeStruct((dim, rows), f32),
@@ -523,15 +501,84 @@
     )(matching, here, *flat, *flat_found)
 
 
+def total_of_peers(value, axis, stride, n):
+    count = lax.axis_size(axis)
+
+    def peer(i, k):
+        digit = (i // stride) % n
+        return i + ((digit ^ k) - digit) * stride
+
+    terms = [value]
+    terms += [
+        lax.ppermute(value, axis, [(i, peer(i, k)) for i in range(count)]) for k in range(1, n)
+    ]
+    while len(terms) > 1:
+        terms = [terms[i] + terms[i + 1] for i in range(0, len(terms), 2)]
+    return terms[0]
+
+
 def total_over_mesh(value):
-    for axis in ("edge", "dom"):
-        count = lax.axis_size(axis)
-        step = 1
-        while step < count:
-            other = lax.ppermute(value, axis, [(i, i ^ step) for i in range(count)])
-            value = value + other
-            step *= 2
-    return value
+    down, across = grid_of(lax.axis_size("dom"))
+    value = total_of_peers(value, "edge", 1, CORES)
+    value = total_of_peers(value, "edge", CORES, lax.axis_size("edge") // CORES)
+    if down * across <= 4:
+        return total_of_peers(value, "dom", 1, down * across)
+    value = total_of_peers(value, "dom", 1, across)
+    return total_of_peers(value, "dom", across, down)
+
+
+def visits(chips):
+    orders = []
+    for z in range(chips):
+        left, order = set(range(chips)) - {z}, []
+        for k in range(1, chips):
+            near = [t for t in left if abs(t - z) <= k]
+            near.sort(key=lambda t: (abs(t - z), (t > z) == (2 * z < chips)))
+            order.append(near[-1])
+            left.remove(near[-1])
+        orders.append(order)
+    return orders
+
+
+def rounds(orders, step):
+    result = []
+    for z, order in enumerate(orders):
+        pair = (z, order[step])
+        for group in result:
+            if all(pair[1] != other[1] for other in group):
+                group.append(pair)
+                break
+        else:
+            result.append([pair])
+    return result
+
+
+def pick_table(candidates, which, chip):
+    if len(candidates) == 1:
+        return candidates[0]
+
+    def body(chip_ref, *refs):
+        out = refs[-1]
+        place = chip_ref[0]
+        for k in range(len(candidates)):
+            hits = [place == z for z in range(len(which)) if which[z] == k]
+            hit = hits[0]
+            for more in hits[1:]:
+                hit = jnp.logical_or(hit, more)
+
+            @pl.when(hit)
+            def _(k=k):
+                out[...] = refs[k][...]
+
+    vmem = pl.BlockSpec(memory_space=pltpu.VMEM)
+    return pl.pallas_call(
+        body,
+        in_specs=[pl.BlockSpec(memory_space=pltpu.SMEM)] + [vmem] * len(candidates),
+        out_specs=vmem,
+        out_shape=jax.ShapeDtypeStruct(candidates[0].shape, bf16),
+        compiler_params=pltpu.CompilerParams(vmem_limit_bytes=16 * MIB),
+        cost_estimate=cost(0, 4 * candidates[0].size),
+    )(chip, *candidates)
 
 
 def shards(
@@ -568,7 +615,7 @@
     rest, part_high = lax.optimization_barrier((rest, part_high))
     low_state = route([rest], matching, place)
 
-    query, query_b = make_queries(src_table, rel_parts, src_ids, rel_ids, rel_count, chunk)
+    query, query_b, src_rows = make_queries(src_table, rel_parts, src_ids, rel_ids, rel_count, chunk)
     query_grad, own_grad = positives(part_high, query, dst_ids, chunk)
 
     swap = [(i, i ^ 1) for i in range(edge_count)]
@@ -576,43 +623,38 @@
     def swapped(array):
         return lax.ppermute(array, "edge", swap)
 
-    near = swapped(part_high)
-    from_below = from_above = part_high
+    orders = visits(chips)
+    chip = here // CORES
+    lane = here % CORES
+    goals = [chip] + [
+        sum(jnp.where(chip == z, orders[z][k], 0) for z in range(chips)) for k in range(chips - 1)
+    ]
+    at_offset = {0: part_high}
     arrived = []
-    for group in groups_of(chips):
-        tables, shifts = [], []
-        for s in group:
-            if s == 0:
-                tables += [part_high, near]
-                shifts += [(True, 0), (False, 0)]
-                continue
+    for k in range(chips):
+        if k:
             last = edge_count - CORES
-            up = [(i, i + CORES) for i in range(CORES * (s - 1), last)]
-            down = [(i + CORES, i) for i in range(0, last - CORES * (s - 1))]
-            from_below = lax.ppermute(from_below, "edge", up)
-            from_above = lax.ppermute(from_above, "edge", down)
-            far = CORES * s
-            tables += [from_below, from_above]
-            tables += [swapped(from_below), swapped(from_above)]
-            shifts += [(True, -far), (True, far), (False, -far), (False, far)]
-        query_grad, *mine, theirs = negative_wave(
-            tables, shifts, here, quotas, neg_ids, query_b, query_grad, wave_chunk
+            up = [(i, i + CORES) for i in range(CORES * (k - 1), last)]
+            down = [(i + CORES, i) for i in range(0, last - CORES * (k - 1))]
+            at_offset[-k] = lax.ppermute(at_offset[1 - k], "edge", up)
+            at_offset[k] = lax.ppermute(at_offset[k - 1], "edge", down)
+        offsets = [orders[z][k - 1] - z if k else 0 for z in range(chips)]
+        kinds = sorted(set(offsets))
+        table = pick_table([at_offset[d] for d in kinds], [kinds.index(d) for d in offsets], chip)
+        tables = [table, swapped(table)]
+        query_grad, mine, theirs = negative_wave(
+            tables, goals[k], quotas, neg_ids, query_b, query_grad, lane, wave_chunk
         )
-        theirs = swapped(theirs).astype(f32)
-        at = 0
-        for s in group:
-            far = CORES * s
-            below = [(i, i - far) for i in range(far, edge_count)]
-            above = [(i, i + far) for i in range(edge_count - far)]
-            for pairs in (below, above):
-                total = mine[at].astype(f32) + theirs[at]
-                at += 1
-                if s == 0:
-                    arrived.append(total)
-                    break
-                arrived.append(lax.ppermute(total.astype(bf16), "edge", pairs))
-
-    rel_grad = relation_side(src_table, src_ids, rel_ids, query_grad, rel_count, chunk)
+        total = mine.astype(f32) + swapped(theirs).astype(f32)
+        if not k:
+            arrived.append(total)
+            continue
+        total = total.astype(bf16)
+        for group in rounds(orders, k - 1):
+            pairs = [(CORES * z + c, CORES * t + c) for z, t in group for c in range(CORES)]
+            arrived.append(lax.ppermute(total, "edge", pairs))
+
+    rel_grad = relation_side(src_rows, rel_ids, query_grad, rel_count, chunk)
     src_out, src_state_out = source_side(
         src_table,
         src_state.reshape(1, row_count),
@@ -632,10 +674,6 @@
         dst_state_out.reshape(row_count),
         relation_out,
     )
-
-
-def groups_of(chips):
-    return [list(range(min(2, chips)))] + [[s] for s in range(2, chips)]
 
 
 def solution(mesh):

time: 168 us -> 172 us (1.024)
  the two profiles are of different devices: /device:TPU:22 before, /device:TPU:0 now
where the time goes in v4:
time: 172 us; the launch traced here: 171 us
  Pallas kernels  84.4 us (49%)
  starting transfers between devices  44.1 us (26%)
  waiting for transfers between devices  37.9 us (22%)
  local copies, waits for them, and re-layouts  2.18 us (1%)
  other arithmetic  1.84 us (1%)
    pallas_call x4, Pallas kernels, negative_wave(): pl.pallas_call(body, grid=(edges // chunk,), in_specs=[smem, smem, smem]...  46.6 us
    ppermute x7, starting transfers between devices, total_of_peers(): lax.ppermute(value, axis, [(i, peer(i, k)) for i in range(count)])  16 us
    ppermute x5, waiting for transfers between devices, shards(): arrived.append(lax.ppermute(total, 'edge', pairs))  14 us
    ppermute x7, waiting for transfers between devices, total_of_peers(): lax.ppermute(value, axis, [(i, peer(i, k)) for i in range(count)])  11.9 us
    pallas_call x1, Pallas kernels, make_queries(): pl.pallas_call(body, name='make_queries', grid=(edges // chunk,), in_spec...  9.63 us
    ppermute x5, starting transfers between devices, shards(): arrived.append(lax.ppermute(total, 'edge', pairs))  9.5 us
    ppermute x6, waiting for transfers between devices, shifted(): lax.ppermute(array, 'dom', [(d, moved(d, n, stride, shift)) for d in rang...  8.77 us
    pallas_call x1, Pallas kernels, positives(): pl.pallas_call(body, name='positives', grid=(edges // chunk,), in_specs=[...  7.99 us
  transfers between devices with their start and end apart: 32, of which 11 were waited for; matrix products, arithmetic and copies ran while one was open for 2% of the time, Pallas kernels for 46%

profile of v4, /device:TPU:0, one launch (start us, length us, event | category | flops | bytes accessed | tf_op | source)
XLA Modules:
  0.0 171.4 jit_solution(10166629183235739155)
XLA Ops:
  1.9 3.0 %collective-permute-start = (bf16[400,256]{1,0:T(8,128)(2,1)S(1)}, bf16[400,256]{1,0:T(8,128)(2,1)S(1)}, u32[]{:S(2)}, u32[]{:S(2)}) collective-permute-start(bf16[400,256]{1,0:T(8,128)(2,1)S(1)} %get-tuple-element.34.refs_0_), channel_id=1, source_target_pairs={{0,8},{8,0},{16,24},{24,16},{1,9},{9,1},{17,25},{25,17},{2,10},{10... | collective-permute-start | bytes 614408 | tf_op jit(solution)/shard_map/ppermute | solution.py:421
  5.0 1.5 collective-permute-start.1
  7.2 2.9 %collective-permute-done.refs_1_ = bf16[400,256]{1,0:T(8,128)(2,1)S(1)} collective-permute-done((bf16[400,256]{1,0:T(8,128)(2,1)S(1)}, bf16[400,256]{1,0:T(8,128)(2,1)S(1)}, u32[]{:S(2)}, u32[]{:S(2)}) %collective-permute-start) | collective-permute-done | bytes 204832 | tf_op jit(solution)/shard_map/ppermute | solution.py:421
  12.8 1.6 collective-permute-start.2
  15.7 2.9 %collective-permute-done.2.refs_4_ = bf16[400,256]{1,0:T(8,128)(2,1)S(1)} collective-permute-done((bf16[400,256]{1,0:T(8,128)(2,1)S(1)}, bf16[400,256]{1,0:T(8,128)(2,1)S(1)}, u32[]{:S(2)}, u32[]{:S(2)}) %collective-permute-start.2) | collective-permute-done | bytes 204832 | tf_op jit(solution)/shard_map/ppermute | solution.py:421
  22.7 4.6 %collective-permute-start.4 = (bf16[400,512]{1,0:T(8,128)(2,1)S(1)}, bf16[400,512]{1,0:T(8,128)(2,1)S(1)}, u32[]{:S(2)}, u32[]{:S(2)}) collective-permute-start(bf16[400,512]{1,0:T(8,128)(2,1)S(1)} %shard_map.147.table.refs_0_), channel_id=1, source_target_pairs={{0,2},{1,3},{2,4},{3,5},{4,6},{5,7},{8,10},{9,11},{10,12},{11,13},... | collective-permute-start | bytes 1228808 | tf_op jit(solution)/shard_map/ppermute | solution.py:639
  27.5 9.6 %make_queries.1 = (f32[400,4096]{1,0:T(8,128)}, bf16[400,4096]{1,0:T(8,128)(2,1)}, f32[400,4096]{1,0:T(8,128)}) custom-call(f32[400,512]{1,0:T(8,128)} %table.3, bf16[400,128]{1,0:T(8,128)(2,1)S(1)} %pad.4.parts, s32[1,4096]{1,0:T(1,128)} %bitcast.16, s32[1,4096]{1,0:T(1,128)} %bitcast.11), custom_call_target="tpu_custom_call" | custom-call | flops 3355443200 | bytes 9830400 | tf_op jit(solution)/shard_map/make_queries/pallas_call | solution.py:108
  39.7 8.0 %positives.1 = (f32[400,4096]{1,0:T(8,128)}, f32[400,512]{1,0:T(8,128)S(1)}) custom-call(bf16[400,512]{1,0:T(8,128)(2,1)S(1)} %shard_map.147.table.refs_0_, f32[400,4096]{1,0:T(8,128)} %get-tuple-element.40.query_in, s32[1,4096]{1,0:T(1,128)} %bitcast.15), custom_call_target="tpu_custom_call" | custom-call | flops 5033164800 | bytes 13107200 | tf_op jit(solution)/shard_map/positives/pallas_call | solution.py:142
  48.0 3.2 %collective-permute-done.8.refs_1_ = bf16[400,512]{1,0:T(8,128)(2,1)S(1)} collective-permute-done((bf16[400,512]{1,0:T(8,128)(2,1)S(1)}, bf16[400,512]{1,0:T(8,128)(2,1)S(1)}, u32[]{:S(2)}, u32[]{:S(2)}) %collective-permute-start.8) | collective-permute-done | bytes 409632 | tf_op jit(solution)/shard_map/ppermute | solution.py:640
  53.2 12.5 %shard_map.151 = (f32[400,4096]{1,0:T(8,128)}, bf16[400,512]{1,0:T(8,128)(2,1)S(1)}, bf16[400,512]{1,0:T(8,128)(2,1)S(1)}) custom-call(s32[1]{0:T(128)S(6)} %select_n.43.chip_ref, s32[1]{0:T(128)S(6)} %select_n.46.lane_ref, s32[1,8]{1,0:T(1,128)S(1)} %copy-done.3, bf16[400,512]{1,0:T(8,128)(2,1)S(1)} %shard_map.147.table.refs_0_, ...), custom_call_target="tpu_custom_call", output_to_operand_aliasing={{0}: (7, {})} | custom-call | flops 3774873600 | bytes 16384000 | tf_op jit(solution)/shard_map/pallas_call | solution.py:243
  67.2 12.5 %shard_map.152 = (f32[400,4096]{1,0:T(8,128)}, bf16[400,512]{1,0:T(8,128)(2,1)S(1)}, bf16[400,512]{1,0:T(8,128)(2,1)S(1)}) custom-call(s32[1]{0:T(128)S(6)} %add.69.chip_ref, s32[1]{0:T(128)S(6)} %select_n.46.lane_ref, s32[1,8]{1,0:T(1,128)S(1)} %copy-done.3, bf16[400,512]{1,0:T(8,128)(2,1)S(1)} %shard_map.150.refs_0_, ...), custom_call_target="tpu_custom_call", output_to_operand_aliasing={{0}: (7, {})} | custom-call | flops 3774873600 | bytes 16384000 | tf_op jit(solution)/shard_map/pallas_call | solution.py:243
  81.1 12.5 %shard_map.153 = (f32[400,4096]{1,0:T(8,128)}, bf16[400,512]{1,0:T(8,128)(2,1)S(1)}, bf16[400,512]{1,0:T(8,128)(2,1)S(1)}) custom-call(s32[1]{0:T(128)S(6)} %add.66.chip_ref, s32[1]{0:T(128)S(6)} %select_n.46.lane_ref, s32[1,8]{1,0:T(1,128)S(1)} %copy-done.3, bf16[400,512]{1,0:T(8,128)(2,1)S(1)} %shard_map.149.refs_0_, ...), custom_call_target="tpu_custom_call", output_to_operand_aliasing={{0}: (7, {})} | custom-call | flops 3774873600 | bytes 16384000 | tf_op jit(solution)/shard_map/pallas_call | solution.py:243
  93.6 9.1 %shard_map.154 = (f32[400,4096]{1,0:T(8,128)}, bf16[400,512]{1,0:T(8,128)(2,1)S(1)}, bf16[400,512]{1,0:T(8,128)(2,1)S(1)}) custom-call(s32[1]{0:T(128)S(6)} %add.63.chip_ref, s32[1]{0:T(128)S(6)} %select_n.46.lane_ref, s32[1,8]{1,0:T(1,128)S(1)} %copy-done.3, bf16[400,512]{1,0:T(8,128)(2,1)S(1)} %shard_map.148.refs_0_, ...), custom_call_target="tpu_custom_call", output_to_operand_aliasing={{0}: (7, {})} | custom-call | flops 3774873600 | bytes 16384000 | tf_op jit(solution)/shard_map/pallas_call | solution.py:243
  102.7 6.4 %relation_side.1 = f32[16,400]{1,0:T(8,128)S(1)} custom-call(f32[400,4096]{1,0:T(8,128)} %get-tuple-element.60.rows_in, s32[1,4096]{1,0:T(1,128)} %bitcast.12, f32[400,4096]{1,0:T(8,128)} %get-tuple-element.45.grad_in), custom_call_target="tpu_custom_call" | custom-call | flops 104857600 | bytes 13107200 | tf_op jit(solution)/shard_map/relation_side/pallas_call | solution.py:274
  109.1 4.0 %collective-permute-start.25 = (f32[16,400]{1,0:T(8,128)S(1)}, f32[16,400]{1,0:T(8,128)S(1)}, u32[]{:S(2)}, u32[]{:S(2)}) collective-permute-start(f32[16,400]{1,0:T(8,128)S(1)} %relation_side.1), channel_id=1, source_target_pairs={{0,1},{1,0},{2,3},{3,2},{4,5},{5,4},{6,7},{7,6},{8,9},{9,8},{10,11... | collective-permute-start | bytes 76808 | tf_op jit(solution)/shard_map/ppermute | solution.py:513
  113.9 7.8 %collective-permute-start.28 = (f32[16,400]{1,0:T(8,128)S(1)}, f32[16,400]{1,0:T(8,128)S(1)}, u32[]{:S(2)}, u32[]{:S(2)}) collective-permute-start(f32[16,400]{1,0:T(8,128)S(1)} %add.74), channel_id=1, source_target_pairs={{0,6},{1,7},{2,4},{3,5},{4,2},{5,3},{6,0},{7,1},{8,14},{9,15},{10,... | collective-permute-start | bytes 76808 | tf_op jit(solution)/shard_map/ppermute | solution.py:513
  122.5 9.8 %collective-permute-done.28 = f32[16,400]{1,0:T(8,128)S(1)} collective-permute-done((f32[16,400]{1,0:T(8,128)S(1)}, f32[16,400]{1,0:T(8,128)S(1)}, u32[]{:S(2)}, u32[]{:S(2)}) %collective-permute-start.28) | collective-permute-done | bytes 25632 | tf_op jit(solution)/shard_map/ppermute | solution.py:513
  132.3 1.7 collective-permute-start.18
  135.3 1.8 %collective-permute-start.30 = (f32[16,400]{1,0:T(8,128)S(1)}, f32[16,400]{1,0:T(8,128)S(1)}, u32[]{:S(2)}, u32[]{:S(2)}) collective-permute-start(f32[16,400]{1,0:T(8,128)S(1)} %add_add_fusion), channel_id=1, source_target_pairs={{0,16},{8,24},{16,0},{24,8},{1,17},{9,25},{17,1},{25,9},{2,18},{10... | collective-permute-start | bytes 76808 | tf_op jit(solution)/shard_map/ppermute | solution.py:513
  141.1 5.9 %collective-permute-start.23 = (bf16[400,512]{1,0:T(8,128)(2,1)S(1)}, bf16[400,512]{1,0:T(8,128)(2,1)S(1)}, u32[]{:S(2)}, u32[]{:S(2)}) collective-permute-start(bf16[400,512]{1,0:T(8,128)(2,1)S(1)} %add_convert_fusion), channel_id=1, source_target_pairs={{0,6},{1,7},{2,0},{3,1},{8,14},{9,15},{10,8},{11,9},{16,22},{17,23... | collective-permute-start | bytes 1228808 | tf_op jit(solution)/shard_map/ppermute | solution.py:655
  146.9 7.4 %source_side.1 = (f32[400,512]{1,0:T(8,128)}, f32[1,512]{1,0:T(1,128)}) custom-call(f32[400,512]{1,0:T(8,128)} %table.3, f32[1,512]{1,0:T(1,128)} %bitcast.18, bf16[400,128]{1,0:T(8,128)(2,1)S(1)} %pad.4.parts, s32[1,4096]{1,0:T(1,128)} %bitcast.17, s32[1,4096]{1,0:T(1,128)} %bitcast.13, f32[400,4096]{1,0:T(8,128)} %get-tuple-element.45.grad_in), custom_call_target="tpu_custom_call" | custom-call | flops 3355443200 | bytes 6553600 | tf_op jit(solution)/shard_map/source_side/pallas_call | solution.py:308
  154.9 10.6 %collective-permute-done.21.refs_6_ = bf16[400,512]{1,0:T(8,128)(2,1)S(1)} collective-permute-done((bf16[400,512]{1,0:T(8,128)(2,1)S(1)}, bf16[400,512]{1,0:T(8,128)(2,1)S(1)}, u32[]{:S(2)}, u32[]{:S(2)}) %collective-permute-start.21) | collective-permute-done | bytes 409632 | tf_op jit(solution)/shard_map/ppermute | solution.py:655
  165.5 3.4 %collective-permute-done.23.refs_7_ = bf16[400,512]{1,0:T(8,128)(2,1)S(1)} collective-permute-done((bf16[400,512]{1,0:T(8,128)(2,1)S(1)}, bf16[400,512]{1,0:T(8,128)(2,1)S(1)}, u32[]{:S(2)}, u32[]{:S(2)}) %collective-permute-start.23) | collective-permute-done | bytes 409632 | tf_op jit(solution)/shard_map/ppermute | solution.py:655
  169.0 2.5 %destination_side.1 = (f32[400,512]{1,0:T(8,128)}, f32[1,512]{1,0:T(1,128)}) custom-call(bf16[400,512]{1,0:T(8,128)(2,1)S(1)} %shard_map.147.table.refs_0_, bf16[416,512]{1,0:T(8,128)(2,1)S(1)} %shard_map.156.refs_1_, f32[400,512]{1,0:T(8,128)S(1)} %get-tuple-element.49.refs_2_, f32[400,512]{1,0:T(8,128)S(1)} %convert_add_fusion.refs_3_, ...), custom_call_target="tpu_custom_call" | custom-call | flops 1638400 | bytes 4915200 | tf_op jit(solution)/shard_map/destination_side/pallas_call | solution.py:358
  (79 shorter events, 25.4 us)
Async XLA Ops:
  21.4 16.2 %collective-permute-start.7 = (bf16[400,512]{1,0:T(8,128)(2,1)S(1)}, bf16[400,512]{1,0:T(8,128)(2,1)S(1)}, u32[]{:S(2)}, u32[]{:S(2)}) collective-permute-start(bf16[400,512]{1,0:T(8,128)(2,1)S(1)} %shard_map.147.table.refs_0_), channel_id=1, source_target_pairs={{2,0},{3,1},{4,2},{5,3},{6,4},{7,5},{10,8},{11,9},{12,10},{13,11},... | collective-permute-start | bytes 1228808 | tf_op jit(solution)/shard_map/ppermute | solution.py:640
  22.7 16.2 %collective-permute-start.4 = (bf16[400,512]{1,0:T(8,128)(2,1)S(1)}, bf16[400,512]{1,0:T(8,128)(2,1)S(1)}, u32[]{:S(2)}, u32[]{:S(2)}) collective-permute-start(bf16[400,512]{1,0:T(8,128)(2,1)S(1)} %shard_map.147.table.refs_0_), channel_id=1, source_target_pairs={{0,2},{1,3},{2,4},{3,5},{4,6},{5,7},{8,10},{9,11},{10,12},{11,13},... | collective-permute-start | bytes 1228808 | tf_op jit(solution)/shard_map/ppermute | solution.py:639
  37.1 16.0 %collective-permute-start.13 = (bf16[400,512]{1,0:T(8,128)(2,1)S(1)}, bf16[400,512]{1,0:T(8,128)(2,1)S(1)}, u32[]{:S(2)}, u32[]{:S(2)}) collective-permute-start(bf16[400,512]{1,0:T(8,128)(2,1)S(1)} %shard_map.147.table.refs_0_), channel_id=1, source_target_pairs={{0,1},{1,0},{2,3},{3,2},{4,5},{5,4},{6,7},{7,6},{8,9},{9,8},{10,11... | collective-permute-start | bytes 1228808 | tf_op jit(solution)/shard_map/ppermute | solution.py:624
  37.1 28.5 %collective-permute-start.14 = (bf16[416,512]{1,0:T(8,128)(2,1)S(1)}, bf16[416,512]{1,0:T(8,128)(2,1)S(1)}, u32[]{:S(2)}, u32[]{:S(2)}) collective-permute-start(bf16[416,512]{1,0:T(8,128)(2,1)S(1)} %get-tuple-element.48.refs_0_), channel_id=1, source_target_pairs={{0,8},{8,0},{16,24},{24,16},{1,9},{9,1},{17,25},{25,17},{2,10},{10... | collective-permute-start | bytes 1277960 | tf_op jit(solution)/shard_map/ppermute | solution.py:421
  37.7 13.5 %collective-permute-start.8 = (bf16[400,512]{1,0:T(8,128)(2,1)S(1)}, bf16[400,512]{1,0:T(8,128)(2,1)S(1)}, u32[]{:S(2)}, u32[]{:S(2)}) collective-permute-start(bf16[400,512]{1,0:T(8,128)(2,1)S(1)} %collective-permute-done.7.refs_2_.refs_1_), channel_id=1, source_target_pairs={{2,0},{3,1},{4,2},{5,3},{10,8},{11,9},{12,10},{13,11},{18,16},{19,... | collective-permute-start | bytes 1228808 | tf_op jit(solution)/shard_map/ppermute | solution.py:640
  39.0 13.5 %collective-permute-start.5 = (bf16[400,512]{1,0:T(8,128)(2,1)S(1)}, bf16[400,512]{1,0:T(8,128)(2,1)S(1)}, u32[]{:S(2)}, u32[]{:S(2)}) collective-permute-start(bf16[400,512]{1,0:T(8,128)(2,1)S(1)} %collective-permute-done.4.refs_1_.refs_0_), channel_id=1, source_target_pairs={{2,4},{3,5},{4,6},{5,7},{10,12},{11,13},{12,14},{13,15},{18,20},{1... | collective-permute-start | bytes 1228808 | tf_op jit(solution)/shard_map/ppermute | solution.py:639
  47.7 19.2 %collective-permute-start.12 = (bf16[400,512]{1,0:T(8,128)(2,1)S(1)}, bf16[400,512]{1,0:T(8,128)(2,1)S(1)}, u32[]{:S(2)}, u32[]{:S(2)}) collective-permute-start(bf16[400,512]{1,0:T(8,128)(2,1)S(1)} %shard_map.150.refs_0_), channel_id=1, source_target_pairs={{0,1},{1,0},{2,3},{3,2},{4,5},{5,4},{6,7},{7,6},{8,9},{9,8},{10,11... | collective-permute-start | bytes 1228808 | tf_op jit(solution)/shard_map/ppermute | solution.py:624
  51.1 28.6 %collective-permute-start.9 = (bf16[400,512]{1,0:T(8,128)(2,1)S(1)}, bf16[400,512]{1,0:T(8,128)(2,1)S(1)}, u32[]{:S(2)}, u32[]{:S(2)}) collective-permute-start(bf16[400,512]{1,0:T(8,128)(2,1)S(1)} %collective-permute-done.8.refs_1_), channel_id=1, source_target_pairs={{2,0},{3,1},{10,8},{11,9},{18,16},{19,17},{26,24},{27,25}} | collective-permute-start | bytes 1228808 | tf_op jit(solution)/shard_map/ppermute | solution.py:640
  52.4 27.3 %collective-permute-start.6 = (bf16[400,512]{1,0:T(8,128)(2,1)S(1)}, bf16[400,512]{1,0:T(8,128)(2,1)S(1)}, u32[]{:S(2)}, u32[]{:S(2)}) collective-permute-start(bf16[400,512]{1,0:T(8,128)(2,1)S(1)} %collective-permute-done.5.refs_0_), channel_id=1, source_target_pairs={{4,6},{5,7},{12,14},{13,15},{20,22},{21,23},{28,30},{29,31}} | collective-permute-start | bytes 1228808 | tf_op jit(solution)/shard_map/ppermute | solution.py:639
  65.6 14.7 %collective-permute-start.16 = (bf16[400,512]{1,0:T(8,128)(2,1)S(1)}, bf16[400,512]{1,0:T(8,128)(2,1)S(1)}, u32[]{:S(2)}, u32[]{:S(2)}) collective-permute-start(bf16[400,512]{1,0:T(8,128)(2,1)S(1)} %get-tuple-element.51), channel_id=1, source_target_pairs={{0,1},{1,0},{2,3},{3,2},{4,5},{5,4},{6,7},{7,6},{8,9},{9,8},{10,11... | collective-permute-start | bytes 1228808 | tf_op jit(solution)/shard_map/ppermute | solution.py:624
  66.3 14.1 %collective-permute-start.15 = (bf16[416,512]{1,0:T(8,128)(2,1)S(1)}, bf16[416,512]{1,0:T(8,128)(2,1)S(1)}, u32[]{:S(2)}, u32[]{:S(2)}) collective-permute-start(bf16[416,512]{1,0:T(8,128)(2,1)S(1)} %shard_map.155), channel_id=1, source_target_pairs={{0,16},{8,24},{16,0},{24,8},{1,17},{9,25},{17,1},{25,9},{2,18},{10... | collective-permute-start | bytes 1277960 | tf_op jit(solution)/shard_map/ppermute | solution.py:421
  66.9 14.1 %collective-permute-start.11 = (bf16[400,512]{1,0:T(8,128)(2,1)S(1)}, bf16[400,512]{1,0:T(8,128)(2,1)S(1)}, u32[]{:S(2)}, u32[]{:S(2)}) collective-permute-start(bf16[400,512]{1,0:T(8,128)(2,1)S(1)} %shard_map.149.refs_0_), channel_id=1, source_target_pairs={{0,1},{1,0},{2,3},{3,2},{4,5},{5,4},{6,7},{7,6},{8,9},{9,8},{10,11... | collective-permute-start | bytes 1228808 | tf_op jit(solution)/shard_map/ppermute | solution.py:624
  79.7 33.3 %collective-permute-start.17 = (bf16[400,512]{1,0:T(8,128)(2,1)S(1)}, bf16[400,512]{1,0:T(8,128)(2,1)S(1)}, u32[]{:S(2)}, u32[]{:S(2)}) collective-permute-start(bf16[400,512]{1,0:T(8,128)(2,1)S(1)} %get-tuple-element.53), channel_id=1, source_target_pairs={{0,1},{1,0},{2,3},{3,2},{4,5},{5,4},{6,7},{7,6},{8,9},{9,8},{10,11... | collective-permute-start | bytes 1228808 | tf_op jit(solution)/shard_map/ppermute | solution.py:624
  79.8 13.8 %collective-permute-start.10 = (bf16[400,512]{1,0:T(8,128)(2,1)S(1)}, bf16[400,512]{1,0:T(8,128)(2,1)S(1)}, u32[]{:S(2)}, u32[]{:S(2)}) collective-permute-start(bf16[400,512]{1,0:T(8,128)(2,1)S(1)} %shard_map.148.refs_0_), channel_id=1, source_target_pairs={{0,1},{1,0},{2,3},{3,2},{4,5},{5,4},{6,7},{7,6},{8,9},{9,8},{10,11... | collective-permute-start | bytes 1228808 | tf_op jit(solution)/shard_map/ppermute | solution.py:624
  93.6 28.2 %collective-permute-start.20 = (bf16[400,512]{1,0:T(8,128)(2,1)S(1)}, bf16[400,512]{1,0:T(8,128)(2,1)S(1)}, u32[]{:S(2)}, u32[]{:S(2)}) collective-permute-start(bf16[400,512]{1,0:T(8,128)(2,1)S(1)} %get-tuple-element.55), channel_id=1, source_target_pairs={{0,1},{1,0},{2,3},{3,2},{4,5},{5,4},{6,7},{7,6},{8,9},{9,8},{10,11... | collective-permute-start | bytes 1228808 | tf_op jit(solution)/shard_map/ppermute | solution.py:624
  113.1 41.8 %collective-permute-start.19 = (bf16[400,512]{1,0:T(8,128)(2,1)S(1)}, bf16[400,512]{1,0:T(8,128)(2,1)S(1)}, u32[]{:S(2)}, u32[]{:S(2)}) collective-permute-start(bf16[400,512]{1,0:T(8,128)(2,1)S(1)} %add_convert_fusion.2), channel_id=1, source_target_pairs={{4,2},{5,3},{6,4},{7,5},{12,10},{13,11},{14,12},{15,13},{20,18},{2... | collective-permute-start | bytes 1228808 | tf_op jit(solution)/shard_map/ppermute | solution.py:655
  113.8 23.3 %collective-permute-start.22 = (bf16[400,512]{1,0:T(8,128)(2,1)S(1)}, bf16[400,512]{1,0:T(8,128)(2,1)S(1)}, u32[]{:S(2)}, u32[]{:S(2)}) collective-permute-start(bf16[400,512]{1,0:T(8,128)(2,1)S(1)} %get-tuple-element.57), channel_id=1, source_target_pairs={{0,1},{1,0},{2,3},{3,2},{4,5},{5,4},{6,7},{7,6},{8,9},{9,8},{10,11... | collective-permute-start | bytes 1228808 | tf_op jit(solution)/shard_map/ppermute | solution.py:624
  113.9 18.4 %collective-permute-start.28 = (f32[16,400]{1,0:T(8,128)S(1)}, f32[16,400]{1,0:T(8,128)S(1)}, u32[]{:S(2)}, u32[]{:S(2)}) collective-permute-start(f32[16,400]{1,0:T(8,128)S(1)} %add.74), channel_id=1, source_target_pairs={{0,6},{1,7},{2,4},{3,5},{4,2},{5,3},{6,0},{7,1},{8,14},{9,15},{10,... | collective-permute-start | bytes 76808 | tf_op jit(solution)/shard_map/ppermute | solution.py:513
  121.8 12.2 %collective-permute-start.27 = (f32[16,400]{1,0:T(8,128)S(1)}, f32[16,400]{1,0:T(8,128)S(1)}, u32[]{:S(2)}, u32[]{:S(2)}) collective-permute-start(f32[16,400]{1,0:T(8,128)S(1)} %add.74), channel_id=1, source_target_pairs={{0,4},{1,5},{2,6},{3,7},{4,0},{5,1},{6,2},{7,3},{8,12},{9,13},{10,... | collective-permute-start | bytes 76808 | tf_op jit(solution)/shard_map/ppermute | solution.py:513
  121.8 12.2 %collective-permute-start.26 = (f32[16,400]{1,0:T(8,128)S(1)}, f32[16,400]{1,0:T(8,128)S(1)}, u32[]{:S(2)}, u32[]{:S(2)}) collective-permute-start(f32[16,400]{1,0:T(8,128)S(1)} %add.74), channel_id=1, source_target_pairs={{0,2},{1,3},{2,0},{3,1},{4,6},{5,7},{6,4},{7,5},{8,10},{9,11},{10,... | collective-permute-start | bytes 76808 | tf_op jit(solution)/shard_map/ppermute | solution.py:513
  132.3 22.6 %collective-permute-start.18 = (bf16[400,512]{1,0:T(8,128)(2,1)S(1)}, bf16[400,512]{1,0:T(8,128)(2,1)S(1)}, u32[]{:S(2)}, u32[]{:S(2)}) collective-permute-start(bf16[400,512]{1,0:T(8,128)(2,1)S(1)} %add_convert_fusion.2), channel_id=1, source_target_pairs={{0,2},{1,3},{2,4},{3,5},{8,10},{9,11},{10,12},{11,13},{16,18},{17,... | collective-permute-start | bytes 1228808 | tf_op jit(solution)/shard_map/ppermute | solution.py:655
  138.9 26.6 %collective-permute-start.21 = (bf16[400,512]{1,0:T(8,128)(2,1)S(1)}, bf16[400,512]{1,0:T(8,128)(2,1)S(1)}, u32[]{:S(2)}, u32[]{:S(2)}) collective-permute-start(bf16[400,512]{1,0:T(8,128)(2,1)S(1)} %add_convert_fusion.1), channel_id=1, source_target_pairs={{0,4},{1,5},{2,6},{3,7},{4,0},{5,1},{6,2},{7,3},{8,12},{9,13},{10,... | collective-permute-start | bytes 1228808 | tf_op jit(solution)/shard_map/ppermute | solution.py:655
  139.3 26.3 %collective-permute-start.24 = (bf16[400,512]{1,0:T(8,128)(2,1)S(1)}, bf16[400,512]{1,0:T(8,128)(2,1)S(1)}, u32[]{:S(2)}, u32[]{:S(2)}) collective-permute-start(bf16[400,512]{1,0:T(8,128)(2,1)S(1)} %add_convert_fusion), channel_id=1, source_target_pairs={{4,6},{5,7},{6,0},{7,1},{12,14},{13,15},{14,8},{15,9},{20,22},{21,... | collective-permute-start | bytes 1228808 | tf_op jit(solution)/shard_map/ppermute | solution.py:655
  141.1 27.9 %collective-permute-start.23 = (bf16[400,512]{1,0:T(8,128)(2,1)S(1)}, bf16[400,512]{1,0:T(8,128)(2,1)S(1)}, u32[]{:S(2)}, u32[]{:S(2)}) collective-permute-start(bf16[400,512]{1,0:T(8,128)(2,1)S(1)} %add_convert_fusion), channel_id=1, source_target_pairs={{0,6},{1,7},{2,0},{3,1},{8,14},{9,15},{10,8},{11,9},{16,22},{17,23... | collective-permute-start | bytes 1228808 | tf_op jit(solution)/shard_map/ppermute | solution.py:655
  (13 other events, 87.8 us)

commit v5 on v4

--- a/solution.py
+++ b/solution.py
@@ -89,11 +89,15 @@
     return dot_nn(rel_parts, jnp.where(hit, 1.0, 0.0).astype(bf16))
 
 
-def make_queries(src_table, rel_parts, src_ids, rel_ids, rel_count, chunk):
+def make_queries(src_table, rel_parts, src_ids, rel_ids, rel_count, chunk, part, parts, before):
     dim, rows = src_table.shape
     edges = src_ids.shape[1]
-
-    def body(table, parts, src, rel, query, query_b, rows_out, high, low):
+    steps = edges // chunk // parts
+    dtypes = (f32, bf16, f32)
+
+    def body(table, parts_ref, src, rel, *refs):
+        query, query_b, rows_out, high, low = refs[len(before) :]
+
         @pl.when(pl.program_id(0) == 0)
         def _():
             high[...], low[...] = split2(table[...])
@@ -101,25 +105,26 @@
         pick = select_rows(src[...], rows)
         src_rows = dot_nn(high[...], pick) + dot_nn(low[...], pick)
         rows_out[...] = src_rows
-        value = product(src_rows, relation_rows(parts[...], rel[...], rel_count))
+        value = product(src_rows, relation_rows(parts_ref[...], rel[...], rel_count))
         query[...] = value
         query_b[...] = value.astype(bf16)
 
+    def columns(height):
+        return pl.BlockSpec((height, chunk), lambda i: (0, i + part * steps))
+
     return pl.pallas_call(
         body,
         name="make_queries",
-        grid=(edges // chunk,),
-        in_specs=[whole((dim, rows)), whole(rel_parts.shape), lanes(1, chunk), lanes(1, chunk)],
-        out_specs=[lanes(dim, chunk)] * 3,
-        out_shape=[
-            pltpu.HBM((dim, edges), f32),
-            pltpu.HBM((dim, edges), bf16),
-            pltpu.HBM((dim, edges), f32),
-        ],
+        grid=(steps,),
+        in_specs=[whole((dim, rows)), whole(rel_parts.shape), columns(1), columns(1)]
+        + [pl.BlockSpec(memory_space=pl.ANY)] * len(before),
+        out_specs=[columns(dim)] * 3,
+        out_shape=[pltpu.HBM((dim, edges), dtype) for dtype in dtypes],
+        input_output_aliases={4 + i: i for i in range(len(before))},
         scratch_shapes=[pltpu.VMEM((dim, rows), bf16)] * 2,
         compiler_params=params(32),
-        cost_estimate=cost(4 * dim * rows * edges, 6 * dim * edges),
-    )(in_hbm(src_table), rel_parts, in_hbm(src_ids), in_hbm(rel_ids))
+        cost_estimate=cost(4 * dim * rows * edges // parts, 10 * dim * edges // parts),
+    )(in_hbm(src_table), rel_parts, in_hbm(src_ids), in_hbm(rel_ids), *map(in_hbm, before))
 
 
 def positives(part_high, query, dst_ids, chunk):
@@ -509,9 +514,8 @@
         return i + ((digit ^ k) - digit) * stride
 
     terms = [value]
-    terms += [
-        lax.ppermute(value, axis, [(i, peer(i, k)) for i in range(count)]) for k in range(1, n)
-    ]
+    for k in range(1, n):
+        terms.append(lax.ppermute(value, axis, [(i, peer(i, k)) for i in range(count)]))
     while len(terms) > 1:
         terms = [terms[i] + terms[i + 1] for i in range(0, len(terms), 2)]
     return terms[0]
@@ -525,60 +529,6 @@
         return total_of_peers(value, "dom", 1, down * across)
     value = total_of_peers(value, "dom", 1, across)
     return total_of_peers(value, "dom", across, down)
-
-
-def visits(chips):
-    orders = []
-    for z in range(chips):
-        left, order = set(range(chips)) - {z}, []
-        for k in range(1, chips):
-            near = [t for t in left if abs(t - z) <= k]
-            near.sort(key=lambda t: (abs(t - z), (t > z) == (2 * z < chips)))
-            order.append(near[-1])
-            left.remove(near[-1])
-        orders.append(order)
-    return orders
-
-
-def rounds(orders, step):
-    result = []
-    for z, order in enumerate(orders):
-        pair = (z, order[step])
-        for group in result:
-            if all(pair[1] != other[1] for other in group):
-                group.append(pair)
-                break
-        else:
-            result.append([pair])
-    return result
-
-
-def pick_table(candidates, which, chip):
-    if len(candidates) == 1:
-        return candidates[0]
-
-    def body(chip_ref, *refs):
-        out = refs[-1]
-        place = chip_ref[0]
-        for k in range(len(candidates)):
-            hits = [place == z for z in range(len(which)) if which[z] == k]
-            hit = hits[0]
-            for more in hits[1:]:
-                hit = jnp.logical_or(hit, more)
-
-            @pl.when(hit)
-            def _(k=k):
-                out[...] = refs[k][...]
-
-    vmem = pl.BlockSpec(memory_space=pltpu.VMEM)
-    return pl.pallas_call(
-        body,
-        in_specs=[pl.BlockSpec(memory_space=pltpu.SMEM)] + [vmem] * len(candidates),
-        out_specs=vmem,
-        out_shape=jax.ShapeDtypeStruct(candidates[0].shape, bf16),
-        compiler_params=pltpu.CompilerParams(vmem_limit_bytes=16 * MIB),
-        cost_estimate=cost(0, 4 * candidates[0].size),
-    )(chip, *candidates)
 
 
 def shards(
@@ -615,7 +565,12 @@
     rest, part_high = lax.optimization_barrier((rest, part_high))
     low_state = route([rest], matching, place)
 
-    query, query_b, src_rows = make_queries(src_table, rel_parts, src_ids, rel_ids, rel_count, chunk)
+    made = []
+    for part in range(2):
+        made = make_queries(
+            src_table, rel_parts, src_ids, rel_ids, rel_count, min(chunk, edges // 2), part, 2, made
+        )
+    query, query_b, src_rows = made
     query_grad, own_grad = positives(part_high, query, dst_ids, chunk)
 
     swap = [(i, i ^ 1) for i in range(edge_count)]
@@ -623,36 +578,31 @@
     def swapped(array):
         return lax.ppermute(array, "edge", swap)
 
-    orders = visits(chips)
     chip = here // CORES
     lane = here % CORES
-    goals = [chip] + [
-        sum(jnp.where(chip == z, orders[z][k], 0) for z in range(chips)) for k in range(chips - 1)
-    ]
-    at_offset = {0: part_high}
-    arrived = []
+    arrived, done = [], []
     for k in range(chips):
+        pairs = [(i, i ^ (CORES * k)) for i in range(edge_count)]
+        table = part_high
         if k:
-            last = edge_count - CORES
-            up = [(i, i + CORES) for i in range(CORES * (k - 1), last)]
-            down = [(i + CORES, i) for i in range(0, last - CORES * (k - 1))]
-            at_offset[-k] = lax.ppermute(at_offset[1 - k], "edge", up)
-            at_offset[k] = lax.ppermute(at_offset[k - 1], "edge", down)
-        offsets = [orders[z][k - 1] - z if k else 0 for z in range(chips)]
-        kinds = sorted(set(offsets))
-        table = pick_table([at_offset[d] for d in kinds], [kinds.index(d) for d in offsets], chip)
-        tables = [table, swapped(table)]
+            if k >= 3:
+                table, _ = lax.optimization_barrier((table, done[k - 3]))
+            table = lax.ppermute(table, "edge", pairs)
         query_grad, mine, theirs = negative_wave(
-            tables, goals[k], quotas, neg_ids, query_b, query_grad, lane, wave_chunk
+            [table, swapped(table)],
+            chip ^ k,
+            quotas,
+            neg_ids,
+            query_b,
+            query_grad,
+            lane,
+            wave_chunk,
         )
         total = mine.astype(f32) + swapped(theirs).astype(f32)
-        if not k:
-            arrived.append(total)
-            continue
-        total = total.astype(bf16)
-        for group in rounds(orders, k - 1):
-            pairs = [(CORES * z + c, CORES * t + c) for z, t in group for c in range(CORES)]
-            arrived.append(lax.ppermute(total, "edge", pairs))
+        if k:
+            total = lax.ppermute(total.astype(bf16), "edge", pairs)
+        arrived.append(total)
+        done.append(mine)
 
     rel_grad = relation_side(src_rows, rel_ids, query_grad, rel_count, chunk)
     src_out, src_state_out = source_side(

time: 172 us -> 164 us (0.953)
  the two profiles are of different devices: /device:TPU:0 before, /device:TPU:10 now
where the time goes in v5:
time: 164 us
  Pallas kernels  87.1 us (53%)
  waiting for transfers between devices  50.5 us (31%)
  starting transfers between devices  22.8 us (14%)
  other arithmetic  1.84 us (1%)
    pallas_call x4, Pallas kernels, negative_wave(): pl.pallas_call(body, grid=(edges // chunk,), in_specs=[smem, smem, smem]...  46.6 us
    ppermute x7, waiting for transfers between devices, total_of_peers(): lax.ppermute(value, axis, [(i, peer(i, k)) for i in range(count)])  19.4 us
    ppermute x3, waiting for transfers between devices, shards(): table = lax.ppermute(table, 'edge', pairs)  17.4 us
    pallas_call x2, Pallas kernels, make_queries(): pl.pallas_call(body, name='make_queries', grid=(steps,), in_specs=[whole(...  12.4 us
    ppermute x7, starting transfers between devices, total_of_peers(): lax.ppermute(value, axis, [(i, peer(i, k)) for i in range(count)])  10.5 us
    ppermute x3, waiting for transfers between devices, shards(): total = lax.ppermute(total.astype(bf16), 'edge', pairs)  9.61 us
    pallas_call x1, Pallas kernels, positives(): pl.pallas_call(body, name='positives', grid=(edges // chunk,), in_specs=[...  8.06 us
    pallas_call x1, Pallas kernels, source_side(): pl.pallas_call(body, name='source_side', grid=(edges // chunk,), in_specs...  7.28 us
  transfers between devices with their start and end apart: 27, of which 10 were waited for; matrix products, arithmetic and copies ran while one was open for 1% of the time, Pallas kernels for 50%

profile of v5, /device:TPU:10, one launch (start us, length us, event | category | flops | bytes accessed | tf_op | source)
XLA Modules:
  0.0 164.0 jit_solution(9626431940958349398)
XLA Ops:
  2.5 1.5 collective-permute-start.1
  5.0 3.8 %collective-permute-done.refs_1_ = bf16[400,256]{1,0:T(8,128)(2,1)S(1)} collective-permute-done((bf16[400,256]{1,0:T(8,128)(2,1)S(1)}, bf16[400,256]{1,0:T(8,128)(2,1)S(1)}, u32[]{:S(2)}, u32[]{:S(2)}) %collective-permute-start) | collective-permute-done | bytes 204832 | tf_op jit(solution)/shard_map/ppermute | solution.py:426
  10.4 1.6 collective-permute-start.2
  12.0 1.5 collective-permute-start.3
  13.4 6.2 %make_queries.2 = (f32[400,4096]{1,0:T(8,128)}, bf16[400,4096]{1,0:T(8,128)(2,1)}, f32[400,4096]{1,0:T(8,128)}) custom-call(f32[400,512]{1,0:T(8,128)} %table.5, bf16[400,128]{1,0:T(8,128)(2,1)S(1)} %pad.4.parts_ref.parts, s32[1,4096]{1,0:T(1,128)} %bitcast.15, s32[1,4096]{1,0:T(1,128)} %bitcast.11), custom_call_target="tpu_custom_call" | custom-call | flops 1677721600 | bytes 8192000 | tf_op jit(solution)/shard_map/make_queries/pallas_call | solution.py:115
  19.7 6.2 %make_queries.3 = (f32[400,4096]{1,0:T(8,128)}, bf16[400,4096]{1,0:T(8,128)(2,1)}, f32[400,4096]{1,0:T(8,128)}) custom-call(f32[400,512]{1,0:T(8,128)} %table.5, bf16[400,128]{1,0:T(8,128)(2,1)S(1)} %pad.4.parts_ref.parts, s32[1,4096]{1,0:T(1,128)} %bitcast.16, s32[1,4096]{1,0:T(1,128)} %bitcast.12, ...), custom_call_target="tpu_custom_call", output_to_operand_aliasing={{0}: (4, {}), {1}: (5, {}), {2}: (6, {})} | custom-call | flops 1677721600 | bytes 8192000 | tf_op jit(solution)/shard_map/make_queries/pallas_call | solution.py:115
  27.1 2.6 %collective-permute-start.7 = (bf16[400,512]{1,0:T(8,128)(2,1)S(1)}, bf16[400,512]{1,0:T(8,128)(2,1)S(1)}, u32[]{:S(2)}, u32[]{:S(2)}) collective-permute-start(bf16[400,512]{1,0:T(8,128)(2,1)S(1)} %shard_map.147.table.refs_0_), channel_id=1, source_target_pairs={{0,4},{1,5},{2,6},{3,7},{4,0},{5,1},{6,2},{7,3},{8,12},{9,13},{10,... | collective-permute-start | bytes 1228808 | tf_op jit(solution)/shard_map/ppermute | solution.py:590
  30.2 8.1 %positives.1 = (f32[400,4096]{1,0:T(8,128)}, f32[400,512]{1,0:T(8,128)S(1)}) custom-call(bf16[400,512]{1,0:T(8,128)(2,1)S(1)} %shard_map.147.table.refs_0_, f32[400,4096]{1,0:T(8,128)} %get-tuple-element.47.query_in, s32[1,4096]{1,0:T(1,128)} %bitcast.19), custom_call_target="tpu_custom_call" | custom-call | flops 5033164800 | bytes 13107200 | tf_op jit(solution)/shard_map/positives/pallas_call | solution.py:147
  38.3 12.5 %shard_map.148 = (f32[400,4096]{1,0:T(8,128)}, bf16[400,512]{1,0:T(8,128)(2,1)S(1)}, bf16[400,512]{1,0:T(8,128)(2,1)S(1)}) custom-call(s32[1]{0:T(128)S(6)} %select_n.12.chip_ref, s32[1]{0:T(128)S(6)} %select_n.13.lane_ref, s32[1,8]{1,0:T(1,128)S(1)} %copy-done.2, bf16[400,512]{1,0:T(8,128)(2,1)S(1)} %shard_map.147.table.refs_0_, ...), custom_call_target="tpu_custom_call", output_to_operand_aliasing={{0}: (7, {})} | custom-call | flops 3774873600 | bytes 16384000 | tf_op jit(solution)/shard_map/pallas_call | solution.py:248
  53.2 17.4 %collective-permute-done.5.refs_0_ = bf16[400,512]{1,0:T(8,128)(2,1)S(1)} collective-permute-done((bf16[400,512]{1,0:T(8,128)(2,1)S(1)}, bf16[400,512]{1,0:T(8,128)(2,1)S(1)}, u32[]{:S(2)}, u32[]{:S(2)}) %collective-permute-start.5) | collective-permute-done | bytes 409632 | tf_op jit(solution)/shard_map/ppermute | solution.py:590
  70.6 12.5 %shard_map.149 = (f32[400,4096]{1,0:T(8,128)}, bf16[400,512]{1,0:T(8,128)(2,1)S(1)}, bf16[400,512]{1,0:T(8,128)(2,1)S(1)}) custom-call(s32[1]{0:T(128)S(6)} %xor.11.chip_ref, s32[1]{0:T(128)S(6)} %select_n.13.lane_ref, s32[1,8]{1,0:T(1,128)S(1)} %copy-done.2, bf16[400,512]{1,0:T(8,128)(2,1)S(1)} %collective-permute-done.9.refs_0_, ...), custom_call_target="tpu_custom_call", output_to_operand_aliasing={{0}: (7, {})} | custom-call | flops 3774873600 | bytes 16384000 | tf_op jit(solution)/shard_map/pallas_call | solution.py:248
  83.1 12.5 %shard_map.150 = (f32[400,4096]{1,0:T(8,128)}, bf16[400,512]{1,0:T(8,128)(2,1)S(1)}, bf16[400,512]{1,0:T(8,128)(2,1)S(1)}) custom-call(s32[1]{0:T(128)S(6)} %xor.10.chip_ref, s32[1]{0:T(128)S(6)} %select_n.13.lane_ref, s32[1,8]{1,0:T(1,128)S(1)} %copy-done.2, bf16[400,512]{1,0:T(8,128)(2,1)S(1)} %collective-permute-done.7.refs_0_, ...), custom_call_target="tpu_custom_call", output_to_operand_aliasing={{0}: (7, {})} | custom-call | flops 3774873600 | bytes 16384000 | tf_op jit(solution)/shard_map/pallas_call | solution.py:248
  97.1 9.1 %shard_map.151 = (f32[400,4096]{1,0:T(8,128)}, bf16[400,512]{1,0:T(8,128)(2,1)S(1)}, bf16[400,512]{1,0:T(8,128)(2,1)S(1)}) custom-call(s32[1]{0:T(128)S(6)} %xor.9.chip_ref, s32[1]{0:T(128)S(6)} %select_n.13.lane_ref, s32[1,8]{1,0:T(1,128)S(1)} %copy-done.2, bf16[400,512]{1,0:T(8,128)(2,1)S(1)} %collective-permute-done.5.refs_0_, ...), custom_call_target="tpu_custom_call", output_to_operand_aliasing={{0}: (7, {})} | custom-call | flops 3774873600 | bytes 16384000 | tf_op jit(solution)/shard_map/pallas_call | solution.py:248
  106.2 6.4 %relation_side.1 = f32[16,400]{1,0:T(8,128)S(1)} custom-call(f32[400,4096]{1,0:T(8,128)} %get-tuple-element.68.rows_in, s32[1,4096]{1,0:T(1,128)} %bitcast.13, f32[400,4096]{1,0:T(8,128)} %get-tuple-element.54.grad_in), custom_call_target="tpu_custom_call" | custom-call | flops 104857600 | bytes 13107200 | tf_op jit(solution)/shard_map/relation_side/pallas_call | solution.py:279
  112.5 3.5 %collective-permute-start.20 = (f32[16,400]{1,0:T(8,128)S(1)}, f32[16,400]{1,0:T(8,128)S(1)}, u32[]{:S(2)}, u32[]{:S(2)}) collective-permute-start(f32[16,400]{1,0:T(8,128)S(1)} %relation_side.1), channel_id=1, source_target_pairs={{0,1},{1,0},{2,3},{3,2},{4,5},{5,4},{6,7},{7,6},{8,9},{9,8},{10,11... | collective-permute-start | bytes 76808 | tf_op jit(solution)/shard_map/ppermute | solution.py:518
  116.9 1.8 %collective-permute-start.21 = (f32[16,400]{1,0:T(8,128)S(1)}, f32[16,400]{1,0:T(8,128)S(1)}, u32[]{:S(2)}, u32[]{:S(2)}) collective-permute-start(f32[16,400]{1,0:T(8,128)S(1)} %add.47), channel_id=1, source_target_pairs={{0,2},{1,3},{2,0},{3,1},{4,6},{5,7},{6,4},{7,5},{8,10},{9,11},{10,... | collective-permute-start | bytes 76808 | tf_op jit(solution)/shard_map/ppermute | solution.py:518
  120.5 9.2 %collective-permute-done.21 = f32[16,400]{1,0:T(8,128)S(1)} collective-permute-done((f32[16,400]{1,0:T(8,128)S(1)}, f32[16,400]{1,0:T(8,128)S(1)}, u32[]{:S(2)}, u32[]{:S(2)}) %collective-permute-start.21) | collective-permute-done | bytes 25632 | tf_op jit(solution)/shard_map/ppermute | solution.py:518
  129.7 7.4 %collective-permute-done.22 = f32[16,400]{1,0:T(8,128)S(1)} collective-permute-done((f32[16,400]{1,0:T(8,128)S(1)}, f32[16,400]{1,0:T(8,128)S(1)}, u32[]{:S(2)}, u32[]{:S(2)}) %collective-permute-start.22) | collective-permute-done | bytes 25632 | tf_op jit(solution)/shard_map/ppermute | solution.py:518
  137.1 1.7 %collective-permute-done.23 = f32[16,400]{1,0:T(8,128)S(1)} collective-permute-done((f32[16,400]{1,0:T(8,128)S(1)}, f32[16,400]{1,0:T(8,128)S(1)}, u32[]{:S(2)}, u32[]{:S(2)}) %collective-permute-start.23) | collective-permute-done | bytes 25632 | tf_op jit(solution)/shard_map/ppermute | solution.py:518
  139.8 2.6 %collective-permute-start.26 = (f32[16,400]{1,0:T(8,128)S(1)}, f32[16,400]{1,0:T(8,128)S(1)}, u32[]{:S(2)}, u32[]{:S(2)}) collective-permute-start(f32[16,400]{1,0:T(8,128)S(1)} %add_add_fusion), channel_id=1, source_target_pairs={{0,24},{8,16},{16,8},{24,0},{1,25},{9,17},{17,9},{25,1},{2,26},{10... | collective-permute-start | bytes 76808 | tf_op jit(solution)/shard_map/ppermute | solution.py:518
  144.2 7.3 %source_side.1 = (f32[400,512]{1,0:T(8,128)}, f32[1,512]{1,0:T(1,128)}) custom-call(f32[400,512]{1,0:T(8,128)} %table.5, f32[1,512]{1,0:T(1,128)} %bitcast.20, bf16[400,128]{1,0:T(8,128)(2,1)S(1)} %pad.4.parts_ref.parts, s32[1,4096]{1,0:T(1,128)} %bitcast.17, s32[1,4096]{1,0:T(1,128)} %bitcast.14, f32[400,4096]{1,0:T(8,128)} %get-tuple-element.54.grad_in), custom_call_target="tpu_custom_call" | custom-call | flops 3355443200 | bytes 6553600 | tf_op jit(solution)/shard_map/source_side/pallas_call | solution.py:313
  152.1 2.2 %collective-permute-done.15.refs_4_ = bf16[400,512]{1,0:T(8,128)(2,1)S(1)} collective-permute-done((bf16[400,512]{1,0:T(8,128)(2,1)S(1)}, bf16[400,512]{1,0:T(8,128)(2,1)S(1)}, u32[]{:S(2)}, u32[]{:S(2)}) %collective-permute-start.15) | collective-permute-done | bytes 409632 | tf_op jit(solution)/shard_map/ppermute | solution.py:603
  154.3 7.4 %collective-permute-done.19.refs_6_ = bf16[400,512]{1,0:T(8,128)(2,1)S(1)} collective-permute-done((bf16[400,512]{1,0:T(8,128)(2,1)S(1)}, bf16[400,512]{1,0:T(8,128)(2,1)S(1)}, u32[]{:S(2)}, u32[]{:S(2)}) %collective-permute-start.19) | collective-permute-done | bytes 409632 | tf_op jit(solution)/shard_map/ppermute | solution.py:603
  161.7 2.3 %destination_side.1 = (f32[400,512]{1,0:T(8,128)}, f32[1,512]{1,0:T(1,128)}) custom-call(bf16[400,512]{1,0:T(8,128)(2,1)S(1)} %shard_map.147.table.refs_0_, bf16[416,512]{1,0:T(8,128)(2,1)S(1)} %shard_map.153.refs_1_, f32[400,512]{1,0:T(8,128)S(1)} %get-tuple-element.58.refs_2_, f32[400,512]{1,0:T(8,128)S(1)} %convert_add_fusion.refs_3_, ...), custom_call_target="tpu_custom_call" | custom-call | flops 1638400 | bytes 4096000 | tf_op jit(solution)/shard_map/destination_side/pallas_call | solution.py:363
  (67 shorter events, 16.0 us)
Async XLA Ops:
  1.9 6.9 %collective-permute-start = (bf16[400,256]{1,0:T(8,128)(2,1)S(1)}, bf16[400,256]{1,0:T(8,128)(2,1)S(1)}, u32[]{:S(2)}, u32[]{:S(2)}) collective-permute-start(bf16[400,256]{1,0:T(8,128)(2,1)S(1)} %get-tuple-element.38.refs_0_), channel_id=1, source_target_pairs={{0,8},{8,0},{16,24},{24,16},{1,9},{9,1},{17,25},{25,17},{2,10},{10... | collective-permute-start | bytes 614408 | tf_op jit(solution)/shard_map/ppermute | solution.py:426
  10.4 15.5 %collective-permute-start.2 = (bf16[400,256]{1,0:T(8,128)(2,1)S(1)}, bf16[400,256]{1,0:T(8,128)(2,1)S(1)}, u32[]{:S(2)}, u32[]{:S(2)}) collective-permute-start(bf16[400,256]{1,0:T(8,128)(2,1)S(1)} %get-tuple-element.40), channel_id=1, source_target_pairs={{0,16},{8,24},{16,0},{24,8},{1,17},{9,25},{17,1},{25,9},{2,18},{10... | collective-permute-start | bytes 614408 | tf_op jit(solution)/shard_map/ppermute | solution.py:426
  12.0 13.9 %collective-permute-start.3 = (bf16[400,256]{1,0:T(8,128)(2,1)S(1)}, bf16[400,256]{1,0:T(8,128)(2,1)S(1)}, u32[]{:S(2)}, u32[]{:S(2)}) collective-permute-start(bf16[400,256]{1,0:T(8,128)(2,1)S(1)} %get-tuple-element.41), channel_id=1, source_target_pairs={{0,8},{8,0},{16,24},{24,16},{1,9},{9,1},{17,25},{25,17},{2,10},{10... | collective-permute-start | bytes 614408 | tf_op jit(solution)/shard_map/ppermute | solution.py:426
  26.5 11.8 %collective-permute-start.4 = (bf16[400,512]{1,0:T(8,128)(2,1)S(1)}, bf16[400,512]{1,0:T(8,128)(2,1)S(1)}, u32[]{:S(2)}, u32[]{:S(2)}) collective-permute-start(bf16[400,512]{1,0:T(8,128)(2,1)S(1)} %shard_map.147.table.refs_0_), channel_id=1, source_target_pairs={{0,1},{1,0},{2,3},{3,2},{4,5},{5,4},{6,7},{7,6},{8,9},{9,8},{10,11... | collective-permute-start | bytes 1228808 | tf_op jit(solution)/shard_map/ppermute | solution.py:579
  26.6 24.3 %collective-permute-start.9 = (bf16[400,512]{1,0:T(8,128)(2,1)S(1)}, bf16[400,512]{1,0:T(8,128)(2,1)S(1)}, u32[]{:S(2)}, u32[]{:S(2)}) collective-permute-start(bf16[400,512]{1,0:T(8,128)(2,1)S(1)} %shard_map.147.table.refs_0_), channel_id=1, source_target_pairs={{0,2},{1,3},{2,0},{3,1},{4,6},{5,7},{6,4},{7,5},{8,10},{9,11},{10,... | collective-permute-start | bytes 1228808 | tf_op jit(solution)/shard_map/ppermute | solution.py:590
  27.1 23.8 %collective-permute-start.7 = (bf16[400,512]{1,0:T(8,128)(2,1)S(1)}, bf16[400,512]{1,0:T(8,128)(2,1)S(1)}, u32[]{:S(2)}, u32[]{:S(2)}) collective-permute-start(bf16[400,512]{1,0:T(8,128)(2,1)S(1)} %shard_map.147.table.refs_0_), channel_id=1, source_target_pairs={{0,4},{1,5},{2,6},{3,7},{4,0},{5,1},{6,2},{7,3},{8,12},{9,13},{10,... | collective-permute-start | bytes 1228808 | tf_op jit(solution)/shard_map/ppermute | solution.py:590
  29.7 21.8 %collective-permute-start.11 = (bf16[416,512]{1,0:T(8,128)(2,1)S(1)}, bf16[416,512]{1,0:T(8,128)(2,1)S(1)}, u32[]{:S(2)}, u32[]{:S(2)}) collective-permute-start(bf16[416,512]{1,0:T(8,128)(2,1)S(1)} %get-tuple-element.57.refs_0_), channel_id=1, source_target_pairs={{0,8},{8,0},{16,24},{24,16},{1,9},{9,1},{17,25},{25,17},{2,10},{10... | collective-permute-start | bytes 1277960 | tf_op jit(solution)/shard_map/ppermute | solution.py:426
  50.9 19.7 %collective-permute-start.5 = (bf16[400,512]{1,0:T(8,128)(2,1)S(1)}, bf16[400,512]{1,0:T(8,128)(2,1)S(1)}, u32[]{:S(2)}, u32[]{:S(2)}) collective-permute-start(bf16[400,512]{1,0:T(8,128)(2,1)S(1)} %shard_map.147.table.refs_0_), channel_id=1, source_target_pairs={{0,6},{1,7},{2,4},{3,5},{4,2},{5,3},{6,0},{7,1},{8,14},{9,15},{10,... | collective-permute-start | bytes 1228808 | tf_op jit(solution)/shard_map/ppermute | solution.py:590
  50.9 19.7 %collective-permute-start.10 = (bf16[400,512]{1,0:T(8,128)(2,1)S(1)}, bf16[400,512]{1,0:T(8,128)(2,1)S(1)}, u32[]{:S(2)}, u32[]{:S(2)}) collective-permute-start(bf16[400,512]{1,0:T(8,128)(2,1)S(1)} %collective-permute-done.9.refs_0_), channel_id=1, source_target_pairs={{0,1},{1,0},{2,3},{3,2},{4,5},{5,4},{6,7},{7,6},{8,9},{9,8},{10,11... | collective-permute-start | bytes 1228808 | tf_op jit(solution)/shard_map/ppermute | solution.py:579
  51.0 32.1 %collective-permute-start.8 = (bf16[400,512]{1,0:T(8,128)(2,1)S(1)}, bf16[400,512]{1,0:T(8,128)(2,1)S(1)}, u32[]{:S(2)}, u32[]{:S(2)}) collective-permute-start(bf16[400,512]{1,0:T(8,128)(2,1)S(1)} %collective-permute-done.7.refs_0_), channel_id=1, source_target_pairs={{0,1},{1,0},{2,3},{3,2},{4,5},{5,4},{6,7},{7,6},{8,9},{9,8},{10,11... | collective-permute-start | bytes 1228808 | tf_op jit(solution)/shard_map/ppermute | solution.py:579
  51.4 44.7 %collective-permute-start.13 = (bf16[400,512]{1,0:T(8,128)(2,1)S(1)}, bf16[400,512]{1,0:T(8,128)(2,1)S(1)}, u32[]{:S(2)}, u32[]{:S(2)}) collective-permute-start(bf16[400,512]{1,0:T(8,128)(2,1)S(1)} %get-tuple-element.59), channel_id=1, source_target_pairs={{0,1},{1,0},{2,3},{3,2},{4,5},{5,4},{6,7},{7,6},{8,9},{9,8},{10,11... | collective-permute-start | bytes 1228808 | tf_op jit(solution)/shard_map/ppermute | solution.py:579
  52.3 43.9 %collective-permute-start.12 = (bf16[416,512]{1,0:T(8,128)(2,1)S(1)}, bf16[416,512]{1,0:T(8,128)(2,1)S(1)}, u32[]{:S(2)}, u32[]{:S(2)}) collective-permute-start(bf16[416,512]{1,0:T(8,128)(2,1)S(1)} %shard_map.152), channel_id=1, source_target_pairs={{0,16},{8,24},{16,0},{24,8},{1,17},{9,25},{17,1},{25,9},{2,18},{10... | collective-permute-start | bytes 1277960 | tf_op jit(solution)/shard_map/ppermute | solution.py:426
  70.6 26.5 %collective-permute-start.6 = (bf16[400,512]{1,0:T(8,128)(2,1)S(1)}, bf16[400,512]{1,0:T(8,128)(2,1)S(1)}, u32[]{:S(2)}, u32[]{:S(2)}) collective-permute-start(bf16[400,512]{1,0:T(8,128)(2,1)S(1)} %collective-permute-done.5.refs_0_), channel_id=1, source_target_pairs={{0,1},{1,0},{2,3},{3,2},{4,5},{5,4},{6,7},{7,6},{8,9},{9,8},{10,11... | collective-permute-start | bytes 1228808 | tf_op jit(solution)/shard_map/ppermute | solution.py:579
  95.6 20.5 %collective-permute-start.16 = (bf16[400,512]{1,0:T(8,128)(2,1)S(1)}, bf16[400,512]{1,0:T(8,128)(2,1)S(1)}, u32[]{:S(2)}, u32[]{:S(2)}) collective-permute-start(bf16[400,512]{1,0:T(8,128)(2,1)S(1)} %get-tuple-element.63), channel_id=1, source_target_pairs={{0,1},{1,0},{2,3},{3,2},{4,5},{5,4},{6,7},{7,6},{8,9},{9,8},{10,11... | collective-permute-start | bytes 1228808 | tf_op jit(solution)/shard_map/ppermute | solution.py:579
  95.6 23.8 %collective-permute-start.14 = (bf16[400,512]{1,0:T(8,128)(2,1)S(1)}, bf16[400,512]{1,0:T(8,128)(2,1)S(1)}, u32[]{:S(2)}, u32[]{:S(2)}) collective-permute-start(bf16[400,512]{1,0:T(8,128)(2,1)S(1)} %get-tuple-element.61), channel_id=1, source_target_pairs={{0,1},{1,0},{2,3},{3,2},{4,5},{5,4},{6,7},{7,6},{8,9},{9,8},{10,11... | collective-permute-start | bytes 1228808 | tf_op jit(solution)/shard_map/ppermute | solution.py:579
  116.0 23.8 %collective-permute-start.18 = (bf16[400,512]{1,0:T(8,128)(2,1)S(1)}, bf16[400,512]{1,0:T(8,128)(2,1)S(1)}, u32[]{:S(2)}, u32[]{:S(2)}) collective-permute-start(bf16[400,512]{1,0:T(8,128)(2,1)S(1)} %get-tuple-element.65), channel_id=1, source_target_pairs={{0,1},{1,0},{2,3},{3,2},{4,5},{5,4},{6,7},{7,6},{8,9},{9,8},{10,11... | collective-permute-start | bytes 1228808 | tf_op jit(solution)/shard_map/ppermute | solution.py:579
  116.2 35.9 %collective-permute-start.17 = (bf16[400,512]{1,0:T(8,128)(2,1)S(1)}, bf16[400,512]{1,0:T(8,128)(2,1)S(1)}, u32[]{:S(2)}, u32[]{:S(2)}) collective-permute-start(bf16[400,512]{1,0:T(8,128)(2,1)S(1)} %add_convert_fusion.1), channel_id=1, source_target_pairs={{0,4},{1,5},{2,6},{3,7},{4,0},{5,1},{6,2},{7,3},{8,12},{9,13},{10,... | collective-permute-start | bytes 1228808 | tf_op jit(solution)/shard_map/ppermute | solution.py:603
  116.9 12.8 %collective-permute-start.21 = (f32[16,400]{1,0:T(8,128)S(1)}, f32[16,400]{1,0:T(8,128)S(1)}, u32[]{:S(2)}, u32[]{:S(2)}) collective-permute-start(f32[16,400]{1,0:T(8,128)S(1)} %add.47), channel_id=1, source_target_pairs={{0,2},{1,3},{2,0},{3,1},{4,6},{5,7},{6,4},{7,5},{8,10},{9,11},{10,... | collective-permute-start | bytes 76808 | tf_op jit(solution)/shard_map/ppermute | solution.py:518
  118.7 18.4 %collective-permute-start.22 = (f32[16,400]{1,0:T(8,128)S(1)}, f32[16,400]{1,0:T(8,128)S(1)}, u32[]{:S(2)}, u32[]{:S(2)}) collective-permute-start(f32[16,400]{1,0:T(8,128)S(1)} %add.47), channel_id=1, source_target_pairs={{0,4},{1,5},{2,6},{3,7},{4,0},{5,1},{6,2},{7,3},{8,12},{9,13},{10,... | collective-permute-start | bytes 76808 | tf_op jit(solution)/shard_map/ppermute | solution.py:518
  119.4 19.5 %collective-permute-start.23 = (f32[16,400]{1,0:T(8,128)S(1)}, f32[16,400]{1,0:T(8,128)S(1)}, u32[]{:S(2)}, u32[]{:S(2)}) collective-permute-start(f32[16,400]{1,0:T(8,128)S(1)} %add.47), channel_id=1, source_target_pairs={{0,6},{1,7},{2,4},{3,5},{4,2},{5,3},{6,0},{7,1},{8,14},{9,15},{10,... | collective-permute-start | bytes 76808 | tf_op jit(solution)/shard_map/ppermute | solution.py:518
  129.7 24.6 %collective-permute-start.15 = (bf16[400,512]{1,0:T(8,128)(2,1)S(1)}, bf16[400,512]{1,0:T(8,128)(2,1)S(1)}, u32[]{:S(2)}, u32[]{:S(2)}) collective-permute-start(bf16[400,512]{1,0:T(8,128)(2,1)S(1)} %add_convert_fusion.2), channel_id=1, source_target_pairs={{0,2},{1,3},{2,0},{3,1},{4,6},{5,7},{6,4},{7,5},{8,10},{9,11},{10,... | collective-permute-start | bytes 1228808 | tf_op jit(solution)/shard_map/ppermute | solution.py:603
  138.9 12.6 %collective-permute-start.25 = (f32[16,400]{1,0:T(8,128)S(1)}, f32[16,400]{1,0:T(8,128)S(1)}, u32[]{:S(2)}, u32[]{:S(2)}) collective-permute-start(f32[16,400]{1,0:T(8,128)S(1)} %add_add_fusion), channel_id=1, source_target_pairs={{0,16},{8,24},{16,0},{24,8},{1,17},{9,25},{17,1},{25,9},{2,18},{10... | collective-permute-start | bytes 76808 | tf_op jit(solution)/shard_map/ppermute | solution.py:518
  139.8 11.7 %collective-permute-start.26 = (f32[16,400]{1,0:T(8,128)S(1)}, f32[16,400]{1,0:T(8,128)S(1)}, u32[]{:S(2)}, u32[]{:S(2)}) collective-permute-start(f32[16,400]{1,0:T(8,128)S(1)} %add_add_fusion), channel_id=1, source_target_pairs={{0,24},{8,16},{16,8},{24,0},{1,25},{9,17},{17,9},{25,1},{2,26},{10... | collective-permute-start | bytes 76808 | tf_op jit(solution)/shard_map/ppermute | solution.py:518
  143.0 18.7 %collective-permute-start.19 = (bf16[400,512]{1,0:T(8,128)(2,1)S(1)}, bf16[400,512]{1,0:T(8,128)(2,1)S(1)}, u32[]{:S(2)}, u32[]{:S(2)}) collective-permute-start(bf16[400,512]{1,0:T(8,128)(2,1)S(1)} %add_convert_fusion), channel_id=1, source_target_pairs={{0,6},{1,7},{2,4},{3,5},{4,2},{5,3},{6,0},{7,1},{8,14},{9,15},{10,... | collective-permute-start | bytes 1228808 | tf_op jit(solution)/shard_map/ppermute | solution.py:603
  (8 other events, 58.1 us)

commit v6 on v5

--- a/solution.py
+++ b/solution.py
@@ -156,17 +156,18 @@
     )(part_high, in_hbm(query), in_hbm(dst_ids))
 
 
-def negative_wave(tables, chip, quota, neg_ids, query_b, query_grad, lane, chunk):
+def negative_wave(tables, chip, quota, neg_ids, query_b, lane, chunk):
     count = len(tables)
     dim, rows = tables[0].shape
     edges = query_b.shape[1]
+    slots = QMAX * count
     half_weight = 0.5 / math.sqrt(NNEG)
 
     def body(chip_ref, lane_ref, quota_ref, *refs):
         table_refs = refs[:count]
-        ids, query_ref, grad_in, grad_out = refs[count : count + 4]
+        ids, query_ref, neg, coef_out = refs[count : count + 4]
         grad_refs = refs[count + 4 : 2 * count + 4]
-        neg, neg_t, neg_grad = refs[2 * count + 4 :]
+        neg_t, neg_grad = refs[2 * count + 4 :]
 
         live, at, base = [], [], [jnp.int32(0)]
         for s in range(count):
@@ -206,19 +207,13 @@
             neg_t[total] = jnp.zeros((BLOCK, dim), bf16)
             neg_grad[total] = jnp.zeros((dim, BLOCK), f32)
 
-        @pl.when(total == 0)
-        def _():
-            grad_out[...] = grad_in[...]
-
         def pair(p, carry):
             left, right = 2 * p, 2 * p + 1
-            columns = jnp.concatenate([neg[left], neg[right]], axis=1)
             columns_t = jnp.concatenate([neg_t[left], neg_t[right]], axis=0)
             query = query_ref[...]
             scores = dot_nn(columns_t, query)
             coef = (half_weight * jnp.tanh(0.5 * scores) + half_weight).astype(bf16)
-            before = jnp.where(p == 0, grad_in[...], grad_out[...])
-            grad_out[...] = before + dot_nn(columns, coef)
+            coef_out[pl.ds(pl.multiple_of(left * BLOCK, 2 * BLOCK), 2 * BLOCK)] = coef
             added = dot_nt(query, coef)
             neg_grad[left] += added[:, :BLOCK]
             neg_grad[right] += added[:, BLOCK:]
@@ -242,7 +237,6 @@
                     pick = picks(s, wide)
                     grad_refs[s][...] = (dot_nt(high, pick) + dot_nt(low, pick)).astype(bf16)
 
-    slots = QMAX * count
     smem = pl.BlockSpec(memory_space=pltpu.SMEM)
     shard = jax.ShapeDtypeStruct((dim, rows), bf16)
     return pl.pallas_call(
@@ -250,42 +244,80 @@
         grid=(edges // chunk,),
         in_specs=[smem, smem, smem]
         + [whole((dim, rows))] * count
-        + [whole(neg_ids.shape), lanes(dim, chunk), lanes(dim, chunk)],
-        out_specs=[lanes(dim, chunk)] + [whole((dim, rows))] * count,
+        + [whole(neg_ids.shape), lanes(dim, chunk)],
+        out_specs=[whole((slots, dim, BLOCK)), lanes(slots * BLOCK, chunk)]
+        + [whole((dim, rows))] * count,
         scratch_shapes=[
-            pltpu.VMEM((slots, dim, BLOCK), bf16),
             pltpu.VMEM((slots, BLOCK, dim), bf16),
             pltpu.VMEM((slots, dim, BLOCK), f32),
         ],
-        out_shape=[pltpu.HBM((dim, edges), f32)] + [shard] * count,
-        input_output_aliases={count + 5: 0},
+        out_shape=[
+            jax.ShapeDtypeStruct((slots, dim, BLOCK), bf16),
+            pltpu.HBM((slots * BLOCK, edges), bf16),
+        ]
+        + [shard] * count,
         compiler_params=params(32),
         cost_estimate=cost(6 * dim * 1.5 * count * BLOCK * edges, 10 * dim * edges),
-    )(chip, lane, quota, *tables, neg_ids, in_hbm(query_b), in_hbm(query_grad))
-
-
-def relation_side(src_rows, rel_ids, query_grad, rel_count, chunk):
+    )(chip, lane, quota, *tables, neg_ids, in_hbm(query_b))
+
+
+def combine(src_rows, rel_ids, query_grad, negatives, coefs, chip, lane, quota, rel_count, chunk):
     dim, edges = src_rows.shape
-
-    def body(rows_in, rel, grad_in, rel_out):
+    count = len(negatives)
+    slots = negatives[0].shape[0]
+    wide = 2 * BLOCK
+
+    def body(chip_ref, lane_ref, quota_ref, rows_in, rel, grad_in, *refs):
+        neg_refs, coef_refs = refs[:count], refs[count : 2 * count]
+        grad_out, rel_out = refs[2 * count :]
+
         @pl.when(pl.program_id(0) == 0)
         def _():
             rel_out[...] = jnp.zeros_like(rel_out)
 
+        grad_out[...] = grad_in[...]
+        for k in range(count):
+            first = CORES * (chip_ref[0] ^ k)
+            total = quota_ref[0, first]
+            for c in range(1, CORES):
+                total = total + quota_ref[0, first + c]
+            for pairs in range(1, slots // 2 + 1):
+
+                @pl.when((total + 1) // 2 == pairs)
+                def _(k=k, pairs=pairs):
+                    columns = [neg_refs[k][j] for j in range(2 * pairs)]
+                    columns = jnp.concatenate(columns, axis=1)
+                    grad_out[...] += dot_nn(columns, coef_refs[k][: pairs * wide])
+
         kinds = select_rows(rel[...], rel_count)
-        upper, lower = split2(back(grad_in[...], rows_in[...]))
+        upper, lower = split2(back(grad_out[...], rows_in[...]))
         rel_out[...] += dot_nt(kinds, upper) + dot_nt(kinds, lower)
 
+    smem = pl.BlockSpec(memory_space=pltpu.SMEM)
     return pl.pallas_call(
         body,
-        name="relation_side",
+        name="combine",
         grid=(edges // chunk,),
-        in_specs=[lanes(dim, chunk), lanes(1, chunk), lanes(dim, chunk)],
-        out_specs=whole((rel_count, dim)),
-        out_shape=jax.ShapeDtypeStruct((rel_count, dim), f32),
-        compiler_params=params(24),
-        cost_estimate=cost(4 * dim * rel_count * edges, 8 * dim * edges),
-    )(in_hbm(src_rows), in_hbm(rel_ids), in_hbm(query_grad))
+        in_specs=[smem, smem, smem, lanes(dim, chunk), lanes(1, chunk), lanes(dim, chunk)]
+        + [whole(negatives[0].shape)] * count
+        + [lanes(slots * BLOCK, chunk)] * count,
+        out_specs=[lanes(dim, chunk), whole((rel_count, dim))],
+        out_shape=[
+            pltpu.HBM((dim, edges), f32),
+            jax.ShapeDtypeStruct((rel_count, dim), f32),
+        ],
+        compiler_params=params(44),
+        cost_estimate=cost(2 * dim * NNEG * edges, 12 * dim * edges + 2 * NNEG * edges),
+    )(
+        chip,
+        lane,
+        quota,
+        in_hbm(src_rows),
+        in_hbm(rel_ids),
+        in_hbm(query_grad),
+        *negatives,
+        *map(in_hbm, coefs),
+    )
 
 
 def source_side(src_table, src_state, rel_parts, src_ids, rel_ids, query_grad, rel_count, chunk):
@@ -580,31 +612,38 @@
 
     chip = here // CORES
     lane = here % CORES
-    arrived, done = [], []
+    arrived, negatives, coefs = [], [], []
+    done = [own_grad]
     for k in range(chips):
         pairs = [(i, i ^ (CORES * k)) for i in range(edge_count)]
         table = part_high
         if k:
-            if k >= 3:
-                table, _ = lax.optimization_barrier((table, done[k - 3]))
+            if k >= 2:
+                table, _ = lax.optimization_barrier((table, done[k - 2]))
             table = lax.ppermute(table, "edge", pairs)
-        query_grad, mine, theirs = negative_wave(
-            [table, swapped(table)],
-            chip ^ k,
-            quotas,
-            neg_ids,
-            query_b,
-            query_grad,
-            lane,
-            wave_chunk,
+        live, coef, mine, theirs = negative_wave(
+            [table, swapped(table)], chip ^ k, quotas, neg_ids, query_b, lane, wave_chunk
         )
         total = mine.astype(f32) + swapped(theirs).astype(f32)
         if k:
             total = lax.ppermute(total.astype(bf16), "edge", pairs)
         arrived.append(total)
         done.append(mine)
-
-    rel_grad = relation_side(src_rows, rel_ids, query_grad, rel_count, chunk)
+        negatives.append(live)
+        coefs.append(coef)
+
+    query_grad, rel_grad = combine(
+        src_rows,
+        rel_ids,
+        query_grad,
+        negatives,
+        coefs,
+        chip,
+        lane,
+        quotas,
+        rel_count,
+        chunk,
+    )
     src_out, src_state_out = source_side(
         src_table,
         src_state.reshape(1, row_count),

time: 164 us -> 167 us (1.018)
  the two profiles are of different devices: /device:TPU:10 before, /device:TPU:13 now
where the time goes in v6:
time: 167 us; the launch traced here: 166 us
  Pallas kernels  85.3 us (51%)
  waiting for transfers between devices  44.7 us (27%)
  starting transfers between devices  32.6 us (20%)
  other arithmetic  1.85 us (1%)
    pallas_call x4, Pallas kernels, negative_wave(): pl.pallas_call(body, grid=(edges // chunk,), in_specs=[smem, smem, smem]...  34.9 us
    ppermute x3, waiting for transfers between devices, shards(): total = lax.ppermute(total.astype(bf16), 'edge', pairs)  22.2 us
    pallas_call x1, Pallas kernels, combine(): pl.pallas_call(body, name='combine', grid=(edges // chunk,), in_specs=[sm...  16.3 us
    ppermute x3, waiting for transfers between devices, shards(): table = lax.ppermute(table, 'edge', pairs)  15.1 us
    pallas_call x2, Pallas kernels, make_queries(): pl.pallas_call(body, name='make_queries', grid=(steps,), in_specs=[whole(...  12.4 us
    ppermute x3, starting transfers between devices, shards(): total = lax.ppermute(total.astype(bf16), 'edge', pairs)  10.7 us
    pallas_call x1, Pallas kernels, positives(): pl.pallas_call(body, name='positives', grid=(edges // chunk,), in_specs=[...  8.01 us
    ppermute x8, starting transfers between devices, swapped(): return lax.ppermute(array, 'edge', swap)  7.64 us
  transfers between devices with their start and end apart: 27, of which 8 were waited for; matrix products, arithmetic and copies ran while one was open for 1% of the time, Pallas kernels for 48%

profile of v6, /device:TPU:13, one launch (start us, length us, event | category | flops | bytes accessed | tf_op | source)
XLA Modules:
  0.0 166.2 jit_solution(7603412845010300368)
XLA Ops:
  4.4 3.6 %collective-permute-done.refs_1_ = bf16[400,256]{1,0:T(8,128)(2,1)S(1)} collective-permute-done((bf16[400,256]{1,0:T(8,128)(2,1)S(1)}, bf16[400,256]{1,0:T(8,128)(2,1)S(1)}, u32[]{:S(2)}, u32[]{:S(2)}) %collective-permute-start) | collective-permute-done | bytes 204832 | tf_op jit(solution)/shard_map/ppermute | solution.py:458
  10.8 6.2 %make_queries.2 = (f32[400,4096]{1,0:T(8,128)}, bf16[400,4096]{1,0:T(8,128)(2,1)}, f32[400,4096]{1,0:T(8,128)}) custom-call(f32[400,512]{1,0:T(8,128)} %table.5, bf16[400,128]{1,0:T(8,128)(2,1)S(1)} %pad.4.parts_ref.parts, s32[1,4096]{1,0:T(1,128)} %bitcast.15, s32[1,4096]{1,0:T(1,128)} %bitcast.11), custom_call_target="tpu_custom_call" | custom-call | flops 1677721600 | bytes 8192000 | tf_op jit(solution)/shard_map/make_queries/pallas_call | solution.py:115
  16.9 6.2 %make_queries.3 = (f32[400,4096]{1,0:T(8,128)}, bf16[400,4096]{1,0:T(8,128)(2,1)}, f32[400,4096]{1,0:T(8,128)}) custom-call(f32[400,512]{1,0:T(8,128)} %table.5, bf16[400,128]{1,0:T(8,128)(2,1)S(1)} %pad.4.parts_ref.parts, s32[1,4096]{1,0:T(1,128)} %bitcast.16, s32[1,4096]{1,0:T(1,128)} %bitcast.12, ...), custom_call_target="tpu_custom_call", output_to_operand_aliasing={{0}: (4, {}), {1}: (5, {}), {2}: (6, {})} | custom-call | flops 1677721600 | bytes 8192000 | tf_op jit(solution)/shard_map/make_queries/pallas_call | solution.py:115
  24.1 2.4 %collective-permute-start.4 = (bf16[400,512]{1,0:T(8,128)(2,1)S(1)}, bf16[400,512]{1,0:T(8,128)(2,1)S(1)}, u32[]{:S(2)}, u32[]{:S(2)}) collective-permute-start(bf16[400,512]{1,0:T(8,128)(2,1)S(1)} %shard_map.147.table.refs_0_), channel_id=1, source_target_pairs={{0,1},{1,0},{2,3},{3,2},{4,5},{5,4},{6,7},{7,6},{8,9},{9,8},{10,11... | collective-permute-start | bytes 1228808 | tf_op jit(solution)/shard_map/ppermute | solution.py:611
  26.4 8.0 %positives.1 = (f32[400,4096]{1,0:T(8,128)}, f32[400,512]{1,0:T(8,128)S(1)}) custom-call(bf16[400,512]{1,0:T(8,128)(2,1)S(1)} %shard_map.147.table.refs_0_, f32[400,4096]{1,0:T(8,128)} %get-tuple-element.54.query_in, s32[1,4096]{1,0:T(1,128)} %bitcast.19), custom_call_target="tpu_custom_call" | custom-call | flops 5033164800 | bytes 13107200 | tf_op jit(solution)/shard_map/positives/pallas_call | solution.py:147
  34.5 2.5 %collective-permute-start.7 = (bf16[400,512]{1,0:T(8,128)(2,1)S(1)}, bf16[400,512]{1,0:T(8,128)(2,1)S(1)}, u32[]{:S(2)}, u32[]{:S(2)}) collective-permute-start(bf16[400,512]{1,0:T(8,128)(2,1)S(1)} %shard_map.147.table.refs_0_), channel_id=1, source_target_pairs={{0,4},{1,5},{2,6},{3,7},{4,0},{5,1},{6,2},{7,3},{8,12},{9,13},{10,... | collective-permute-start | bytes 1228808 | tf_op jit(solution)/shard_map/ppermute | solution.py:623
  38.8 9.3 %shard_map.148 = (bf16[4,400,128]{2,1,0:T(8,128)(2,1)S(1)}, bf16[512,4096]{1,0:T(8,128)(2,1)}, bf16[400,512]{1,0:T(8,128)(2,1)S(1)}, bf16[400,512]{1,0:T(8,128)(2,1)S(1)}) custom-call(s32[1]{0:T(128)S(6)} %select_n.12.chip_ref, s32[1]{0:T(128)S(6)} %select_n.13.lane_ref, s32[1,8]{1,0:T(1,128)S(1)} %copy-done.2, ...), custom_call_target="tpu_custom_call" | custom-call | flops 3774873600 | bytes 16384000 | tf_op jit(solution)/shard_map/pallas_call | solution.py:242
  48.2 15.1 %collective-permute-done.7.refs_0_ = bf16[400,512]{1,0:T(8,128)(2,1)S(1)} collective-permute-done((bf16[400,512]{1,0:T(8,128)(2,1)S(1)}, bf16[400,512]{1,0:T(8,128)(2,1)S(1)}, u32[]{:S(2)}, u32[]{:S(2)}) %collective-permute-start.7) | collective-permute-done | bytes 409632 | tf_op jit(solution)/shard_map/ppermute | solution.py:623
  63.3 1.3 collective-permute-start.8
  66.7 9.3 %shard_map.149 = (bf16[4,400,128]{2,1,0:T(8,128)(2,1)S(1)}, bf16[512,4096]{1,0:T(8,128)(2,1)}, bf16[400,512]{1,0:T(8,128)(2,1)S(1)}, bf16[400,512]{1,0:T(8,128)(2,1)S(1)}) custom-call(s32[1]{0:T(128)S(6)} %xor.9.chip_ref, s32[1]{0:T(128)S(6)} %select_n.13.lane_ref, s32[1,8]{1,0:T(1,128)S(1)} %copy-done.2, ...), custom_call_target="tpu_custom_call" | custom-call | flops 3774873600 | bytes 16384000 | tf_op jit(solution)/shard_map/pallas_call | solution.py:242
  76.6 6.9 %shard_map.150 = (bf16[4,400,128]{2,1,0:T(8,128)(2,1)S(1)}, bf16[512,4096]{1,0:T(8,128)(2,1)}, bf16[400,512]{1,0:T(8,128)(2,1)S(1)}, bf16[400,512]{1,0:T(8,128)(2,1)S(1)}) custom-call(s32[1]{0:T(128)S(6)} %xor.10.chip_ref, s32[1]{0:T(128)S(6)} %select_n.13.lane_ref, s32[1,8]{1,0:T(1,128)S(1)} %copy-done.2, ...), custom_call_target="tpu_custom_call" | custom-call | flops 3774873600 | bytes 16384000 | tf_op jit(solution)/shard_map/pallas_call | solution.py:242
  83.4 2.5 %collective-permute-start.16 = (bf16[400,512]{1,0:T(8,128)(2,1)S(1)}, bf16[400,512]{1,0:T(8,128)(2,1)S(1)}, u32[]{:S(2)}, u32[]{:S(2)}) collective-permute-start(bf16[400,512]{1,0:T(8,128)(2,1)S(1)} %get-tuple-element.77), channel_id=1, source_target_pairs={{0,1},{1,0},{2,3},{3,2},{4,5},{5,4},{6,7},{7,6},{8,9},{9,8},{10,11... | collective-permute-start | bytes 1228808 | tf_op jit(solution)/shard_map/ppermute | solution.py:611
  86.9 9.4 %shard_map.151 = (bf16[4,400,128]{2,1,0:T(8,128)(2,1)S(1)}, bf16[512,4096]{1,0:T(8,128)(2,1)}, bf16[400,512]{1,0:T(8,128)(2,1)S(1)}, bf16[400,512]{1,0:T(8,128)(2,1)S(1)}) custom-call(s32[1]{0:T(128)S(6)} %xor.11.chip_ref, s32[1]{0:T(128)S(6)} %select_n.13.lane_ref, s32[1,8]{1,0:T(1,128)S(1)} %copy-done.2, ...), custom_call_target="tpu_custom_call" | custom-call | flops 3774873600 | bytes 16384000 | tf_op jit(solution)/shard_map/pallas_call | solution.py:242
  96.3 16.3 %combine.1 = (f32[400,4096]{1,0:T(8,128)}, f32[16,400]{1,0:T(8,128)S(1)}) custom-call(s32[1]{0:T(128)S(6)} %select_n.12.chip_ref, s32[1]{0:T(128)S(6)} %select_n.13.lane_ref, s32[1,8]{1,0:T(1,128)S(1)} %copy-done.2, f32[400,4096]{1,0:T(8,128)} %get-tuple-element.47.rows_in, s32[1,4096]{1,0:T(1,128)} %bitcast.13, f32[400,4096]{1,0:T(8,128)} %get-tuple-element.55.grad_in, ...), custom_call_target="tpu_custom_call" | custom-call | flops 5033164800 | bytes 32243712 | tf_op jit(solution)/shard_map/combine/pallas_call | solution.py:297
  112.8 1.5 collective-permute-start.15
  114.6 2.9 %collective-permute-start.23 = (f32[16,400]{1,0:T(8,128)S(1)}, f32[16,400]{1,0:T(8,128)S(1)}, u32[]{:S(2)}, u32[]{:S(2)}) collective-permute-start(f32[16,400]{1,0:T(8,128)S(1)} %add.47), channel_id=1, source_target_pairs={{0,6},{1,7},{2,4},{3,5},{4,2},{5,3},{6,0},{7,1},{8,14},{9,15},{10,... | collective-permute-start | bytes 76808 | tf_op jit(solution)/shard_map/ppermute | solution.py:550
  119.0 7.5 %collective-permute-start.17 = (bf16[400,512]{1,0:T(8,128)(2,1)S(1)}, bf16[400,512]{1,0:T(8,128)(2,1)S(1)}, u32[]{:S(2)}, u32[]{:S(2)}) collective-permute-start(bf16[400,512]{1,0:T(8,128)(2,1)S(1)} %add_convert_fusion.1), channel_id=1, source_target_pairs={{0,4},{1,5},{2,6},{3,7},{4,0},{5,1},{6,2},{7,3},{8,12},{9,13},{10,... | collective-permute-start | bytes 1228808 | tf_op jit(solution)/shard_map/ppermute | solution.py:629
  126.6 1.4 collective-permute-done.22
  128.1 2.7 %collective-permute-start.25 = (f32[16,400]{1,0:T(8,128)S(1)}, f32[16,400]{1,0:T(8,128)S(1)}, u32[]{:S(2)}, u32[]{:S(2)}) collective-permute-start(f32[16,400]{1,0:T(8,128)S(1)} %add_add_fusion), channel_id=1, source_target_pairs={{0,16},{8,24},{16,0},{24,8},{1,17},{9,25},{17,1},{25,9},{2,18},{10... | collective-permute-start | bytes 76808 | tf_op jit(solution)/shard_map/ppermute | solution.py:550
  132.1 1.7 %collective-permute-start.19 = (bf16[400,512]{1,0:T(8,128)(2,1)S(1)}, bf16[400,512]{1,0:T(8,128)(2,1)S(1)}, u32[]{:S(2)}, u32[]{:S(2)}) collective-permute-start(bf16[400,512]{1,0:T(8,128)(2,1)S(1)} %add_convert_fusion), channel_id=1, source_target_pairs={{0,6},{1,7},{2,4},{3,5},{4,2},{5,3},{6,0},{7,1},{8,14},{9,15},{10,... | collective-permute-start | bytes 1228808 | tf_op jit(solution)/shard_map/ppermute | solution.py:629
  133.7 7.3 %source_side.1 = (f32[400,512]{1,0:T(8,128)}, f32[1,512]{1,0:T(1,128)}) custom-call(f32[400,512]{1,0:T(8,128)} %table.5, f32[1,512]{1,0:T(1,128)} %bitcast.20, bf16[400,128]{1,0:T(8,128)(2,1)S(1)} %pad.4.parts_ref.parts, s32[1,4096]{1,0:T(1,128)} %bitcast.17, s32[1,4096]{1,0:T(1,128)} %bitcast.14, f32[400,4096]{1,0:T(8,128)} %get-tuple-element.69.grad_in), custom_call_target="tpu_custom_call" | custom-call | flops 3355443200 | bytes 6553600 | tf_op jit(solution)/shard_map/source_side/pallas_call | solution.py:345
  141.7 10.1 %collective-permute-done.17.refs_5_ = bf16[400,512]{1,0:T(8,128)(2,1)S(1)} collective-permute-done((bf16[400,512]{1,0:T(8,128)(2,1)S(1)}, bf16[400,512]{1,0:T(8,128)(2,1)S(1)}, u32[]{:S(2)}, u32[]{:S(2)}) %collective-permute-start.17) | collective-permute-done | bytes 409632 | tf_op jit(solution)/shard_map/ppermute | solution.py:629
  151.8 12.2 %collective-permute-done.19.refs_6_ = bf16[400,512]{1,0:T(8,128)(2,1)S(1)} collective-permute-done((bf16[400,512]{1,0:T(8,128)(2,1)S(1)}, bf16[400,512]{1,0:T(8,128)(2,1)S(1)}, u32[]{:S(2)}, u32[]{:S(2)}) %collective-permute-start.19) | collective-permute-done | bytes 409632 | tf_op jit(solution)/shard_map/ppermute | solution.py:629
  163.9 2.3 %destination_side.1 = (f32[400,512]{1,0:T(8,128)}, f32[1,512]{1,0:T(1,128)}) custom-call(bf16[400,512]{1,0:T(8,128)(2,1)S(1)} %shard_map.147.table.refs_0_, bf16[416,512]{1,0:T(8,128)(2,1)S(1)} %shard_map.153.refs_1_, f32[400,512]{1,0:T(8,128)S(1)} %get-tuple-element.59.refs_2_, f32[400,512]{1,0:T(8,128)S(1)} %convert_add_fusion.refs_3_, ...), custom_call_target="tpu_custom_call" | custom-call | flops 1638400 | bytes 4096000 | tf_op jit(solution)/shard_map/destination_side/pallas_call | solution.py:395
  (67 shorter events, 16.9 us)
Async XLA Ops:
  1.9 6.0 %collective-permute-start = (bf16[400,256]{1,0:T(8,128)(2,1)S(1)}, bf16[400,256]{1,0:T(8,128)(2,1)S(1)}, u32[]{:S(2)}, u32[]{:S(2)}) collective-permute-start(bf16[400,256]{1,0:T(8,128)(2,1)S(1)} %get-tuple-element.49.refs_0_), channel_id=1, source_target_pairs={{0,8},{8,0},{16,24},{24,16},{1,9},{9,1},{17,25},{25,17},{2,10},{10... | collective-permute-start | bytes 614408 | tf_op jit(solution)/shard_map/ppermute | solution.py:458
  3.2 5.7 %collective-permute-start.1 = (bf16[400,256]{1,0:T(8,128)(2,1)S(1)}, bf16[400,256]{1,0:T(8,128)(2,1)S(1)}, u32[]{:S(2)}, u32[]{:S(2)}) collective-permute-start(bf16[400,256]{1,0:T(8,128)(2,1)S(1)} %get-tuple-element.50.refs_2_), channel_id=1, source_target_pairs={{0,16},{8,24},{16,0},{24,8},{1,17},{9,25},{17,1},{25,9},{2,18},{10... | collective-permute-start | bytes 614408 | tf_op jit(solution)/shard_map/ppermute | solution.py:458
  10.2 12.9 %collective-permute-start.2 = (bf16[400,256]{1,0:T(8,128)(2,1)S(1)}, bf16[400,256]{1,0:T(8,128)(2,1)S(1)}, u32[]{:S(2)}, u32[]{:S(2)}) collective-permute-start(bf16[400,256]{1,0:T(8,128)(2,1)S(1)} %get-tuple-element.51), channel_id=1, source_target_pairs={{0,16},{8,24},{16,0},{24,8},{1,17},{9,25},{17,1},{25,9},{2,18},{10... | collective-permute-start | bytes 614408 | tf_op jit(solution)/shard_map/ppermute | solution.py:458
  10.5 12.6 %collective-permute-start.3 = (bf16[400,256]{1,0:T(8,128)(2,1)S(1)}, bf16[400,256]{1,0:T(8,128)(2,1)S(1)}, u32[]{:S(2)}, u32[]{:S(2)}) collective-permute-start(bf16[400,256]{1,0:T(8,128)(2,1)S(1)} %get-tuple-element.52), channel_id=1, source_target_pairs={{0,8},{8,0},{16,24},{24,16},{1,9},{9,1},{17,25},{25,17},{2,10},{10... | collective-permute-start | bytes 614408 | tf_op jit(solution)/shard_map/ppermute | solution.py:458
  23.8 14.4 %collective-permute-start.5 = (bf16[400,512]{1,0:T(8,128)(2,1)S(1)}, bf16[400,512]{1,0:T(8,128)(2,1)S(1)}, u32[]{:S(2)}, u32[]{:S(2)}) collective-permute-start(bf16[400,512]{1,0:T(8,128)(2,1)S(1)} %shard_map.147.table.refs_0_), channel_id=1, source_target_pairs={{0,2},{1,3},{2,0},{3,1},{4,6},{5,7},{6,4},{7,5},{8,10},{9,11},{10,... | collective-permute-start | bytes 1228808 | tf_op jit(solution)/shard_map/ppermute | solution.py:623
  24.1 14.8 %collective-permute-start.4 = (bf16[400,512]{1,0:T(8,128)(2,1)S(1)}, bf16[400,512]{1,0:T(8,128)(2,1)S(1)}, u32[]{:S(2)}, u32[]{:S(2)}) collective-permute-start(bf16[400,512]{1,0:T(8,128)(2,1)S(1)} %shard_map.147.table.refs_0_), channel_id=1, source_target_pairs={{0,1},{1,0},{2,3},{3,2},{4,5},{5,4},{6,7},{7,6},{8,9},{9,8},{10,11... | collective-permute-start | bytes 1228808 | tf_op jit(solution)/shard_map/ppermute | solution.py:611
  34.5 28.9 %collective-permute-start.7 = (bf16[400,512]{1,0:T(8,128)(2,1)S(1)}, bf16[400,512]{1,0:T(8,128)(2,1)S(1)}, u32[]{:S(2)}, u32[]{:S(2)}) collective-permute-start(bf16[400,512]{1,0:T(8,128)(2,1)S(1)} %shard_map.147.table.refs_0_), channel_id=1, source_target_pairs={{0,4},{1,5},{2,6},{3,7},{4,0},{5,1},{6,2},{7,3},{8,12},{9,13},{10,... | collective-permute-start | bytes 1228808 | tf_op jit(solution)/shard_map/ppermute | solution.py:623
  36.9 27.7 %collective-permute-start.11 = (bf16[416,512]{1,0:T(8,128)(2,1)S(1)}, bf16[416,512]{1,0:T(8,128)(2,1)S(1)}, u32[]{:S(2)}, u32[]{:S(2)}) collective-permute-start(bf16[416,512]{1,0:T(8,128)(2,1)S(1)} %get-tuple-element.72.refs_0_), channel_id=1, source_target_pairs={{0,8},{8,0},{16,24},{24,16},{1,9},{9,1},{17,25},{25,17},{2,10},{10... | collective-permute-start | bytes 1277960 | tf_op jit(solution)/shard_map/ppermute | solution.py:458
  38.2 28.5 %collective-permute-start.6 = (bf16[400,512]{1,0:T(8,128)(2,1)S(1)}, bf16[400,512]{1,0:T(8,128)(2,1)S(1)}, u32[]{:S(2)}, u32[]{:S(2)}) collective-permute-start(bf16[400,512]{1,0:T(8,128)(2,1)S(1)} %collective-permute-done.5.refs_0_), channel_id=1, source_target_pairs={{0,1},{1,0},{2,3},{3,2},{4,5},{5,4},{6,7},{7,6},{8,9},{9,8},{10,11... | collective-permute-start | bytes 1228808 | tf_op jit(solution)/shard_map/ppermute | solution.py:611
  48.2 27.9 %collective-permute-start.9 = (bf16[400,512]{1,0:T(8,128)(2,1)S(1)}, bf16[400,512]{1,0:T(8,128)(2,1)S(1)}, u32[]{:S(2)}, u32[]{:S(2)}) collective-permute-start(bf16[400,512]{1,0:T(8,128)(2,1)S(1)} %shard_map.147.table.refs_0_), channel_id=1, source_target_pairs={{0,6},{1,7},{2,4},{3,5},{4,2},{5,3},{6,0},{7,1},{8,14},{9,15},{10,... | collective-permute-start | bytes 1228808 | tf_op jit(solution)/shard_map/ppermute | solution.py:623
  63.3 13.2 %collective-permute-start.8 = (bf16[400,512]{1,0:T(8,128)(2,1)S(1)}, bf16[400,512]{1,0:T(8,128)(2,1)S(1)}, u32[]{:S(2)}, u32[]{:S(2)}) collective-permute-start(bf16[400,512]{1,0:T(8,128)(2,1)S(1)} %collective-permute-done.7.refs_0_), channel_id=1, source_target_pairs={{0,1},{1,0},{2,3},{3,2},{4,5},{5,4},{6,7},{7,6},{8,9},{9,8},{10,11... | collective-permute-start | bytes 1228808 | tf_op jit(solution)/shard_map/ppermute | solution.py:611
  64.6 21.3 %collective-permute-start.13 = (bf16[400,512]{1,0:T(8,128)(2,1)S(1)}, bf16[400,512]{1,0:T(8,128)(2,1)S(1)}, u32[]{:S(2)}, u32[]{:S(2)}) collective-permute-start(bf16[400,512]{1,0:T(8,128)(2,1)S(1)} %get-tuple-element.73), channel_id=1, source_target_pairs={{0,1},{1,0},{2,3},{3,2},{4,5},{5,4},{6,7},{7,6},{8,9},{9,8},{10,11... | collective-permute-start | bytes 1228808 | tf_op jit(solution)/shard_map/ppermute | solution.py:611
  65.4 20.6 %collective-permute-start.12 = (bf16[416,512]{1,0:T(8,128)(2,1)S(1)}, bf16[416,512]{1,0:T(8,128)(2,1)S(1)}, u32[]{:S(2)}, u32[]{:S(2)}) collective-permute-start(bf16[416,512]{1,0:T(8,128)(2,1)S(1)} %shard_map.152), channel_id=1, source_target_pairs={{0,16},{8,24},{16,0},{24,8},{1,17},{9,25},{17,1},{25,9},{2,18},{10... | collective-permute-start | bytes 1277960 | tf_op jit(solution)/shard_map/ppermute | solution.py:458
  76.0 36.6 %collective-permute-start.14 = (bf16[400,512]{1,0:T(8,128)(2,1)S(1)}, bf16[400,512]{1,0:T(8,128)(2,1)S(1)}, u32[]{:S(2)}, u32[]{:S(2)}) collective-permute-start(bf16[400,512]{1,0:T(8,128)(2,1)S(1)} %get-tuple-element.75), channel_id=1, source_target_pairs={{0,1},{1,0},{2,3},{3,2},{4,5},{5,4},{6,7},{7,6},{8,9},{9,8},{10,11... | collective-permute-start | bytes 1228808 | tf_op jit(solution)/shard_map/ppermute | solution.py:611
  76.1 10.8 %collective-permute-start.10 = (bf16[400,512]{1,0:T(8,128)(2,1)S(1)}, bf16[400,512]{1,0:T(8,128)(2,1)S(1)}, u32[]{:S(2)}, u32[]{:S(2)}) collective-permute-start(bf16[400,512]{1,0:T(8,128)(2,1)S(1)} %collective-permute-done.9.refs_0_), channel_id=1, source_target_pairs={{0,1},{1,0},{2,3},{3,2},{4,5},{5,4},{6,7},{7,6},{8,9},{9,8},{10,11... | collective-permute-start | bytes 1228808 | tf_op jit(solution)/shard_map/ppermute | solution.py:611
  83.4 34.1 %collective-permute-start.16 = (bf16[400,512]{1,0:T(8,128)(2,1)S(1)}, bf16[400,512]{1,0:T(8,128)(2,1)S(1)}, u32[]{:S(2)}, u32[]{:S(2)}) collective-permute-start(bf16[400,512]{1,0:T(8,128)(2,1)S(1)} %get-tuple-element.77), channel_id=1, source_target_pairs={{0,1},{1,0},{2,3},{3,2},{4,5},{5,4},{6,7},{7,6},{8,9},{9,8},{10,11... | collective-permute-start | bytes 1228808 | tf_op jit(solution)/shard_map/ppermute | solution.py:611
  112.8 28.9 %collective-permute-start.15 = (bf16[400,512]{1,0:T(8,128)(2,1)S(1)}, bf16[400,512]{1,0:T(8,128)(2,1)S(1)}, u32[]{:S(2)}, u32[]{:S(2)}) collective-permute-start(bf16[400,512]{1,0:T(8,128)(2,1)S(1)} %add_convert_fusion.2), channel_id=1, source_target_pairs={{0,2},{1,3},{2,0},{3,1},{4,6},{5,7},{6,4},{7,5},{8,10},{9,11},{10,... | collective-permute-start | bytes 1228808 | tf_op jit(solution)/shard_map/ppermute | solution.py:629
  114.3 16.5 %collective-permute-start.18 = (bf16[400,512]{1,0:T(8,128)(2,1)S(1)}, bf16[400,512]{1,0:T(8,128)(2,1)S(1)}, u32[]{:S(2)}, u32[]{:S(2)}) collective-permute-start(bf16[400,512]{1,0:T(8,128)(2,1)S(1)} %get-tuple-element.79), channel_id=1, source_target_pairs={{0,1},{1,0},{2,3},{3,2},{4,5},{5,4},{6,7},{7,6},{8,9},{9,8},{10,11... | collective-permute-start | bytes 1228808 | tf_op jit(solution)/shard_map/ppermute | solution.py:611
  117.4 10.6 %collective-permute-start.22 = (f32[16,400]{1,0:T(8,128)S(1)}, f32[16,400]{1,0:T(8,128)S(1)}, u32[]{:S(2)}, u32[]{:S(2)}) collective-permute-start(f32[16,400]{1,0:T(8,128)S(1)} %add.47), channel_id=1, source_target_pairs={{0,4},{1,5},{2,6},{3,7},{4,0},{5,1},{6,2},{7,3},{8,12},{9,13},{10,... | collective-permute-start | bytes 76808 | tf_op jit(solution)/shard_map/ppermute | solution.py:550
  117.6 10.5 %collective-permute-start.21 = (f32[16,400]{1,0:T(8,128)S(1)}, f32[16,400]{1,0:T(8,128)S(1)}, u32[]{:S(2)}, u32[]{:S(2)}) collective-permute-start(f32[16,400]{1,0:T(8,128)S(1)} %add.47), channel_id=1, source_target_pairs={{0,2},{1,3},{2,0},{3,1},{4,6},{5,7},{6,4},{7,5},{8,10},{9,11},{10,... | collective-permute-start | bytes 76808 | tf_op jit(solution)/shard_map/ppermute | solution.py:550
  119.0 32.7 %collective-permute-start.17 = (bf16[400,512]{1,0:T(8,128)(2,1)S(1)}, bf16[400,512]{1,0:T(8,128)(2,1)S(1)}, u32[]{:S(2)}, u32[]{:S(2)}) collective-permute-start(bf16[400,512]{1,0:T(8,128)(2,1)S(1)} %add_convert_fusion.1), channel_id=1, source_target_pairs={{0,4},{1,5},{2,6},{3,7},{4,0},{5,1},{6,2},{7,3},{8,12},{9,13},{10,... | collective-permute-start | bytes 1228808 | tf_op jit(solution)/shard_map/ppermute | solution.py:629
  128.1 12.9 %collective-permute-start.25 = (f32[16,400]{1,0:T(8,128)S(1)}, f32[16,400]{1,0:T(8,128)S(1)}, u32[]{:S(2)}, u32[]{:S(2)}) collective-permute-start(f32[16,400]{1,0:T(8,128)S(1)} %add_add_fusion), channel_id=1, source_target_pairs={{0,16},{8,24},{16,0},{24,8},{1,17},{9,25},{17,1},{25,9},{2,18},{10... | collective-permute-start | bytes 76808 | tf_op jit(solution)/shard_map/ppermute | solution.py:550
  130.8 10.2 %collective-permute-start.24 = (f32[16,400]{1,0:T(8,128)S(1)}, f32[16,400]{1,0:T(8,128)S(1)}, u32[]{:S(2)}, u32[]{:S(2)}) collective-permute-start(f32[16,400]{1,0:T(8,128)S(1)} %add_add_fusion), channel_id=1, source_target_pairs={{0,8},{8,0},{16,24},{24,16},{1,9},{9,1},{17,25},{25,17},{2,10},{10... | collective-permute-start | bytes 76808 | tf_op jit(solution)/shard_map/ppermute | solution.py:550
  132.1 31.9 %collective-permute-start.19 = (bf16[400,512]{1,0:T(8,128)(2,1)S(1)}, bf16[400,512]{1,0:T(8,128)(2,1)S(1)}, u32[]{:S(2)}, u32[]{:S(2)}) collective-permute-start(bf16[400,512]{1,0:T(8,128)(2,1)S(1)} %add_convert_fusion), channel_id=1, source_target_pairs={{0,6},{1,7},{2,4},{3,5},{4,2},{5,3},{6,0},{7,1},{8,14},{9,15},{10,... | collective-permute-start | bytes 1228808 | tf_op jit(solution)/shard_map/ppermute | solution.py:629
  (8 other events, 51.6 us)

commit v7 on v6

--- a/solution.py
+++ b/solution.py
@@ -131,7 +131,7 @@
     dim, rows = part_high.shape
     edges = dst_ids.shape[1]
 
-    def body(table, query_in, dst, query_grad, dst_grad):
+    def body(table, query_in, dst, coefs, dst_grad):
         @pl.when(pl.program_id(0) == 0)
         def _():
             dst_grad[...] = jnp.zeros_like(dst_grad)
@@ -141,7 +141,7 @@
         value = query_in[...]
         positive = jnp.sum(value * dst_rows, axis=0, keepdims=True)
         coef = -jax.nn.sigmoid(-positive)
-        query_grad[...] = coef * dst_rows
+        coefs[...] = coef
         dst_grad[...] += dot_nt((coef * value).astype(bf16), pick)
 
     return pl.pallas_call(
@@ -149,8 +149,8 @@
         name="positives",
         grid=(edges // chunk,),
         in_specs=[whole((dim, rows)), lanes(dim, chunk), lanes(1, chunk)],
-        out_specs=[lanes(dim, chunk), whole((dim, rows))],
-        out_shape=[pltpu.HBM((dim, edges), f32), jax.ShapeDtypeStruct((dim, rows), f32)],
+        out_specs=[lanes(1, chunk), whole((dim, rows))],
+        out_shape=[pltpu.HBM((1, edges), f32), jax.ShapeDtypeStruct((dim, rows), f32)],
         compiler_params=params(32),
         cost_estimate=cost(6 * dim * rows * edges, 8 * dim * edges),
     )(part_high, in_hbm(query), in_hbm(dst_ids))
@@ -261,13 +261,16 @@
     )(chip, lane, quota, *tables, neg_ids, in_hbm(query_b))
 
 
-def combine(src_rows, rel_ids, query_grad, negatives, coefs, chip, lane, quota, rel_count, chunk):
+def combine(
+    src_rows, rel_ids, part_high, dst_ids, pos_coef, negatives, coefs, chip, lane, quota, rel_count, chunk
+):
     dim, edges = src_rows.shape
+    rows = part_high.shape[1]
     count = len(negatives)
     slots = negatives[0].shape[0]
     wide = 2 * BLOCK
 
-    def body(chip_ref, lane_ref, quota_ref, rows_in, rel, grad_in, *refs):
+    def body(chip_ref, lane_ref, quota_ref, rows_in, rel, table, dst, pos, *refs):
         neg_refs, coef_refs = refs[:count], refs[count : 2 * count]
         grad_out, rel_out = refs[2 * count :]
 
@@ -275,7 +278,8 @@
         def _():
             rel_out[...] = jnp.zeros_like(rel_out)
 
-        grad_out[...] = grad_in[...]
+        dst_rows = dot_nn(table[...], select_rows(dst[...], rows))
+        grad_out[...] = pos[...] * dst_rows
         for k in range(count):
             first = CORES * (chip_ref[0] ^ k)
             total = quota_ref[0, first]
@@ -298,7 +302,8 @@
         body,
         name="combine",
         grid=(edges // chunk,),
-        in_specs=[smem, smem, smem, lanes(dim, chunk), lanes(1, chunk), lanes(dim, chunk)]
+        in_specs=[smem, smem, smem, lanes(dim, chunk), lanes(1, chunk)]
+        + [whole((dim, rows)), lanes(1, chunk), lanes(1, chunk)]
         + [whole(negatives[0].shape)] * count
         + [lanes(slots * BLOCK, chunk)] * count,
         out_specs=[lanes(dim, chunk), whole((rel_count, dim))],
@@ -314,7 +319,9 @@
         quota,
         in_hbm(src_rows),
         in_hbm(rel_ids),
-        in_hbm(query_grad),
+        part_high,
+        in_hbm(dst_ids),
+        in_hbm(pos_coef),
         *negatives,
         *map(in_hbm, coefs),
     )
@@ -603,7 +610,7 @@
             src_table, rel_parts, src_ids, rel_ids, rel_count, min(chunk, edges // 2), part, 2, made
         )
     query, query_b, src_rows = made
-    query_grad, own_grad = positives(part_high, query, dst_ids, chunk)
+    pos_coef, own_grad = positives(part_high, query, dst_ids, chunk)
 
     swap = [(i, i ^ 1) for i in range(edge_count)]
 
@@ -613,14 +620,17 @@
     chip = here // CORES
     lane = here % CORES
     arrived, negatives, coefs = [], [], []
-    done = [own_grad]
+    done, brought = [own_grad], {}
     for k in range(chips):
         pairs = [(i, i ^ (CORES * k)) for i in range(edge_count)]
-        table = part_high
+        near = k & -k
+        table = brought.get(k - near, part_high)
         if k:
-            if k >= 2:
-                table, _ = lax.optimization_barrier((table, done[k - 2]))
-            table = lax.ppermute(table, "edge", pairs)
+            if k == near >= 2:
+                table, _ = lax.optimization_barrier((table, done[k // 2 - 1]))
+            hop = [(i, i ^ (CORES * near)) for i in range(edge_count)]
+            table = lax.ppermute(table, "edge", hop)
+        brought[k] = table
         live, coef, mine, theirs = negative_wave(
             [table, swapped(table)], chip ^ k, quotas, neg_ids, query_b, lane, wave_chunk
         )
@@ -635,7 +645,9 @@
     query_grad, rel_grad = combine(
         src_rows,
         rel_ids,
-        query_grad,
+        part_high,
+        dst_ids,
+        pos_coef,
         negatives,
         coefs,
         chip,

time: 167 us -> 162 us (0.970)
  the two profiles are of different devices: /device:TPU:13 before, /device:TPU:0 now
where the time goes in v7:
time: 162 us; the launch traced here: 160 us
  Pallas kernels  85.4 us (53%)
  starting transfers between devices  41.8 us (26%)
  waiting for transfers between devices  29.1 us (18%)
  other arithmetic  1.84 us (1%)
    pallas_call x4, Pallas kernels, negative_wave(): pl.pallas_call(body, grid=(edges // chunk,), in_specs=[smem, smem, smem]...  35.1 us
    pallas_call x1, Pallas kernels, combine(): pl.pallas_call(body, name='combine', grid=(edges // chunk,), in_specs=[sm...  17.5 us
    ppermute x3, starting transfers between devices, shards(): total = lax.ppermute(total.astype(bf16), 'edge', pairs)  16 us
    ppermute x3, waiting for transfers between devices, shards(): table = lax.ppermute(table, 'edge', hop)  13.7 us
    pallas_call x2, Pallas kernels, make_queries(): pl.pallas_call(body, name='make_queries', grid=(steps,), in_specs=[whole(...  12.4 us
    ppermute x7, starting transfers between devices, total_of_peers(): lax.ppermute(value, axis, [(i, peer(i, k)) for i in range(count)])  11.1 us
    ppermute x6, starting transfers between devices, shifted(): lax.ppermute(array, 'dom', [(d, moved(d, n, stride, shift)) for d in rang...  8.74 us
    ppermute x7, waiting for transfers between devices, total_of_peers(): lax.ppermute(value, axis, [(i, peer(i, k)) for i in range(count)])  7.48 us
  transfers between devices with their start and end apart: 27, of which 7 were waited for; matrix products, arithmetic and copies ran while one was open for 1% of the time, Pallas kernels for 46%

profile of v7, /device:TPU:0, one launch (start us, length us, event | category | flops | bytes accessed | tf_op | source)
XLA Modules:
  0.0 159.8 jit_solution(12595131771835984047)
XLA Ops:
  1.9 3.0 %collective-permute-start = (bf16[400,256]{1,0:T(8,128)(2,1)S(1)}, bf16[400,256]{1,0:T(8,128)(2,1)S(1)}, u32[]{:S(2)}, u32[]{:S(2)}) collective-permute-start(bf16[400,256]{1,0:T(8,128)(2,1)S(1)} %get-tuple-element.48.refs_0_), channel_id=1, source_target_pairs={{0,8},{8,0},{16,24},{24,16},{1,9},{9,1},{17,25},{25,17},{2,10},{10... | collective-permute-start | bytes 614408 | tf_op jit(solution)/shard_map/ppermute | solution.py:465
  7.4 2.6 %collective-permute-done.refs_1_ = bf16[400,256]{1,0:T(8,128)(2,1)S(1)} collective-permute-done((bf16[400,256]{1,0:T(8,128)(2,1)S(1)}, bf16[400,256]{1,0:T(8,128)(2,1)S(1)}, u32[]{:S(2)}, u32[]{:S(2)}) %collective-permute-start) | collective-permute-done | bytes 204832 | tf_op jit(solution)/shard_map/ppermute | solution.py:465
  12.8 1.6 collective-permute-start.2
  14.9 6.2 %make_queries.2 = (f32[400,4096]{1,0:T(8,128)}, bf16[400,4096]{1,0:T(8,128)(2,1)}, f32[400,4096]{1,0:T(8,128)}) custom-call(f32[400,512]{1,0:T(8,128)} %table.5, bf16[400,128]{1,0:T(8,128)(2,1)S(1)} %pad.4.parts_ref.parts, s32[1,4096]{1,0:T(1,128)} %bitcast.15, s32[1,4096]{1,0:T(1,128)} %bitcast.11), custom_call_target="tpu_custom_call" | custom-call | flops 1677721600 | bytes 8192000 | tf_op jit(solution)/shard_map/make_queries/pallas_call | solution.py:115
  21.2 6.2 %make_queries.3 = (f32[400,4096]{1,0:T(8,128)}, bf16[400,4096]{1,0:T(8,128)(2,1)}, f32[400,4096]{1,0:T(8,128)}) custom-call(f32[400,512]{1,0:T(8,128)} %table.5, bf16[400,128]{1,0:T(8,128)(2,1)S(1)} %pad.4.parts_ref.parts, s32[1,4096]{1,0:T(1,128)} %bitcast.16, s32[1,4096]{1,0:T(1,128)} %bitcast.12, ...), custom_call_target="tpu_custom_call", output_to_operand_aliasing={{0}: (4, {}), {1}: (5, {}), {2}: (6, {})} | custom-call | flops 1677721600 | bytes 8192000 | tf_op jit(solution)/shard_map/make_queries/pallas_call | solution.py:115
  28.0 6.7 %positives.1 = (f32[1,4096]{1,0:T(1,128)}, f32[400,512]{1,0:T(8,128)S(1)}) custom-call(bf16[400,512]{1,0:T(8,128)(2,1)S(1)} %shard_map.147.table.refs_0_, f32[400,4096]{1,0:T(8,128)} %get-tuple-element.53.query_in, s32[1,4096]{1,0:T(1,128)} %bitcast.18), custom_call_target="tpu_custom_call" | custom-call | flops 5033164800 | bytes 13107200 | tf_op jit(solution)/shard_map/positives/pallas_call | solution.py:147
  34.7 2.6 %collective-permute-start.7 = (bf16[400,512]{1,0:T(8,128)(2,1)S(1)}, bf16[400,512]{1,0:T(8,128)(2,1)S(1)}, u32[]{:S(2)}, u32[]{:S(2)}) collective-permute-start(bf16[400,512]{1,0:T(8,128)(2,1)S(1)} %shard_map.147.table.refs_0_), channel_id=1, source_target_pairs={{0,4},{1,5},{2,6},{3,7},{4,0},{5,1},{6,2},{7,3},{8,12},{9,13},{10,... | collective-permute-start | bytes 1228808 | tf_op jit(solution)/shard_map/ppermute | solution.py:632
  37.3 1.6 collective-permute-start.5
  40.3 13.7 %collective-permute-done.7.refs_0_ = bf16[400,512]{1,0:T(8,128)(2,1)S(1)} collective-permute-done((bf16[400,512]{1,0:T(8,128)(2,1)S(1)}, bf16[400,512]{1,0:T(8,128)(2,1)S(1)}, u32[]{:S(2)}, u32[]{:S(2)}) %collective-permute-start.7) | collective-permute-done | bytes 409632 | tf_op jit(solution)/shard_map/ppermute | solution.py:632
  54.9 9.4 %shard_map.148 = (bf16[4,400,128]{2,1,0:T(8,128)(2,1)S(1)}, bf16[512,4096]{1,0:T(8,128)(2,1)}, bf16[400,512]{1,0:T(8,128)(2,1)S(1)}, bf16[400,512]{1,0:T(8,128)(2,1)S(1)}) custom-call(s32[1]{0:T(128)S(6)} %select_n.12.chip_ref, s32[1]{0:T(128)S(6)} %select_n.13.lane_ref, s32[1,8]{1,0:T(1,128)S(1)} %copy-done.2, ...), custom_call_target="tpu_custom_call" | custom-call | flops 3774873600 | bytes 16384000 | tf_op jit(solution)/shard_map/pallas_call | solution.py:242
  66.0 9.4 %shard_map.150 = (bf16[4,400,128]{2,1,0:T(8,128)(2,1)S(1)}, bf16[512,4096]{1,0:T(8,128)(2,1)}, bf16[400,512]{1,0:T(8,128)(2,1)S(1)}, bf16[400,512]{1,0:T(8,128)(2,1)S(1)}) custom-call(s32[1]{0:T(128)S(6)} %xor.10.chip_ref, s32[1]{0:T(128)S(6)} %select_n.13.lane_ref, s32[1,8]{1,0:T(1,128)S(1)} %copy-done.2, ...), custom_call_target="tpu_custom_call" | custom-call | flops 3774873600 | bytes 16384000 | tf_op jit(solution)/shard_map/pallas_call | solution.py:242
  75.9 9.4 %shard_map.149 = (bf16[4,400,128]{2,1,0:T(8,128)(2,1)S(1)}, bf16[512,4096]{1,0:T(8,128)(2,1)}, bf16[400,512]{1,0:T(8,128)(2,1)S(1)}, bf16[400,512]{1,0:T(8,128)(2,1)S(1)}) custom-call(s32[1]{0:T(128)S(6)} %xor.9.chip_ref, s32[1]{0:T(128)S(6)} %select_n.13.lane_ref, s32[1,8]{1,0:T(1,128)S(1)} %copy-done.2, ...), custom_call_target="tpu_custom_call" | custom-call | flops 3774873600 | bytes 16384000 | tf_op jit(solution)/shard_map/pallas_call | solution.py:242
  86.3 6.9 %shard_map.151 = (bf16[4,400,128]{2,1,0:T(8,128)(2,1)S(1)}, bf16[512,4096]{1,0:T(8,128)(2,1)}, bf16[400,512]{1,0:T(8,128)(2,1)S(1)}, bf16[400,512]{1,0:T(8,128)(2,1)S(1)}) custom-call(s32[1]{0:T(128)S(6)} %xor.11.chip_ref, s32[1]{0:T(128)S(6)} %select_n.13.lane_ref, s32[1,8]{1,0:T(1,128)S(1)} %copy-done.2, ...), custom_call_target="tpu_custom_call" | custom-call | flops 3774873600 | bytes 16384000 | tf_op jit(solution)/shard_map/pallas_call | solution.py:242
  93.2 17.5 %combine.1 = (f32[400,4096]{1,0:T(8,128)}, f32[16,400]{1,0:T(8,128)S(1)}) custom-call(s32[1]{0:T(128)S(6)} %select_n.12.chip_ref, s32[1]{0:T(128)S(6)} %select_n.13.lane_ref, s32[1,8]{1,0:T(1,128)S(1)} %copy-done.2, f32[400,4096]{1,0:T(8,128)} %get-tuple-element.46.rows_in, s32[1,4096]{1,0:T(1,128)} %bitcast.13, ...), custom_call_target="tpu_custom_call" | custom-call | flops 5033164800 | bytes 32243712 | tf_op jit(solution)/shard_map/combine/pallas_call | solution.py:301
  110.7 3.0 %collective-permute-start.20 = (f32[16,400]{1,0:T(8,128)S(1)}, f32[16,400]{1,0:T(8,128)S(1)}, u32[]{:S(2)}, u32[]{:S(2)}) collective-permute-start(f32[16,400]{1,0:T(8,128)S(1)} %get-tuple-element.80), channel_id=1, source_target_pairs={{0,1},{1,0},{2,3},{3,2},{4,5},{5,4},{6,7},{7,6},{8,9},{9,8},{10,11... | collective-permute-start | bytes 76808 | tf_op jit(solution)/shard_map/ppermute | solution.py:557
  113.8 3.1 %collective-permute-start.17 = (bf16[400,512]{1,0:T(8,128)(2,1)S(1)}, bf16[400,512]{1,0:T(8,128)(2,1)S(1)}, u32[]{:S(2)}, u32[]{:S(2)}) collective-permute-start(bf16[400,512]{1,0:T(8,128)(2,1)S(1)} %add_convert_fusion.1), channel_id=1, source_target_pairs={{0,4},{1,5},{2,6},{3,7},{4,0},{5,1},{6,2},{7,3},{8,12},{9,13},{10,... | collective-permute-start | bytes 1228808 | tf_op jit(solution)/shard_map/ppermute | solution.py:639
  118.8 2.6 %collective-permute-start.21 = (f32[16,400]{1,0:T(8,128)S(1)}, f32[16,400]{1,0:T(8,128)S(1)}, u32[]{:S(2)}, u32[]{:S(2)}) collective-permute-start(f32[16,400]{1,0:T(8,128)S(1)} %add.47), channel_id=1, source_target_pairs={{0,2},{1,3},{2,0},{3,1},{4,6},{5,7},{6,4},{7,5},{8,10},{9,11},{10,... | collective-permute-start | bytes 76808 | tf_op jit(solution)/shard_map/ppermute | solution.py:557
  121.5 6.3 %collective-permute-done.23 = f32[16,400]{1,0:T(8,128)S(1)} collective-permute-done((f32[16,400]{1,0:T(8,128)S(1)}, f32[16,400]{1,0:T(8,128)S(1)}, u32[]{:S(2)}, u32[]{:S(2)}) %collective-permute-start.23) | collective-permute-done | bytes 25632 | tf_op jit(solution)/shard_map/ppermute | solution.py:557
  127.7 10.1 %collective-permute-start.15 = (bf16[400,512]{1,0:T(8,128)(2,1)S(1)}, bf16[400,512]{1,0:T(8,128)(2,1)S(1)}, u32[]{:S(2)}, u32[]{:S(2)}) collective-permute-start(bf16[400,512]{1,0:T(8,128)(2,1)S(1)} %add_convert_fusion.2), channel_id=1, source_target_pairs={{0,2},{1,3},{2,0},{3,1},{4,6},{5,7},{6,4},{7,5},{8,10},{9,11},{10,... | collective-permute-start | bytes 1228808 | tf_op jit(solution)/shard_map/ppermute | solution.py:639
  138.7 2.9 %collective-permute-start.25 = (f32[16,400]{1,0:T(8,128)S(1)}, f32[16,400]{1,0:T(8,128)S(1)}, u32[]{:S(2)}, u32[]{:S(2)}) collective-permute-start(f32[16,400]{1,0:T(8,128)S(1)} %add_add_fusion), channel_id=1, source_target_pairs={{0,16},{8,24},{16,0},{24,8},{1,17},{9,25},{17,1},{25,9},{2,18},{10... | collective-permute-start | bytes 76808 | tf_op jit(solution)/shard_map/ppermute | solution.py:557
  142.9 2.8 %collective-permute-start.19 = (bf16[400,512]{1,0:T(8,128)(2,1)S(1)}, bf16[400,512]{1,0:T(8,128)(2,1)S(1)}, u32[]{:S(2)}, u32[]{:S(2)}) collective-permute-start(bf16[400,512]{1,0:T(8,128)(2,1)S(1)} %add_convert_fusion), channel_id=1, source_target_pairs={{0,6},{1,7},{2,4},{3,5},{4,2},{5,3},{6,0},{7,1},{8,14},{9,15},{10,... | collective-permute-start | bytes 1228808 | tf_op jit(solution)/shard_map/ppermute | solution.py:639
  145.7 7.3 %source_side.1 = (f32[400,512]{1,0:T(8,128)}, f32[1,512]{1,0:T(1,128)}) custom-call(f32[400,512]{1,0:T(8,128)} %table.5, f32[1,512]{1,0:T(1,128)} %bitcast.21, bf16[400,128]{1,0:T(8,128)(2,1)S(1)} %pad.4.parts_ref.parts, s32[1,4096]{1,0:T(1,128)} %bitcast.17, s32[1,4096]{1,0:T(1,128)} %bitcast.14, f32[400,4096]{1,0:T(8,128)} %get-tuple-element.66.grad_in), custom_call_target="tpu_custom_call" | custom-call | flops 3355443200 | bytes 6553600 | tf_op jit(solution)/shard_map/source_side/pallas_call | solution.py:352
  153.6 3.9 %collective-permute-done.19.refs_6_ = bf16[400,512]{1,0:T(8,128)(2,1)S(1)} collective-permute-done((bf16[400,512]{1,0:T(8,128)(2,1)S(1)}, bf16[400,512]{1,0:T(8,128)(2,1)S(1)}, u32[]{:S(2)}, u32[]{:S(2)}) %collective-permute-start.19) | collective-permute-done | bytes 409632 | tf_op jit(solution)/shard_map/ppermute | solution.py:639
  157.5 2.3 %destination_side.1 = (f32[400,512]{1,0:T(8,128)}, f32[1,512]{1,0:T(1,128)}) custom-call(bf16[400,512]{1,0:T(8,128)(2,1)S(1)} %shard_map.147.table.refs_0_, bf16[416,512]{1,0:T(8,128)(2,1)S(1)} %shard_map.153.refs_1_, f32[400,512]{1,0:T(8,128)S(1)} %get-tuple-element.58.refs_2_, f32[400,512]{1,0:T(8,128)S(1)} %convert_add_fusion.refs_3_, ...), custom_call_target="tpu_custom_call" | custom-call | flops 1638400 | bytes 4096000 | tf_op jit(solution)/shard_map/destination_side/pallas_call | solution.py:402
  (67 shorter events, 18.1 us)
Async XLA Ops:
  1.9 8.1 %collective-permute-start = (bf16[400,256]{1,0:T(8,128)(2,1)S(1)}, bf16[400,256]{1,0:T(8,128)(2,1)S(1)}, u32[]{:S(2)}, u32[]{:S(2)}) collective-permute-start(bf16[400,256]{1,0:T(8,128)(2,1)S(1)} %get-tuple-element.48.refs_0_), channel_id=1, source_target_pairs={{0,8},{8,0},{16,24},{24,16},{1,9},{9,1},{17,25},{25,17},{2,10},{10... | collective-permute-start | bytes 614408 | tf_op jit(solution)/shard_map/ppermute | solution.py:465
  12.8 14.6 %collective-permute-start.2 = (bf16[400,256]{1,0:T(8,128)(2,1)S(1)}, bf16[400,256]{1,0:T(8,128)(2,1)S(1)}, u32[]{:S(2)}, u32[]{:S(2)}) collective-permute-start(bf16[400,256]{1,0:T(8,128)(2,1)S(1)} %get-tuple-element.50), channel_id=1, source_target_pairs={{0,16},{8,24},{16,0},{24,8},{1,17},{9,25},{17,1},{25,9},{2,18},{10... | collective-permute-start | bytes 614408 | tf_op jit(solution)/shard_map/ppermute | solution.py:465
  14.4 13.0 %collective-permute-start.3 = (bf16[400,256]{1,0:T(8,128)(2,1)S(1)}, bf16[400,256]{1,0:T(8,128)(2,1)S(1)}, u32[]{:S(2)}, u32[]{:S(2)}) collective-permute-start(bf16[400,256]{1,0:T(8,128)(2,1)S(1)} %get-tuple-element.51), channel_id=1, source_target_pairs={{0,8},{8,0},{16,24},{24,16},{1,9},{9,1},{17,25},{25,17},{2,10},{10... | collective-permute-start | bytes 614408 | tf_op jit(solution)/shard_map/ppermute | solution.py:465
  34.7 19.3 %collective-permute-start.7 = (bf16[400,512]{1,0:T(8,128)(2,1)S(1)}, bf16[400,512]{1,0:T(8,128)(2,1)S(1)}, u32[]{:S(2)}, u32[]{:S(2)}) collective-permute-start(bf16[400,512]{1,0:T(8,128)(2,1)S(1)} %shard_map.147.table.refs_0_), channel_id=1, source_target_pairs={{0,4},{1,5},{2,6},{3,7},{4,0},{5,1},{6,2},{7,3},{8,12},{9,13},{10,... | collective-permute-start | bytes 1228808 | tf_op jit(solution)/shard_map/ppermute | solution.py:632
  37.3 17.4 %collective-permute-start.5 = (bf16[400,512]{1,0:T(8,128)(2,1)S(1)}, bf16[400,512]{1,0:T(8,128)(2,1)S(1)}, u32[]{:S(2)}, u32[]{:S(2)}) collective-permute-start(bf16[400,512]{1,0:T(8,128)(2,1)S(1)} %shard_map.147.table.refs_0_), channel_id=1, source_target_pairs={{0,2},{1,3},{2,0},{3,1},{4,6},{5,7},{6,4},{7,5},{8,10},{9,11},{10,... | collective-permute-start | bytes 1228808 | tf_op jit(solution)/shard_map/ppermute | solution.py:632
  38.8 16.0 %collective-permute-start.4 = (bf16[400,512]{1,0:T(8,128)(2,1)S(1)}, bf16[400,512]{1,0:T(8,128)(2,1)}, u32[]{:S(2)}, u32[]{:S(2)}) collective-permute-start(bf16[400,512]{1,0:T(8,128)(2,1)S(1)} %shard_map.147.table.refs_0_), channel_id=1, source_target_pairs={{0,1},{1,0},{2,3},{3,2},{4,5},{5,4},{6,7},{7,6},{8,9},{9,8},{10,11... | collective-permute-start | bytes 1228808 | tf_op jit(solution)/shard_map/ppermute | solution.py:618
  38.8 25.8 %collective-permute-start.11 = (bf16[416,512]{1,0:T(8,128)(2,1)S(1)}, bf16[416,512]{1,0:T(8,128)(2,1)S(1)}, u32[]{:S(2)}, u32[]{:S(2)}) collective-permute-start(bf16[416,512]{1,0:T(8,128)(2,1)S(1)} %get-tuple-element.69.refs_0_), channel_id=1, source_target_pairs={{0,8},{8,0},{16,24},{24,16},{1,9},{9,1},{17,25},{25,17},{2,10},{10... | collective-permute-start | bytes 1277960 | tf_op jit(solution)/shard_map/ppermute | solution.py:465
  54.0 12.0 %collective-permute-start.8 = (bf16[400,512]{1,0:T(8,128)(2,1)S(1)}, bf16[400,512]{1,0:T(8,128)(2,1)S(1)}, u32[]{:S(2)}, u32[]{:S(2)}) collective-permute-start(bf16[400,512]{1,0:T(8,128)(2,1)S(1)} %collective-permute-done.7.refs_0_), channel_id=1, source_target_pairs={{0,1},{1,0},{2,3},{3,2},{4,5},{5,4},{6,7},{7,6},{8,9},{9,8},{10,11... | collective-permute-start | bytes 1228808 | tf_op jit(solution)/shard_map/ppermute | solution.py:618
  54.0 21.4 %collective-permute-start.9 = (bf16[400,512]{1,0:T(8,128)(2,1)S(1)}, bf16[400,512]{1,0:T(8,128)(2,1)S(1)}, u32[]{:S(2)}, u32[]{:S(2)}) collective-permute-start(bf16[400,512]{1,0:T(8,128)(2,1)S(1)} %collective-permute-done.7.refs_0_), channel_id=1, source_target_pairs={{0,2},{1,3},{2,0},{3,1},{4,6},{5,7},{6,4},{7,5},{8,10},{9,11},{10,... | collective-permute-start | bytes 1228808 | tf_op jit(solution)/shard_map/ppermute | solution.py:632
  54.7 21.3 %collective-permute-start.6 = (bf16[400,512]{1,0:T(8,128)(2,1)S(1)}, bf16[400,512]{1,0:T(8,128)(2,1)S(1)}, u32[]{:S(2)}, u32[]{:S(2)}) collective-permute-start(bf16[400,512]{1,0:T(8,128)(2,1)S(1)} %collective-permute-done.5.refs_0_), channel_id=1, source_target_pairs={{0,1},{1,0},{2,3},{3,2},{4,5},{5,4},{6,7},{7,6},{8,9},{9,8},{10,11... | collective-permute-start | bytes 1228808 | tf_op jit(solution)/shard_map/ppermute | solution.py:618
  64.3 21.0 %collective-permute-start.13 = (bf16[400,512]{1,0:T(8,128)(2,1)S(1)}, bf16[400,512]{1,0:T(8,128)(2,1)S(1)}, u32[]{:S(2)}, u32[]{:S(2)}) collective-permute-start(bf16[400,512]{1,0:T(8,128)(2,1)S(1)} %get-tuple-element.71), channel_id=1, source_target_pairs={{0,1},{1,0},{2,3},{3,2},{4,5},{5,4},{6,7},{7,6},{8,9},{9,8},{10,11... | collective-permute-start | bytes 1228808 | tf_op jit(solution)/shard_map/ppermute | solution.py:618
  65.4 20.0 %collective-permute-start.12 = (bf16[416,512]{1,0:T(8,128)(2,1)S(1)}, bf16[416,512]{1,0:T(8,128)(2,1)S(1)}, u32[]{:S(2)}, u32[]{:S(2)}) collective-permute-start(bf16[416,512]{1,0:T(8,128)(2,1)S(1)} %shard_map.152), channel_id=1, source_target_pairs={{0,16},{8,24},{16,0},{24,8},{1,17},{9,25},{17,1},{25,9},{2,18},{10... | collective-permute-start | bytes 1277960 | tf_op jit(solution)/shard_map/ppermute | solution.py:465
  75.4 38.3 %collective-permute-start.16 = (bf16[400,512]{1,0:T(8,128)(2,1)S(1)}, bf16[400,512]{1,0:T(8,128)(2,1)S(1)}, u32[]{:S(2)}, u32[]{:S(2)}) collective-permute-start(bf16[400,512]{1,0:T(8,128)(2,1)S(1)} %get-tuple-element.75), channel_id=1, source_target_pairs={{0,1},{1,0},{2,3},{3,2},{4,5},{5,4},{6,7},{7,6},{8,9},{9,8},{10,11... | collective-permute-start | bytes 1228808 | tf_op jit(solution)/shard_map/ppermute | solution.py:618
  75.4 10.8 %collective-permute-start.10 = (bf16[400,512]{1,0:T(8,128)(2,1)S(1)}, bf16[400,512]{1,0:T(8,128)(2,1)S(1)}, u32[]{:S(2)}, u32[]{:S(2)}) collective-permute-start(bf16[400,512]{1,0:T(8,128)(2,1)S(1)} %collective-permute-done.9.refs_0_), channel_id=1, source_target_pairs={{0,1},{1,0},{2,3},{3,2},{4,5},{5,4},{6,7},{7,6},{8,9},{9,8},{10,11... | collective-permute-start | bytes 1228808 | tf_op jit(solution)/shard_map/ppermute | solution.py:618
  85.3 33.5 %collective-permute-start.14 = (bf16[400,512]{1,0:T(8,128)(2,1)S(1)}, bf16[400,512]{1,0:T(8,128)(2,1)S(1)}, u32[]{:S(2)}, u32[]{:S(2)}) collective-permute-start(bf16[400,512]{1,0:T(8,128)(2,1)S(1)} %get-tuple-element.73), channel_id=1, source_target_pairs={{0,1},{1,0},{2,3},{3,2},{4,5},{5,4},{6,7},{7,6},{8,9},{9,8},{10,11... | collective-permute-start | bytes 1228808 | tf_op jit(solution)/shard_map/ppermute | solution.py:618
  113.8 39.8 %collective-permute-start.17 = (bf16[400,512]{1,0:T(8,128)(2,1)S(1)}, bf16[400,512]{1,0:T(8,128)(2,1)S(1)}, u32[]{:S(2)}, u32[]{:S(2)}) collective-permute-start(bf16[400,512]{1,0:T(8,128)(2,1)S(1)} %add_convert_fusion.1), channel_id=1, source_target_pairs={{0,4},{1,5},{2,6},{3,7},{4,0},{5,1},{6,2},{7,3},{8,12},{9,13},{10,... | collective-permute-start | bytes 1228808 | tf_op jit(solution)/shard_map/ppermute | solution.py:639
  116.9 24.6 %collective-permute-start.18 = (bf16[400,512]{1,0:T(8,128)(2,1)S(1)}, bf16[400,512]{1,0:T(8,128)(2,1)S(1)}, u32[]{:S(2)}, u32[]{:S(2)}) collective-permute-start(bf16[400,512]{1,0:T(8,128)(2,1)S(1)} %get-tuple-element.77), channel_id=1, source_target_pairs={{0,1},{1,0},{2,3},{3,2},{4,5},{5,4},{6,7},{7,6},{8,9},{9,8},{10,11... | collective-permute-start | bytes 1228808 | tf_op jit(solution)/shard_map/ppermute | solution.py:618
  116.9 10.8 %collective-permute-start.23 = (f32[16,400]{1,0:T(8,128)S(1)}, f32[16,400]{1,0:T(8,128)S(1)}, u32[]{:S(2)}, u32[]{:S(2)}) collective-permute-start(f32[16,400]{1,0:T(8,128)S(1)} %add.47), channel_id=1, source_target_pairs={{0,6},{1,7},{2,4},{3,5},{4,2},{5,3},{6,0},{7,1},{8,14},{9,15},{10,... | collective-permute-start | bytes 76808 | tf_op jit(solution)/shard_map/ppermute | solution.py:557
  117.4 20.5 %collective-permute-start.22 = (f32[16,400]{1,0:T(8,128)S(1)}, f32[16,400]{1,0:T(8,128)S(1)}, u32[]{:S(2)}, u32[]{:S(2)}) collective-permute-start(f32[16,400]{1,0:T(8,128)S(1)} %add.47), channel_id=1, source_target_pairs={{0,4},{1,5},{2,6},{3,7},{4,0},{5,1},{6,2},{7,3},{8,12},{9,13},{10,... | collective-permute-start | bytes 76808 | tf_op jit(solution)/shard_map/ppermute | solution.py:557
  118.8 19.1 %collective-permute-start.21 = (f32[16,400]{1,0:T(8,128)S(1)}, f32[16,400]{1,0:T(8,128)S(1)}, u32[]{:S(2)}, u32[]{:S(2)}) collective-permute-start(f32[16,400]{1,0:T(8,128)S(1)} %add.47), channel_id=1, source_target_pairs={{0,2},{1,3},{2,0},{3,1},{4,6},{5,7},{6,4},{7,5},{8,10},{9,11},{10,... | collective-permute-start | bytes 76808 | tf_op jit(solution)/shard_map/ppermute | solution.py:557
  127.7 25.9 %collective-permute-start.15 = (bf16[400,512]{1,0:T(8,128)(2,1)S(1)}, bf16[400,512]{1,0:T(8,128)(2,1)S(1)}, u32[]{:S(2)}, u32[]{:S(2)}) collective-permute-start(bf16[400,512]{1,0:T(8,128)(2,1)S(1)} %add_convert_fusion.2), channel_id=1, source_target_pairs={{0,2},{1,3},{2,0},{3,1},{4,6},{5,7},{6,4},{7,5},{8,10},{9,11},{10,... | collective-permute-start | bytes 1228808 | tf_op jit(solution)/shard_map/ppermute | solution.py:639
  138.7 14.3 %collective-permute-start.25 = (f32[16,400]{1,0:T(8,128)S(1)}, f32[16,400]{1,0:T(8,128)S(1)}, u32[]{:S(2)}, u32[]{:S(2)}) collective-permute-start(f32[16,400]{1,0:T(8,128)S(1)} %add_add_fusion), channel_id=1, source_target_pairs={{0,16},{8,24},{16,0},{24,8},{1,17},{9,25},{17,1},{25,9},{2,18},{10... | collective-permute-start | bytes 76808 | tf_op jit(solution)/shard_map/ppermute | solution.py:557
  141.5 11.4 %collective-permute-start.24 = (f32[16,400]{1,0:T(8,128)S(1)}, f32[16,400]{1,0:T(8,128)S(1)}, u32[]{:S(2)}, u32[]{:S(2)}) collective-permute-start(f32[16,400]{1,0:T(8,128)S(1)} %add_add_fusion), channel_id=1, source_target_pairs={{0,8},{8,0},{16,24},{24,16},{1,9},{9,1},{17,25},{25,17},{2,10},{10... | collective-permute-start | bytes 76808 | tf_op jit(solution)/shard_map/ppermute | solution.py:557
  142.9 14.6 %collective-permute-start.19 = (bf16[400,512]{1,0:T(8,128)(2,1)S(1)}, bf16[400,512]{1,0:T(8,128)(2,1)S(1)}, u32[]{:S(2)}, u32[]{:S(2)}) collective-permute-start(bf16[400,512]{1,0:T(8,128)(2,1)S(1)} %add_convert_fusion), channel_id=1, source_target_pairs={{0,6},{1,7},{2,4},{3,5},{4,2},{5,3},{6,0},{7,1},{8,14},{9,15},{10,... | collective-permute-start | bytes 1228808 | tf_op jit(solution)/shard_map/ppermute | solution.py:639
  (8 other events, 84.7 us)

commit v8 on v7

--- a/solution.py
+++ b/solution.py
@@ -14,6 +14,7 @@
 CORES = 2
 LEARN_RATE = 0.1
 REL_RATE = 0.02
+SUB = 1024
 
 
 bf16 = jnp.bfloat16
@@ -207,19 +208,26 @@
             neg_t[total] = jnp.zeros((BLOCK, dim), bf16)
             neg_grad[total] = jnp.zeros((dim, BLOCK), f32)
 
-        def pair(p, carry):
-            left, right = 2 * p, 2 * p + 1
-            columns_t = jnp.concatenate([neg_t[left], neg_t[right]], axis=0)
-            query = query_ref[...]
-            scores = dot_nn(columns_t, query)
-            coef = (half_weight * jnp.tanh(0.5 * scores) + half_weight).astype(bf16)
-            coef_out[pl.ds(pl.multiple_of(left * BLOCK, 2 * BLOCK), 2 * BLOCK)] = coef
-            added = dot_nt(query, coef)
-            neg_grad[left] += added[:, :BLOCK]
-            neg_grad[right] += added[:, BLOCK:]
-            return carry
-
-        lax.fori_loop(0, (total + 1) // 2, pair, 0)
+        for pairs in range(1, slots // 2 + 1):
+
+            @pl.when((total + 1) // 2 == pairs)
+            def _(blocks=2 * pairs):
+                query = query_ref[...]
+                rows_t = jnp.concatenate([neg_t[j] for j in range(blocks)], axis=0)
+                scores = dot_nn(rows_t, query)
+                coef = (half_weight * jnp.tanh(0.5 * scores) + half_weight).astype(bf16)
+                coef_out[: blocks * BLOCK] = coef
+                added = dot_nt(query, coef)
+                for j in range(blocks):
+                    neg_grad[j] += added[:, j * BLOCK : (j + 1) * BLOCK]
+
+        for p in range(slots // 2):
+
+            @pl.when(p >= (total + 1) // 2)
+            def _(p=p):
+                coef_out[2 * p * BLOCK : 2 * (p + 1) * BLOCK] = jnp.zeros((2 * BLOCK, chunk), bf16)
+                neg[2 * p] = jnp.zeros((dim, BLOCK), bf16)
+                neg[2 * p + 1] = jnp.zeros((dim, BLOCK), bf16)
 
         for s in range(count):
 
@@ -233,9 +241,7 @@
                 def _(s=s, wide=wide):
                     parts = [neg_grad[base[s] + b] for b in range(wide)]
                     value = jnp.concatenate(parts, axis=1) if wide > 1 else parts[0]
-                    high, low = split2(value)
-                    pick = picks(s, wide)
-                    grad_refs[s][...] = (dot_nt(high, pick) + dot_nt(low, pick)).astype(bf16)
+                    grad_refs[s][...] = dot_nt(value.astype(bf16), picks(s, wide)).astype(bf16)
 
     smem = pl.BlockSpec(memory_space=pltpu.SMEM)
     shard = jax.ShapeDtypeStruct((dim, rows), bf16)
@@ -262,47 +268,43 @@
 
 
 def combine(
-    src_rows, rel_ids, part_high, dst_ids, pos_coef, negatives, coefs, chip, lane, quota, rel_count, chunk
+    src_rows, rel_ids, part_high, dst_ids, pos_coef, negatives, coefs, rel_count, chunk
 ):
     dim, edges = src_rows.shape
     rows = part_high.shape[1]
     count = len(negatives)
     slots = negatives[0].shape[0]
-    wide = 2 * BLOCK
-
-    def body(chip_ref, lane_ref, quota_ref, rows_in, rel, table, dst, pos, *refs):
+    sub = min(SUB, chunk)
+
+    def body(rows_in, rel, table, dst, pos, *refs):
         neg_refs, coef_refs = refs[:count], refs[count : 2 * count]
-        grad_out, rel_out = refs[2 * count :]
+        grad_out, rel_out, all_neg = refs[2 * count :]
 
         @pl.when(pl.program_id(0) == 0)
         def _():
             rel_out[...] = jnp.zeros_like(rel_out)
-
-        dst_rows = dot_nn(table[...], select_rows(dst[...], rows))
-        grad_out[...] = pos[...] * dst_rows
-        for k in range(count):
-            first = CORES * (chip_ref[0] ^ k)
-            total = quota_ref[0, first]
-            for c in range(1, CORES):
-                total = total + quota_ref[0, first + c]
-            for pairs in range(1, slots // 2 + 1):
-
-                @pl.when((total + 1) // 2 == pairs)
-                def _(k=k, pairs=pairs):
-                    columns = [neg_refs[k][j] for j in range(2 * pairs)]
-                    columns = jnp.concatenate(columns, axis=1)
-                    grad_out[...] += dot_nn(columns, coef_refs[k][: pairs * wide])
-
-        kinds = select_rows(rel[...], rel_count)
-        upper, lower = split2(back(grad_out[...], rows_in[...]))
-        rel_out[...] += dot_nt(kinds, upper) + dot_nt(kinds, lower)
-
-    smem = pl.BlockSpec(memory_space=pltpu.SMEM)
+            for k in range(count):
+                for j in range(slots):
+                    all_neg[k, :, j * BLOCK : (j + 1) * BLOCK] = neg_refs[k][j]
+
+        found = None
+        for h in range(chunk // sub):
+            part = slice(h * sub, (h + 1) * sub)
+            grad = pos[:, part] * dot_nn(table[...], select_rows(dst[:, part], rows))
+            for k in range(count):
+                grad = grad + dot_nn(all_neg[k], coef_refs[k][:, part])
+            grad_out[:, part] = grad
+            kinds = select_rows(rel[:, part], rel_count)
+            upper, lower = split2(back(grad, rows_in[:, part]))
+            more = dot_nt(kinds, upper) + dot_nt(kinds, lower)
+            found = more if found is None else found + more
+        rel_out[...] += found
+
     return pl.pallas_call(
         body,
         name="combine",
         grid=(edges // chunk,),
-        in_specs=[smem, smem, smem, lanes(dim, chunk), lanes(1, chunk)]
+        in_specs=[lanes(dim, chunk), lanes(1, chunk)]
         + [whole((dim, rows)), lanes(1, chunk), lanes(1, chunk)]
         + [whole(negatives[0].shape)] * count
         + [lanes(slots * BLOCK, chunk)] * count,
@@ -311,12 +313,10 @@
             pltpu.HBM((dim, edges), f32),
             jax.ShapeDtypeStruct((rel_count, dim), f32),
         ],
-        compiler_params=params(44),
+        scratch_shapes=[pltpu.VMEM((count, dim, slots * BLOCK), bf16)],
+        compiler_params=params(48),
         cost_estimate=cost(2 * dim * NNEG * edges, 12 * dim * edges + 2 * NNEG * edges),
     )(
-        chip,
-        lane,
-        quota,
         in_hbm(src_rows),
         in_hbm(rel_ids),
         part_high,
@@ -330,6 +330,7 @@
 def source_side(src_table, src_state, rel_parts, src_ids, rel_ids, query_grad, rel_count, chunk):
     dim, rows = src_table.shape
     edges = src_ids.shape[1]
+    sub = min(SUB, chunk)
 
     def body(table, state, parts, src, rel, grad_in, out, state_out, acc):
         step = pl.program_id(0)
@@ -338,9 +339,15 @@
         def _():
             acc[...] = jnp.zeros_like(acc)
 
-        pick = select_rows(src[...], rows)
-        term = back(grad_in[...], relation_rows(parts[...], rel[...], rel_count))
-        acc[...] += dot_nt(term.astype(bf16), pick)
+        found = None
+        for h in range(chunk // sub):
+            part = slice(h * sub, (h + 1) * sub)
+            pick = select_rows(src[:, part], rows)
+            rel_rows = relation_rows(parts[...], rel[:, part], rel_count)
+            term = back(grad_in[:, part], rel_rows).astype(bf16)
+            more = dot_nt(term, pick)
+            found = more if found is None else found + more
+        acc[...] += found
 
         @pl.when(step == pl.num_programs(0) - 1)
         def _():
@@ -650,9 +657,6 @@
         pos_coef,
         negatives,
         coefs,
-        chip,
-        lane,
-        quotas,
         rel_count,
         chunk,
     )

time: 162 us -> 159 us (0.981)
  Pallas kernels: 85.4 us -> 82.4 us
  transfers between devices with their start and end apart: 27 -> 27, of which waited for: 7 -> 7; matrix products, arithmetic and copies ran while one was open for 1% -> 1% of each run, Pallas kernels for 46% -> 45%
where the time goes in v8:
time: 159 us; the launch traced here: 156 us
  Pallas kernels  82.4 us (52%)
  starting transfers between devices  41.4 us (26%)
  waiting for transfers between devices  29.2 us (18%)
  other arithmetic  1.84 us (1%)
    pallas_call x4, Pallas kernels, negative_wave(): pl.pallas_call(body, grid=(edges // chunk,), in_specs=[smem, smem, smem]...  33.8 us
    ppermute x3, starting transfers between devices, shards(): total = lax.ppermute(total.astype(bf16), 'edge', pairs)  16.1 us
    pallas_call x1, Pallas kernels, combine(): pl.pallas_call(body, name='combine', grid=(edges // chunk,), in_specs=[la...  15.9 us
    ppermute x3, waiting for transfers between devices, shards(): table = lax.ppermute(table, 'edge', hop)  13.7 us
    pallas_call x2, Pallas kernels, make_queries(): pl.pallas_call(body, name='make_queries', grid=(steps,), in_specs=[whole(...  12.4 us
    ppermute x7, starting transfers between devices, total_of_peers(): lax.ppermute(value, axis, [(i, peer(i, k)) for i in range(count)])  10.7 us
    ppermute x6, starting transfers between devices, shifted(): lax.ppermute(array, 'dom', [(d, moved(d, n, stride, shift)) for d in rang...  8.74 us
    ppermute x7, waiting for transfers between devices, total_of_peers(): lax.ppermute(value, axis, [(i, peer(i, k)) for i in range(count)])  7.46 us
  transfers between devices with their start and end apart: 27, of which 7 were waited for; matrix products, arithmetic and copies ran while one was open for 1% of the time, Pallas kernels for 45%

profile of v8, /device:TPU:0, one launch (start us, length us, event | category | flops | bytes accessed | tf_op | source)
XLA Modules:
  0.0 156.4 jit_solution(18361882123965863516)
XLA Ops:
  1.9 3.0 %collective-permute-start = (bf16[400,256]{1,0:T(8,128)(2,1)S(1)}, bf16[400,256]{1,0:T(8,128)(2,1)S(1)}, u32[]{:S(2)}, u32[]{:S(2)}) collective-permute-start(bf16[400,256]{1,0:T(8,128)(2,1)S(1)} %get-tuple-element.48.refs_0_), channel_id=1, source_target_pairs={{0,8},{8,0},{16,24},{24,16},{1,9},{9,1},{17,25},{25,17},{2,10},{10... | collective-permute-start | bytes 614408 | tf_op jit(solution)/shard_map/ppermute | solution.py:472
  7.4 2.6 %collective-permute-done.refs_1_ = bf16[400,256]{1,0:T(8,128)(2,1)S(1)} collective-permute-done((bf16[400,256]{1,0:T(8,128)(2,1)S(1)}, bf16[400,256]{1,0:T(8,128)(2,1)S(1)}, u32[]{:S(2)}, u32[]{:S(2)}) %collective-permute-start) | collective-permute-done | bytes 204832 | tf_op jit(solution)/shard_map/ppermute | solution.py:472
  12.8 1.6 %collective-permute-start.2 = (bf16[400,256]{1,0:T(8,128)(2,1)S(1)}, bf16[400,256]{1,0:T(8,128)(2,1)S(1)}, u32[]{:S(2)}, u32[]{:S(2)}) collective-permute-start(bf16[400,256]{1,0:T(8,128)(2,1)S(1)} %get-tuple-element.50), channel_id=1, source_target_pairs={{0,16},{8,24},{16,0},{24,8},{1,17},{9,25},{17,1},{25,9},{2,18},{10... | collective-permute-start | bytes 614408 | tf_op jit(solution)/shard_map/ppermute | solution.py:472
  14.9 6.2 %make_queries.2 = (f32[400,4096]{1,0:T(8,128)}, bf16[400,4096]{1,0:T(8,128)(2,1)}, f32[400,4096]{1,0:T(8,128)}) custom-call(f32[400,512]{1,0:T(8,128)} %table.5, bf16[400,128]{1,0:T(8,128)(2,1)S(1)} %pad.4.parts_ref.parts, s32[1,4096]{1,0:T(1,128)} %bitcast.17, s32[1,4096]{1,0:T(1,128)} %bitcast.11), custom_call_target="tpu_custom_call" | custom-call | flops 1677721600 | bytes 8192000 | tf_op jit(solution)/shard_map/make_queries/pallas_call | solution.py:116
  21.2 6.2 %make_queries.3 = (f32[400,4096]{1,0:T(8,128)}, bf16[400,4096]{1,0:T(8,128)(2,1)}, f32[400,4096]{1,0:T(8,128)}) custom-call(f32[400,512]{1,0:T(8,128)} %table.5, bf16[400,128]{1,0:T(8,128)(2,1)S(1)} %pad.4.parts_ref.parts, s32[1,4096]{1,0:T(1,128)} %bitcast.18, s32[1,4096]{1,0:T(1,128)} %bitcast.12, ...), custom_call_target="tpu_custom_call", output_to_operand_aliasing={{0}: (4, {}), {1}: (5, {}), {2}: (6, {})} | custom-call | flops 1677721600 | bytes 8192000 | tf_op jit(solution)/shard_map/make_queries/pallas_call | solution.py:116
  28.0 6.7 %positives.1 = (f32[1,4096]{1,0:T(1,128)}, f32[400,512]{1,0:T(8,128)S(1)}) custom-call(bf16[400,512]{1,0:T(8,128)(2,1)S(1)} %shard_map.147.table.refs_0_, f32[400,4096]{1,0:T(8,128)} %get-tuple-element.53.query_in, s32[1,4096]{1,0:T(1,128)} %bitcast.15), custom_call_target="tpu_custom_call" | custom-call | flops 5033164800 | bytes 13107200 | tf_op jit(solution)/shard_map/positives/pallas_call | solution.py:148
  34.7 2.6 %collective-permute-start.7 = (bf16[400,512]{1,0:T(8,128)(2,1)S(1)}, bf16[400,512]{1,0:T(8,128)(2,1)S(1)}, u32[]{:S(2)}, u32[]{:S(2)}) collective-permute-start(bf16[400,512]{1,0:T(8,128)(2,1)S(1)} %shard_map.147.table.refs_0_), channel_id=1, source_target_pairs={{0,4},{1,5},{2,6},{3,7},{4,0},{5,1},{6,2},{7,3},{8,12},{9,13},{10,... | collective-permute-start | bytes 1228808 | tf_op jit(solution)/shard_map/ppermute | solution.py:639
  37.3 1.6 %collective-permute-start.5 = (bf16[400,512]{1,0:T(8,128)(2,1)S(1)}, bf16[400,512]{1,0:T(8,128)(2,1)S(1)}, u32[]{:S(2)}, u32[]{:S(2)}) collective-permute-start(bf16[400,512]{1,0:T(8,128)(2,1)S(1)} %shard_map.147.table.refs_0_), channel_id=1, source_target_pairs={{0,2},{1,3},{2,0},{3,1},{4,6},{5,7},{6,4},{7,5},{8,10},{9,11},{10,... | collective-permute-start | bytes 1228808 | tf_op jit(solution)/shard_map/ppermute | solution.py:639
  40.3 13.7 %collective-permute-done.7.refs_0_ = bf16[400,512]{1,0:T(8,128)(2,1)S(1)} collective-permute-done((bf16[400,512]{1,0:T(8,128)(2,1)S(1)}, bf16[400,512]{1,0:T(8,128)(2,1)S(1)}, u32[]{:S(2)}, u32[]{:S(2)}) %collective-permute-start.7) | collective-permute-done | bytes 409632 | tf_op jit(solution)/shard_map/ppermute | solution.py:639
  54.9 9.0 %shard_map.148 = (bf16[4,400,128]{2,1,0:T(8,128)(2,1)S(1)}, bf16[512,4096]{1,0:T(8,128)(2,1)}, bf16[400,512]{1,0:T(8,128)(2,1)S(1)}, bf16[400,512]{1,0:T(8,128)(2,1)S(1)}) custom-call(s32[1]{0:T(128)S(6)} %select_n.12.chip_ref, s32[1]{0:T(128)S(6)} %select_n.13.lane_ref, s32[1,8]{1,0:T(1,128)S(1)} %copy-done.2, ...), custom_call_target="tpu_custom_call" | custom-call | flops 3774873600 | bytes 16384000 | tf_op jit(solution)/shard_map/pallas_call | solution.py:248
  65.6 9.0 %shard_map.150 = (bf16[4,400,128]{2,1,0:T(8,128)(2,1)S(1)}, bf16[512,4096]{1,0:T(8,128)(2,1)}, bf16[400,512]{1,0:T(8,128)(2,1)S(1)}, bf16[400,512]{1,0:T(8,128)(2,1)S(1)}) custom-call(s32[1]{0:T(128)S(6)} %xor.10.chip_ref, s32[1]{0:T(128)S(6)} %select_n.13.lane_ref, s32[1,8]{1,0:T(1,128)S(1)} %copy-done.2, ...), custom_call_target="tpu_custom_call" | custom-call | flops 3774873600 | bytes 16384000 | tf_op jit(solution)/shard_map/pallas_call | solution.py:248
  75.1 8.9 %shard_map.149 = (bf16[4,400,128]{2,1,0:T(8,128)(2,1)S(1)}, bf16[512,4096]{1,0:T(8,128)(2,1)}, bf16[400,512]{1,0:T(8,128)(2,1)S(1)}, bf16[400,512]{1,0:T(8,128)(2,1)S(1)}) custom-call(s32[1]{0:T(128)S(6)} %xor.9.chip_ref, s32[1]{0:T(128)S(6)} %select_n.13.lane_ref, s32[1,8]{1,0:T(1,128)S(1)} %copy-done.2, ...), custom_call_target="tpu_custom_call" | custom-call | flops 3774873600 | bytes 16384000 | tf_op jit(solution)/shard_map/pallas_call | solution.py:248
  85.0 6.9 %shard_map.151 = (bf16[4,400,128]{2,1,0:T(8,128)(2,1)S(1)}, bf16[512,4096]{1,0:T(8,128)(2,1)}, bf16[400,512]{1,0:T(8,128)(2,1)S(1)}, bf16[400,512]{1,0:T(8,128)(2,1)S(1)}) custom-call(s32[1]{0:T(128)S(6)} %xor.11.chip_ref, s32[1]{0:T(128)S(6)} %select_n.13.lane_ref, s32[1,8]{1,0:T(1,128)S(1)} %copy-done.2, ...), custom_call_target="tpu_custom_call" | custom-call | flops 3774873600 | bytes 16384000 | tf_op jit(solution)/shard_map/pallas_call | solution.py:248
  91.9 15.9 %combine.1 = (f32[400,4096]{1,0:T(8,128)}, f32[16,400]{1,0:T(8,128)S(1)}) custom-call(f32[400,4096]{1,0:T(8,128)} %get-tuple-element.46.rows_in, s32[1,4096]{1,0:T(1,128)} %bitcast.13, bf16[400,512]{1,0:T(8,128)(2,1)S(1)} %shard_map.147.table.refs_0_, s32[1,4096]{1,0:T(1,128)} %bitcast.16, f32[1,4096]{1,0:T(1,128)} %get-tuple-element.54.pos, ...), custom_call_target="tpu_custom_call" | custom-call | flops 5033164800 | bytes 32243712 | tf_op jit(solution)/shard_map/combine/pallas_call | solution.py:303
  107.8 2.5 %collective-permute-start.20 = (f32[16,400]{1,0:T(8,128)S(1)}, f32[16,400]{1,0:T(8,128)S(1)}, u32[]{:S(2)}, u32[]{:S(2)}) collective-permute-start(f32[16,400]{1,0:T(8,128)S(1)} %get-tuple-element.80), channel_id=1, source_target_pairs={{0,1},{1,0},{2,3},{3,2},{4,5},{5,4},{6,7},{7,6},{8,9},{9,8},{10,11... | collective-permute-start | bytes 76808 | tf_op jit(solution)/shard_map/ppermute | solution.py:564
  110.4 3.1 %collective-permute-start.17 = (bf16[400,512]{1,0:T(8,128)(2,1)S(1)}, bf16[400,512]{1,0:T(8,128)(2,1)S(1)}, u32[]{:S(2)}, u32[]{:S(2)}) collective-permute-start(bf16[400,512]{1,0:T(8,128)(2,1)S(1)} %add_convert_fusion.1), channel_id=1, source_target_pairs={{0,4},{1,5},{2,6},{3,7},{4,0},{5,1},{6,2},{7,3},{8,12},{9,13},{10,... | collective-permute-start | bytes 1228808 | tf_op jit(solution)/shard_map/ppermute | solution.py:646
  115.5 2.6 %collective-permute-start.21 = (f32[16,400]{1,0:T(8,128)S(1)}, f32[16,400]{1,0:T(8,128)S(1)}, u32[]{:S(2)}, u32[]{:S(2)}) collective-permute-start(f32[16,400]{1,0:T(8,128)S(1)} %add.47), channel_id=1, source_target_pairs={{0,2},{1,3},{2,0},{3,1},{4,6},{5,7},{6,4},{7,5},{8,10},{9,11},{10,... | collective-permute-start | bytes 76808 | tf_op jit(solution)/shard_map/ppermute | solution.py:564
  118.1 6.3 %collective-permute-done.23 = f32[16,400]{1,0:T(8,128)S(1)} collective-permute-done((f32[16,400]{1,0:T(8,128)S(1)}, f32[16,400]{1,0:T(8,128)S(1)}, u32[]{:S(2)}, u32[]{:S(2)}) %collective-permute-start.23) | collective-permute-done | bytes 25632 | tf_op jit(solution)/shard_map/ppermute | solution.py:564
  124.4 10.1 %collective-permute-start.15 = (bf16[400,512]{1,0:T(8,128)(2,1)S(1)}, bf16[400,512]{1,0:T(8,128)(2,1)S(1)}, u32[]{:S(2)}, u32[]{:S(2)}) collective-permute-start(bf16[400,512]{1,0:T(8,128)(2,1)S(1)} %add_convert_fusion.2), channel_id=1, source_target_pairs={{0,2},{1,3},{2,0},{3,1},{4,6},{5,7},{6,4},{7,5},{8,10},{9,11},{10,... | collective-permute-start | bytes 1228808 | tf_op jit(solution)/shard_map/ppermute | solution.py:646
  135.7 2.4 %collective-permute-start.25 = (f32[16,400]{1,0:T(8,128)S(1)}, f32[16,400]{1,0:T(8,128)S(1)}, u32[]{:S(2)}, u32[]{:S(2)}) collective-permute-start(f32[16,400]{1,0:T(8,128)S(1)} %add_add_fusion), channel_id=1, source_target_pairs={{0,16},{8,24},{16,0},{24,8},{1,17},{9,25},{17,1},{25,9},{2,18},{10... | collective-permute-start | bytes 76808 | tf_op jit(solution)/shard_map/ppermute | solution.py:564
  139.5 2.9 %collective-permute-start.19 = (bf16[400,512]{1,0:T(8,128)(2,1)S(1)}, bf16[400,512]{1,0:T(8,128)(2,1)S(1)}, u32[]{:S(2)}, u32[]{:S(2)}) collective-permute-start(bf16[400,512]{1,0:T(8,128)(2,1)S(1)} %add_convert_fusion), channel_id=1, source_target_pairs={{0,6},{1,7},{2,4},{3,5},{4,2},{5,3},{6,0},{7,1},{8,14},{9,15},{10,... | collective-permute-start | bytes 1228808 | tf_op jit(solution)/shard_map/ppermute | solution.py:646
  142.3 7.2 %source_side.1 = (f32[400,512]{1,0:T(8,128)}, f32[1,512]{1,0:T(1,128)}) custom-call(f32[400,512]{1,0:T(8,128)} %table.5, f32[1,512]{1,0:T(1,128)} %bitcast.21, bf16[400,128]{1,0:T(8,128)(2,1)S(1)} %pad.4.parts_ref.parts, s32[1,4096]{1,0:T(1,128)} %bitcast.19, s32[1,4096]{1,0:T(1,128)} %bitcast.14, f32[400,4096]{1,0:T(8,128)} %get-tuple-element.66.grad_in), custom_call_target="tpu_custom_call" | custom-call | flops 3355443200 | bytes 6553600 | tf_op jit(solution)/shard_map/source_side/pallas_call | solution.py:359
  150.2 3.9 %collective-permute-done.19.refs_6_ = bf16[400,512]{1,0:T(8,128)(2,1)S(1)} collective-permute-done((bf16[400,512]{1,0:T(8,128)(2,1)S(1)}, bf16[400,512]{1,0:T(8,128)(2,1)S(1)}, u32[]{:S(2)}, u32[]{:S(2)}) %collective-permute-start.19) | collective-permute-done | bytes 409632 | tf_op jit(solution)/shard_map/ppermute | solution.py:646
  154.2 2.3 %destination_side.1 = (f32[400,512]{1,0:T(8,128)}, f32[1,512]{1,0:T(1,128)}) custom-call(bf16[400,512]{1,0:T(8,128)(2,1)S(1)} %shard_map.147.table.refs_0_, bf16[416,512]{1,0:T(8,128)(2,1)S(1)} %shard_map.153.refs_1_, f32[400,512]{1,0:T(8,128)S(1)} %get-tuple-element.58.refs_2_, f32[400,512]{1,0:T(8,128)S(1)} %convert_add_fusion.refs_3_, ...), custom_call_target="tpu_custom_call" | custom-call | flops 1638400 | bytes 4096000 | tf_op jit(solution)/shard_map/destination_side/pallas_call | solution.py:409
  (67 shorter events, 18.5 us)
Async XLA Ops:
  1.9 8.1 %collective-permute-start = (bf16[400,256]{1,0:T(8,128)(2,1)S(1)}, bf16[400,256]{1,0:T(8,128)(2,1)S(1)}, u32[]{:S(2)}, u32[]{:S(2)}) collective-permute-start(bf16[400,256]{1,0:T(8,128)(2,1)S(1)} %get-tuple-element.48.refs_0_), channel_id=1, source_target_pairs={{0,8},{8,0},{16,24},{24,16},{1,9},{9,1},{17,25},{25,17},{2,10},{10... | collective-permute-start | bytes 614408 | tf_op jit(solution)/shard_map/ppermute | solution.py:472
  12.8 14.6 %collective-permute-start.2 = (bf16[400,256]{1,0:T(8,128)(2,1)S(1)}, bf16[400,256]{1,0:T(8,128)(2,1)S(1)}, u32[]{:S(2)}, u32[]{:S(2)}) collective-permute-start(bf16[400,256]{1,0:T(8,128)(2,1)S(1)} %get-tuple-element.50), channel_id=1, source_target_pairs={{0,16},{8,24},{16,0},{24,8},{1,17},{9,25},{17,1},{25,9},{2,18},{10... | collective-permute-start | bytes 614408 | tf_op jit(solution)/shard_map/ppermute | solution.py:472
  14.4 13.0 %collective-permute-start.3 = (bf16[400,256]{1,0:T(8,128)(2,1)S(1)}, bf16[400,256]{1,0:T(8,128)(2,1)S(1)}, u32[]{:S(2)}, u32[]{:S(2)}) collective-permute-start(bf16[400,256]{1,0:T(8,128)(2,1)S(1)} %get-tuple-element.51), channel_id=1, source_target_pairs={{0,8},{8,0},{16,24},{24,16},{1,9},{9,1},{17,25},{25,17},{2,10},{10... | collective-permute-start | bytes 614408 | tf_op jit(solution)/shard_map/ppermute | solution.py:472
  34.7 19.3 %collective-permute-start.7 = (bf16[400,512]{1,0:T(8,128)(2,1)S(1)}, bf16[400,512]{1,0:T(8,128)(2,1)S(1)}, u32[]{:S(2)}, u32[]{:S(2)}) collective-permute-start(bf16[400,512]{1,0:T(8,128)(2,1)S(1)} %shard_map.147.table.refs_0_), channel_id=1, source_target_pairs={{0,4},{1,5},{2,6},{3,7},{4,0},{5,1},{6,2},{7,3},{8,12},{9,13},{10,... | collective-permute-start | bytes 1228808 | tf_op jit(solution)/shard_map/ppermute | solution.py:639
  37.3 17.4 %collective-permute-start.5 = (bf16[400,512]{1,0:T(8,128)(2,1)S(1)}, bf16[400,512]{1,0:T(8,128)(2,1)S(1)}, u32[]{:S(2)}, u32[]{:S(2)}) collective-permute-start(bf16[400,512]{1,0:T(8,128)(2,1)S(1)} %shard_map.147.table.refs_0_), channel_id=1, source_target_pairs={{0,2},{1,3},{2,0},{3,1},{4,6},{5,7},{6,4},{7,5},{8,10},{9,11},{10,... | collective-permute-start | bytes 1228808 | tf_op jit(solution)/shard_map/ppermute | solution.py:639
  38.8 16.0 %collective-permute-start.4 = (bf16[400,512]{1,0:T(8,128)(2,1)S(1)}, bf16[400,512]{1,0:T(8,128)(2,1)}, u32[]{:S(2)}, u32[]{:S(2)}) collective-permute-start(bf16[400,512]{1,0:T(8,128)(2,1)S(1)} %shard_map.147.table.refs_0_), channel_id=1, source_target_pairs={{0,1},{1,0},{2,3},{3,2},{4,5},{5,4},{6,7},{7,6},{8,9},{9,8},{10,11... | collective-permute-start | bytes 1228808 | tf_op jit(solution)/shard_map/ppermute | solution.py:625
  38.8 25.4 %collective-permute-start.11 = (bf16[416,512]{1,0:T(8,128)(2,1)S(1)}, bf16[416,512]{1,0:T(8,128)(2,1)S(1)}, u32[]{:S(2)}, u32[]{:S(2)}) collective-permute-start(bf16[416,512]{1,0:T(8,128)(2,1)S(1)} %get-tuple-element.69.refs_0_), channel_id=1, source_target_pairs={{0,8},{8,0},{16,24},{24,16},{1,9},{9,1},{17,25},{25,17},{2,10},{10... | collective-permute-start | bytes 1277960 | tf_op jit(solution)/shard_map/ppermute | solution.py:472
  54.0 11.6 %collective-permute-start.8 = (bf16[400,512]{1,0:T(8,128)(2,1)S(1)}, bf16[400,512]{1,0:T(8,128)(2,1)S(1)}, u32[]{:S(2)}, u32[]{:S(2)}) collective-permute-start(bf16[400,512]{1,0:T(8,128)(2,1)S(1)} %collective-permute-done.7.refs_0_), channel_id=1, source_target_pairs={{0,1},{1,0},{2,3},{3,2},{4,5},{5,4},{6,7},{7,6},{8,9},{9,8},{10,11... | collective-permute-start | bytes 1228808 | tf_op jit(solution)/shard_map/ppermute | solution.py:625
  54.0 20.5 %collective-permute-start.9 = (bf16[400,512]{1,0:T(8,128)(2,1)S(1)}, bf16[400,512]{1,0:T(8,128)(2,1)S(1)}, u32[]{:S(2)}, u32[]{:S(2)}) collective-permute-start(bf16[400,512]{1,0:T(8,128)(2,1)S(1)} %collective-permute-done.7.refs_0_), channel_id=1, source_target_pairs={{0,2},{1,3},{2,0},{3,1},{4,6},{5,7},{6,4},{7,5},{8,10},{9,11},{10,... | collective-permute-start | bytes 1228808 | tf_op jit(solution)/shard_map/ppermute | solution.py:639
  54.7 20.4 %collective-permute-start.6 = (bf16[400,512]{1,0:T(8,128)(2,1)S(1)}, bf16[400,512]{1,0:T(8,128)(2,1)S(1)}, u32[]{:S(2)}, u32[]{:S(2)}) collective-permute-start(bf16[400,512]{1,0:T(8,128)(2,1)S(1)} %collective-permute-done.5.refs_0_), channel_id=1, source_target_pairs={{0,1},{1,0},{2,3},{3,2},{4,5},{5,4},{6,7},{7,6},{8,9},{9,8},{10,11... | collective-permute-start | bytes 1228808 | tf_op jit(solution)/shard_map/ppermute | solution.py:625
  63.9 20.1 %collective-permute-start.13 = (bf16[400,512]{1,0:T(8,128)(2,1)S(1)}, bf16[400,512]{1,0:T(8,128)(2,1)S(1)}, u32[]{:S(2)}, u32[]{:S(2)}) collective-permute-start(bf16[400,512]{1,0:T(8,128)(2,1)S(1)} %get-tuple-element.71), channel_id=1, source_target_pairs={{0,1},{1,0},{2,3},{3,2},{4,5},{5,4},{6,7},{7,6},{8,9},{9,8},{10,11... | collective-permute-start | bytes 1228808 | tf_op jit(solution)/shard_map/ppermute | solution.py:625
  65.0 19.1 %collective-permute-start.12 = (bf16[416,512]{1,0:T(8,128)(2,1)S(1)}, bf16[416,512]{1,0:T(8,128)(2,1)S(1)}, u32[]{:S(2)}, u32[]{:S(2)}) collective-permute-start(bf16[416,512]{1,0:T(8,128)(2,1)S(1)} %shard_map.152), channel_id=1, source_target_pairs={{0,16},{8,24},{16,0},{24,8},{1,17},{9,25},{17,1},{25,9},{2,18},{10... | collective-permute-start | bytes 1277960 | tf_op jit(solution)/shard_map/ppermute | solution.py:472
  74.6 35.7 %collective-permute-start.16 = (bf16[400,512]{1,0:T(8,128)(2,1)S(1)}, bf16[400,512]{1,0:T(8,128)(2,1)S(1)}, u32[]{:S(2)}, u32[]{:S(2)}) collective-permute-start(bf16[400,512]{1,0:T(8,128)(2,1)S(1)} %get-tuple-element.75), channel_id=1, source_target_pairs={{0,1},{1,0},{2,3},{3,2},{4,5},{5,4},{6,7},{7,6},{8,9},{9,8},{10,11... | collective-permute-start | bytes 1228808 | tf_op jit(solution)/shard_map/ppermute | solution.py:625
  74.6 10.4 %collective-permute-start.10 = (bf16[400,512]{1,0:T(8,128)(2,1)S(1)}, bf16[400,512]{1,0:T(8,128)(2,1)S(1)}, u32[]{:S(2)}, u32[]{:S(2)}) collective-permute-start(bf16[400,512]{1,0:T(8,128)(2,1)S(1)} %collective-permute-done.9.refs_0_), channel_id=1, source_target_pairs={{0,1},{1,0},{2,3},{3,2},{4,5},{5,4},{6,7},{7,6},{8,9},{9,8},{10,11... | collective-permute-start | bytes 1228808 | tf_op jit(solution)/shard_map/ppermute | solution.py:625
  84.0 31.5 %collective-permute-start.14 = (bf16[400,512]{1,0:T(8,128)(2,1)S(1)}, bf16[400,512]{1,0:T(8,128)(2,1)S(1)}, u32[]{:S(2)}, u32[]{:S(2)}) collective-permute-start(bf16[400,512]{1,0:T(8,128)(2,1)S(1)} %get-tuple-element.73), channel_id=1, source_target_pairs={{0,1},{1,0},{2,3},{3,2},{4,5},{5,4},{6,7},{7,6},{8,9},{9,8},{10,11... | collective-permute-start | bytes 1228808 | tf_op jit(solution)/shard_map/ppermute | solution.py:625
  110.4 39.8 %collective-permute-start.17 = (bf16[400,512]{1,0:T(8,128)(2,1)S(1)}, bf16[400,512]{1,0:T(8,128)(2,1)S(1)}, u32[]{:S(2)}, u32[]{:S(2)}) collective-permute-start(bf16[400,512]{1,0:T(8,128)(2,1)S(1)} %add_convert_fusion.1), channel_id=1, source_target_pairs={{0,4},{1,5},{2,6},{3,7},{4,0},{5,1},{6,2},{7,3},{8,12},{9,13},{10,... | collective-permute-start | bytes 1228808 | tf_op jit(solution)/shard_map/ppermute | solution.py:646
  113.5 24.6 %collective-permute-start.18 = (bf16[400,512]{1,0:T(8,128)(2,1)S(1)}, bf16[400,512]{1,0:T(8,128)(2,1)S(1)}, u32[]{:S(2)}, u32[]{:S(2)}) collective-permute-start(bf16[400,512]{1,0:T(8,128)(2,1)S(1)} %get-tuple-element.77), channel_id=1, source_target_pairs={{0,1},{1,0},{2,3},{3,2},{4,5},{5,4},{6,7},{7,6},{8,9},{9,8},{10,11... | collective-permute-start | bytes 1228808 | tf_op jit(solution)/shard_map/ppermute | solution.py:625
  113.6 10.8 %collective-permute-start.23 = (f32[16,400]{1,0:T(8,128)S(1)}, f32[16,400]{1,0:T(8,128)S(1)}, u32[]{:S(2)}, u32[]{:S(2)}) collective-permute-start(f32[16,400]{1,0:T(8,128)S(1)} %add.47), channel_id=1, source_target_pairs={{0,6},{1,7},{2,4},{3,5},{4,2},{5,3},{6,0},{7,1},{8,14},{9,15},{10,... | collective-permute-start | bytes 76808 | tf_op jit(solution)/shard_map/ppermute | solution.py:564
  114.0 20.5 %collective-permute-start.22 = (f32[16,400]{1,0:T(8,128)S(1)}, f32[16,400]{1,0:T(8,128)S(1)}, u32[]{:S(2)}, u32[]{:S(2)}) collective-permute-start(f32[16,400]{1,0:T(8,128)S(1)} %add.47), channel_id=1, source_target_pairs={{0,4},{1,5},{2,6},{3,7},{4,0},{5,1},{6,2},{7,3},{8,12},{9,13},{10,... | collective-permute-start | bytes 76808 | tf_op jit(solution)/shard_map/ppermute | solution.py:564
  115.5 19.1 %collective-permute-start.21 = (f32[16,400]{1,0:T(8,128)S(1)}, f32[16,400]{1,0:T(8,128)S(1)}, u32[]{:S(2)}, u32[]{:S(2)}) collective-permute-start(f32[16,400]{1,0:T(8,128)S(1)} %add.47), channel_id=1, source_target_pairs={{0,2},{1,3},{2,0},{3,1},{4,6},{5,7},{6,4},{7,5},{8,10},{9,11},{10,... | collective-permute-start | bytes 76808 | tf_op jit(solution)/shard_map/ppermute | solution.py:564
  124.4 25.8 %collective-permute-start.15 = (bf16[400,512]{1,0:T(8,128)(2,1)S(1)}, bf16[400,512]{1,0:T(8,128)(2,1)S(1)}, u32[]{:S(2)}, u32[]{:S(2)}) collective-permute-start(bf16[400,512]{1,0:T(8,128)(2,1)S(1)} %add_convert_fusion.2), channel_id=1, source_target_pairs={{0,2},{1,3},{2,0},{3,1},{4,6},{5,7},{6,4},{7,5},{8,10},{9,11},{10,... | collective-permute-start | bytes 1228808 | tf_op jit(solution)/shard_map/ppermute | solution.py:646
  135.7 13.8 %collective-permute-start.25 = (f32[16,400]{1,0:T(8,128)S(1)}, f32[16,400]{1,0:T(8,128)S(1)}, u32[]{:S(2)}, u32[]{:S(2)}) collective-permute-start(f32[16,400]{1,0:T(8,128)S(1)} %add_add_fusion), channel_id=1, source_target_pairs={{0,16},{8,24},{16,0},{24,8},{1,17},{9,25},{17,1},{25,9},{2,18},{10... | collective-permute-start | bytes 76808 | tf_op jit(solution)/shard_map/ppermute | solution.py:564
  138.2 11.4 %collective-permute-start.24 = (f32[16,400]{1,0:T(8,128)S(1)}, f32[16,400]{1,0:T(8,128)S(1)}, u32[]{:S(2)}, u32[]{:S(2)}) collective-permute-start(f32[16,400]{1,0:T(8,128)S(1)} %add_add_fusion), channel_id=1, source_target_pairs={{0,8},{8,0},{16,24},{24,16},{1,9},{9,1},{17,25},{25,17},{2,10},{10... | collective-permute-start | bytes 76808 | tf_op jit(solution)/shard_map/ppermute | solution.py:564
  139.5 14.7 %collective-permute-start.19 = (bf16[400,512]{1,0:T(8,128)(2,1)S(1)}, bf16[400,512]{1,0:T(8,128)(2,1)S(1)}, u32[]{:S(2)}, u32[]{:S(2)}) collective-permute-start(bf16[400,512]{1,0:T(8,128)(2,1)S(1)} %add_convert_fusion), channel_id=1, source_target_pairs={{0,6},{1,7},{2,4},{3,5},{4,2},{5,3},{6,0},{7,1},{8,14},{9,15},{10,... | collective-permute-start | bytes 1228808 | tf_op jit(solution)/shard_map/ppermute | solution.py:646
  (8 other events, 84.2 us)

commit v9 on v8

--- a/solution.py
+++ b/solution.py
@@ -386,15 +386,23 @@
     )
 
 
-def destination_side(high, low_state, own_grad, grads):
+def destination_side(high, low_options, low_order, matching, place, own_grad, grads):
     dim, rows = own_grad.shape
     count = len(grads)
-
-    def body(*refs):
-        high_ref, low_ref, own_ref = refs[:3]
-        out, state_out = refs[3 + count :]
+    options = len(low_options)
+    (n1, stride1), (n2, stride2) = low_order
+
+    def body(match_ref, here_ref, *refs):
+        high_ref, own_ref = refs[:2]
+        low_refs = refs[2 : 2 + options]
+        out, state_out, low_ref = refs[2 + options + count :]
+        source = match_ref[here_ref[0]]
+        near = behind(here_ref[0], source, n1, stride1)
+        far = behind(here_ref[0], source, n2, stride2)
+        index = jnp.where(far == 0, near, n1 - 1 + far)
+        copy_chosen(index, low_refs, low_ref, slice(None))
         total = own_ref[...]
-        for ref in refs[3 : 3 + count]:
+        for ref in refs[2 + options : 2 + options + count]:
             total = total + ref[...].astype(f32)
         packed = low_ref[...].astype(f32)
         state = packed[dim : dim + 1] + packed[dim + 1 : dim + 2] + packed[dim + 2 : dim + 3]
@@ -405,20 +413,22 @@
 
     width = min(rows, 128)
 
-    operands = [high, low_state, own_grad, *grads]
+    operands = [high, own_grad, *low_options, *grads]
+    smem = pl.BlockSpec(memory_space=pltpu.SMEM)
     return pl.pallas_call(
         body,
         name="destination_side",
         grid=(rows // width,),
-        in_specs=[lanes(array.shape[0], width) for array in operands],
+        in_specs=[smem, smem] + [lanes(array.shape[0], width) for array in operands],
         out_specs=[lanes(dim, width), lanes(1, width)],
+        scratch_shapes=[pltpu.VMEM((low_options[0].shape[0], width), bf16)],
         out_shape=[
             jax.ShapeDtypeStruct((dim, rows), f32),
             jax.ShapeDtypeStruct((1, rows), f32),
         ],
         compiler_params=params(16),
         cost_estimate=cost(8 * dim * rows, (12 + 2 * count) * dim * rows),
-    )(*operands)
+    )(matching, place, *operands)
 
 
 def split_table(table, state):
@@ -472,6 +482,10 @@
     return lax.ppermute(array, "dom", [(d, moved(d, n, stride, shift)) for d in range(count)])
 
 
+def behind(place, source, n, stride):
+    return ((place // stride) % n - (source // stride) % n + n) % n
+
+
 def copy_chosen(index, options, out, columns):
     for k in range(len(options)):
 
@@ -480,7 +494,7 @@
             out[:, columns] = options[k][...]
 
 
-def route(values, matching, here):
+def route(values, matching, here, join=True):
     down, across = grid_of(lax.axis_size("dom"))
     axes = [(across, 1), (down, across)]
     orders = [axes, axes[::-1]][: len(values)]
@@ -501,9 +515,6 @@
             result.append(refs[used : used + len(group)])
             used += len(group)
         return result, refs[used:]
-
-    def behind(place, source, n, stride):
-        return ((place // stride) % n - (source // stride) % n + n) % n
 
     def pass_on(match_ref, here_ref, *refs):
         place = here_ref[0]
@@ -529,6 +540,9 @@
     for (i, m), array in zip(hops, passed):
         found[i].append(shifted(array, *orders[i][1], m))
     flat_found = [array for group in found for array in group]
+
+    if not join:
+        return [*held[0], *found[0]], orders[0]
 
     def merge(match_ref, here_ref, *refs):
         place = here_ref[0]
@@ -609,7 +623,7 @@
     left, right, rest = split_table(dst_table, dst_state.reshape(1, row_count))
     part_high = route([left, right], matching, place)
     rest, part_high = lax.optimization_barrier((rest, part_high))
-    low_state = route([rest], matching, place)
+    low_options, low_order = route([rest], matching, place, join=False)
 
     made = []
     for part in range(2):
@@ -671,7 +685,9 @@
         chunk,
     )
     relation_out = relation - REL_RATE * total_over_mesh(rel_grad).T
-    dst_out, dst_state_out = destination_side(part_high, low_state, own_grad, arrived)
+    dst_out, dst_state_out = destination_side(
+        part_high, low_options, low_order, matching, place, own_grad, arrived
+    )
     return (
         src_out,
         src_state_out.reshape(row_count),

time: 159 us -> 155 us (0.975)
  the two profiles are of different devices: /device:TPU:0 before, /device:TPU:21 now
where the time goes in v9:
time: 155 us
  Pallas kernels  79.9 us (52%)
  waiting for transfers between devices  43.3 us (28%)
  starting transfers between devices  28.2 us (18%)
  other arithmetic  1.84 us (1%)
    pallas_call x4, Pallas kernels, negative_wave(): pl.pallas_call(body, grid=(edges // chunk,), in_specs=[smem, smem, smem]...  31.5 us
    ppermute x3, waiting for transfers between devices, shards(): total = lax.ppermute(total.astype(bf16), 'edge', pairs)  22.7 us
    pallas_call x1, Pallas kernels, combine(): pl.pallas_call(body, name='combine', grid=(edges // chunk,), in_specs=[la...  15.9 us
    pallas_call x2, Pallas kernels, make_queries(): pl.pallas_call(body, name='make_queries', grid=(steps,), in_specs=[whole(...  12.4 us
    ppermute x3, waiting for transfers between devices, shards(): table = lax.ppermute(table, 'edge', hop)  11.7 us
    ppermute x8, starting transfers between devices, swapped(): return lax.ppermute(array, 'edge', swap)  10.8 us
    pallas_call x1, Pallas kernels, source_side(): pl.pallas_call(body, name='source_side', grid=(edges // chunk,), in_specs...  7.25 us
    pallas_call x1, Pallas kernels, positives(): pl.pallas_call(body, name='positives', grid=(edges // chunk,), in_specs=[...  6.65 us
  transfers between devices with their start and end apart: 27, of which 9 were waited for; matrix products, arithmetic and copies ran while one was open for 1% of the time, Pallas kernels for 44%

profile of v9, /device:TPU:21, one launch (start us, length us, event | category | flops | bytes accessed | tf_op | source)
XLA Modules:
  0.0 154.9 jit_solution(4073281622394223990)
XLA Ops:
  0.6 1.3 split_table.1
  4.4 3.6 %collective-permute-done.refs_1_ = bf16[400,256]{1,0:T(8,128)(2,1)S(1)} collective-permute-done((bf16[400,256]{1,0:T(8,128)(2,1)S(1)}, bf16[400,256]{1,0:T(8,128)(2,1)S(1)}, u32[]{:S(2)}, u32[]{:S(2)}) %collective-permute-start) | collective-permute-done | bytes 204832 | tf_op jit(solution)/shard_map/ppermute | solution.py:482
  10.8 6.2 %make_queries.2 = (f32[400,4096]{1,0:T(8,128)}, bf16[400,4096]{1,0:T(8,128)(2,1)}, f32[400,4096]{1,0:T(8,128)}) custom-call(f32[400,512]{1,0:T(8,128)} %table.5, bf16[400,128]{1,0:T(8,128)(2,1)S(1)} %pad.4.parts_ref.parts, s32[1,4096]{1,0:T(1,128)} %bitcast.17, s32[1,4096]{1,0:T(1,128)} %bitcast.11), custom_call_target="tpu_custom_call" | custom-call | flops 1677721600 | bytes 8192000 | tf_op jit(solution)/shard_map/make_queries/pallas_call | solution.py:116
  17.0 6.2 %make_queries.3 = (f32[400,4096]{1,0:T(8,128)}, bf16[400,4096]{1,0:T(8,128)(2,1)}, f32[400,4096]{1,0:T(8,128)}) custom-call(f32[400,512]{1,0:T(8,128)} %table.5, bf16[400,128]{1,0:T(8,128)(2,1)S(1)} %pad.4.parts_ref.parts, s32[1,4096]{1,0:T(1,128)} %bitcast.18, s32[1,4096]{1,0:T(1,128)} %bitcast.12, ...), custom_call_target="tpu_custom_call", output_to_operand_aliasing={{0}: (4, {}), {1}: (5, {}), {2}: (6, {})} | custom-call | flops 1677721600 | bytes 8192000 | tf_op jit(solution)/shard_map/make_queries/pallas_call | solution.py:116
  23.9 6.7 %positives.1 = (f32[1,4096]{1,0:T(1,128)}, f32[400,512]{1,0:T(8,128)S(1)}) custom-call(bf16[400,512]{1,0:T(8,128)(2,1)S(1)} %shard_map.147.table.refs_0_, f32[400,4096]{1,0:T(8,128)} %get-tuple-element.53.query_in, s32[1,4096]{1,0:T(1,128)} %bitcast.15), custom_call_target="tpu_custom_call" | custom-call | flops 5033164800 | bytes 13107200 | tf_op jit(solution)/shard_map/positives/pallas_call | solution.py:148
  31.9 2.9 %collective-permute-start.4 = (bf16[400,512]{1,0:T(8,128)(2,1)S(1)}, bf16[400,512]{1,0:T(8,128)(2,1)}, u32[]{:S(2)}, u32[]{:S(2)}) collective-permute-start(bf16[400,512]{1,0:T(8,128)(2,1)S(1)} %shard_map.147.table.refs_0_), channel_id=1, source_target_pairs={{0,1},{1,0},{2,3},{3,2},{4,5},{5,4},{6,7},{7,6},{8,9},{9,8},{10,11... | collective-permute-start | bytes 1228808 | tf_op jit(solution)/shard_map/ppermute | solution.py:639
  36.0 11.7 %collective-permute-done.7.refs_0_ = bf16[400,512]{1,0:T(8,128)(2,1)S(1)} collective-permute-done((bf16[400,512]{1,0:T(8,128)(2,1)S(1)}, bf16[400,512]{1,0:T(8,128)(2,1)S(1)}, u32[]{:S(2)}, u32[]{:S(2)}) %collective-permute-start.7) | collective-permute-done | bytes 409632 | tf_op jit(solution)/shard_map/ppermute | solution.py:653
  47.7 1.4 collective-permute-start.8
  49.2 4.2 %collective-permute-start.9 = (bf16[400,512]{1,0:T(8,128)(2,1)S(1)}, bf16[400,512]{1,0:T(8,128)(2,1)S(1)}, u32[]{:S(2)}, u32[]{:S(2)}) collective-permute-start(bf16[400,512]{1,0:T(8,128)(2,1)S(1)} %collective-permute-done.7.refs_0_), channel_id=1, source_target_pairs={{0,2},{1,3},{2,0},{3,1},{4,6},{5,7},{6,4},{7,5},{8,10},{9,11},{10,... | collective-permute-start | bytes 1228808 | tf_op jit(solution)/shard_map/ppermute | solution.py:653
  53.6 7.0 %shard_map.148 = (bf16[4,400,128]{2,1,0:T(8,128)(2,1)S(1)}, bf16[512,4096]{1,0:T(8,128)(2,1)}, bf16[400,512]{1,0:T(8,128)(2,1)S(1)}, bf16[400,512]{1,0:T(8,128)(2,1)S(1)}) custom-call(s32[1]{0:T(128)S(6)} %select_n.12.chip_ref, s32[1]{0:T(128)S(6)} %select_n.13.lane_ref, s32[1,8]{1,0:T(1,128)S(1)} %copy-done.2, ...), custom_call_target="tpu_custom_call" | custom-call | flops 3774873600 | bytes 16384000 | tf_op jit(solution)/shard_map/pallas_call | solution.py:248
  60.6 2.3 %collective-permute-start.13 = (bf16[400,512]{1,0:T(8,128)(2,1)S(1)}, bf16[400,512]{1,0:T(8,128)(2,1)S(1)}, u32[]{:S(2)}, u32[]{:S(2)}) collective-permute-start(bf16[400,512]{1,0:T(8,128)(2,1)S(1)} %get-tuple-element.71), channel_id=1, source_target_pairs={{0,1},{1,0},{2,3},{3,2},{4,5},{5,4},{6,7},{7,6},{8,9},{9,8},{10,11... | collective-permute-start | bytes 1228808 | tf_op jit(solution)/shard_map/ppermute | solution.py:639
  64.8 9.0 %shard_map.150 = (bf16[4,400,128]{2,1,0:T(8,128)(2,1)S(1)}, bf16[512,4096]{1,0:T(8,128)(2,1)}, bf16[400,512]{1,0:T(8,128)(2,1)S(1)}, bf16[400,512]{1,0:T(8,128)(2,1)S(1)}) custom-call(s32[1]{0:T(128)S(6)} %xor.10.chip_ref, s32[1]{0:T(128)S(6)} %select_n.13.lane_ref, s32[1,8]{1,0:T(1,128)S(1)} %copy-done.2, ...), custom_call_target="tpu_custom_call" | custom-call | flops 3774873600 | bytes 16384000 | tf_op jit(solution)/shard_map/pallas_call | solution.py:248
  74.6 9.0 %shard_map.149 = (bf16[4,400,128]{2,1,0:T(8,128)(2,1)S(1)}, bf16[512,4096]{1,0:T(8,128)(2,1)}, bf16[400,512]{1,0:T(8,128)(2,1)S(1)}, bf16[400,512]{1,0:T(8,128)(2,1)S(1)}) custom-call(s32[1]{0:T(128)S(6)} %xor.9.chip_ref, s32[1]{0:T(128)S(6)} %select_n.13.lane_ref, s32[1,8]{1,0:T(1,128)S(1)} %copy-done.2, ...), custom_call_target="tpu_custom_call" | custom-call | flops 3774873600 | bytes 16384000 | tf_op jit(solution)/shard_map/pallas_call | solution.py:248
  83.7 6.6 %shard_map.151 = (bf16[4,400,128]{2,1,0:T(8,128)(2,1)S(1)}, bf16[512,4096]{1,0:T(8,128)(2,1)}, bf16[400,512]{1,0:T(8,128)(2,1)S(1)}, bf16[400,512]{1,0:T(8,128)(2,1)S(1)}) custom-call(s32[1]{0:T(128)S(6)} %xor.11.chip_ref, s32[1]{0:T(128)S(6)} %select_n.13.lane_ref, s32[1,8]{1,0:T(1,128)S(1)} %copy-done.2, ...), custom_call_target="tpu_custom_call" | custom-call | flops 3774873600 | bytes 16384000 | tf_op jit(solution)/shard_map/pallas_call | solution.py:248
  90.3 3.1 %collective-permute-start.18 = (bf16[400,512]{1,0:T(8,128)(2,1)S(1)}, bf16[400,512]{1,0:T(8,128)(2,1)S(1)}, u32[]{:S(2)}, u32[]{:S(2)}) collective-permute-start(bf16[400,512]{1,0:T(8,128)(2,1)S(1)} %get-tuple-element.77), channel_id=1, source_target_pairs={{0,1},{1,0},{2,3},{3,2},{4,5},{5,4},{6,7},{7,6},{8,9},{9,8},{10,11... | collective-permute-start | bytes 1228808 | tf_op jit(solution)/shard_map/ppermute | solution.py:639
  93.4 15.9 %combine.1 = (f32[400,4096]{1,0:T(8,128)}, f32[16,400]{1,0:T(8,128)S(1)}) custom-call(f32[400,4096]{1,0:T(8,128)} %get-tuple-element.46.rows_in, s32[1,4096]{1,0:T(1,128)} %bitcast.13, bf16[400,512]{1,0:T(8,128)(2,1)S(1)} %shard_map.147.table.refs_0_, s32[1,4096]{1,0:T(1,128)} %bitcast.16, f32[1,4096]{1,0:T(1,128)} %get-tuple-element.54.pos, ...), custom_call_target="tpu_custom_call" | custom-call | flops 5033164800 | bytes 32243712 | tf_op jit(solution)/shard_map/combine/pallas_call | solution.py:303
  110.5 1.7 %collective-permute-start.22 = (f32[16,400]{1,0:T(8,128)S(1)}, f32[16,400]{1,0:T(8,128)S(1)}, u32[]{:S(2)}, u32[]{:S(2)}) collective-permute-start(f32[16,400]{1,0:T(8,128)S(1)} %add.47), channel_id=1, source_target_pairs={{0,4},{1,5},{2,6},{3,7},{4,0},{5,1},{6,2},{7,3},{8,12},{9,13},{10,... | collective-permute-start | bytes 76808 | tf_op jit(solution)/shard_map/ppermute | solution.py:578
  114.5 2.0 %collective-permute-start.15 = (bf16[400,512]{1,0:T(8,128)(2,1)S(1)}, bf16[400,512]{1,0:T(8,128)(2,1)S(1)}, u32[]{:S(2)}, u32[]{:S(2)}) collective-permute-start(bf16[400,512]{1,0:T(8,128)(2,1)S(1)} %add_convert_fusion.2), channel_id=1, source_target_pairs={{0,2},{1,3},{2,0},{3,1},{4,6},{5,7},{6,4},{7,5},{8,10},{9,11},{10,... | collective-permute-start | bytes 1228808 | tf_op jit(solution)/shard_map/ppermute | solution.py:660
  117.7 2.9 %collective-permute-done.26 = f32[16,400]{1,0:T(8,128)S(1)} collective-permute-done((f32[16,400]{1,0:T(8,128)S(1)}, f32[16,400]{1,0:T(8,128)S(1)}, u32[]{:S(2)}, u32[]{:S(2)}) %collective-permute-start.26) | collective-permute-done | bytes 25632 | tf_op jit(solution)/shard_map/ppermute | solution.py:578
  121.4 7.2 %source_side.1 = (f32[400,512]{1,0:T(8,128)}, f32[1,512]{1,0:T(1,128)}) custom-call(f32[400,512]{1,0:T(8,128)} %table.5, f32[1,512]{1,0:T(1,128)} %bitcast.21, bf16[400,128]{1,0:T(8,128)(2,1)S(1)} %pad.4.parts_ref.parts, s32[1,4096]{1,0:T(1,128)} %bitcast.19, s32[1,4096]{1,0:T(1,128)} %bitcast.14, f32[400,4096]{1,0:T(8,128)} %get-tuple-element.66.grad_in), custom_call_target="tpu_custom_call" | custom-call | flops 3355443200 | bytes 6553600 | tf_op jit(solution)/shard_map/source_side/pallas_call | solution.py:359
  129.3 1.5 collective-permute-done.17.refs_7_
  130.8 2.5 %collective-permute-done.15.refs_6_ = bf16[400,512]{1,0:T(8,128)(2,1)S(1)} collective-permute-done((bf16[400,512]{1,0:T(8,128)(2,1)S(1)}, bf16[400,512]{1,0:T(8,128)(2,1)S(1)}, u32[]{:S(2)}, u32[]{:S(2)}) %collective-permute-start.15) | collective-permute-done | bytes 409632 | tf_op jit(solution)/shard_map/ppermute | solution.py:660
  133.4 18.6 %collective-permute-done.19.refs_8_ = bf16[400,512]{1,0:T(8,128)(2,1)S(1)} collective-permute-done((bf16[400,512]{1,0:T(8,128)(2,1)S(1)}, bf16[400,512]{1,0:T(8,128)(2,1)S(1)}, u32[]{:S(2)}, u32[]{:S(2)}) %collective-permute-start.19) | collective-permute-done | bytes 409632 | tf_op jit(solution)/shard_map/ppermute | solution.py:660
  152.0 2.9 %destination_side.1 = (f32[400,512]{1,0:T(8,128)}, f32[1,512]{1,0:T(1,128)}) custom-call(s32[4]{0:T(128)S(1)} %copy-done.1, s32[1]{0:T(128)} %bitcast.4.here_ref, bf16[400,512]{1,0:T(8,128)(2,1)S(1)} %shard_map.147.table.refs_0_, f32[400,512]{1,0:T(8,128)S(1)} %get-tuple-element.58.refs_1_, bf16[416,512]{1,0:T(8,128)(2,1)S(1)} %get-tuple-element.69.refs_0_.refs_2_, ...), custom_call_target="tpu_custom_call" | custom-call | flops 1638400 | bytes 4096000 | tf_op jit(solution)/shard_map/destination_side/pallas_call | solution.py:418
  (66 shorter events, 17.7 us)
Async XLA Ops:
  1.9 6.0 %collective-permute-start = (bf16[400,256]{1,0:T(8,128)(2,1)S(1)}, bf16[400,256]{1,0:T(8,128)(2,1)S(1)}, u32[]{:S(2)}, u32[]{:S(2)}) collective-permute-start(bf16[400,256]{1,0:T(8,128)(2,1)S(1)} %get-tuple-element.48.refs_0_), channel_id=1, source_target_pairs={{0,8},{8,0},{16,24},{24,16},{1,9},{9,1},{17,25},{25,17},{2,10},{10... | collective-permute-start | bytes 614408 | tf_op jit(solution)/shard_map/ppermute | solution.py:482
  3.2 5.7 %collective-permute-start.1 = (bf16[400,256]{1,0:T(8,128)(2,1)S(1)}, bf16[400,256]{1,0:T(8,128)(2,1)S(1)}, u32[]{:S(2)}, u32[]{:S(2)}) collective-permute-start(bf16[400,256]{1,0:T(8,128)(2,1)S(1)} %get-tuple-element.49.refs_2_), channel_id=1, source_target_pairs={{0,16},{8,24},{16,0},{24,8},{1,17},{9,25},{17,1},{25,9},{2,18},{10... | collective-permute-start | bytes 614408 | tf_op jit(solution)/shard_map/ppermute | solution.py:482
  10.2 13.0 %collective-permute-start.2 = (bf16[400,256]{1,0:T(8,128)(2,1)S(1)}, bf16[400,256]{1,0:T(8,128)(2,1)S(1)}, u32[]{:S(2)}, u32[]{:S(2)}) collective-permute-start(bf16[400,256]{1,0:T(8,128)(2,1)S(1)} %get-tuple-element.50), channel_id=1, source_target_pairs={{0,16},{8,24},{16,0},{24,8},{1,17},{9,25},{17,1},{25,9},{2,18},{10... | collective-permute-start | bytes 614408 | tf_op jit(solution)/shard_map/ppermute | solution.py:482
  10.5 12.7 %collective-permute-start.3 = (bf16[400,256]{1,0:T(8,128)(2,1)S(1)}, bf16[400,256]{1,0:T(8,128)(2,1)S(1)}, u32[]{:S(2)}, u32[]{:S(2)}) collective-permute-start(bf16[400,256]{1,0:T(8,128)(2,1)S(1)} %get-tuple-element.51), channel_id=1, source_target_pairs={{0,8},{8,0},{16,24},{24,16},{1,9},{9,1},{17,25},{25,17},{2,10},{10... | collective-permute-start | bytes 614408 | tf_op jit(solution)/shard_map/ppermute | solution.py:482
  30.5 17.2 %collective-permute-start.7 = (bf16[400,512]{1,0:T(8,128)(2,1)S(1)}, bf16[400,512]{1,0:T(8,128)(2,1)S(1)}, u32[]{:S(2)}, u32[]{:S(2)}) collective-permute-start(bf16[400,512]{1,0:T(8,128)(2,1)S(1)} %shard_map.147.table.refs_0_), channel_id=1, source_target_pairs={{0,4},{1,5},{2,6},{3,7},{4,0},{5,1},{6,2},{7,3},{8,12},{9,13},{10,... | collective-permute-start | bytes 1228808 | tf_op jit(solution)/shard_map/ppermute | solution.py:653
  30.6 22.7 %collective-permute-start.5 = (bf16[400,512]{1,0:T(8,128)(2,1)S(1)}, bf16[400,512]{1,0:T(8,128)(2,1)S(1)}, u32[]{:S(2)}, u32[]{:S(2)}) collective-permute-start(bf16[400,512]{1,0:T(8,128)(2,1)S(1)} %shard_map.147.table.refs_0_), channel_id=1, source_target_pairs={{0,2},{1,3},{2,0},{3,1},{4,6},{5,7},{6,4},{7,5},{8,10},{9,11},{10,... | collective-permute-start | bytes 1228808 | tf_op jit(solution)/shard_map/ppermute | solution.py:653
  31.9 21.8 %collective-permute-start.4 = (bf16[400,512]{1,0:T(8,128)(2,1)S(1)}, bf16[400,512]{1,0:T(8,128)(2,1)}, u32[]{:S(2)}, u32[]{:S(2)}) collective-permute-start(bf16[400,512]{1,0:T(8,128)(2,1)S(1)} %shard_map.147.table.refs_0_), channel_id=1, source_target_pairs={{0,1},{1,0},{2,3},{3,2},{4,5},{5,4},{6,7},{7,6},{8,9},{9,8},{10,11... | collective-permute-start | bytes 1228808 | tf_op jit(solution)/shard_map/ppermute | solution.py:639
  34.8 28.1 %collective-permute-start.11 = (bf16[416,512]{1,0:T(8,128)(2,1)S(1)}, bf16[416,512]{1,0:T(8,128)(2,1)S(1)}, u32[]{:S(2)}, u32[]{:S(2)}) collective-permute-start(bf16[416,512]{1,0:T(8,128)(2,1)S(1)} %get-tuple-element.69.refs_0_.refs_2_), channel_id=1, source_target_pairs={{0,8},{8,0},{16,24},{24,16},{1,9},{9,1},{17,25},{25,17},{2,10},{10... | collective-permute-start | bytes 1277960 | tf_op jit(solution)/shard_map/ppermute | solution.py:482
  47.7 17.1 %collective-permute-start.8 = (bf16[400,512]{1,0:T(8,128)(2,1)S(1)}, bf16[400,512]{1,0:T(8,128)(2,1)S(1)}, u32[]{:S(2)}, u32[]{:S(2)}) collective-permute-start(bf16[400,512]{1,0:T(8,128)(2,1)S(1)} %collective-permute-done.7.refs_0_), channel_id=1, source_target_pairs={{0,1},{1,0},{2,3},{3,2},{4,5},{5,4},{6,7},{7,6},{8,9},{9,8},{10,11... | collective-permute-start | bytes 1228808 | tf_op jit(solution)/shard_map/ppermute | solution.py:639
  49.2 25.4 %collective-permute-start.9 = (bf16[400,512]{1,0:T(8,128)(2,1)S(1)}, bf16[400,512]{1,0:T(8,128)(2,1)S(1)}, u32[]{:S(2)}, u32[]{:S(2)}) collective-permute-start(bf16[400,512]{1,0:T(8,128)(2,1)S(1)} %collective-permute-done.7.refs_0_), channel_id=1, source_target_pairs={{0,2},{1,3},{2,0},{3,1},{4,6},{5,7},{6,4},{7,5},{8,10},{9,11},{10,... | collective-permute-start | bytes 1228808 | tf_op jit(solution)/shard_map/ppermute | solution.py:653
  53.3 21.3 %collective-permute-start.6 = (bf16[400,512]{1,0:T(8,128)(2,1)S(1)}, bf16[400,512]{1,0:T(8,128)(2,1)S(1)}, u32[]{:S(2)}, u32[]{:S(2)}) collective-permute-start(bf16[400,512]{1,0:T(8,128)(2,1)S(1)} %collective-permute-done.5.refs_0_), channel_id=1, source_target_pairs={{0,1},{1,0},{2,3},{3,2},{4,5},{5,4},{6,7},{7,6},{8,9},{9,8},{10,11... | collective-permute-start | bytes 1228808 | tf_op jit(solution)/shard_map/ppermute | solution.py:639
  60.6 23.0 %collective-permute-start.13 = (bf16[400,512]{1,0:T(8,128)(2,1)S(1)}, bf16[400,512]{1,0:T(8,128)(2,1)S(1)}, u32[]{:S(2)}, u32[]{:S(2)}) collective-permute-start(bf16[400,512]{1,0:T(8,128)(2,1)S(1)} %get-tuple-element.71), channel_id=1, source_target_pairs={{0,1},{1,0},{2,3},{3,2},{4,5},{5,4},{6,7},{7,6},{8,9},{9,8},{10,11... | collective-permute-start | bytes 1228808 | tf_op jit(solution)/shard_map/ppermute | solution.py:639
  63.7 65.7 %collective-permute-start.12 = (bf16[416,512]{1,0:T(8,128)(2,1)S(1)}, bf16[416,512]{1,0:T(8,128)(2,1)S(1)}, u32[]{:S(2)}, u32[]{:S(2)}) collective-permute-start(bf16[416,512]{1,0:T(8,128)(2,1)S(1)} %shard_map.152), channel_id=1, source_target_pairs={{0,16},{8,24},{16,0},{24,8},{1,17},{9,25},{17,1},{25,9},{2,18},{10... | collective-permute-start | bytes 1277960 | tf_op jit(solution)/shard_map/ppermute | solution.py:482
  73.8 35.5 %collective-permute-start.16 = (bf16[400,512]{1,0:T(8,128)(2,1)S(1)}, bf16[400,512]{1,0:T(8,128)(2,1)S(1)}, u32[]{:S(2)}, u32[]{:S(2)}) collective-permute-start(bf16[400,512]{1,0:T(8,128)(2,1)S(1)} %get-tuple-element.75), channel_id=1, source_target_pairs={{0,1},{1,0},{2,3},{3,2},{4,5},{5,4},{6,7},{7,6},{8,9},{9,8},{10,11... | collective-permute-start | bytes 1228808 | tf_op jit(solution)/shard_map/ppermute | solution.py:639
  74.6 9.2 %collective-permute-start.10 = (bf16[400,512]{1,0:T(8,128)(2,1)S(1)}, bf16[400,512]{1,0:T(8,128)(2,1)S(1)}, u32[]{:S(2)}, u32[]{:S(2)}) collective-permute-start(bf16[400,512]{1,0:T(8,128)(2,1)S(1)} %collective-permute-done.9.refs_0_), channel_id=1, source_target_pairs={{0,1},{1,0},{2,3},{3,2},{4,5},{5,4},{6,7},{7,6},{8,9},{9,8},{10,11... | collective-permute-start | bytes 1228808 | tf_op jit(solution)/shard_map/ppermute | solution.py:639
  83.6 28.7 %collective-permute-start.14 = (bf16[400,512]{1,0:T(8,128)(2,1)S(1)}, bf16[400,512]{1,0:T(8,128)(2,1)S(1)}, u32[]{:S(2)}, u32[]{:S(2)}) collective-permute-start(bf16[400,512]{1,0:T(8,128)(2,1)S(1)} %get-tuple-element.73), channel_id=1, source_target_pairs={{0,1},{1,0},{2,3},{3,2},{4,5},{5,4},{6,7},{7,6},{8,9},{9,8},{10,11... | collective-permute-start | bytes 1228808 | tf_op jit(solution)/shard_map/ppermute | solution.py:639
  90.3 26.5 %collective-permute-start.18 = (bf16[400,512]{1,0:T(8,128)(2,1)S(1)}, bf16[400,512]{1,0:T(8,128)(2,1)S(1)}, u32[]{:S(2)}, u32[]{:S(2)}) collective-permute-start(bf16[400,512]{1,0:T(8,128)(2,1)S(1)} %get-tuple-element.77), channel_id=1, source_target_pairs={{0,1},{1,0},{2,3},{3,2},{4,5},{5,4},{6,7},{7,6},{8,9},{9,8},{10,11... | collective-permute-start | bytes 1228808 | tf_op jit(solution)/shard_map/ppermute | solution.py:639
  110.5 4.0 %collective-permute-start.22 = (f32[16,400]{1,0:T(8,128)S(1)}, f32[16,400]{1,0:T(8,128)S(1)}, u32[]{:S(2)}, u32[]{:S(2)}) collective-permute-start(f32[16,400]{1,0:T(8,128)S(1)} %add.47), channel_id=1, source_target_pairs={{0,4},{1,5},{2,6},{3,7},{4,0},{5,1},{6,2},{7,3},{8,12},{9,13},{10,... | collective-permute-start | bytes 76808 | tf_op jit(solution)/shard_map/ppermute | solution.py:578
  112.2 4.3 %collective-permute-start.21 = (f32[16,400]{1,0:T(8,128)S(1)}, f32[16,400]{1,0:T(8,128)S(1)}, u32[]{:S(2)}, u32[]{:S(2)}) collective-permute-start(f32[16,400]{1,0:T(8,128)S(1)} %add.47), channel_id=1, source_target_pairs={{0,2},{1,3},{2,0},{3,1},{4,6},{5,7},{6,4},{7,5},{8,10},{9,11},{10,... | collective-permute-start | bytes 76808 | tf_op jit(solution)/shard_map/ppermute | solution.py:578
  113.3 17.6 %collective-permute-start.17 = (bf16[400,512]{1,0:T(8,128)(2,1)S(1)}, bf16[400,512]{1,0:T(8,128)(2,1)S(1)}, u32[]{:S(2)}, u32[]{:S(2)}) collective-permute-start(bf16[400,512]{1,0:T(8,128)(2,1)S(1)} %add_convert_fusion.1), channel_id=1, source_target_pairs={{0,4},{1,5},{2,6},{3,7},{4,0},{5,1},{6,2},{7,3},{8,12},{9,13},{10,... | collective-permute-start | bytes 1228808 | tf_op jit(solution)/shard_map/ppermute | solution.py:660
  114.5 18.9 %collective-permute-start.15 = (bf16[400,512]{1,0:T(8,128)(2,1)S(1)}, bf16[400,512]{1,0:T(8,128)(2,1)S(1)}, u32[]{:S(2)}, u32[]{:S(2)}) collective-permute-start(bf16[400,512]{1,0:T(8,128)(2,1)S(1)} %add_convert_fusion.2), channel_id=1, source_target_pairs={{0,2},{1,3},{2,0},{3,1},{4,6},{5,7},{6,4},{7,5},{8,10},{9,11},{10,... | collective-permute-start | bytes 1228808 | tf_op jit(solution)/shard_map/ppermute | solution.py:660
  116.5 4.0 %collective-permute-start.26 = (f32[16,400]{1,0:T(8,128)S(1)}, f32[16,400]{1,0:T(8,128)S(1)}, u32[]{:S(2)}, u32[]{:S(2)}) collective-permute-start(f32[16,400]{1,0:T(8,128)S(1)} %add_add_fusion), channel_id=1, source_target_pairs={{0,24},{8,16},{16,8},{24,0},{1,25},{9,17},{17,9},{25,1},{2,26},{10... | collective-permute-start | bytes 76808 | tf_op jit(solution)/shard_map/ppermute | solution.py:578
  120.6 8.1 %collective-permute-start.24 = (f32[16,400]{1,0:T(8,128)S(1)}, f32[16,400]{1,0:T(8,128)S(1)}, u32[]{:S(2)}, u32[]{:S(2)}) collective-permute-start(f32[16,400]{1,0:T(8,128)S(1)} %add_add_fusion), channel_id=1, source_target_pairs={{0,8},{8,0},{16,24},{24,16},{1,9},{9,1},{17,25},{25,17},{2,10},{10... | collective-permute-start | bytes 76808 | tf_op jit(solution)/shard_map/ppermute | solution.py:578
  120.6 31.4 %collective-permute-start.19 = (bf16[400,512]{1,0:T(8,128)(2,1)S(1)}, bf16[400,512]{1,0:T(8,128)(2,1)S(1)}, u32[]{:S(2)}, u32[]{:S(2)}) collective-permute-start(bf16[400,512]{1,0:T(8,128)(2,1)S(1)} %add_convert_fusion), channel_id=1, source_target_pairs={{0,6},{1,7},{2,4},{3,5},{4,2},{5,3},{6,0},{7,1},{8,14},{9,15},{10,... | collective-permute-start | bytes 1228808 | tf_op jit(solution)/shard_map/ppermute | solution.py:660
  (8 other events, 77.0 us)

commit v10 on v8

--- a/solution.py
+++ b/solution.py
@@ -293,7 +293,7 @@
             grad = pos[:, part] * dot_nn(table[...], select_rows(dst[:, part], rows))
             for k in range(count):
                 grad = grad + dot_nn(all_neg[k], coef_refs[k][:, part])
-            grad_out[:, part] = grad
+            grad_out[:, part] = grad.astype(bf16)
             kinds = select_rows(rel[:, part], rel_count)
             upper, lower = split2(back(grad, rows_in[:, part]))
             more = dot_nt(kinds, upper) + dot_nt(kinds, lower)
@@ -310,7 +310,7 @@
         + [lanes(slots * BLOCK, chunk)] * count,
         out_specs=[lanes(dim, chunk), whole((rel_count, dim))],
         out_shape=[
-            pltpu.HBM((dim, edges), f32),
+            pltpu.HBM((dim, edges), bf16),
             jax.ShapeDtypeStruct((rel_count, dim), f32),
         ],
         scratch_shapes=[pltpu.VMEM((count, dim, slots * BLOCK), bf16)],
@@ -344,7 +344,7 @@
             part = slice(h * sub, (h + 1) * sub)
             pick = select_rows(src[:, part], rows)
             rel_rows = relation_rows(parts[...], rel[:, part], rel_count)
-            term = back(grad_in[:, part], rel_rows).astype(bf16)
+            term = back(grad_in[:, part].astype(f32), rel_rows).astype(bf16)
             more = dot_nt(term, pick)
             found = more if found is None else found + more
         acc[...] += found

time: 159 us -> 158 us (level)
  the two profiles are of different devices: /device:TPU:0 before, /device:TPU:10 now
where the time goes in v10:
time: 158 us
  Pallas kernels  81.7 us (52%)
  waiting for transfers between devices  49.4 us (31%)
  starting transfers between devices  23.3 us (15%)
  other arithmetic  1.84 us (1%)
    pallas_call x4, Pallas kernels, negative_wave(): pl.pallas_call(body, grid=(edges // chunk,), in_specs=[smem, smem, smem]...  33.7 us
    ppermute x7, waiting for transfers between devices, total_of_peers(): lax.ppermute(value, axis, [(i, peer(i, k)) for i in range(count)])  19.4 us
    pallas_call x1, Pallas kernels, combine(): pl.pallas_call(body, name='combine', grid=(edges // chunk,), in_specs=[la...  15.6 us
    ppermute x3, waiting for transfers between devices, shards(): table = lax.ppermute(table, 'edge', hop)  14.7 us
    pallas_call x2, Pallas kernels, make_queries(): pl.pallas_call(body, name='make_queries', grid=(steps,), in_specs=[whole(...  12.4 us
    ppermute x3, waiting for transfers between devices, shards(): total = lax.ppermute(total.astype(bf16), 'edge', pairs)  11.2 us
    ppermute x7, starting transfers between devices, total_of_peers(): lax.ppermute(value, axis, [(i, peer(i, k)) for i in range(count)])  11.1 us
    pallas_call x1, Pallas kernels, source_side(): pl.pallas_call(body, name='source_side', grid=(edges // chunk,), in_specs...  6.95 us
  transfers between devices with their start and end apart: 27, of which 10 were waited for; matrix products, arithmetic and copies ran while one was open for 1% of the time, Pallas kernels for 44%

profile of v10, /device:TPU:10, one launch (start us, length us, event | category | flops | bytes accessed | tf_op | source)
XLA Modules:
  0.0 157.9 jit_solution(230982859300916846)
XLA Ops:
  2.5 1.5 collective-permute-start.1
  5.0 3.8 %collective-permute-done.refs_1_ = bf16[400,256]{1,0:T(8,128)(2,1)S(1)} collective-permute-done((bf16[400,256]{1,0:T(8,128)(2,1)S(1)}, bf16[400,256]{1,0:T(8,128)(2,1)S(1)}, u32[]{:S(2)}, u32[]{:S(2)}) %collective-permute-start) | collective-permute-done | bytes 204832 | tf_op jit(solution)/shard_map/ppermute | solution.py:472
  10.4 1.6 %collective-permute-start.2 = (bf16[400,256]{1,0:T(8,128)(2,1)S(1)}, bf16[400,256]{1,0:T(8,128)(2,1)S(1)}, u32[]{:S(2)}, u32[]{:S(2)}) collective-permute-start(bf16[400,256]{1,0:T(8,128)(2,1)S(1)} %get-tuple-element.50), channel_id=1, source_target_pairs={{0,16},{8,24},{16,0},{24,8},{1,17},{9,25},{17,1},{25,9},{2,18},{10... | collective-permute-start | bytes 614408 | tf_op jit(solution)/shard_map/ppermute | solution.py:472
  13.4 6.3 %make_queries.2 = (f32[400,4096]{1,0:T(8,128)}, bf16[400,4096]{1,0:T(8,128)(2,1)}, f32[400,4096]{1,0:T(8,128)}) custom-call(f32[400,512]{1,0:T(8,128)} %table.5, bf16[400,128]{1,0:T(8,128)(2,1)S(1)} %pad.4.parts_ref.parts, s32[1,4096]{1,0:T(1,128)} %bitcast.17, s32[1,4096]{1,0:T(1,128)} %bitcast.11), custom_call_target="tpu_custom_call" | custom-call | flops 1677721600 | bytes 8192000 | tf_op jit(solution)/shard_map/make_queries/pallas_call | solution.py:116
  19.7 6.2 %make_queries.3 = (f32[400,4096]{1,0:T(8,128)}, bf16[400,4096]{1,0:T(8,128)(2,1)}, f32[400,4096]{1,0:T(8,128)}) custom-call(f32[400,512]{1,0:T(8,128)} %table.5, bf16[400,128]{1,0:T(8,128)(2,1)S(1)} %pad.4.parts_ref.parts, s32[1,4096]{1,0:T(1,128)} %bitcast.18, s32[1,4096]{1,0:T(1,128)} %bitcast.12, ...), custom_call_target="tpu_custom_call", output_to_operand_aliasing={{0}: (4, {}), {1}: (5, {}), {2}: (6, {})} | custom-call | flops 1677721600 | bytes 8192000 | tf_op jit(solution)/shard_map/make_queries/pallas_call | solution.py:116
  26.5 6.7 %positives.1 = (f32[1,4096]{1,0:T(1,128)}, f32[400,512]{1,0:T(8,128)S(1)}) custom-call(bf16[400,512]{1,0:T(8,128)(2,1)S(1)} %shard_map.147.table.refs_0_, f32[400,4096]{1,0:T(8,128)} %get-tuple-element.53.query_in, s32[1,4096]{1,0:T(1,128)} %bitcast.15), custom_call_target="tpu_custom_call" | custom-call | flops 5033164800 | bytes 13107200 | tf_op jit(solution)/shard_map/positives/pallas_call | solution.py:148
  33.2 2.6 %collective-permute-start.7 = (bf16[400,512]{1,0:T(8,128)(2,1)S(1)}, bf16[400,512]{1,0:T(8,128)(2,1)S(1)}, u32[]{:S(2)}, u32[]{:S(2)}) collective-permute-start(bf16[400,512]{1,0:T(8,128)(2,1)S(1)} %shard_map.147.table.refs_0_), channel_id=1, source_target_pairs={{0,4},{1,5},{2,6},{3,7},{4,0},{5,1},{6,2},{7,3},{8,12},{9,13},{10,... | collective-permute-start | bytes 1228808 | tf_op jit(solution)/shard_map/ppermute | solution.py:639
  36.7 14.7 %collective-permute-done.7.refs_0_ = bf16[400,512]{1,0:T(8,128)(2,1)S(1)} collective-permute-done((bf16[400,512]{1,0:T(8,128)(2,1)S(1)}, bf16[400,512]{1,0:T(8,128)(2,1)S(1)}, u32[]{:S(2)}, u32[]{:S(2)}) %collective-permute-start.7) | collective-permute-done | bytes 409632 | tf_op jit(solution)/shard_map/ppermute | solution.py:639
  53.2 9.1 %shard_map.148 = (bf16[4,400,128]{2,1,0:T(8,128)(2,1)S(1)}, bf16[512,4096]{1,0:T(8,128)(2,1)}, bf16[400,512]{1,0:T(8,128)(2,1)S(1)}, bf16[400,512]{1,0:T(8,128)(2,1)S(1)}) custom-call(s32[1]{0:T(128)S(6)} %select_n.12.chip_ref, s32[1]{0:T(128)S(6)} %select_n.13.lane_ref, s32[1,8]{1,0:T(1,128)S(1)} %copy-done.2, ...), custom_call_target="tpu_custom_call" | custom-call | flops 3774873600 | bytes 16384000 | tf_op jit(solution)/shard_map/pallas_call | solution.py:248
  63.9 8.9 %shard_map.150 = (bf16[4,400,128]{2,1,0:T(8,128)(2,1)S(1)}, bf16[512,4096]{1,0:T(8,128)(2,1)}, bf16[400,512]{1,0:T(8,128)(2,1)S(1)}, bf16[400,512]{1,0:T(8,128)(2,1)S(1)}) custom-call(s32[1]{0:T(128)S(6)} %xor.10.chip_ref, s32[1]{0:T(128)S(6)} %select_n.13.lane_ref, s32[1,8]{1,0:T(1,128)S(1)} %copy-done.2, ...), custom_call_target="tpu_custom_call" | custom-call | flops 3774873600 | bytes 16384000 | tf_op jit(solution)/shard_map/pallas_call | solution.py:248
  73.4 8.8 %shard_map.149 = (bf16[4,400,128]{2,1,0:T(8,128)(2,1)S(1)}, bf16[512,4096]{1,0:T(8,128)(2,1)}, bf16[400,512]{1,0:T(8,128)(2,1)S(1)}, bf16[400,512]{1,0:T(8,128)(2,1)S(1)}) custom-call(s32[1]{0:T(128)S(6)} %xor.9.chip_ref, s32[1]{0:T(128)S(6)} %select_n.13.lane_ref, s32[1,8]{1,0:T(1,128)S(1)} %copy-done.2, ...), custom_call_target="tpu_custom_call" | custom-call | flops 3774873600 | bytes 16384000 | tf_op jit(solution)/shard_map/pallas_call | solution.py:248
  83.2 6.9 %shard_map.151 = (bf16[4,400,128]{2,1,0:T(8,128)(2,1)S(1)}, bf16[512,4096]{1,0:T(8,128)(2,1)}, bf16[400,512]{1,0:T(8,128)(2,1)S(1)}, bf16[400,512]{1,0:T(8,128)(2,1)S(1)}) custom-call(s32[1]{0:T(128)S(6)} %xor.11.chip_ref, s32[1]{0:T(128)S(6)} %select_n.13.lane_ref, s32[1,8]{1,0:T(1,128)S(1)} %copy-done.2, ...), custom_call_target="tpu_custom_call" | custom-call | flops 3774873600 | bytes 16384000 | tf_op jit(solution)/shard_map/pallas_call | solution.py:248
  90.1 15.6 %combine.1 = (bf16[400,4096]{1,0:T(8,128)(2,1)}, f32[16,400]{1,0:T(8,128)S(1)}) custom-call(f32[400,4096]{1,0:T(8,128)} %get-tuple-element.46.rows_in, s32[1,4096]{1,0:T(1,128)} %bitcast.13, bf16[400,512]{1,0:T(8,128)(2,1)S(1)} %shard_map.147.table.refs_0_, s32[1,4096]{1,0:T(1,128)} %bitcast.16, f32[1,4096]{1,0:T(1,128)} %get-tuple-element.54.pos, ...), custom_call_target="tpu_custom_call" | custom-call | flops 5033164800 | bytes 32243712 | tf_op jit(solution)/shard_map/combine/pallas_call | solution.py:303
  105.7 2.5 %collective-permute-start.20 = (f32[16,400]{1,0:T(8,128)S(1)}, f32[16,400]{1,0:T(8,128)S(1)}, u32[]{:S(2)}, u32[]{:S(2)}) collective-permute-start(f32[16,400]{1,0:T(8,128)S(1)} %get-tuple-element.80), channel_id=1, source_target_pairs={{0,1},{1,0},{2,3},{3,2},{4,5},{5,4},{6,7},{7,6},{8,9},{9,8},{10,11... | collective-permute-start | bytes 76808 | tf_op jit(solution)/shard_map/ppermute | solution.py:564
  109.1 3.5 %collective-permute-start.21 = (f32[16,400]{1,0:T(8,128)S(1)}, f32[16,400]{1,0:T(8,128)S(1)}, u32[]{:S(2)}, u32[]{:S(2)}) collective-permute-start(f32[16,400]{1,0:T(8,128)S(1)} %add.47), channel_id=1, source_target_pairs={{0,2},{1,3},{2,0},{3,1},{4,6},{5,7},{6,4},{7,5},{8,10},{9,11},{10,... | collective-permute-start | bytes 76808 | tf_op jit(solution)/shard_map/ppermute | solution.py:564
  114.2 9.3 %collective-permute-done.21 = f32[16,400]{1,0:T(8,128)S(1)} collective-permute-done((f32[16,400]{1,0:T(8,128)S(1)}, f32[16,400]{1,0:T(8,128)S(1)}, u32[]{:S(2)}, u32[]{:S(2)}) %collective-permute-start.21) | collective-permute-done | bytes 25632 | tf_op jit(solution)/shard_map/ppermute | solution.py:564
  123.5 5.8 %collective-permute-done.22 = f32[16,400]{1,0:T(8,128)S(1)} collective-permute-done((f32[16,400]{1,0:T(8,128)S(1)}, f32[16,400]{1,0:T(8,128)S(1)}, u32[]{:S(2)}, u32[]{:S(2)}) %collective-permute-start.22) | collective-permute-done | bytes 25632 | tf_op jit(solution)/shard_map/ppermute | solution.py:564
  129.3 3.4 %collective-permute-done.23 = f32[16,400]{1,0:T(8,128)S(1)} collective-permute-done((f32[16,400]{1,0:T(8,128)S(1)}, f32[16,400]{1,0:T(8,128)S(1)}, u32[]{:S(2)}, u32[]{:S(2)}) %collective-permute-start.23) | collective-permute-done | bytes 25632 | tf_op jit(solution)/shard_map/ppermute | solution.py:564
  132.8 1.7 %collective-permute-start.25 = (f32[16,400]{1,0:T(8,128)S(1)}, f32[16,400]{1,0:T(8,128)S(1)}, u32[]{:S(2)}, u32[]{:S(2)}) collective-permute-start(f32[16,400]{1,0:T(8,128)S(1)} %add_add_fusion), channel_id=1, source_target_pairs={{0,16},{8,24},{16,0},{24,8},{1,17},{9,25},{17,1},{25,9},{2,18},{10... | collective-permute-start | bytes 76808 | tf_op jit(solution)/shard_map/ppermute | solution.py:564
  134.6 1.7 %collective-permute-start.26 = (f32[16,400]{1,0:T(8,128)S(1)}, f32[16,400]{1,0:T(8,128)S(1)}, u32[]{:S(2)}, u32[]{:S(2)}) collective-permute-start(f32[16,400]{1,0:T(8,128)S(1)} %add_add_fusion), channel_id=1, source_target_pairs={{0,24},{8,16},{16,8},{24,0},{1,25},{9,17},{17,9},{25,1},{2,26},{10... | collective-permute-start | bytes 76808 | tf_op jit(solution)/shard_map/ppermute | solution.py:564
  136.8 7.0 %source_side.1 = (f32[400,512]{1,0:T(8,128)}, f32[1,512]{1,0:T(1,128)}) custom-call(f32[400,512]{1,0:T(8,128)} %table.5, f32[1,512]{1,0:T(1,128)} %bitcast.21, bf16[400,128]{1,0:T(8,128)(2,1)S(1)} %pad.4.parts_ref.parts, s32[1,4096]{1,0:T(1,128)} %bitcast.19, s32[1,4096]{1,0:T(1,128)} %bitcast.14, bf16[400,4096]{1,0:T(8,128)(2,1)} %get-tuple-element.66.grad_in), custom_call_target="tpu_custom_call" | custom-call | flops 3355443200 | bytes 6553600 | tf_op jit(solution)/shard_map/source_side/pallas_call | solution.py:359
  144.5 4.0 %collective-permute-done.15.refs_4_ = bf16[400,512]{1,0:T(8,128)(2,1)S(1)} collective-permute-done((bf16[400,512]{1,0:T(8,128)(2,1)S(1)}, bf16[400,512]{1,0:T(8,128)(2,1)S(1)}, u32[]{:S(2)}, u32[]{:S(2)}) %collective-permute-start.15) | collective-permute-done | bytes 409632 | tf_op jit(solution)/shard_map/ppermute | solution.py:646
  148.5 7.2 %collective-permute-done.19.refs_6_ = bf16[400,512]{1,0:T(8,128)(2,1)S(1)} collective-permute-done((bf16[400,512]{1,0:T(8,128)(2,1)S(1)}, bf16[400,512]{1,0:T(8,128)(2,1)S(1)}, u32[]{:S(2)}, u32[]{:S(2)}) %collective-permute-start.19) | collective-permute-done | bytes 409632 | tf_op jit(solution)/shard_map/ppermute | solution.py:646
  155.7 2.3 %destination_side.1 = (f32[400,512]{1,0:T(8,128)}, f32[1,512]{1,0:T(1,128)}) custom-call(bf16[400,512]{1,0:T(8,128)(2,1)S(1)} %shard_map.147.table.refs_0_, bf16[416,512]{1,0:T(8,128)(2,1)S(1)} %shard_map.153.refs_1_, f32[400,512]{1,0:T(8,128)S(1)} %get-tuple-element.58.refs_2_, f32[400,512]{1,0:T(8,128)S(1)} %convert_add_fusion.refs_3_, ...), custom_call_target="tpu_custom_call" | custom-call | flops 1638400 | bytes 4096000 | tf_op jit(solution)/shard_map/destination_side/pallas_call | solution.py:409
  (67 shorter events, 16.2 us)
Async XLA Ops:
  1.9 6.9 %collective-permute-start = (bf16[400,256]{1,0:T(8,128)(2,1)S(1)}, bf16[400,256]{1,0:T(8,128)(2,1)S(1)}, u32[]{:S(2)}, u32[]{:S(2)}) collective-permute-start(bf16[400,256]{1,0:T(8,128)(2,1)S(1)} %get-tuple-element.48.refs_0_), channel_id=1, source_target_pairs={{0,8},{8,0},{16,24},{24,16},{1,9},{9,1},{17,25},{25,17},{2,10},{10... | collective-permute-start | bytes 614408 | tf_op jit(solution)/shard_map/ppermute | solution.py:472
  10.4 15.5 %collective-permute-start.2 = (bf16[400,256]{1,0:T(8,128)(2,1)S(1)}, bf16[400,256]{1,0:T(8,128)(2,1)S(1)}, u32[]{:S(2)}, u32[]{:S(2)}) collective-permute-start(bf16[400,256]{1,0:T(8,128)(2,1)S(1)} %get-tuple-element.50), channel_id=1, source_target_pairs={{0,16},{8,24},{16,0},{24,8},{1,17},{9,25},{17,1},{25,9},{2,18},{10... | collective-permute-start | bytes 614408 | tf_op jit(solution)/shard_map/ppermute | solution.py:472
  11.9 13.9 %collective-permute-start.3 = (bf16[400,256]{1,0:T(8,128)(2,1)S(1)}, bf16[400,256]{1,0:T(8,128)(2,1)S(1)}, u32[]{:S(2)}, u32[]{:S(2)}) collective-permute-start(bf16[400,256]{1,0:T(8,128)(2,1)S(1)} %get-tuple-element.51), channel_id=1, source_target_pairs={{0,8},{8,0},{16,24},{24,16},{1,9},{9,1},{17,25},{25,17},{2,10},{10... | collective-permute-start | bytes 614408 | tf_op jit(solution)/shard_map/ppermute | solution.py:472
  33.2 18.3 %collective-permute-start.7 = (bf16[400,512]{1,0:T(8,128)(2,1)S(1)}, bf16[400,512]{1,0:T(8,128)(2,1)S(1)}, u32[]{:S(2)}, u32[]{:S(2)}) collective-permute-start(bf16[400,512]{1,0:T(8,128)(2,1)S(1)} %shard_map.147.table.refs_0_), channel_id=1, source_target_pairs={{0,4},{1,5},{2,6},{3,7},{4,0},{5,1},{6,2},{7,3},{8,12},{9,13},{10,... | collective-permute-start | bytes 1228808 | tf_op jit(solution)/shard_map/ppermute | solution.py:639
  35.8 17.2 %collective-permute-start.5 = (bf16[400,512]{1,0:T(8,128)(2,1)S(1)}, bf16[400,512]{1,0:T(8,128)(2,1)S(1)}, u32[]{:S(2)}, u32[]{:S(2)}) collective-permute-start(bf16[400,512]{1,0:T(8,128)(2,1)S(1)} %shard_map.147.table.refs_0_), channel_id=1, source_target_pairs={{0,2},{1,3},{2,0},{3,1},{4,6},{5,7},{6,4},{7,5},{8,10},{9,11},{10,... | collective-permute-start | bytes 1228808 | tf_op jit(solution)/shard_map/ppermute | solution.py:639
  36.2 17.0 %collective-permute-start.4 = (bf16[400,512]{1,0:T(8,128)(2,1)S(1)}, bf16[400,512]{1,0:T(8,128)(2,1)}, u32[]{:S(2)}, u32[]{:S(2)}) collective-permute-start(bf16[400,512]{1,0:T(8,128)(2,1)S(1)} %shard_map.147.table.refs_0_), channel_id=1, source_target_pairs={{0,1},{1,0},{2,3},{3,2},{4,5},{5,4},{6,7},{7,6},{8,9},{9,8},{10,11... | collective-permute-start | bytes 1228808 | tf_op jit(solution)/shard_map/ppermute | solution.py:625
  36.2 26.4 %collective-permute-start.11 = (bf16[416,512]{1,0:T(8,128)(2,1)S(1)}, bf16[416,512]{1,0:T(8,128)(2,1)S(1)}, u32[]{:S(2)}, u32[]{:S(2)}) collective-permute-start(bf16[416,512]{1,0:T(8,128)(2,1)S(1)} %get-tuple-element.69.refs_0_), channel_id=1, source_target_pairs={{0,8},{8,0},{16,24},{24,16},{1,9},{9,1},{17,25},{25,17},{2,10},{10... | collective-permute-start | bytes 1277960 | tf_op jit(solution)/shard_map/ppermute | solution.py:472
  51.5 12.5 %collective-permute-start.8 = (bf16[400,512]{1,0:T(8,128)(2,1)S(1)}, bf16[400,512]{1,0:T(8,128)(2,1)S(1)}, u32[]{:S(2)}, u32[]{:S(2)}) collective-permute-start(bf16[400,512]{1,0:T(8,128)(2,1)S(1)} %collective-permute-done.7.refs_0_), channel_id=1, source_target_pairs={{0,1},{1,0},{2,3},{3,2},{4,5},{5,4},{6,7},{7,6},{8,9},{9,8},{10,11... | collective-permute-start | bytes 1228808 | tf_op jit(solution)/shard_map/ppermute | solution.py:625
  51.5 21.4 %collective-permute-start.9 = (bf16[400,512]{1,0:T(8,128)(2,1)S(1)}, bf16[400,512]{1,0:T(8,128)(2,1)S(1)}, u32[]{:S(2)}, u32[]{:S(2)}) collective-permute-start(bf16[400,512]{1,0:T(8,128)(2,1)S(1)} %collective-permute-done.7.refs_0_), channel_id=1, source_target_pairs={{0,2},{1,3},{2,0},{3,1},{4,6},{5,7},{6,4},{7,5},{8,10},{9,11},{10,... | collective-permute-start | bytes 1228808 | tf_op jit(solution)/shard_map/ppermute | solution.py:639
  53.0 20.4 %collective-permute-start.6 = (bf16[400,512]{1,0:T(8,128)(2,1)S(1)}, bf16[400,512]{1,0:T(8,128)(2,1)S(1)}, u32[]{:S(2)}, u32[]{:S(2)}) collective-permute-start(bf16[400,512]{1,0:T(8,128)(2,1)S(1)} %collective-permute-done.5.refs_0_), channel_id=1, source_target_pairs={{0,1},{1,0},{2,3},{3,2},{4,5},{5,4},{6,7},{7,6},{8,9},{9,8},{10,11... | collective-permute-start | bytes 1228808 | tf_op jit(solution)/shard_map/ppermute | solution.py:625
  62.3 19.9 %collective-permute-start.13 = (bf16[400,512]{1,0:T(8,128)(2,1)S(1)}, bf16[400,512]{1,0:T(8,128)(2,1)S(1)}, u32[]{:S(2)}, u32[]{:S(2)}) collective-permute-start(bf16[400,512]{1,0:T(8,128)(2,1)S(1)} %get-tuple-element.71), channel_id=1, source_target_pairs={{0,1},{1,0},{2,3},{3,2},{4,5},{5,4},{6,7},{7,6},{8,9},{9,8},{10,11... | collective-permute-start | bytes 1228808 | tf_op jit(solution)/shard_map/ppermute | solution.py:625
  63.4 19.0 %collective-permute-start.12 = (bf16[416,512]{1,0:T(8,128)(2,1)S(1)}, bf16[416,512]{1,0:T(8,128)(2,1)S(1)}, u32[]{:S(2)}, u32[]{:S(2)}) collective-permute-start(bf16[416,512]{1,0:T(8,128)(2,1)S(1)} %shard_map.152), channel_id=1, source_target_pairs={{0,16},{8,24},{16,0},{24,8},{1,17},{9,25},{17,1},{25,9},{2,18},{10... | collective-permute-start | bytes 1277960 | tf_op jit(solution)/shard_map/ppermute | solution.py:472
  72.8 35.5 %collective-permute-start.16 = (bf16[400,512]{1,0:T(8,128)(2,1)S(1)}, bf16[400,512]{1,0:T(8,128)(2,1)S(1)}, u32[]{:S(2)}, u32[]{:S(2)}) collective-permute-start(bf16[400,512]{1,0:T(8,128)(2,1)S(1)} %get-tuple-element.75), channel_id=1, source_target_pairs={{0,1},{1,0},{2,3},{3,2},{4,5},{5,4},{6,7},{7,6},{8,9},{9,8},{10,11... | collective-permute-start | bytes 1228808 | tf_op jit(solution)/shard_map/ppermute | solution.py:625
  72.8 10.3 %collective-permute-start.10 = (bf16[400,512]{1,0:T(8,128)(2,1)S(1)}, bf16[400,512]{1,0:T(8,128)(2,1)S(1)}, u32[]{:S(2)}, u32[]{:S(2)}) collective-permute-start(bf16[400,512]{1,0:T(8,128)(2,1)S(1)} %collective-permute-done.9.refs_0_), channel_id=1, source_target_pairs={{0,1},{1,0},{2,3},{3,2},{4,5},{5,4},{6,7},{7,6},{8,9},{9,8},{10,11... | collective-permute-start | bytes 1228808 | tf_op jit(solution)/shard_map/ppermute | solution.py:625
  82.2 30.9 %collective-permute-start.14 = (bf16[400,512]{1,0:T(8,128)(2,1)S(1)}, bf16[400,512]{1,0:T(8,128)(2,1)S(1)}, u32[]{:S(2)}, u32[]{:S(2)}) collective-permute-start(bf16[400,512]{1,0:T(8,128)(2,1)S(1)} %get-tuple-element.73), channel_id=1, source_target_pairs={{0,1},{1,0},{2,3},{3,2},{4,5},{5,4},{6,7},{7,6},{8,9},{9,8},{10,11... | collective-permute-start | bytes 1228808 | tf_op jit(solution)/shard_map/ppermute | solution.py:625
  108.2 26.3 %collective-permute-start.18 = (bf16[400,512]{1,0:T(8,128)(2,1)S(1)}, bf16[400,512]{1,0:T(8,128)(2,1)S(1)}, u32[]{:S(2)}, u32[]{:S(2)}) collective-permute-start(bf16[400,512]{1,0:T(8,128)(2,1)S(1)} %get-tuple-element.77), channel_id=1, source_target_pairs={{0,1},{1,0},{2,3},{3,2},{4,5},{5,4},{6,7},{7,6},{8,9},{9,8},{10,11... | collective-permute-start | bytes 1228808 | tf_op jit(solution)/shard_map/ppermute | solution.py:625
  108.4 36.1 %collective-permute-start.17 = (bf16[400,512]{1,0:T(8,128)(2,1)S(1)}, bf16[400,512]{1,0:T(8,128)(2,1)S(1)}, u32[]{:S(2)}, u32[]{:S(2)}) collective-permute-start(bf16[400,512]{1,0:T(8,128)(2,1)S(1)} %add_convert_fusion.1), channel_id=1, source_target_pairs={{0,4},{1,5},{2,6},{3,7},{4,0},{5,1},{6,2},{7,3},{8,12},{9,13},{10,... | collective-permute-start | bytes 1228808 | tf_op jit(solution)/shard_map/ppermute | solution.py:646
  109.1 14.4 %collective-permute-start.21 = (f32[16,400]{1,0:T(8,128)S(1)}, f32[16,400]{1,0:T(8,128)S(1)}, u32[]{:S(2)}, u32[]{:S(2)}) collective-permute-start(f32[16,400]{1,0:T(8,128)S(1)} %add.47), channel_id=1, source_target_pairs={{0,2},{1,3},{2,0},{3,1},{4,6},{5,7},{6,4},{7,5},{8,10},{9,11},{10,... | collective-permute-start | bytes 76808 | tf_op jit(solution)/shard_map/ppermute | solution.py:564
  112.5 16.8 %collective-permute-start.22 = (f32[16,400]{1,0:T(8,128)S(1)}, f32[16,400]{1,0:T(8,128)S(1)}, u32[]{:S(2)}, u32[]{:S(2)}) collective-permute-start(f32[16,400]{1,0:T(8,128)S(1)} %add.47), channel_id=1, source_target_pairs={{0,4},{1,5},{2,6},{3,7},{4,0},{5,1},{6,2},{7,3},{8,12},{9,13},{10,... | collective-permute-start | bytes 76808 | tf_op jit(solution)/shard_map/ppermute | solution.py:564
  113.1 19.6 %collective-permute-start.23 = (f32[16,400]{1,0:T(8,128)S(1)}, f32[16,400]{1,0:T(8,128)S(1)}, u32[]{:S(2)}, u32[]{:S(2)}) collective-permute-start(f32[16,400]{1,0:T(8,128)S(1)} %add.47), channel_id=1, source_target_pairs={{0,6},{1,7},{2,4},{3,5},{4,2},{5,3},{6,0},{7,1},{8,14},{9,15},{10,... | collective-permute-start | bytes 76808 | tf_op jit(solution)/shard_map/ppermute | solution.py:564
  123.5 25.0 %collective-permute-start.15 = (bf16[400,512]{1,0:T(8,128)(2,1)S(1)}, bf16[400,512]{1,0:T(8,128)(2,1)S(1)}, u32[]{:S(2)}, u32[]{:S(2)}) collective-permute-start(bf16[400,512]{1,0:T(8,128)(2,1)S(1)} %add_convert_fusion.2), channel_id=1, source_target_pairs={{0,2},{1,3},{2,0},{3,1},{4,6},{5,7},{6,4},{7,5},{8,10},{9,11},{10,... | collective-permute-start | bytes 1228808 | tf_op jit(solution)/shard_map/ppermute | solution.py:646
  132.8 11.0 %collective-permute-start.25 = (f32[16,400]{1,0:T(8,128)S(1)}, f32[16,400]{1,0:T(8,128)S(1)}, u32[]{:S(2)}, u32[]{:S(2)}) collective-permute-start(f32[16,400]{1,0:T(8,128)S(1)} %add_add_fusion), channel_id=1, source_target_pairs={{0,16},{8,24},{16,0},{24,8},{1,17},{9,25},{17,1},{25,9},{2,18},{10... | collective-permute-start | bytes 76808 | tf_op jit(solution)/shard_map/ppermute | solution.py:564
  134.6 9.2 %collective-permute-start.26 = (f32[16,400]{1,0:T(8,128)S(1)}, f32[16,400]{1,0:T(8,128)S(1)}, u32[]{:S(2)}, u32[]{:S(2)}) collective-permute-start(f32[16,400]{1,0:T(8,128)S(1)} %add_add_fusion), channel_id=1, source_target_pairs={{0,24},{8,16},{16,8},{24,0},{1,25},{9,17},{17,9},{25,1},{2,26},{10... | collective-permute-start | bytes 76808 | tf_op jit(solution)/shard_map/ppermute | solution.py:564
  136.8 18.8 %collective-permute-start.19 = (bf16[400,512]{1,0:T(8,128)(2,1)S(1)}, bf16[400,512]{1,0:T(8,128)(2,1)S(1)}, u32[]{:S(2)}, u32[]{:S(2)}) collective-permute-start(bf16[400,512]{1,0:T(8,128)(2,1)S(1)} %add_convert_fusion), channel_id=1, source_target_pairs={{0,6},{1,7},{2,4},{3,5},{4,2},{5,3},{6,0},{7,1},{8,14},{9,15},{10,... | collective-permute-start | bytes 1228808 | tf_op jit(solution)/shard_map/ppermute | solution.py:646
  (8 other events, 79.6 us)
